TPU v7x, 32 devices: a whole 2x2x4 slice. The times are simulated.
32 devices in a mesh: groups: 2 (over y), seq: 16 (over z, x, core).
Axes of the slice: x: 2, y: 2, z: 4, core: 2. Of those that a mesh axis runs over, the one named last changes fastest.
Arguments:
- queries: bfloat16 [4, 128, 128, 128], P('groups', 'seq'), parts along dimension 0, may hold values from -64 to 64
- new_k: bfloat16 [4, 128, 8, 128], P('groups', 'seq'), parts along dimension 0, may hold values from -15 to 15
- new_v: bfloat16 [4, 128, 8, 128], P('groups', 'seq'), parts along dimension 0, may hold values from -6 to 6
- cache_k: bfloat16 [4, 8192, 8, 128], P('groups', 'seq'), parts along dimension 0, may hold values from -12 to 12
- cache_v: bfloat16 [4, 8192, 8, 128], P('groups', 'seq'), parts along dimension 0, may hold values from -6 to 6
- cache_len: int32 [4], P('groups'), parts along dimension 0, may hold values from 2048 to 8192
Outputs:
- attended: bfloat16 [4, 128, 128, 128], P('groups', 'seq'), parts along dimension 0
There are 2 independent parts, one for each index of `groups`. A program takes and returns all parts, laid end to end along the dimension named above; each array names one. Nothing has to cross between parts.
Inputs may be any that keep to these rules, and one draw needn't show every extreme that they name: The first cache_len[r] of the 8192 cache slots of request r hold keys and values; the rest are to be ignored.
All inputs are finite; a program needn't handle non-finite values.
Results may differ from a plain program's by a relative error of at most 0.004.
Values may be sent and summed in bfloat16 or wider, within the bound.
No kernel may reach another device: no remote copies, remote signals or barrier semaphores. Data moves between devices by JAX's collectives and lax.ppermute only.
A program may use at most 128 MiB of HBM per device.

v0:
```python
import math

import jax
import jax.numpy as jnp
from jax import lax
from jax.sharding import PartitionSpec as P


def shards(queries, new_k, new_v, cache_k, cache_v, cache_len):
    requests, local_rows, heads, head_dim = queries.shape
    slots = cache_k.shape[1]
    kv_heads = cache_k.shape[2]
    group_size = heads // kv_heads
    devices_seq = lax.axis_size("seq")
    seq_index = lax.axis_index("seq")
    scaling = 1.0 / math.sqrt(head_dim)
    all_rows = local_rows * devices_seq
    spread = devices_seq // kv_heads
    piece = slots // spread
    part_id = seq_index % spread

    def to_heads(cache):
        moved = cache.reshape(requests, spread, piece, kv_heads, head_dim)
        return jnp.transpose(moved, (3, 1, 0, 2, 4)).reshape(devices_seq, requests, piece, head_dim)

    moved_k, moved_v = (
        lax.all_to_all(to_heads(cache_k), "seq", split_axis=0, concat_axis=0, tiled=True),
        lax.all_to_all(to_heads(cache_v), "seq", split_axis=0, concat_axis=0, tiled=True),
    )
    grouped = jnp.transpose(
        queries.reshape(requests, local_rows, kv_heads, group_size, head_dim), (2, 1, 0, 3, 4)
    )
    grouped = jnp.broadcast_to(
        grouped[:, None], (kv_heads, spread, local_rows, requests, group_size, head_dim)
    )
    grouped = grouped.reshape(devices_seq, local_rows, requests, group_size, head_dim)

    def head_spread(fresh):
        turned = jnp.transpose(fresh, (2, 1, 0, 3))
        turned = jnp.broadcast_to(
            turned[:, None], (kv_heads, spread, local_rows, requests, head_dim)
        )
        return turned.reshape(devices_seq, local_rows, requests, head_dim)

    head_q, head_k, head_v = (
        lax.all_to_all(grouped, "seq", split_axis=0, concat_axis=1, tiled=True),
        lax.all_to_all(head_spread(new_k), "seq", split_axis=0, concat_axis=1, tiled=True),
        lax.all_to_all(head_spread(new_v), "seq", split_axis=0, concat_axis=1, tiled=True),
    )
    head_q = head_q[0]
    head_k = head_k[0]
    head_v = head_v[0]
    slot_pos = (
        jnp.arange(devices_seq, dtype=jnp.int32)[:, None] * slots
        + part_id * piece
        + jnp.arange(piece, dtype=jnp.int32)[None, :]
    ).reshape(-1)
    head_valid = (slot_pos[None, :] < cache_len[:, None])[:, None, None, :]
    fresh_pos = jnp.arange(all_rows, dtype=jnp.int32)
    held_slots = devices_seq * piece
    block_rows = max((width for width in range(1, min(all_rows, 16) + 1) if all_rows % width == 0))

    def head_block(block, state):
        start = block * block_rows
        sub_rows = lax.dynamic_slice_in_dim(head_q, start, block_rows, 0)
        cache_scores = jnp.einsum(
            "prgd,srjd->rpgsj", sub_rows, moved_k, preferred_element_type=jnp.float32
        )
        cache_scores = cache_scores.reshape(requests, block_rows, group_size, held_slots) * scaling
        fresh_scores = (
            jnp.einsum("prgd,urd->rpgu", sub_rows, head_k, preferred_element_type=jnp.float32)
            * scaling
        )
        row_pos = start + jnp.arange(block_rows, dtype=jnp.int32)
        fresh_valid = ((fresh_pos[None, :] <= row_pos[:, None]) & (part_id == 0))[None, :, None, :]
        cache_scores = jnp.where(head_valid, cache_scores, -1e30)
        fresh_scores = jnp.where(fresh_valid, fresh_scores, -1e30)
        row_max = jnp.maximum(jnp.max(cache_scores, axis=-1), jnp.max(fresh_scores, axis=-1))
        cache_weights = jnp.where(head_valid, jnp.exp(cache_scores - row_max[..., None]), 0.0)
        fresh_weights = jnp.where(fresh_valid, jnp.exp(fresh_scores - row_max[..., None]), 0.0)
        row_sum = jnp.sum(cache_weights, axis=-1) + jnp.sum(fresh_weights, axis=-1)
        cache_weights = cache_weights.astype(jnp.bfloat16).reshape(
            requests, block_rows, group_size, devices_seq, piece
        )
        partial_value = jnp.einsum(
            "rpgsj,srjd->prgd", cache_weights, moved_v, preferred_element_type=jnp.float32
        )
        partial_value = partial_value + jnp.einsum(
            "rpgu,urd->prgd",
            fresh_weights.astype(jnp.bfloat16),
            head_v,
            preferred_element_type=jnp.float32,
        )
        results = (
            partial_value,
            jnp.transpose(row_max, (1, 0, 2)),
            jnp.transpose(row_sum, (1, 0, 2)),
        )
        return tuple(
            (
                lax.dynamic_update_slice_in_dim(whole, piece_out, start, 0)
                for whole, piece_out in zip(state, results)
            )
        )

    start_state = (
        jnp.zeros((all_rows, requests, group_size, head_dim), jnp.float32),
        jnp.full((all_rows, requests, group_size), -1e30, jnp.float32),
        jnp.zeros((all_rows, requests, group_size), jnp.float32),
    )
    partial_value, row_max, row_sum = lax.fori_loop(
        0, all_rows // block_rows, head_block, start_state
    )
    partial_value = partial_value.reshape(devices_seq, local_rows, requests, group_size, head_dim)
    row_max = row_max.reshape(devices_seq, local_rows, requests, group_size)
    row_sum = row_sum.reshape(devices_seq, local_rows, requests, group_size)
    partial_value, row_max, row_sum = (
        lax.all_to_all(partial_value, "seq", split_axis=0, concat_axis=0, tiled=True),
        lax.all_to_all(row_max, "seq", split_axis=0, concat_axis=0, tiled=True),
        lax.all_to_all(row_sum, "seq", split_axis=0, concat_axis=0, tiled=True),
    )
    partial_value = partial_value.reshape(
        kv_heads, spread, local_rows, requests, group_size, head_dim
    )
    row_max = row_max.reshape(kv_heads, spread, local_rows, requests, group_size)
    row_sum = row_sum.reshape(kv_heads, spread, local_rows, requests, group_size)
    global_max = jnp.max(row_max, axis=1)
    rescale = jnp.exp(row_max - global_max[:, None])
    numerator = jnp.sum(partial_value * rescale[..., None], axis=1)
    denominator = jnp.sum(row_sum * rescale, axis=1)
    merged = numerator / denominator[..., None]
    merged = jnp.transpose(merged, (2, 1, 0, 3, 4)).reshape(requests, local_rows, heads, head_dim)
    return merged.astype(jnp.bfloat16)


def solution(mesh):
    in_specs = (
        P("groups", "seq", None, None),
        P("groups", "seq", None, None),
        P("groups", "seq", None, None),
        P("groups", "seq", None, None),
        P("groups", "seq", None, None),
        P("groups"),
    )
    out_specs = P("groups", "seq", None, None)
    return jax.shard_map(shards, mesh=mesh, in_specs=in_specs, out_specs=out_specs, check_vma=False)
```

profile of v0, /device:TPU:11, one launch (start us, length us, event | category | flops | bytes accessed | tf_op | source)
XLA Modules:
  0.0 311.1 jit_solution(9602894458382184402)
XLA Ops:
  1.4 6.5 %all-to-all-start.4 = ((bf16[16,8,2,128]{3,1,2,0:T(8,128)(2,1)}), bf16[16,8,2,128]{3,1,2,0:T(8,128)(2,1)S(1)}, u32[]{:S(2)}, u32[]{:S(2)}) async-start(bf16[16,8,2,128]{3,1,2,0:T(8,128)(2,1)} %bitcast.14), calls=%async_computation.4 | async-start | bytes 131072 | tf_op jit(solution)/shard_map/all_to_all | solution.py:48
  8.7 3.5 %all-to-all-done.4 = bf16[16,8,2,128]{3,1,2,0:T(8,128)(2,1)S(1)} async-done(((bf16[16,8,2,128]{3,1,2,0:T(8,128)(2,1)}), bf16[16,8,2,128]{3,1,2,0:T(8,128)(2,1)S(1)}, u32[]{:S(2)}, u32[]{:S(2)}) %all-to-all-start.4) | async-done | bytes 65568 | tf_op jit(solution)/shard_map/all_to_all | solution.py:48
  12.8 6.0 %all-to-all-start.2 = ((bf16[16,8,2,128]{3,1,2,0:T(8,128)(2,1)}), bf16[16,8,2,128]{3,1,2,0:T(8,128)(2,1)S(1)}, u32[]{:S(2)}, u32[]{:S(2)}) async-start(bf16[16,8,2,128]{3,1,2,0:T(8,128)(2,1)} %bitcast.8), calls=%async_computation.2 | async-start | bytes 131072 | tf_op jit(solution)/shard_map/all_to_all | solution.py:47
  20.0 3.2 %all-to-all-done.2 = bf16[16,8,2,128]{3,1,2,0:T(8,128)(2,1)S(1)} async-done(((bf16[16,8,2,128]{3,1,2,0:T(8,128)(2,1)}), bf16[16,8,2,128]{3,1,2,0:T(8,128)(2,1)S(1)}, u32[]{:S(2)}, u32[]{:S(2)}) %all-to-all-start.2) | async-done | bytes 65568 | tf_op jit(solution)/shard_map/all_to_all | solution.py:47
  24.4 6.2 %all-to-all-start = ((bf16[16,8,2,16,128]{4,3,1,2,0:T(8,128)(2,1)}), bf16[16,8,2,16,128]{4,3,1,2,0:T(8,128)(2,1)S(1)}, u32[]{:S(2)}, u32[]{:S(2)}) async-start(bf16[16,8,2,16,128]{4,3,1,2,0:T(8,128)(2,1)} %bitcast.2), calls=%async_computation | async-start | bytes 2097152 | tf_op jit(solution)/shard_map/all_to_all | solution.py:46
  30.6 3.4 %copy.52 = bf16[2,2,256,8,128]{4,2,0,1,3:T(8,128)(2,1)} copy(bf16[2,2,256,8,128]{4,3,2,1,0:T(8,128)(2,1)} %bitcast.129) | data formatting | bytes 4194304 | tf_op jit(solution)/shard_map/reshape | solution.py:23
  34.0 21.5 %all-to-all-done = bf16[16,8,2,16,128]{4,3,1,2,0:T(8,128)(2,1)S(1)} async-done(((bf16[16,8,2,16,128]{4,3,1,2,0:T(8,128)(2,1)}), bf16[16,8,2,16,128]{4,3,1,2,0:T(8,128)(2,1)S(1)}, u32[]{:S(2)}, u32[]{:S(2)}) %all-to-all-start) | async-done | bytes 1048608 | tf_op jit(solution)/shard_map/all_to_all | solution.py:46
  55.5 4.8 %all-to-all-start.1 = ((bf16[16,2,256,128]{3,2,1,0:T(8,128)(2,1)}), bf16[16,2,256,128]{3,2,1,0:T(8,128)(2,1)S(1)}, u32[]{:S(2)}, u32[]{:S(2)}) async-start(bf16[16,2,256,128]{3,2,1,0:T(8,128)(2,1)} %bitcast.125), calls=%async_computation.1 | async-start | bytes 4194304 | tf_op jit(solution)/shard_map/all_to_all | solution.py:27
  60.3 3.4 %copy.55 = bf16[2,2,256,8,128]{4,2,0,1,3:T(8,128)(2,1)} copy(bf16[2,2,256,8,128]{4,3,2,1,0:T(8,128)(2,1)} %bitcast.130) | data formatting | bytes 4194304 | tf_op jit(solution)/shard_map/reshape | solution.py:23
  63.7 44.0 %all-to-all-done.1 = bf16[16,2,256,128]{3,2,1,0:T(8,128)(2,1)S(1)} async-done(((bf16[16,2,256,128]{3,2,1,0:T(8,128)(2,1)}), bf16[16,2,256,128]{3,2,1,0:T(8,128)(2,1)S(1)}, u32[]{:S(2)}, u32[]{:S(2)}) %all-to-all-start.1) | async-done | bytes 2097184 | tf_op jit(solution)/shard_map/all_to_all | solution.py:27
  109.1 4.8 %all-to-all-start.3 = ((bf16[16,2,256,128]{3,2,1,0:T(8,128)(2,1)}), bf16[16,2,256,128]{3,2,1,0:T(8,128)(2,1)}, u32[]{:S(2)}, u32[]{:S(2)}) async-start(bf16[16,2,256,128]{3,2,1,0:T(8,128)(2,1)} %bitcast.122), calls=%async_computation.3 | async-start | bytes 4194304 | tf_op jit(solution)/shard_map/all_to_all | solution.py:28
  115.6 45.8 %all-to-all-done.3 = bf16[16,2,256,128]{3,2,1,0:T(8,128)(2,1)} async-done(((bf16[16,2,256,128]{3,2,1,0:T(8,128)(2,1)}), bf16[16,2,256,128]{3,2,1,0:T(8,128)(2,1)}, u32[]{:S(2)}, u32[]{:S(2)}) %all-to-all-start.3) | async-done | bytes 2097184 | tf_op jit(solution)/shard_map/all_to_all | solution.py:28
  161.4 3.2 %copy.60 = bf16[16,2,256,128]{3,2,0,1:T(8,128)(2,1)} copy(bf16[16,2,256,128]{3,2,1,0:T(8,128)(2,1)} %all-to-all-done.3) | data formatting | bytes 4194304
  166.0 70.1 %while.20 = (s32[]{:T(128)}, f32[128,2,16,128]{3,2,0,1:T(8,128)}, f32[128,2,16]{2,0,1:T(8,128)S(1)}, f32[128,2,16]{2,0,1:T(8,128)S(1)}, bf16[128,2,16,128]{3,2,1...) while((s32[]{:T(128)}, f32[128,2,16,128]{3,2,0,1:T(8,128)}, ...), condition=%wide.region_5.6_spmd.clone, body=%wide.region_0.5_spmd.clone.sunk | while | flops 1135225856 | bytes 39920000 | solution.py:111
  168.6 2.5 fusion.66
  177.4 2.5 fusion.66
  186.2 2.5 fusion.66
  212.4 2.5 fusion.66
  236.8 4.8 %all-to-all-start.6 = ((f32[16,1,256]{2,1,0:T(1,128)}), f32[16,1,256]{2,1,0:T(1,128)S(1)}, u32[]{:S(2)}, u32[]{:S(2)}) async-start(f32[16,1,256]{2,1,0:T(1,128)} %reshape.224), calls=%async_computation.6 | async-start | bytes 32768 | tf_op jit(solution)/shard_map/all_to_all | solution.py:119
  242.3 3.4 %all-to-all-done.6 = f32[16,1,256]{2,1,0:T(1,128)S(1)} async-done(((f32[16,1,256]{2,1,0:T(1,128)}), f32[16,1,256]{2,1,0:T(1,128)S(1)}, u32[]{:S(2)}, u32[]{:S(2)}) %all-to-all-start.6) | async-done | bytes 16416 | tf_op jit(solution)/shard_map/all_to_all | solution.py:119
  245.7 5.8 %all-to-all-start.7 = ((f32[16,1,256]{2,1,0:T(1,128)}), f32[16,1,256]{2,1,0:T(1,128)S(1)}, u32[]{:S(2)}, u32[]{:S(2)}) async-start(f32[16,1,256]{2,1,0:T(1,128)} %reshape.226), calls=%async_computation.7 | async-start | bytes 32768 | tf_op jit(solution)/shard_map/all_to_all | solution.py:120
  251.5 3.2 %copy.62 = f32[16,8,2,16,128]{4,3,1,2,0:T(8,128)} copy(f32[16,8,2,16,128]{4,3,1,0,2:T(8,128)} %bitcast.124) | data formatting | bytes 4194304 | tf_op jit(solution)/shard_map/reshape | solution.py:114
  255.7 6.0 %all-to-all-start.5 = ((f32[16,8,2,16,128]{4,3,1,2,0:T(8,128)}), f32[16,8,2,16,128]{4,3,1,2,0:T(8,128)S(1)}, u32[]{:S(2)}, u32[]{:S(2)}) async-start(f32[16,8,2,16,128]{4,3,1,2,0:T(8,128)} %copy.62), calls=%async_computation.5 | async-start | bytes 4194304 | tf_op jit(solution)/shard_map/all_to_all | solution.py:118
  263.8 45.3 %all-to-all-done.5 = f32[16,8,2,16,128]{4,3,1,2,0:T(8,128)S(1)} async-done(((f32[16,8,2,16,128]{4,3,1,2,0:T(8,128)}), f32[16,8,2,16,128]{4,3,1,2,0:T(8,128)S(1)}, u32[]{:S(2)}, u32[]{:S(2)}) %all-to-all-start.5) | async-done | bytes 2097184 | tf_op jit(solution)/shard_map/all_to_all | solution.py:118
  (143 shorter events, 75.8 us)
Async XLA Ops:
  1.4 10.8 %all-to-all-start.4 = ((bf16[16,8,2,128]{3,1,2,0:T(8,128)(2,1)}), bf16[16,8,2,128]{3,1,2,0:T(8,128)(2,1)S(1)}, u32[]{:S(2)}, u32[]{:S(2)}) async-start(bf16[16,8,2,128]{3,1,2,0:T(8,128)(2,1)} %bitcast.14), calls=%async_computation.4 | async-start | bytes 131072 | tf_op jit(solution)/shard_map/all_to_all | solution.py:48
  12.8 10.4 %all-to-all-start.2 = ((bf16[16,8,2,128]{3,1,2,0:T(8,128)(2,1)}), bf16[16,8,2,128]{3,1,2,0:T(8,128)(2,1)S(1)}, u32[]{:S(2)}, u32[]{:S(2)}) async-start(bf16[16,8,2,128]{3,1,2,0:T(8,128)(2,1)} %bitcast.8), calls=%async_computation.2 | async-start | bytes 131072 | tf_op jit(solution)/shard_map/all_to_all | solution.py:47
  24.4 31.1 %all-to-all-start = ((bf16[16,8,2,16,128]{4,3,1,2,0:T(8,128)(2,1)}), bf16[16,8,2,16,128]{4,3,1,2,0:T(8,128)(2,1)S(1)}, u32[]{:S(2)}, u32[]{:S(2)}) async-start(bf16[16,8,2,16,128]{4,3,1,2,0:T(8,128)(2,1)} %bitcast.2), calls=%async_computation | async-start | bytes 2097152 | tf_op jit(solution)/shard_map/all_to_all | solution.py:46
  55.5 52.2 %all-to-all-start.1 = ((bf16[16,2,256,128]{3,2,1,0:T(8,128)(2,1)}), bf16[16,2,256,128]{3,2,1,0:T(8,128)(2,1)S(1)}, u32[]{:S(2)}, u32[]{:S(2)}) async-start(bf16[16,2,256,128]{3,2,1,0:T(8,128)(2,1)} %bitcast.125), calls=%async_computation.1 | async-start | bytes 4194304 | tf_op jit(solution)/shard_map/all_to_all | solution.py:27
  107.7 1.3 copy-start
  109.1 52.3 %all-to-all-start.3 = ((bf16[16,2,256,128]{3,2,1,0:T(8,128)(2,1)}), bf16[16,2,256,128]{3,2,1,0:T(8,128)(2,1)}, u32[]{:S(2)}, u32[]{:S(2)}) async-start(bf16[16,2,256,128]{3,2,1,0:T(8,128)(2,1)} %bitcast.122), calls=%async_computation.3 | async-start | bytes 4194304 | tf_op jit(solution)/shard_map/all_to_all | solution.py:28
  113.8 1.6 copy-start.1
  168.6 2.7 copy-start.2
  177.4 2.7 copy-start.2
  186.1 2.7 copy-start.2
  194.9 2.7 copy-start.2
  203.7 2.7 copy-start.2
  212.4 2.7 copy-start.2
  221.2 2.7 copy-start.2
  229.9 2.7 copy-start.2
  236.8 8.9 %all-to-all-start.6 = ((f32[16,1,256]{2,1,0:T(1,128)}), f32[16,1,256]{2,1,0:T(1,128)S(1)}, u32[]{:S(2)}, u32[]{:S(2)}) async-start(f32[16,1,256]{2,1,0:T(1,128)} %reshape.224), calls=%async_computation.6 | async-start | bytes 32768 | tf_op jit(solution)/shard_map/all_to_all | solution.py:119
  245.7 10.0 %all-to-all-start.7 = ((f32[16,1,256]{2,1,0:T(1,128)}), f32[16,1,256]{2,1,0:T(1,128)S(1)}, u32[]{:S(2)}, u32[]{:S(2)}) async-start(f32[16,1,256]{2,1,0:T(1,128)} %reshape.226), calls=%async_computation.7 | async-start | bytes 32768 | tf_op jit(solution)/shard_map/all_to_all | solution.py:120
  255.7 53.4 %all-to-all-start.5 = ((f32[16,8,2,16,128]{4,3,1,2,0:T(8,128)}), f32[16,8,2,16,128]{4,3,1,2,0:T(8,128)S(1)}, u32[]{:S(2)}, u32[]{:S(2)}) async-start(f32[16,8,2,16,128]{4,3,1,2,0:T(8,128)} %copy.62), calls=%async_computation.5 | async-start | bytes 4194304 | tf_op jit(solution)/shard_map/all_to_all | solution.py:118
where the time goes:
time: 312 us; the launch traced here: 311 us
  waiting for transfers between devices  168 us (54%)
  starting transfers between devices  44.9 us (14%)
  matrix products  41 us (13%)
  other arithmetic  31 us (10%)
  local copies, waits for them, and re-layouts  25.7 us (8%)
    all_to_all x1, waiting for transfers between devices, shards(): lax.all_to_all(to_heads(cache_v), 'seq', split_axis=0, concat_axis=0, til...  45.8 us
    all_to_all x1, waiting for transfers between devices, shards(): lax.all_to_all(partial_value, 'seq', split_axis=0, concat_axis=0, tiled=T...  45.3 us
    all_to_all x1, waiting for transfers between devices, shards(): lax.all_to_all(to_heads(cache_k), 'seq', split_axis=0, concat_axis=0, til...  44 us
    reduce_sum x16, other arithmetic, head_block(): row_sum = jnp.sum(cache_weights, axis=-1) + jnp.sum(fresh_weights, axis=-1)  21.7 us
    all_to_all x1, waiting for transfers between devices, shards(): lax.all_to_all(grouped, 'seq', split_axis=0, concat_axis=1, tiled=True)  21.5 us
    dot_general x8, matrix products, head_block(): jnp.einsum('rpgsj,srjd->prgd', cache_weights, moved_v, preferred_element_...  19.3 us
    dot_general x8, matrix products, head_block(): jnp.einsum('prgd,srjd->rpgsj', sub_rows, moved_k, preferred_element_type=...  11.5 us
    dot_general x8, matrix products, head_block(): jnp.einsum('rpgu,urd->prgd', fresh_weights.astype(jnp.bfloat16), head_v,...  7.78 us
  transfers between devices with their start and end apart: 8, of which 8 were waited for; matrix products, arithmetic and copies ran while one was open for 5% of the time, Pallas kernels for 0%

commit v1 on v0

v1 whole, which is shorter than its diff:
```python
import functools
import math

import jax
import jax.numpy as jnp
from jax import lax
from jax.experimental import pallas as pl
from jax.experimental.pallas import tpu as pltpu
from jax.sharding import PartitionSpec as P

NEG = -1e30
STAT_ROWS = 8
VMEM_BYTES = 58 * 2**20


def attend_kernel(
    info_ref, q_ref, k_ref, v_ref, fk_ref, fv_ref, out_ref, vals, fvals, s0, s1, m0, m1, *, chunk, tile, group_size
):
    sources, per_source, dim = q_ref.shape
    slots = k_ref.shape[0] * k_ref.shape[1]
    per_chunk = chunk // k_ref.shape[1]
    fresh = fk_ref.shape[0]
    rows = sources * per_source
    tiles = rows // tile
    span = tile // per_source
    scale = math.log2(math.e) / math.sqrt(dim)
    valid = info_ref[0]
    fresh_shift = info_ref[1]

    vals[:, :dim] = v_ref[...].reshape(slots, dim)
    vals[:, dim:] = jnp.ones((slots, dim), jnp.bfloat16)
    fvals[:, :dim] = fv_ref[...]
    fvals[:, dim:] = jnp.ones((fresh, dim), jnp.bfloat16)

    def product(a, b):
        return lax.dot_general(a, b, (((1,), (1,)), ((), ())), preferred_element_type=jnp.float32)

    def lane_max(scores, best):
        for lane in range(scores.shape[1] // dim):
            part = scores[:, lane * dim : (lane + 1) * dim]
            best = part if best is None else jnp.maximum(best, part)
        return best

    def score_chunk(t, j, count, s_ref, best):
        q = q_ref[pl.ds(t * span, span)].reshape(tile, dim)
        if j < count:
            keys = k_ref[j * per_chunk : (j + 1) * per_chunk].reshape(chunk, dim)
            scores = product(q, keys)
            if j == count - 1:
                pos = j * chunk + lax.broadcasted_iota(jnp.int32, (1, chunk), 1)
                scores = scores + jnp.where(pos < valid, 0.0, NEG)
            s_ref[:, j * chunk : (j + 1) * chunk] = scores
            return lane_max(scores, best)
        scores = product(q, fk_ref[...])
        token = (t * tile + lax.broadcasted_iota(jnp.int32, (tile, 1), 0)) // group_size
        unit = lax.broadcasted_iota(jnp.int32, (tile, fresh), 1)
        scores = jnp.where(unit <= token + fresh_shift, scores, NEG)
        s_ref[:, slots : slots + fresh] = scores
        return lane_max(scores, best)

    def value_chunk(j, count, s_ref, top, acc):
        if j < count:
            scores = s_ref[:, j * chunk : (j + 1) * chunk]
            values = vals[j * chunk : (j + 1) * chunk, :]
        else:
            scores = s_ref[:, slots : slots + fresh]
            values = fvals[...]
        weights = jnp.exp2((scores - top) * scale).astype(jnp.bfloat16)
        part = jnp.dot(weights, values, preferred_element_type=jnp.float32)
        return part if acc is None else acc + part

    def stage(t_next, s_next, m_next, t_now, s_now, m_now, count):
        best = None
        acc = None
        if t_now is not None:
            top = jnp.max(m_now[...], axis=1, keepdims=True)
        for j in range(count + 1):
            if t_next is not None:
                best = score_chunk(t_next, j, count, s_next, best)
            if t_now is not None:
                acc = value_chunk(j, count, s_now, top, acc)
        if t_next is not None:
            m_next[...] = best
        if t_now is not None:
            total = acc[:, dim:]
            out = (acc[:, :dim] / total).astype(jnp.bfloat16)
            out_ref[pl.ds(t_now * span, span), :per_source, :] = out.reshape(span, per_source, dim)
            level = top * scale + jnp.log2(total)
            for first in range(0, tile, dim):
                flat = jnp.transpose(level[first : first + dim, :])[:STAT_ROWS]
                high = flat.astype(jnp.bfloat16)
                rest = flat - high.astype(jnp.float32)
                mid = rest.astype(jnp.bfloat16)
                low = (rest - mid.astype(jnp.float32)).astype(jnp.bfloat16)
                which = lax.broadcasted_iota(jnp.int32, flat.shape, 0)
                stats = jnp.where(
                    which == 0,
                    high.astype(jnp.float32),
                    jnp.where(which == 1, mid.astype(jnp.float32), low.astype(jnp.float32)),
                ).astype(jnp.bfloat16)
                width = min(per_source, dim)
                for part in range(dim // width):
                    row = first + part * width
                    out_ref[
                        t_now * span + row // per_source, per_source:, :width
                    ] = stats[:, part * width : (part + 1) * width]

    for count in range(slots // chunk + 1):

        @pl.when((valid > (count - 1) * chunk) & (valid <= count * chunk))
        def _(count=count):
            stage(0, s0, m0, None, None, None, count)

            def pair(i, carry):
                stage(2 * i + 1, s1, m1, 2 * i, s0, m0, count)
                stage(jnp.minimum(2 * i + 2, tiles - 1), s0, m0, 2 * i + 1, s1, m1, count)
                return carry

            lax.fori_loop(0, tiles // 2, pair, 0)


def attend(request, info, head_q, keys, values, fresh_k, fresh_v, per_source, group_size):
    sources, _, dim = head_q.shape
    slots = keys.shape[0] * keys.shape[1]
    rows = sources * per_source
    fresh = fresh_k.shape[0]
    tile = min(256, rows // 2)
    chunk = min(1024, slots)

    def whole(array):
        return pl.BlockSpec(array.shape, lambda i, s: (0,) * array.ndim)

    return pl.pallas_call(
        functools.partial(attend_kernel, chunk=chunk, tile=tile, group_size=group_size),
        grid_spec=pltpu.PrefetchScalarGridSpec(
            num_scalar_prefetch=1,
            grid=(1,),
            in_specs=[
                pl.BlockSpec((sources, per_source, dim), lambda i, s: (0, request, 0)),
                whole(keys),
                whole(values),
                whole(fresh_k),
                whole(fresh_v),
            ],
            out_specs=pl.BlockSpec((sources, per_source + STAT_ROWS, dim), lambda i, s: (0, 0, 0)),
            scratch_shapes=[
                pltpu.VMEM((slots, 2 * dim), jnp.bfloat16),
                pltpu.VMEM((fresh, 2 * dim), jnp.bfloat16),
                pltpu.VMEM((tile, slots + fresh), jnp.float32),
                pltpu.VMEM((tile, slots + fresh), jnp.float32),
                pltpu.VMEM((tile, dim), jnp.float32),
                pltpu.VMEM((tile, dim), jnp.float32),
            ],
        ),
        out_shape=jax.ShapeDtypeStruct((sources, per_source + STAT_ROWS, dim), jnp.bfloat16),
        compiler_params=pltpu.CompilerParams(vmem_limit_bytes=VMEM_BYTES),
        cost_estimate=pl.CostEstimate(
            flops=4 * rows * slots * dim,
            bytes_accessed=4 * slots * dim + 4 * rows * dim,
            transcendentals=rows * slots,
        ),
    )(info, head_q, keys, values, fresh_k, fresh_v)


def merge_kernel(part_ref, out_ref, *, group_size):
    spread, heads, _, dim = part_ref.shape
    local_rows = out_ref.shape[0]
    per_source = local_rows * group_size
    for h in range(heads):
        levels = []
        for b in range(spread):
            stats = part_ref[b, h, per_source : per_source + STAT_ROWS, :].astype(jnp.float32)
            level = stats[0:1] + stats[1:2] + stats[2:3]
            levels.append(jnp.transpose(jnp.broadcast_to(level, (dim, dim)))[:per_source])
        top = functools.reduce(jnp.maximum, levels)
        weights = [jnp.exp2(level - top) for level in levels]
        total = functools.reduce(jnp.add, weights)
        mixed = functools.reduce(
            jnp.add,
            [w * part_ref[b, h, :per_source, :].astype(jnp.float32) for b, w in enumerate(weights)],
        )
        out = (mixed / total).astype(jnp.bfloat16)
        out_ref[:, h * group_size : (h + 1) * group_size, :] = out.reshape(local_rows, group_size, dim)


def merge(parts, local_rows, group_size):
    spread, heads, _, dim = parts.shape
    return pl.pallas_call(
        functools.partial(merge_kernel, group_size=group_size),
        out_shape=jax.ShapeDtypeStruct((local_rows, heads * group_size, dim), jnp.bfloat16),
        compiler_params=pltpu.CompilerParams(vmem_limit_bytes=VMEM_BYTES),
    )(parts)


def shards(queries, new_k, new_v, cache_k, cache_v, cache_len):
    requests, local_rows, heads, head_dim = queries.shape
    slots = cache_k.shape[1]
    kv_heads = cache_k.shape[2]
    group_size = heads // kv_heads
    devices_seq = lax.axis_size("seq")
    seq_index = lax.axis_index("seq")
    spread = devices_seq // kv_heads
    block = seq_index // kv_heads
    per_source = local_rows * group_size
    blocks = [[b * kv_heads + h for h in range(kv_heads)] for b in range(spread)]

    grouped = jnp.transpose(
        queries.reshape(requests, local_rows, kv_heads, group_size, head_dim), (2, 0, 1, 3, 4)
    ).reshape(kv_heads, requests * per_source, head_dim)
    fresh = jnp.transpose(jnp.stack([new_k, new_v]), (3, 0, 1, 2, 4)).reshape(
        kv_heads, 2 * requests * local_rows, head_dim
    )
    sent = jnp.concatenate([grouped, fresh], axis=1)
    sent = jnp.broadcast_to(sent[None], (spread,) + sent.shape).reshape((devices_seq,) + sent.shape[1:])
    head_q = lax.all_to_all(sent, "seq", split_axis=0, concat_axis=0, tiled=True)
    head_fresh = head_q[:, requests * per_source :, :].reshape(
        devices_seq, 2, requests, local_rows, head_dim
    )
    head_fresh = jnp.transpose(head_fresh, (1, 2, 0, 3, 4)).reshape(
        2, requests, devices_seq * local_rows, head_dim
    )

    def to_heads(cache):
        return lax.all_to_all(
            jnp.transpose(cache, (1, 0, 2)), "seq", split_axis=0, concat_axis=0, axis_index_groups=blocks, tiled=True
        )

    outs = []
    for r in range(requests):
        keys = to_heads(cache_k[r])
        values = to_heads(cache_v[r])
        held = kv_heads * slots
        valid = jnp.clip(cache_len[r] - block * held, 0, held)
        fresh_shift = jnp.where(block == spread - 1, 0, -devices_seq * local_rows)
        info = jnp.stack([valid, fresh_shift]).astype(jnp.int32)
        part = attend(r, info, head_q, keys, values, head_fresh[0, r], head_fresh[1, r], per_source, group_size)
        part = lax.all_to_all(part, "seq", split_axis=0, concat_axis=0, tiled=True)
        outs.append(merge(part.reshape(spread, kv_heads, per_source + STAT_ROWS, head_dim), local_rows, group_size))
    return jnp.stack(outs)


def solution(mesh):
    in_specs = (
        P("groups", "seq", None, None),
        P("groups", "seq", None, None),
        P("groups", "seq", None, None),
        P("groups", "seq", None, None),
        P("groups", "seq", None, None),
        P("groups"),
    )
    out_specs = P("groups", "seq", None, None)
    return jax.shard_map(shards, mesh=mesh, in_specs=in_specs, out_specs=out_specs, check_vma=False)
```

time: 312 us -> 161 us (0.52)
  the two profiles are of different devices: /device:TPU:11 before, /device:TPU:0 now
where the time goes in v1:
time: 161 us; the launch traced here: 159 us
  waiting for transfers between devices  75.7 us (47%)
  Pallas kernels  34.3 us (21%)
  starting transfers between devices  33.1 us (21%)
  local copies, waits for them, and re-layouts  11.5 us (7%)
  other arithmetic  3.14 us (2%)
    all_to_all x4, waiting for transfers between devices, to_heads(): lax.all_to_all(jnp.transpose(cache, (1, 0, 2)), 'seq', split_axis=0, conc...  39.2 us
    pallas_call x2, Pallas kernels, attend(): pl.pallas_call(functools.partial(attend_kernel, chunk=chunk, tile=tile, g...  30 us
    all_to_all x1, waiting for transfers between devices, shards(): lax.all_to_all(sent, 'seq', split_axis=0, concat_axis=0, tiled=True)  23.8 us
    all_to_all x4, starting transfers between devices, to_heads(): lax.all_to_all(jnp.transpose(cache, (1, 0, 2)), 'seq', split_axis=0, conc...  19.7 us
    all_to_all x2, waiting for transfers between devices, shards(): part = lax.all_to_all(part, 'seq', split_axis=0, concat_axis=0, tiled=True)  12.7 us
    all_to_all x2, starting transfers between devices, shards(): part = lax.all_to_all(part, 'seq', split_axis=0, concat_axis=0, tiled=True)  8.51 us
    unnamed x24, local copies, waits for them, and re-layouts  5.52 us
    all_to_all x1, starting transfers between devices, shards(): lax.all_to_all(sent, 'seq', split_axis=0, concat_axis=0, tiled=True)  4.88 us
  transfers between devices with their start and end apart: 7, of which 5 were waited for; matrix products, arithmetic and copies ran while one was open for 5% of the time, Pallas kernels for 20%

profile of v1, /device:TPU:0, one launch (start us, length us, event | category | flops | bytes accessed | tf_op | source)
XLA Modules:
  0.0 159.2 jit_solution(12222365259954477437)
XLA Ops:
  0.0 1.7 %fusion.1 = (bf16[1,512,8,128]{3,2,1,0:T(8,128)(2,1)S(1)}, bf16[1,512,8,128]{3,2,1,0:T(8,128)(2,1)S(1)}) fusion(bf16[2,512,8,128]{3,2,1,0:T(8,128)(2,1)} %param.9), kind=kLoop, calls=%fused_computation.15 | loop fusion | bytes 4194304 | tf_op jit(solution)/shard_map/slice | solution.py:230
  1.7 1.1 copy.36
  2.8 5.3 %all-to-all-start.4 = ((bf16[8,512,128]{2,1,0:T(8,128)(2,1)}), bf16[8,512,128]{2,1,0:T(8,128)(2,1)S(1)}, u32[]{:S(2)}, u32[]{:S(2)}) async-start(bf16[8,512,128]{2,1,0:T(8,128)(2,1)} %bitcast.49), calls=%async_computation.4 | async-start | bytes 2097152 | tf_op jit(solution)/shard_map/all_to_all | solution.py:224
  8.1 1.7 %fusion = (bf16[1,512,8,128]{3,2,1,0:T(8,128)(2,1)S(1)}, bf16[1,512,8,128]{3,2,1,0:T(8,128)(2,1)S(1)}) fusion(bf16[2,512,8,128]{3,2,1,0:T(8,128)(2,1)} %param.10), kind=kLoop, calls=%fused_computation.14 | loop fusion | bytes 4194304 | tf_op jit(solution)/shard_map/slice | solution.py:231
  9.7 1.2 copy.35
  10.9 11.6 %all-to-all-done.4.k_ref = bf16[8,512,128]{2,1,0:T(8,128)(2,1)S(1)} async-done(((bf16[8,512,128]{2,1,0:T(8,128)(2,1)}), bf16[8,512,128]{2,1,0:T(8,128)(2,1)S(1)}, u32[]{:S(2)}, u32[]{:S(2)}) %all-to-all-start.4) | async-done | bytes 1048608 | tf_op jit(solution)/shard_map/all_to_all | solution.py:224
  22.5 4.2 %all-to-all-start.5 = ((bf16[8,512,128]{2,1,0:T(8,128)(2,1)}), bf16[8,512,128]{2,1,0:T(8,128)(2,1)}, u32[]{:S(2)}, u32[]{:S(2)}) async-start(bf16[8,512,128]{2,1,0:T(8,128)(2,1)} %bitcast.48), calls=%async_computation.5 | async-start | bytes 2097152 | tf_op jit(solution)/shard_map/all_to_all | solution.py:224
  26.8 1.1 copy.38
  27.9 13.4 %all-to-all-done.5.v_ref = bf16[8,512,128]{2,1,0:T(8,128)(2,1)} async-done(((bf16[8,512,128]{2,1,0:T(8,128)(2,1)}), bf16[8,512,128]{2,1,0:T(8,128)(2,1)}, u32[]{:S(2)}, u32[]{:S(2)}) %all-to-all-start.5) | async-done | bytes 1048608 | tf_op jit(solution)/shard_map/all_to_all | solution.py:224
  41.3 3.7 %all-to-all-start.1 = ((bf16[8,512,128]{2,1,0:T(8,128)(2,1)}), bf16[8,512,128]{2,1,0:T(8,128)(2,1)S(1)}, u32[]{:S(2)}, u32[]{:S(2)}) async-start(bf16[8,512,128]{2,1,0:T(8,128)(2,1)} %bitcast.51), calls=%async_computation.1 | async-start | bytes 2097152 | tf_op jit(solution)/shard_map/all_to_all | solution.py:224
  45.1 14.2 %all-to-all-done.1.k_ref = bf16[8,512,128]{2,1,0:T(8,128)(2,1)S(1)} async-done(((bf16[8,512,128]{2,1,0:T(8,128)(2,1)}), bf16[8,512,128]{2,1,0:T(8,128)(2,1)S(1)}, u32[]{:S(2)}, u32[]{:S(2)}) %all-to-all-start.1) | async-done | bytes 1048608 | tf_op jit(solution)/shard_map/all_to_all | solution.py:224
  59.4 1.3 broadcast_in_dim.2
  60.7 4.9 %all-to-all-start = ((bf16[16,288,128]{2,1,0:T(8,128)(2,1)}), bf16[16,288,128]{2,1,0:T(8,128)(2,1)S(1)}, u32[]{:S(2)}, u32[]{:S(2)}) async-start(bf16[16,288,128]{2,1,0:T(8,128)(2,1)} %bitcast.10), calls=%async_computation | async-start | bytes 2359296 | tf_op jit(solution)/shard_map/all_to_all | solution.py:215
  65.6 1.2 copy.37
  66.8 23.8 %all-to-all-done.q_ref = bf16[16,288,128]{2,1,0:T(8,128)(2,1)S(1)} async-done(((bf16[16,288,128]{2,1,0:T(8,128)(2,1)}), bf16[16,288,128]{2,1,0:T(8,128)(2,1)S(1)}, u32[]{:S(2)}, u32[]{:S(2)}) %all-to-all-start) | async-done | bytes 1179680 | tf_op jit(solution)/shard_map/all_to_all | solution.py:215
  90.6 6.5 %all-to-all-start.2 = ((bf16[8,512,128]{2,1,0:T(8,128)(2,1)}), bf16[8,512,128]{2,1,0:T(8,128)(2,1)S(1)}, u32[]{:S(2)}, u32[]{:S(2)}) async-start(bf16[8,512,128]{2,1,0:T(8,128)(2,1)} %bitcast.50), calls=%async_computation.2 | async-start | bytes 2097152 | tf_op jit(solution)/shard_map/all_to_all | solution.py:224
  99.8 15.0 %shard_map.66 = bf16[16,136,128]{2,1,0:T(8,128)(2,1)} custom-call(s32[2]{0:T(128)} %pad_add_fusion.1.info_ref, bf16[16,288,128]{2,1,0:T(8,128)(2,1)} %copy-done.2, bf16[8,512,128]{2,1,0:T(8,128)(2,1)} %copy-done.4, bf16[8,512,128]{2,1,0:T(8,128)(2,1)} %all-to-all-done.5.v_ref, bf16[128,128]{1,0:T(8,128)(2,1)} %get-tuple-element.11.fk_ref, ...), custom_call_target="tpu_custom_call" | custom-call | flops 4294967296 | bytes 3145728 | tf_op jit(solution)/shard_map/pallas_call | solution.py:133
  114.8 4.3 %all-to-all-start.6 = ((bf16[16,136,128]{2,1,0:T(8,128)(2,1)}), bf16[16,136,128]{2,1,0:T(8,128)(2,1)S(1)}, u32[]{:S(2)}, u32[]{:S(2)}) async-start(bf16[16,136,128]{2,1,0:T(8,128)(2,1)} %shard_map.66), calls=%async_computation.6 | async-start | bytes 1114112 | tf_op jit(solution)/shard_map/all_to_all | solution.py:237
  120.3 15.0 %shard_map.64 = bf16[16,136,128]{2,1,0:T(8,128)(2,1)} custom-call(s32[2]{0:T(128)} %pad_add_fusion.info_ref, bf16[16,288,128]{2,1,0:T(8,128)(2,1)} %copy-done.2, bf16[8,512,128]{2,1,0:T(8,128)(2,1)} %copy-done.3, bf16[8,512,128]{2,1,0:T(8,128)(2,1)} %copy-done.5, bf16[128,128]{1,0:T(8,128)(2,1)} %get-tuple-element.12.fk_ref, ...), custom_call_target="tpu_custom_call" | custom-call | flops 4294967296 | bytes 3145728 | tf_op jit(solution)/shard_map/pallas_call | solution.py:133
  135.3 4.2 %all-to-all-start.3 = ((bf16[16,136,128]{2,1,0:T(8,128)(2,1)}), bf16[16,136,128]{2,1,0:T(8,128)(2,1)S(1)}, u32[]{:S(2)}, u32[]{:S(2)}) async-start(bf16[16,136,128]{2,1,0:T(8,128)(2,1)} %shard_map.64), calls=%async_computation.3 | async-start | bytes 1114112 | tf_op jit(solution)/shard_map/all_to_all | solution.py:237
  139.6 2.1 %shard_map.67 = bf16[8,128,128]{2,1,0:T(8,128)(2,1)} custom-call(bf16[2,8,136,128]{3,2,1,0:T(8,128)(2,1)} %bitcast.53), custom_call_target="tpu_custom_call" | custom-call | tf_op jit(solution)/shard_map/pallas_call | solution.py:188
  141.7 12.7 %all-to-all-done.3 = bf16[16,136,128]{2,1,0:T(8,128)(2,1)S(1)} async-done(((bf16[16,136,128]{2,1,0:T(8,128)(2,1)}), bf16[16,136,128]{2,1,0:T(8,128)(2,1)S(1)}, u32[]{:S(2)}, u32[]{:S(2)}) %all-to-all-start.3) | async-done | bytes 557088 | tf_op jit(solution)/shard_map/all_to_all | solution.py:237
  155.2 2.1 %shard_map.65 = bf16[8,128,128]{2,1,0:T(8,128)(2,1)} custom-call(bf16[2,8,136,128]{3,2,1,0:T(8,128)(2,1)} %bitcast.54), custom_call_target="tpu_custom_call" | custom-call | tf_op jit(solution)/shard_map/pallas_call | solution.py:188
  157.3 1.9 %pad_maximum_fusion.1 = bf16[2,8,128,128]{3,2,1,0:T(8,128)(2,1)} fusion(bf16[1,8,128,128]{3,2,1,0:T(8,128)(2,1)} %bitcast.56, bf16[1,8,128,128]{3,2,1,0:T(8,128)(2,1)} %bitcast.57), kind=kLoop, calls=%fused_computation.5 | loop fusion | flops 262144 | bytes 1048576 | tf_op jit(solution)/shard_map/stack | solution.py:239
  (32 shorter events, 3.5 us)
Async XLA Ops:
  2.8 19.7 %all-to-all-start.4 = ((bf16[8,512,128]{2,1,0:T(8,128)(2,1)}), bf16[8,512,128]{2,1,0:T(8,128)(2,1)S(1)}, u32[]{:S(2)}, u32[]{:S(2)}) async-start(bf16[8,512,128]{2,1,0:T(8,128)(2,1)} %bitcast.49), calls=%async_computation.4 | async-start | bytes 2097152 | tf_op jit(solution)/shard_map/all_to_all | solution.py:224
  22.5 5.4 %copy-start.4 = (bf16[8,512,128]{2,1,0:T(8,128)(2,1)}, bf16[8,512,128]{2,1,0:T(8,128)(2,1)S(1)}, u32[]{:S(2)}) copy-start(bf16[8,512,128]{2,1,0:T(8,128)(2,1)S(1)} %all-to-all-done.4.k_ref) | copy-start | bytes 3145732
  22.5 18.7 %all-to-all-start.5 = ((bf16[8,512,128]{2,1,0:T(8,128)(2,1)}), bf16[8,512,128]{2,1,0:T(8,128)(2,1)}, u32[]{:S(2)}, u32[]{:S(2)}) async-start(bf16[8,512,128]{2,1,0:T(8,128)(2,1)} %bitcast.48), calls=%async_computation.5 | async-start | bytes 2097152 | tf_op jit(solution)/shard_map/all_to_all | solution.py:224
  27.9 17.1 %copy-start.7 = (bf16[2,8,8,128]{3,2,1,0:T(8,128)(2,1)S(1)}, bf16[2,8,8,128]{3,2,1,0:T(8,128)(2,1)}, u32[]{:S(2)}) copy-start(bf16[2,8,8,128]{3,2,1,0:T(8,128)(2,1)} %param.8) | copy-start | bytes 98308
  27.9 17.1 %copy-start.8 = (bf16[2,8,8,128]{3,2,1,0:T(8,128)(2,1)S(1)}, bf16[2,8,8,128]{3,2,1,0:T(8,128)(2,1)}, u32[]{:S(2)}) copy-start(bf16[2,8,8,128]{3,2,1,0:T(8,128)(2,1)} %param.7) | copy-start | bytes 98308
  41.2 3.8 %copy-start.6 = (bf16[2,8,128,128]{3,2,1,0:T(8,128)(2,1)S(1)}, bf16[2,8,128,128]{3,2,1,0:T(8,128)(2,1)}, u32[]{:S(2)}) copy-start(bf16[2,8,128,128]{3,2,1,0:T(8,128)(2,1)} %param.6) | copy-start | bytes 1572868
  41.3 18.1 %all-to-all-start.1 = ((bf16[8,512,128]{2,1,0:T(8,128)(2,1)}), bf16[8,512,128]{2,1,0:T(8,128)(2,1)S(1)}, u32[]{:S(2)}, u32[]{:S(2)}) async-start(bf16[8,512,128]{2,1,0:T(8,128)(2,1)} %bitcast.51), calls=%async_computation.1 | async-start | bytes 2097152 | tf_op jit(solution)/shard_map/all_to_all | solution.py:224
  59.3 1.4 copy-start.3
  60.7 29.9 %all-to-all-start = ((bf16[16,288,128]{2,1,0:T(8,128)(2,1)}), bf16[16,288,128]{2,1,0:T(8,128)(2,1)S(1)}, u32[]{:S(2)}, u32[]{:S(2)}) async-start(bf16[16,288,128]{2,1,0:T(8,128)(2,1)} %bitcast.10), calls=%async_computation | async-start | bytes 2359296 | tf_op jit(solution)/shard_map/all_to_all | solution.py:215
  66.8 30.4 %copy-start.9 = (s32[2]{0:T(128)S(1)}, s32[2]{0:T(128)}, u32[]{:S(2)}) copy-start(s32[2]{0:T(128)} %param.11) | copy-start | bytes 28
  90.6 8.5 %copy-start.2 = (bf16[16,288,128]{2,1,0:T(8,128)(2,1)}, bf16[16,288,128]{2,1,0:T(8,128)(2,1)S(1)}, u32[]{:S(2)}) copy-start(bf16[16,288,128]{2,1,0:T(8,128)(2,1)S(1)} %all-to-all-done.q_ref) | copy-start | bytes 3538948
  90.6 24.1 %all-to-all-start.2 = ((bf16[8,512,128]{2,1,0:T(8,128)(2,1)}), bf16[8,512,128]{2,1,0:T(8,128)(2,1)S(1)}, u32[]{:S(2)}, u32[]{:S(2)}) async-start(bf16[8,512,128]{2,1,0:T(8,128)(2,1)} %bitcast.50), calls=%async_computation.2 | async-start | bytes 2097152 | tf_op jit(solution)/shard_map/all_to_all | solution.py:224
  114.8 5.5 %copy-start.5 = (bf16[8,512,128]{2,1,0:T(8,128)(2,1)}, bf16[8,512,128]{2,1,0:T(8,128)(2,1)S(1)}, u32[]{:S(2)}) copy-start(bf16[8,512,128]{2,1,0:T(8,128)(2,1)S(1)} %all-to-all-done.2.v_ref) | copy-start | bytes 3145732
  114.8 20.5 %all-to-all-start.6 = ((bf16[16,136,128]{2,1,0:T(8,128)(2,1)}), bf16[16,136,128]{2,1,0:T(8,128)(2,1)S(1)}, u32[]{:S(2)}, u32[]{:S(2)}) async-start(bf16[16,136,128]{2,1,0:T(8,128)(2,1)} %shard_map.66), calls=%async_computation.6 | async-start | bytes 1114112 | tf_op jit(solution)/shard_map/all_to_all | solution.py:237
  135.3 4.2 %copy-start = (bf16[16,136,128]{2,1,0:T(8,128)(2,1)}, bf16[16,136,128]{2,1,0:T(8,128)(2,1)S(1)}, u32[]{:S(2)}) copy-start(bf16[16,136,128]{2,1,0:T(8,128)(2,1)S(1)} %all-to-all-done.6) | copy-start | bytes 1671172
  135.3 19.0 %all-to-all-start.3 = ((bf16[16,136,128]{2,1,0:T(8,128)(2,1)}), bf16[16,136,128]{2,1,0:T(8,128)(2,1)S(1)}, u32[]{:S(2)}, u32[]{:S(2)}) async-start(bf16[16,136,128]{2,1,0:T(8,128)(2,1)} %shard_map.64), calls=%async_computation.3 | async-start | bytes 1114112 | tf_op jit(solution)/shard_map/all_to_all | solution.py:237
  154.4 0.8 copy-start.1

commit v2 on v1

--- a/solution.py
+++ b/solution.py
@@ -14,23 +14,28 @@
 
 
 def attend_kernel(
-    info_ref, q_ref, k_ref, v_ref, fk_ref, fv_ref, out_ref, vals, fvals, s0, s1, m0, m1, *, chunk, tile, group_size
+    info_ref, q_ref, kv_ref, fk_ref, fv_ref, out_ref, vals, fvals, s0, s1, m0, m1, *, chunk, tile, group_size
 ):
     sources, per_source, dim = q_ref.shape
-    slots = k_ref.shape[0] * k_ref.shape[1]
-    per_chunk = chunk // k_ref.shape[1]
+    slots = kv_ref.shape[0] * kv_ref.shape[2]
+    per_chunk = chunk // kv_ref.shape[2]
     fresh = fk_ref.shape[0]
+    local_rows = per_source // group_size
     rows = sources * per_source
     tiles = rows // tile
     span = tile // per_source
     scale = math.log2(math.e) / math.sqrt(dim)
     valid = info_ref[0]
     fresh_shift = info_ref[1]
-
-    vals[:, :dim] = v_ref[...].reshape(slots, dim)
+    me = info_ref[2]
+
+    vals[:, :dim] = kv_ref[:, 1].reshape(slots, dim)
     vals[:, dim:] = jnp.ones((slots, dim), jnp.bfloat16)
     fvals[:, :dim] = fv_ref[...]
     fvals[:, dim:] = jnp.ones((fresh, dim), jnp.bfloat16)
+
+    def position(order):
+        return ((order // local_rows) ^ me) * local_rows + order % local_rows
 
     def product(a, b):
         return lax.dot_general(a, b, (((1,), (1,)), ((), ())), preferred_element_type=jnp.float32)
@@ -44,7 +49,7 @@
     def score_chunk(t, j, count, s_ref, best):
         q = q_ref[pl.ds(t * span, span)].reshape(tile, dim)
         if j < count:
-            keys = k_ref[j * per_chunk : (j + 1) * per_chunk].reshape(chunk, dim)
+            keys = kv_ref[j * per_chunk : (j + 1) * per_chunk, 0].reshape(chunk, dim)
             scores = product(q, keys)
             if j == count - 1:
                 pos = j * chunk + lax.broadcasted_iota(jnp.int32, (1, chunk), 1)
@@ -52,8 +57,8 @@
             s_ref[:, j * chunk : (j + 1) * chunk] = scores
             return lane_max(scores, best)
         scores = product(q, fk_ref[...])
-        token = (t * tile + lax.broadcasted_iota(jnp.int32, (tile, 1), 0)) // group_size
-        unit = lax.broadcasted_iota(jnp.int32, (tile, fresh), 1)
+        token = position((t * tile + lax.broadcasted_iota(jnp.int32, (tile, 1), 0)) // group_size)
+        unit = position(lax.broadcasted_iota(jnp.int32, (1, fresh), 1))
         scores = jnp.where(unit <= token + fresh_shift, scores, NEG)
         s_ref[:, slots : slots + fresh] = scores
         return lane_max(scores, best)
@@ -84,7 +89,10 @@
         if t_now is not None:
             total = acc[:, dim:]
             out = (acc[:, :dim] / total).astype(jnp.bfloat16)
-            out_ref[pl.ds(t_now * span, span), :per_source, :] = out.reshape(span, per_source, dim)
+            for part in range(span):
+                out_ref[(t_now * span + part) ^ me, :per_source, :] = out[
+                    part * per_source : (part + 1) * per_source
+                ]
             level = top * scale + jnp.log2(total)
             for first in range(0, tile, dim):
                 flat = jnp.transpose(level[first : first + dim, :])[:STAT_ROWS]
@@ -101,9 +109,9 @@
                 width = min(per_source, dim)
                 for part in range(dim // width):
                     row = first + part * width
-                    out_ref[
-                        t_now * span + row // per_source, per_source:, :width
-                    ] = stats[:, part * width : (part + 1) * width]
+                    out_ref[(t_now * span + row // per_source) ^ me, per_source:, :width] = stats[
+                        :, part * width : (part + 1) * width
+                    ]
 
     for count in range(slots // chunk + 1):
 
@@ -119,9 +127,9 @@
             lax.fori_loop(0, tiles // 2, pair, 0)
 
 
-def attend(request, info, head_q, keys, values, fresh_k, fresh_v, per_source, group_size):
+def attend(request, info, head_q, keys_values, fresh_k, fresh_v, per_source, group_size):
     sources, _, dim = head_q.shape
-    slots = keys.shape[0] * keys.shape[1]
+    slots = keys_values.shape[0] * keys_values.shape[2]
     rows = sources * per_source
     fresh = fresh_k.shape[0]
     tile = min(256, rows // 2)
@@ -137,8 +145,7 @@
             grid=(1,),
             in_specs=[
                 pl.BlockSpec((sources, per_source, dim), lambda i, s: (0, request, 0)),
-                whole(keys),
-                whole(values),
+                whole(keys_values),
                 whole(fresh_k),
                 whole(fresh_v),
             ],
@@ -159,12 +166,13 @@
             bytes_accessed=4 * slots * dim + 4 * rows * dim,
             transcendentals=rows * slots,
         ),
-    )(info, head_q, keys, values, fresh_k, fresh_v)
-
-
-def merge_kernel(part_ref, out_ref, *, group_size):
+    )(info, head_q, keys_values, fresh_k, fresh_v)
+
+
+def merge_kernel(part_ref, *refs, group_size):
+    out_ref = refs[-1]
     spread, heads, _, dim = part_ref.shape
-    local_rows = out_ref.shape[0]
+    local_rows = out_ref.shape[1]
     per_source = local_rows * group_size
     for h in range(heads):
         levels = []
@@ -180,16 +188,48 @@
             [w * part_ref[b, h, :per_source, :].astype(jnp.float32) for b, w in enumerate(weights)],
         )
         out = (mixed / total).astype(jnp.bfloat16)
-        out_ref[:, h * group_size : (h + 1) * group_size, :] = out.reshape(local_rows, group_size, dim)
-
-
-def merge(parts, local_rows, group_size):
-    spread, heads, _, dim = parts.shape
+        out_ref[0, :, h * group_size : (h + 1) * group_size, :] = out.reshape(local_rows, group_size, dim)
+
+
+def merge(parts, request, requests, local_rows, group_size, earlier):
+    heads, dim = parts.shape[1], parts.shape[3]
+    rest = [] if earlier is None else [earlier]
     return pl.pallas_call(
         functools.partial(merge_kernel, group_size=group_size),
-        out_shape=jax.ShapeDtypeStruct((local_rows, heads * group_size, dim), jnp.bfloat16),
+        grid=(1,),
+        in_specs=[pl.BlockSpec(parts.shape, lambda i: (0, 0, 0, 0))]
+        + [pl.BlockSpec(memory_space=pl.ANY) for _ in rest],
+        out_specs=pl.BlockSpec((1, local_rows, heads * group_size, dim), lambda i: (request, 0, 0, 0)),
+        out_shape=jax.ShapeDtypeStruct((requests, local_rows, heads * group_size, dim), jnp.bfloat16),
+        input_output_aliases={1: 0} if rest else {},
         compiler_params=pltpu.CompilerParams(vmem_limit_bytes=VMEM_BYTES),
-    )(parts)
+    )(parts, *rest)
+
+
+def pack_kernel(me_ref, q_ref, fresh_ref, out_ref):
+    requests, local_rows, group_size, dim = q_ref.shape
+    rows = requests * local_rows * group_size
+    out_ref[0, :rows, :] = q_ref[...].reshape(rows, dim)
+    out_ref[0, rows:, :] = fresh_ref[0]
+
+
+def pack(queries, fresh, me, kv_heads):
+    requests, local_rows, heads, dim = queries.shape
+    group_size = heads // kv_heads
+    rows = requests * local_rows * group_size + fresh.shape[1]
+    return pl.pallas_call(
+        pack_kernel,
+        grid_spec=pltpu.PrefetchScalarGridSpec(
+            num_scalar_prefetch=1,
+            grid=(kv_heads,),
+            in_specs=[
+                pl.BlockSpec((requests, local_rows, group_size, dim), lambda d, me: (0, 0, d ^ me[0], 0)),
+                pl.BlockSpec((1,) + fresh.shape[1:], lambda d, me: (d ^ me[0], 0, 0)),
+            ],
+            out_specs=pl.BlockSpec((1, rows, dim), lambda d, me: (d, 0, 0)),
+        ),
+        out_shape=jax.ShapeDtypeStruct((kv_heads, rows, dim), jnp.bfloat16),
+    )(me, queries, fresh)
 
 
 def shards(queries, new_k, new_v, cache_k, cache_v, cache_len):
@@ -204,15 +244,25 @@
     per_source = local_rows * group_size
     blocks = [[b * kv_heads + h for h in range(kv_heads)] for b in range(spread)]
 
-    grouped = jnp.transpose(
-        queries.reshape(requests, local_rows, kv_heads, group_size, head_dim), (2, 0, 1, 3, 4)
-    ).reshape(kv_heads, requests * per_source, head_dim)
+    def partner(bit):
+        return [(i, i ^ bit) for i in range(devices_seq)]
+
     fresh = jnp.transpose(jnp.stack([new_k, new_v]), (3, 0, 1, 2, 4)).reshape(
         kv_heads, 2 * requests * local_rows, head_dim
     )
-    sent = jnp.concatenate([grouped, fresh], axis=1)
-    sent = jnp.broadcast_to(sent[None], (spread,) + sent.shape).reshape((devices_seq,) + sent.shape[1:])
-    head_q = lax.all_to_all(sent, "seq", split_axis=0, concat_axis=0, tiled=True)
+    own_head = (seq_index % kv_heads).astype(jnp.int32)[None]
+    head_q = pack(queries, fresh, own_head, kv_heads)[None]
+    bit = 1
+    while bit < kv_heads:
+        halves = head_q.reshape((head_q.shape[0], -1, 2) + head_q.shape[2:])
+        received = lax.ppermute(halves[:, :, 1], "seq", partner(bit))
+        head_q = jnp.concatenate([halves[:, :, 0], received], axis=0)
+        bit *= 2
+    head_q = head_q[:, 0]
+    in_block = head_q
+    while bit < devices_seq:
+        head_q = jnp.concatenate([head_q, lax.ppermute(head_q, "seq", partner(bit))], axis=0)
+        bit *= 2
     head_fresh = head_q[:, requests * per_source :, :].reshape(
         devices_seq, 2, requests, local_rows, head_dim
     )
@@ -220,23 +270,23 @@
         2, requests, devices_seq * local_rows, head_dim
     )
 
-    def to_heads(cache):
-        return lax.all_to_all(
-            jnp.transpose(cache, (1, 0, 2)), "seq", split_axis=0, concat_axis=0, axis_index_groups=blocks, tiled=True
+    out = None
+    for r in range(requests):
+        keys_values = jnp.transpose(jnp.stack([cache_k[r], cache_v[r]]), (2, 0, 1, 3))
+        if r > 0:
+            keys_values, _ = lax.optimization_barrier((keys_values, in_block))
+        keys_values = lax.all_to_all(
+            keys_values, "seq", split_axis=0, concat_axis=0, axis_index_groups=blocks, tiled=True
         )
-
-    outs = []
-    for r in range(requests):
-        keys = to_heads(cache_k[r])
-        values = to_heads(cache_v[r])
         held = kv_heads * slots
         valid = jnp.clip(cache_len[r] - block * held, 0, held)
         fresh_shift = jnp.where(block == spread - 1, 0, -devices_seq * local_rows)
-        info = jnp.stack([valid, fresh_shift]).astype(jnp.int32)
-        part = attend(r, info, head_q, keys, values, head_fresh[0, r], head_fresh[1, r], per_source, group_size)
+        info = jnp.stack([valid, fresh_shift, seq_index]).astype(jnp.int32)
+        part = attend(r, info, head_q, keys_values, head_fresh[0, r], head_fresh[1, r], per_source, group_size)
         part = lax.all_to_all(part, "seq", split_axis=0, concat_axis=0, tiled=True)
-        outs.append(merge(part.reshape(spread, kv_heads, per_source + STAT_ROWS, head_dim), local_rows, group_size))
-    return jnp.stack(outs)
+        part = part.reshape(spread, kv_heads, per_source + STAT_ROWS, head_dim)
+        out = merge(part, r, requests, local_rows, group_size, out)
+    return out
 
 
 def solution(mesh):

time: 161 us -> 157 us (0.975)
  Pallas kernels: 34.3 us -> 40.7 us
  starting transfers between devices: 33.1 us -> 27.8 us
  waiting for transfers between devices: 75.7 us -> 71.9 us
  local copies, waits for them, and re-layouts: 11.5 us -> 7.72 us
  other arithmetic: 3.14 us -> 5.59 us
    all_to_all x5 -> x2, waiting for transfers between devices: 63 us -> 0.01 us  [shards(): lax.all_to_all(keys_values, 'seq', split_axis=0, concat_axis=0, axis_inde...]
    ppermute x0 -> x4, waiting for transfers between devices: none -> 59.2 us  [the longest x1 31.1 us: shards(): lax.ppermute(head_q, 'seq', partner(bit))]
    all_to_all x5 -> x2, starting transfers between devices: 24.6 us -> 9 us  [shards(): lax.all_to_all(keys_values, 'seq', split_axis=0, concat_axis=0, axis_inde...]
    ppermute x0 -> x4, starting transfers between devices: none -> 7.18 us  [the longest x3 4.06 us: shards(): received = lax.ppermute(halves[:, :, 1], 'seq', partner(bit))]
    pallas_call x2 -> x3, Pallas kernels: 4.25 us -> 8.98 us  [the longest x1 4.76 us: pack(): pl.pallas_call(pack_kernel, grid_spec=pltpu.PrefetchScalarGridSpec(num_sc...]
    all_to_all x2, starting transfers between devices: 8.51 us -> 11.7 us  [shards(): part = lax.all_to_all(part, 'seq', split_axis=0, concat_axis=0, tiled=True)]
    transpose x0 -> x2, other arithmetic: none -> 3.02 us  [shards(): jnp.transpose(jnp.stack([cache_k[r], cache_v[r]]), (2, 0, 1, 3))]
    unnamed x24 -> x20, local copies, waits for them, and re-layouts: 5.52 us -> 2.87 us
  transfers between devices with their start and end apart: 7 -> 8, of which waited for: 5 -> 5; matrix products, arithmetic and copies ran while one was open for 5% -> 5% of each run, Pallas kernels for 20% -> 25%
where the time goes in v2:
time: 157 us; the launch traced here: 155 us
  waiting for transfers between devices  71.9 us (46%)
  Pallas kernels  40.7 us (26%)
  starting transfers between devices  27.8 us (18%)
  local copies, waits for them, and re-layouts  7.72 us (5%)
  other arithmetic  5.59 us (4%)
    pallas_call x2, Pallas kernels, attend(): pl.pallas_call(functools.partial(attend_kernel, chunk=chunk, tile=tile, g...  31.7 us
    ppermute x1, waiting for transfers between devices, shards(): lax.ppermute(head_q, 'seq', partner(bit))  31.1 us
    ppermute x3, waiting for transfers between devices, shards(): received = lax.ppermute(halves[:, :, 1], 'seq', partner(bit))  28 us
    all_to_all x2, waiting for transfers between devices, shards(): part = lax.all_to_all(part, 'seq', split_axis=0, concat_axis=0, tiled=True)  12.7 us
    all_to_all x2, starting transfers between devices, shards(): part = lax.all_to_all(part, 'seq', split_axis=0, concat_axis=0, tiled=True)  11.7 us
    all_to_all x2, starting transfers between devices, shards(): lax.all_to_all(keys_values, 'seq', split_axis=0, concat_axis=0, axis_inde...  9 us
    pallas_call x1, Pallas kernels, pack(): pl.pallas_call(pack_kernel, grid_spec=pltpu.PrefetchScalarGridSpec(num_sc...  4.76 us
    pallas_call x2, Pallas kernels, merge(): pl.pallas_call(functools.partial(merge_kernel, group_size=group_size), gr...  4.23 us
  transfers between devices with their start and end apart: 8, of which 5 were waited for; matrix products, arithmetic and copies ran while one was open for 5% of the time, Pallas kernels for 25%

profile of v2, /device:TPU:0, one launch (start us, length us, event | category | flops | bytes accessed | tf_op | source)
XLA Modules:
  0.0 155.2 jit_solution(13584353828523847806)
XLA Ops:
  0.0 1.7 %fusion.2 = (bf16[1,512,8,128]{3,2,1,0:T(8,128)(2,1)S(1)}, bf16[1,512,8,128]{3,2,1,0:T(8,128)(2,1)S(1)}) fusion(bf16[2,512,8,128]{3,2,1,0:T(8,128)(2,1)} %param.9), kind=kLoop, calls=%fused_computation.25 | loop fusion | bytes 4194304 | tf_op jit(solution)/shard_map/slice | solution.py:275
  1.8 1.4 copy-done.2
  3.6 1.5 maximum_bitcast_fusion.1
  5.1 5.4 %all-to-all-start.2 = ((bf16[8,2,512,128]{3,2,1,0:T(8,128)(2,1)}), bf16[8,2,512,128]{3,2,1,0:T(8,128)(2,1)}, u32[]{:S(2)}, u32[]{:S(2)}) async-start(bf16[8,2,512,128]{3,2,1,0:T(8,128)(2,1)} %maximum_bitcast_fusion.1), calls=%async_computation.2 | async-start | bytes 4194304 | tf_op jit(solution)/shard_map/all_to_all | solution.py:278
  11.2 4.8 %shard_map.64 = bf16[8,288,128]{2,1,0:T(8,128)(2,1)} custom-call(s32[1]{0:T(128)} %bitcast.4.me_ref, bf16[2,8,128,128]{3,2,1,0:T(8,128)(2,1)} %q_ref.1, bf16[8,32,128]{2,1,0:T(8,128)(2,1)} %bitcast.64), custom_call_target="tpu_custom_call" | custom-call | tf_op jit(solution)/shard_map/pallas_call | solution.py:220
  15.9 1.1 fusion.4
  17.6 1.2 collective-permute-done
  18.9 2.0 %collective-permute-start.1 = (bf16[2,2,288,128]{3,2,0,1:T(8,128)(2,1)S(1)}, bf16[2,2,288,128]{3,2,0,1:T(8,128)(2,1)S(1)}, u32[]{:S(2)}, u32[]{:S(2)}) collective-permute-start(bf16[2,2,288,128]{3,2,0,1:T(8,128)(2,1)S(1)} %bitcast.62), channel_id=1, source_target_pairs={{0,2},{1,3},{2,0},{3,1},{4,6},{5,7},{6,4},{7,5},{8,10},{9,11},{10,... | collective-permute-start | bytes 884744 | tf_op jit(solution)/shard_map/ppermute | solution.py:258
  20.9 21.6 %collective-permute-done.1 = bf16[2,2,288,128]{3,2,0,1:T(8,128)(2,1)S(1)} collective-permute-done((bf16[2,2,288,128]{3,2,0,1:T(8,128)(2,1)S(1)}, bf16[2,2,288,128]{3,2,0,1:T(8,128)(2,1)S(1)}, u32[]{:S(2)}, u32[]{:S(2)}) %collective-permute-start.1) | collective-permute-done | bytes 294944 | tf_op jit(solution)/shard_map/ppermute | solution.py:258
  42.6 1.5 collective-permute-start.2
  44.4 1.5 maximum_bitcast_fusion
  45.9 5.2 %collective-permute-done.2 = bf16[4,1,288,128]{3,2,0,1:T(8,128)(2,1)S(1)} collective-permute-done((bf16[4,1,288,128]{3,2,0,1:T(8,128)(2,1)S(1)}, bf16[4,1,288,128]{3,2,0,1:T(8,128)(2,1)S(1)}, u32[]{:S(2)}, u32[]{:S(2)}) %collective-permute-start.2) | collective-permute-done | bytes 294944 | tf_op jit(solution)/shard_map/ppermute | solution.py:258
  51.2 3.6 %all-to-all-start = ((bf16[8,2,512,128]{3,2,1,0:T(8,128)(2,1)}), bf16[8,2,512,128]{3,2,1,0:T(8,128)(2,1)S(1)}, u32[]{:S(2)}, u32[]{:S(2)}) async-start(bf16[8,2,512,128]{3,2,1,0:T(8,128)(2,1)} %maximum_bitcast_fusion), calls=%async_computation | async-start | bytes 4194304 | tf_op jit(solution)/shard_map/all_to_all | solution.py:278
  54.8 3.1 %collective-permute-start.3 = (bf16[8,288,128]{2,1,0:T(8,128)(2,1)S(1)}, bf16[8,288,128]{2,1,0:T(8,128)(2,1)S(1)}, u32[]{:S(2)}, u32[]{:S(2)}) collective-permute-start(bf16[8,288,128]{2,1,0:T(8,128)(2,1)S(1)} %maximum_bitcast_fusion.3), channel_id=1, source_target_pairs={{0,8},{1,9},{2,10},{3,11},{4,12},{5,13},{6,14},{7,15},{8,0},{9,1},... | collective-permute-start | bytes 1769480 | tf_op jit(solution)/shard_map/ppermute | solution.py:264
  59.8 31.1 %collective-permute-done.3 = bf16[8,288,128]{2,1,0:T(8,128)(2,1)S(1)} collective-permute-done((bf16[8,288,128]{2,1,0:T(8,128)(2,1)S(1)}, bf16[8,288,128]{2,1,0:T(8,128)(2,1)S(1)}, u32[]{:S(2)}, u32[]{:S(2)}) %collective-permute-start.3) | collective-permute-done | bytes 589856 | tf_op jit(solution)/shard_map/ppermute | solution.py:264
  91.0 1.2 pad_maximum_fusion.q_ref
  92.8 15.8 %shard_map.66 = bf16[16,136,128]{2,1,0:T(8,128)(2,1)} custom-call(s32[3]{0:T(128)} %add_add_fusion.1.info_ref, bf16[16,288,128]{2,1,0:T(8,128)(2,1)} %pad_maximum_fusion.q_ref, bf16[8,2,512,128]{3,2,1,0:T(8,128)(2,1)} %all-to-all-done.2.kv_ref, bf16[128,128]{1,0:T(8,128)(2,1)} %get-tuple-element.18.fk_ref, bf16[128,128]{1,0:T(8,128)(2,1)} %get-tuple-element.17.fv_ref), custom_call_target="tpu_custom_call" | custom-call | flops 4294967296 | bytes 3145728 | tf_op jit(solution)/shard_map/pallas_call | solution.py:141
  108.7 7.5 %all-to-all-start.3 = ((bf16[16,136,128]{2,1,0:T(8,128)(2,1)}), bf16[16,136,128]{2,1,0:T(8,128)(2,1)S(1)}, u32[]{:S(2)}, u32[]{:S(2)}) async-start(bf16[16,136,128]{2,1,0:T(8,128)(2,1)} %shard_map.66), calls=%async_computation.3 | async-start | bytes 1114112 | tf_op jit(solution)/shard_map/all_to_all | solution.py:286
  117.3 15.9 %shard_map.65 = bf16[16,136,128]{2,1,0:T(8,128)(2,1)} custom-call(s32[3]{0:T(128)} %add_add_fusion.info_ref, bf16[16,288,128]{2,1,0:T(8,128)(2,1)} %pad_maximum_fusion.q_ref, bf16[8,2,512,128]{3,2,1,0:T(8,128)(2,1)} %copy-done.3, bf16[128,128]{1,0:T(8,128)(2,1)} %get-tuple-element.20.fk_ref, bf16[128,128]{1,0:T(8,128)(2,1)} %get-tuple-element.19.fv_ref), custom_call_target="tpu_custom_call" | custom-call | flops 4294967296 | bytes 3145728 | tf_op jit(solution)/shard_map/pallas_call | solution.py:141
  133.2 4.2 %all-to-all-start.1 = ((bf16[16,136,128]{2,1,0:T(8,128)(2,1)}), bf16[16,136,128]{2,1,0:T(8,128)(2,1)S(1)}, u32[]{:S(2)}, u32[]{:S(2)}) async-start(bf16[16,136,128]{2,1,0:T(8,128)(2,1)} %shard_map.65), calls=%async_computation.1 | async-start | bytes 1114112 | tf_op jit(solution)/shard_map/all_to_all | solution.py:286
  137.5 2.1 %shard_map.67.refs_0_ = bf16[2,8,128,128]{3,2,1,0:T(8,128)(2,1)} custom-call(bf16[2,8,136,128]{3,2,1,0:T(8,128)(2,1)} %bitcast.56), custom_call_target="tpu_custom_call" | custom-call | tf_op jit(solution)/shard_map/pallas_call | solution.py:197
  139.6 12.7 %all-to-all-done.1 = bf16[16,136,128]{2,1,0:T(8,128)(2,1)S(1)} async-done(((bf16[16,136,128]{2,1,0:T(8,128)(2,1)}), bf16[16,136,128]{2,1,0:T(8,128)(2,1)S(1)}, u32[]{:S(2)}, u32[]{:S(2)}) %all-to-all-start.1) | async-done | bytes 557088 | tf_op jit(solution)/shard_map/all_to_all | solution.py:286
  152.3 0.8 copy-done.1
  153.1 2.1 %shard_map.68 = bf16[2,8,128,128]{3,2,1,0:T(8,128)(2,1)} custom-call(bf16[2,8,136,128]{3,2,1,0:T(8,128)(2,1)} %bitcast.57, bf16[2,8,128,128]{3,2,1,0:T(8,128)(2,1)} %shard_map.67.refs_0_), custom_call_target="tpu_custom_call", output_to_operand_aliasing={{}: (1, {})} | custom-call | tf_op jit(solution)/shard_map/pallas_call | solution.py:197
  (35 shorter events, 4.7 us)
Async XLA Ops:
  1.7 1.6 %copy-start.2 = (bf16[2,512,8,128]{3,2,1,0:T(8,128)(2,1)S(1)}, bf16[2,512,8,128]{3,2,1,0:T(8,128)(2,1)}, u32[]{:S(2)}) copy-start(bf16[2,512,8,128]{3,2,1,0:T(8,128)(2,1)} %param.10) | copy-start | bytes 6291460
  5.1 5.4 %copy-start.4 = (bf16[2,8,8,128]{3,2,1,0:T(8,128)(2,1)S(1)}, bf16[2,8,8,128]{3,2,1,0:T(8,128)(2,1)}, u32[]{:S(2)}) copy-start(bf16[2,8,8,128]{3,2,1,0:T(8,128)(2,1)} %param.8) | copy-start | bytes 98308
  5.1 5.4 %copy-start.5 = (bf16[2,8,8,128]{3,2,1,0:T(8,128)(2,1)S(1)}, bf16[2,8,8,128]{3,2,1,0:T(8,128)(2,1)}, u32[]{:S(2)}) copy-start(bf16[2,8,8,128]{3,2,1,0:T(8,128)(2,1)} %param.7) | copy-start | bytes 98308
  5.1 46.1 %all-to-all-start.2 = ((bf16[8,2,512,128]{3,2,1,0:T(8,128)(2,1)}), bf16[8,2,512,128]{3,2,1,0:T(8,128)(2,1)}, u32[]{:S(2)}, u32[]{:S(2)}) async-start(bf16[8,2,512,128]{3,2,1,0:T(8,128)(2,1)} %maximum_bitcast_fusion.1), calls=%async_computation.2 | async-start | bytes 4194304 | tf_op jit(solution)/shard_map/all_to_all | solution.py:278
  17.0 1.8 %collective-permute-start = (bf16[1,4,288,128]{3,2,1,0:T(8,128)(2,1)S(1)}, bf16[1,4,288,128]{3,2,1,0:T(8,128)(2,1)S(1)}, u32[]{:S(2)}, u32[]{:S(2)}) collective-permute-start(bf16[1,4,288,128]{3,2,1,0:T(8,128)(2,1)S(1)} %get-tuple-element.16), channel_id=1, source_target_pairs={{0,1},{1,0},{2,3},{3,2},{4,5},{5,4},{6,7},{7,6},{8,9},{9,8},{10,11... | collective-permute-start | bytes 884744 | tf_op jit(solution)/shard_map/ppermute | solution.py:258
  18.9 23.6 %collective-permute-start.1 = (bf16[2,2,288,128]{3,2,0,1:T(8,128)(2,1)S(1)}, bf16[2,2,288,128]{3,2,0,1:T(8,128)(2,1)S(1)}, u32[]{:S(2)}, u32[]{:S(2)}) collective-permute-start(bf16[2,2,288,128]{3,2,0,1:T(8,128)(2,1)S(1)} %bitcast.62), channel_id=1, source_target_pairs={{0,2},{1,3},{2,0},{3,1},{4,6},{5,7},{6,4},{7,5},{8,10},{9,11},{10,... | collective-permute-start | bytes 884744 | tf_op jit(solution)/shard_map/ppermute | solution.py:258
  42.6 8.5 %collective-permute-start.2 = (bf16[4,1,288,128]{3,2,0,1:T(8,128)(2,1)S(1)}, bf16[4,1,288,128]{3,2,0,1:T(8,128)(2,1)S(1)}, u32[]{:S(2)}, u32[]{:S(2)}) collective-permute-start(bf16[4,1,288,128]{3,2,0,1:T(8,128)(2,1)S(1)} %get-tuple-element.12), channel_id=1, source_target_pairs={{0,4},{1,5},{2,6},{3,7},{4,0},{5,1},{6,2},{7,3},{8,12},{9,13},{10,... | collective-permute-start | bytes 884744 | tf_op jit(solution)/shard_map/ppermute | solution.py:258
  51.1 6.8 %copy-start.6 = (s32[2]{0:T(128)S(1)}, s32[2]{0:T(128)}, u32[]{:S(2)}) copy-start(s32[2]{0:T(128)} %param.11) | copy-start | bytes 28
  51.2 57.5 %all-to-all-start = ((bf16[8,2,512,128]{3,2,1,0:T(8,128)(2,1)}), bf16[8,2,512,128]{3,2,1,0:T(8,128)(2,1)S(1)}, u32[]{:S(2)}, u32[]{:S(2)}) async-start(bf16[8,2,512,128]{3,2,1,0:T(8,128)(2,1)} %maximum_bitcast_fusion), calls=%async_computation | async-start | bytes 4194304 | tf_op jit(solution)/shard_map/all_to_all | solution.py:278
  54.8 36.2 %collective-permute-start.3 = (bf16[8,288,128]{2,1,0:T(8,128)(2,1)S(1)}, bf16[8,288,128]{2,1,0:T(8,128)(2,1)S(1)}, u32[]{:S(2)}, u32[]{:S(2)}) collective-permute-start(bf16[8,288,128]{2,1,0:T(8,128)(2,1)S(1)} %maximum_bitcast_fusion.3), channel_id=1, source_target_pairs={{0,8},{1,9},{2,10},{3,11},{4,12},{5,13},{6,14},{7,15},{8,0},{9,1},... | collective-permute-start | bytes 1769480 | tf_op jit(solution)/shard_map/ppermute | solution.py:264
  108.7 8.7 %copy-start.3 = (bf16[8,2,512,128]{3,2,1,0:T(8,128)(2,1)}, bf16[8,2,512,128]{3,2,1,0:T(8,128)(2,1)S(1)}, u32[]{:S(2)}) copy-start(bf16[8,2,512,128]{3,2,1,0:T(8,128)(2,1)S(1)} %all-to-all-done.kv_ref) | copy-start | bytes 6291460
  108.7 24.6 %all-to-all-start.3 = ((bf16[16,136,128]{2,1,0:T(8,128)(2,1)}), bf16[16,136,128]{2,1,0:T(8,128)(2,1)S(1)}, u32[]{:S(2)}, u32[]{:S(2)}) async-start(bf16[16,136,128]{2,1,0:T(8,128)(2,1)} %shard_map.66), calls=%async_computation.3 | async-start | bytes 1114112 | tf_op jit(solution)/shard_map/all_to_all | solution.py:286
  133.2 4.2 %copy-start = (bf16[16,136,128]{2,1,0:T(8,128)(2,1)}, bf16[16,136,128]{2,1,0:T(8,128)(2,1)S(1)}, u32[]{:S(2)}) copy-start(bf16[16,136,128]{2,1,0:T(8,128)(2,1)S(1)} %all-to-all-done.3) | copy-start | bytes 1671172
  133.2 19.0 %all-to-all-start.1 = ((bf16[16,136,128]{2,1,0:T(8,128)(2,1)}), bf16[16,136,128]{2,1,0:T(8,128)(2,1)S(1)}, u32[]{:S(2)}, u32[]{:S(2)}) async-start(bf16[16,136,128]{2,1,0:T(8,128)(2,1)} %shard_map.65), calls=%async_computation.1 | async-start | bytes 1114112 | tf_op jit(solution)/shard_map/all_to_all | solution.py:286
  152.3 0.8 copy-start.1

commit v3 on v2

--- a/solution.py
+++ b/solution.py
@@ -8,9 +8,10 @@
 from jax.experimental.pallas import tpu as pltpu
 from jax.sharding import PartitionSpec as P
 
+
 NEG = -1e30
 STAT_ROWS = 8
-VMEM_BYTES = 58 * 2**20
+SMALL_VMEM = 8 * 2**20
 
 
 def attend_kernel(
@@ -95,7 +96,7 @@
                 ]
             level = top * scale + jnp.log2(total)
             for first in range(0, tile, dim):
-                flat = jnp.transpose(level[first : first + dim, :])[:STAT_ROWS]
+                flat = jnp.transpose(level[first : first + dim, :STAT_ROWS])
                 high = flat.astype(jnp.bfloat16)
                 rest = flat - high.astype(jnp.float32)
                 mid = rest.astype(jnp.bfloat16)
@@ -135,8 +136,10 @@
     tile = min(256, rows // 2)
     chunk = min(1024, slots)
 
-    def whole(array):
-        return pl.BlockSpec(array.shape, lambda i, s: (0,) * array.ndim)
+    grant = 4 * (2 * tile * (slots + fresh) + slots * dim + 2 * slots * dim + 2 * rows * dim) + SMALL_VMEM
+
+    def whole():
+        return pl.BlockSpec(memory_space=pltpu.VMEM)
 
     return pl.pallas_call(
         functools.partial(attend_kernel, chunk=chunk, tile=tile, group_size=group_size),
@@ -144,10 +147,7 @@
             num_scalar_prefetch=1,
             grid=(1,),
             in_specs=[
-                pl.BlockSpec((sources, per_source, dim), lambda i, s: (0, request, 0)),
-                whole(keys_values),
-                whole(fresh_k),
-                whole(fresh_v),
+                pl.BlockSpec((sources, per_source, dim), lambda i, s: (0, request, 0)), whole(), whole(), whole()
             ],
             out_specs=pl.BlockSpec((sources, per_source + STAT_ROWS, dim), lambda i, s: (0, 0, 0)),
             scratch_shapes=[
@@ -160,7 +160,7 @@
             ],
         ),
         out_shape=jax.ShapeDtypeStruct((sources, per_source + STAT_ROWS, dim), jnp.bfloat16),
-        compiler_params=pltpu.CompilerParams(vmem_limit_bytes=VMEM_BYTES),
+        compiler_params=pltpu.CompilerParams(vmem_limit_bytes=grant),
         cost_estimate=pl.CostEstimate(
             flops=4 * rows * slots * dim,
             bytes_accessed=4 * slots * dim + 4 * rows * dim,
@@ -174,21 +174,25 @@
     spread, heads, _, dim = part_ref.shape
     local_rows = out_ref.shape[1]
     per_source = local_rows * group_size
+    levels = []
+    for b in range(spread):
+        stats = [
+            part_ref[b, h, per_source : per_source + STAT_ROWS, :].astype(jnp.float32) for h in range(heads)
+        ]
+        levels.append(jnp.concatenate([x[0:1] + x[1:2] + x[2:3] for x in stats], axis=0))
+    top = functools.reduce(jnp.maximum, levels)
+    weights = [jnp.exp2(level - top) for level in levels]
+    total = functools.reduce(jnp.add, weights)
+    weights = [jnp.transpose(w / total) for w in weights]
     for h in range(heads):
-        levels = []
-        for b in range(spread):
-            stats = part_ref[b, h, per_source : per_source + STAT_ROWS, :].astype(jnp.float32)
-            level = stats[0:1] + stats[1:2] + stats[2:3]
-            levels.append(jnp.transpose(jnp.broadcast_to(level, (dim, dim)))[:per_source])
-        top = functools.reduce(jnp.maximum, levels)
-        weights = [jnp.exp2(level - top) for level in levels]
-        total = functools.reduce(jnp.add, weights)
         mixed = functools.reduce(
             jnp.add,
-            [w * part_ref[b, h, :per_source, :].astype(jnp.float32) for b, w in enumerate(weights)],
-        )
-        out = (mixed / total).astype(jnp.bfloat16)
-        out_ref[0, :, h * group_size : (h + 1) * group_size, :] = out.reshape(local_rows, group_size, dim)
+            [
+                w[:per_source, h : h + 1] * part_ref[b, h, :per_source, :].astype(jnp.float32)
+                for b, w in enumerate(weights)
+            ],
+        ).astype(jnp.bfloat16)
+        out_ref[0, :, h * group_size : (h + 1) * group_size, :] = mixed.reshape(local_rows, group_size, dim)
 
 
 def merge(parts, request, requests, local_rows, group_size, earlier):
@@ -202,37 +206,39 @@
         out_specs=pl.BlockSpec((1, local_rows, heads * group_size, dim), lambda i: (request, 0, 0, 0)),
         out_shape=jax.ShapeDtypeStruct((requests, local_rows, heads * group_size, dim), jnp.bfloat16),
         input_output_aliases={1: 0} if rest else {},
-        compiler_params=pltpu.CompilerParams(vmem_limit_bytes=VMEM_BYTES),
+        compiler_params=pltpu.CompilerParams(vmem_limit_bytes=SMALL_VMEM),
     )(parts, *rest)
 
 
 def pack_kernel(me_ref, q_ref, fresh_ref, out_ref):
-    requests, local_rows, group_size, dim = q_ref.shape
+    requests, local_rows, heads, dim = q_ref.shape
+    kv_heads = out_ref.shape[0]
+    group_size = heads // kv_heads
     rows = requests * local_rows * group_size
-    out_ref[0, :rows, :] = q_ref[...].reshape(rows, dim)
-    out_ref[0, rows:, :] = fresh_ref[0]
+    for d in range(kv_heads):
+        head = d ^ me_ref[0]
+        first = pl.multiple_of(head * group_size, group_size)
+        out_ref[d, :rows, :] = q_ref[:, :, pl.ds(first, group_size), :].reshape(rows, dim)
+        out_ref[d, rows:, :] = fresh_ref[head]
 
 
 def pack(queries, fresh, me, kv_heads):
     requests, local_rows, heads, dim = queries.shape
-    group_size = heads // kv_heads
-    rows = requests * local_rows * group_size + fresh.shape[1]
+    rows = requests * local_rows * (heads // kv_heads) + fresh.shape[1]
     return pl.pallas_call(
         pack_kernel,
-        grid_spec=pltpu.PrefetchScalarGridSpec(
-            num_scalar_prefetch=1,
-            grid=(kv_heads,),
-            in_specs=[
-                pl.BlockSpec((requests, local_rows, group_size, dim), lambda d, me: (0, 0, d ^ me[0], 0)),
-                pl.BlockSpec((1,) + fresh.shape[1:], lambda d, me: (d ^ me[0], 0, 0)),
-            ],
-            out_specs=pl.BlockSpec((1, rows, dim), lambda d, me: (d, 0, 0)),
-        ),
+        in_specs=[
+            pl.BlockSpec(memory_space=pltpu.SMEM),
+            pl.BlockSpec(memory_space=pltpu.VMEM),
+            pl.BlockSpec(memory_space=pltpu.VMEM),
+        ],
+        out_specs=pl.BlockSpec(memory_space=pltpu.VMEM),
         out_shape=jax.ShapeDtypeStruct((kv_heads, rows, dim), jnp.bfloat16),
+        compiler_params=pltpu.CompilerParams(vmem_limit_bytes=SMALL_VMEM),
     )(me, queries, fresh)
 
 
-def shards(queries, new_k, new_v, cache_k, cache_v, cache_len):
+def attention(queries, new_k, new_v, cache_k, cache_v, cache_len):
     requests, local_rows, heads, head_dim = queries.shape
     slots = cache_k.shape[1]
     kv_heads = cache_k.shape[2]
@@ -255,13 +261,16 @@
     bit = 1
     while bit < kv_heads:
         halves = head_q.reshape((head_q.shape[0], -1, 2) + head_q.shape[2:])
+        if 2 * bit == kv_heads:
+            before_last = halves
         received = lax.ppermute(halves[:, :, 1], "seq", partner(bit))
         head_q = jnp.concatenate([halves[:, :, 0], received], axis=0)
         bit *= 2
     head_q = head_q[:, 0]
     in_block = head_q
     while bit < devices_seq:
-        head_q = jnp.concatenate([head_q, lax.ppermute(head_q, "seq", partner(bit))], axis=0)
+        received = lax.ppermute(head_q, "seq", partner(bit))
+        head_q = jnp.concatenate([head_q, received], axis=0)
         bit *= 2
     head_fresh = head_q[:, requests * per_source :, :].reshape(
         devices_seq, 2, requests, local_rows, head_dim
@@ -273,8 +282,7 @@
     out = None
     for r in range(requests):
         keys_values = jnp.transpose(jnp.stack([cache_k[r], cache_v[r]]), (2, 0, 1, 3))
-        if r > 0:
-            keys_values, _ = lax.optimization_barrier((keys_values, in_block))
+        keys_values, _ = lax.optimization_barrier((keys_values, before_last if r == 0 else in_block))
         keys_values = lax.all_to_all(
             keys_values, "seq", split_axis=0, concat_axis=0, axis_index_groups=blocks, tiled=True
         )
@@ -299,4 +307,4 @@
         P("groups"),
     )
     out_specs = P("groups", "seq", None, None)
-    return jax.shard_map(shards, mesh=mesh, in_specs=in_specs, out_specs=out_specs, check_vma=False)
+    return jax.shard_map(attention, mesh=mesh, in_specs=in_specs, out_specs=out_specs, check_vma=False)

time: 157 us -> 153 us (0.975)
  Pallas kernels: 40.7 us -> 28.8 us
  waiting for transfers between devices: 71.9 us -> 78.2 us
    pallas_call x2, Pallas kernels: 31.7 us -> 26.2 us  [attend(): pl.pallas_call(functools.partial(attend_kernel, chunk=chunk, tile=tile, g...]
    pallas_call x1, Pallas kernels: 4.76 us -> 0.07 us  [pack(): pl.pallas_call(pack_kernel, in_specs=[pl.BlockSpec(memory_space=pltpu.SME...]
    ppermute x4, waiting for transfers between devices: 59.2 us -> 63.6 us  [the longest x1 32.1 us: attention(): received = lax.ppermute(head_q, 'seq', partner(bit))]
    all_to_all x4, waiting for transfers between devices: 12.7 us -> 14.6 us  [the longest x2 14.6 us: attention(): part = lax.all_to_all(part, 'seq', split_axis=0, concat_axis=0, tiled=True)]
    pallas_call x2, Pallas kernels: 4.23 us -> 2.52 us  [merge(): pl.pallas_call(functools.partial(merge_kernel, group_size=group_size), gr...]
    slice x4, local copies, waits for them, and re-layouts: 3.5 us -> 1.9 us  [the longest x1 1.12 us: attention(): cache_v[r]]
    unnamed x20 -> x22, local copies, waits for them, and re-layouts: 2.87 us -> 4.2 us
  transfers between devices with their start and end apart: 8 -> 8, of which waited for: 5 -> 6; matrix products, arithmetic and copies ran while one was open for 5% -> 5% of each run, Pallas kernels for 25% -> 18%
where the time goes in v3:
time: 153 us; the launch traced here: 150 us
  waiting for transfers between devices  78.2 us (51%)
  Pallas kernels  28.8 us (19%)
  starting transfers between devices  28.1 us (18%)
  local copies, waits for them, and re-layouts  7.32 us (5%)
  other arithmetic  6.29 us (4%)
    ppermute x1, waiting for transfers between devices, attention(): received = lax.ppermute(head_q, 'seq', partner(bit))  32.1 us
    ppermute x3, waiting for transfers between devices, attention(): received = lax.ppermute(halves[:, :, 1], 'seq', partner(bit))  31.5 us
    pallas_call x2, Pallas kernels, attend(): pl.pallas_call(functools.partial(attend_kernel, chunk=chunk, tile=tile, g...  26.2 us
    all_to_all x2, waiting for transfers between devices, attention(): part = lax.all_to_all(part, 'seq', split_axis=0, concat_axis=0, tiled=True)  14.6 us
    all_to_all x2, starting transfers between devices, attention(): part = lax.all_to_all(part, 'seq', split_axis=0, concat_axis=0, tiled=True)  11.3 us
    all_to_all x2, starting transfers between devices, attention(): lax.all_to_all(keys_values, 'seq', split_axis=0, concat_axis=0, axis_inde...  8.52 us
    ppermute x3, starting transfers between devices, attention(): received = lax.ppermute(halves[:, :, 1], 'seq', partner(bit))  5.55 us
    unnamed x22, local copies, waits for them, and re-layouts  4.2 us
  transfers between devices with their start and end apart: 8, of which 6 were waited for; matrix products, arithmetic and copies ran while one was open for 5% of the time, Pallas kernels for 18%

profile of v3, /device:TPU:0, one launch (start us, length us, event | category | flops | bytes accessed | tf_op | source)
XLA Modules:
  0.0 150.2 jit_solution(9535847467173592664)
XLA Ops:
  0.8 1.0 copy-done.1
  2.5 0.9 copy-done.5
  3.8 2.9 %collective-permute-start.1 = (bf16[2,2,288,128]{3,2,0,1:T(8,128)(2,1)S(1)}, bf16[2,2,288,128]{3,2,0,1:T(8,128)(2,1)S(1)}, u32[]{:S(2)}, u32[]{:S(2)}) collective-permute-start(bf16[2,2,288,128]{3,2,0,1:T(8,128)(2,1)S(1)} %bitcast.63), channel_id=1, source_target_pairs={{0,2},{1,3},{2,0},{3,1},{4,6},{5,7},{6,4},{7,5},{8,10},{9,11},{10,... | collective-permute-start | bytes 884744 | tf_op jit(solution)/shard_map/ppermute | solution.py:266
  6.8 1.1 fusion.3
  8.2 1.5 %maximum_bitcast_fusion.1 = bf16[8,2,512,128]{3,2,1,0:T(8,128)(2,1)} fusion(bf16[1,512,8,128]{3,1,0,2:T(8,128)(2,1)S(1)} %copy.32, bf16[1,512,8,128]{3,1,0,2:T(8,128)(2,1)S(1)} %copy.31), kind=kLoop, calls=%fused_computation.1 | loop fusion | flops 1048576 | bytes 4194304 | tf_op jit(solution)/shard_map/transpose | solution.py:284
  9.7 4.4 %collective-permute-done.1 = bf16[2,2,288,128]{3,2,0,1:T(8,128)(2,1)S(1)} collective-permute-done((bf16[2,2,288,128]{3,2,0,1:T(8,128)(2,1)S(1)}, bf16[2,2,288,128]{3,2,0,1:T(8,128)(2,1)S(1)}, u32[]{:S(2)}, u32[]{:S(2)}) %collective-permute-start.1) | collective-permute-done | bytes 294944 | tf_op jit(solution)/shard_map/ppermute | solution.py:266
  14.1 0.9 maximum_bitcast_fusion.2
  15.0 4.0 %all-to-all-start.2 = ((bf16[8,2,512,128]{3,2,1,0:T(8,128)(2,1)}), bf16[8,2,512,128]{3,2,1,0:T(8,128)(2,1)S(1)}, u32[]{:S(2)}, u32[]{:S(2)}) async-start(bf16[8,2,512,128]{3,2,1,0:T(8,128)(2,1)} %maximum_bitcast_fusion.1), calls=%async_computation.2 | async-start | bytes 4194304 | tf_op jit(solution)/shard_map/all_to_all | solution.py:286
  19.0 1.2 slice_bitcast_fusion.1
  20.2 2.1 %collective-permute-start.2 = (bf16[4,1,288,128]{3,2,0,1:T(8,128)(2,1)S(1)}, bf16[4,1,288,128]{3,2,0,1:T(8,128)(2,1)S(1)}, u32[]{:S(2)}, u32[]{:S(2)}) collective-permute-start(bf16[4,1,288,128]{3,2,0,1:T(8,128)(2,1)S(1)} %get-tuple-element.14), channel_id=1, source_target_pairs={{0,4},{1,5},{2,6},{3,7},{4,0},{5,1},{6,2},{7,3},{8,12},{9,13},{10,... | collective-permute-start | bytes 884744 | tf_op jit(solution)/shard_map/ppermute | solution.py:266
  22.6 1.5 maximum_bitcast_fusion
  24.0 27.0 %collective-permute-done.2 = bf16[4,1,288,128]{3,2,0,1:T(8,128)(2,1)S(1)} collective-permute-done((bf16[4,1,288,128]{3,2,0,1:T(8,128)(2,1)S(1)}, bf16[4,1,288,128]{3,2,0,1:T(8,128)(2,1)S(1)}, u32[]{:S(2)}, u32[]{:S(2)}) %collective-permute-start.2) | collective-permute-done | bytes 294944 | tf_op jit(solution)/shard_map/ppermute | solution.py:266
  51.1 4.5 %all-to-all-start = ((bf16[8,2,512,128]{3,2,1,0:T(8,128)(2,1)}), bf16[8,2,512,128]{3,2,1,0:T(8,128)(2,1)}, u32[]{:S(2)}, u32[]{:S(2)}) async-start(bf16[8,2,512,128]{3,2,1,0:T(8,128)(2,1)} %maximum_bitcast_fusion), calls=%async_computation | async-start | bytes 4194304 | tf_op jit(solution)/shard_map/all_to_all | solution.py:286
  55.6 2.7 %collective-permute-start.3 = (bf16[8,288,128]{2,1,0:T(8,128)(2,1)S(1)}, bf16[8,288,128]{2,1,0:T(8,128)(2,1)S(1)}, u32[]{:S(2)}, u32[]{:S(2)}) collective-permute-start(bf16[8,288,128]{2,1,0:T(8,128)(2,1)S(1)} %maximum_bitcast_fusion.3), channel_id=1, source_target_pairs={{0,8},{1,9},{2,10},{3,11},{4,12},{5,13},{6,14},{7,15},{8,0},{9,1},... | collective-permute-start | bytes 1769480 | tf_op jit(solution)/shard_map/ppermute | solution.py:272
  59.6 32.1 %collective-permute-done.3 = bf16[8,288,128]{2,1,0:T(8,128)(2,1)S(1)} collective-permute-done((bf16[8,288,128]{2,1,0:T(8,128)(2,1)S(1)}, bf16[8,288,128]{2,1,0:T(8,128)(2,1)S(1)}, u32[]{:S(2)}, u32[]{:S(2)}) %collective-permute-start.3) | collective-permute-done | bytes 589856 | tf_op jit(solution)/shard_map/ppermute | solution.py:272
  92.6 1.3 pad_maximum_fusion.q_ref
  94.0 13.2 %shard_map.66 = bf16[16,136,128]{2,1,0:T(8,128)(2,1)S(1)} custom-call(s32[3]{0:T(128)S(1)} %add_add_fusion.1.info_ref, bf16[16,288,128]{2,1,0:T(8,128)(2,1)S(1)} %pad_maximum_fusion.q_ref, bf16[8,2,512,128]{3,2,1,0:T(8,128)(2,1)S(1)} %all-to-all-done.2.kv_ref, bf16[128,128]{1,0:T(8,128)(2,1)S(1)} %get-tuple-element.20.fk_ref, ...), custom_call_target="tpu_custom_call" | custom-call | flops 4294967296 | bytes 3145728 | tf_op jit(solution)/shard_map/pallas_call | solution.py:144
  108.0 7.0 %all-to-all-start.3 = ((bf16[16,136,128]{2,1,0:T(8,128)(2,1)}), bf16[16,136,128]{2,1,0:T(8,128)(2,1)S(1)}, u32[]{:S(2)}, u32[]{:S(2)}) async-start(bf16[16,136,128]{2,1,0:T(8,128)(2,1)} %copy-done), calls=%async_computation.3 | async-start | bytes 1114112 | tf_op jit(solution)/shard_map/all_to_all | solution.py:294
  115.7 13.1 %shard_map.65 = bf16[16,136,128]{2,1,0:T(8,128)(2,1)} custom-call(s32[3]{0:T(128)S(1)} %add_add_fusion.info_ref, bf16[16,288,128]{2,1,0:T(8,128)(2,1)S(1)} %pad_maximum_fusion.q_ref, bf16[8,2,512,128]{3,2,1,0:T(8,128)(2,1)} %all-to-all-done.kv_ref, bf16[128,128]{1,0:T(8,128)(2,1)S(1)} %get-tuple-element.22.fk_ref, bf16[128,128]{1,0:T(8,128)(2,1)S(1)} %get-tuple-element.21.fv_ref), custom_call_target="tpu_custom_call" | custom-call | flops 4294967296 | bytes 3145728 | tf_op jit(solution)/shard_map/pallas_call | solution.py:144
  128.8 1.0 all-to-all-done.3
  129.8 4.3 %all-to-all-start.1 = ((bf16[16,136,128]{2,1,0:T(8,128)(2,1)}), bf16[16,136,128]{2,1,0:T(8,128)(2,1)S(1)}, u32[]{:S(2)}, u32[]{:S(2)}) async-start(bf16[16,136,128]{2,1,0:T(8,128)(2,1)} %shard_map.65), calls=%async_computation.1 | async-start | bytes 1114112 | tf_op jit(solution)/shard_map/all_to_all | solution.py:294
  134.1 1.3 shard_map.67.refs_0_
  135.4 13.5 %all-to-all-done.1 = bf16[16,136,128]{2,1,0:T(8,128)(2,1)S(1)} async-done(((bf16[16,136,128]{2,1,0:T(8,128)(2,1)}), bf16[16,136,128]{2,1,0:T(8,128)(2,1)S(1)}, u32[]{:S(2)}, u32[]{:S(2)}) %all-to-all-start.1) | async-done | bytes 557088 | tf_op jit(solution)/shard_map/all_to_all | solution.py:294
  148.9 1.3 shard_map.68
  (37 shorter events, 5.0 us)
Async XLA Ops:
  0.8 1.0 copy-start.1
  1.9 1.6 %copy-start.5 = (bf16[2,512,8,128]{3,2,1,0:T(8,128)(2,1)S(1)}, bf16[2,512,8,128]{3,2,1,0:T(8,128)(2,1)}, u32[]{:S(2)}) copy-start(bf16[2,512,8,128]{3,2,1,0:T(8,128)(2,1)} %param.9) | copy-start | bytes 6291460
  2.0 4.8 %copy-start.6 = (bf16[2,512,8,128]{3,2,1,0:T(8,128)(2,1)S(1)}, bf16[2,512,8,128]{3,2,1,0:T(8,128)(2,1)}, u32[]{:S(2)}) copy-start(bf16[2,512,8,128]{3,2,1,0:T(8,128)(2,1)} %param.10) | copy-start | bytes 6291460
  2.0 1.8 %collective-permute-start = (bf16[1,4,288,128]{3,2,1,0:T(8,128)(2,1)S(1)}, bf16[1,4,288,128]{3,2,1,0:T(8,128)(2,1)S(1)}, u32[]{:S(2)}, u32[]{:S(2)}) collective-permute-start(bf16[1,4,288,128]{3,2,1,0:T(8,128)(2,1)S(1)} %get-tuple-element.18), channel_id=1, source_target_pairs={{0,1},{1,0},{2,3},{3,2},{4,5},{5,4},{6,7},{7,6},{8,9},{9,8},{10,11... | collective-permute-start | bytes 884744 | tf_op jit(solution)/shard_map/ppermute | solution.py:266
  3.8 10.2 %collective-permute-start.1 = (bf16[2,2,288,128]{3,2,0,1:T(8,128)(2,1)S(1)}, bf16[2,2,288,128]{3,2,0,1:T(8,128)(2,1)S(1)}, u32[]{:S(2)}, u32[]{:S(2)}) collective-permute-start(bf16[2,2,288,128]{3,2,0,1:T(8,128)(2,1)S(1)} %bitcast.63), channel_id=1, source_target_pairs={{0,2},{1,3},{2,0},{3,1},{4,6},{5,7},{6,4},{7,5},{8,10},{9,11},{10,... | collective-permute-start | bytes 884744 | tf_op jit(solution)/shard_map/ppermute | solution.py:266
  15.0 36.1 %all-to-all-start.2 = ((bf16[8,2,512,128]{3,2,1,0:T(8,128)(2,1)}), bf16[8,2,512,128]{3,2,1,0:T(8,128)(2,1)S(1)}, u32[]{:S(2)}, u32[]{:S(2)}) async-start(bf16[8,2,512,128]{3,2,1,0:T(8,128)(2,1)} %maximum_bitcast_fusion.1), calls=%async_computation.2 | async-start | bytes 4194304 | tf_op jit(solution)/shard_map/all_to_all | solution.py:286
  19.0 3.4 %copy-start.3 = (bf16[1,512,8,128]{3,2,1,0:T(8,128)(2,1)S(1)}, bf16[1,512,8,128]{3,2,1,0:T(8,128)(2,1)}, u32[]{:S(2)}) copy-start(bf16[1,512,8,128]{3,2,1,0:T(8,128)(2,1)} %get-tuple-element.12) | copy-start | bytes 3145732
  20.2 30.8 %collective-permute-start.2 = (bf16[4,1,288,128]{3,2,0,1:T(8,128)(2,1)S(1)}, bf16[4,1,288,128]{3,2,0,1:T(8,128)(2,1)S(1)}, u32[]{:S(2)}, u32[]{:S(2)}) collective-permute-start(bf16[4,1,288,128]{3,2,0,1:T(8,128)(2,1)S(1)} %get-tuple-element.14), channel_id=1, source_target_pairs={{0,4},{1,5},{2,6},{3,7},{4,0},{5,1},{6,2},{7,3},{8,12},{9,13},{10,... | collective-permute-start | bytes 884744 | tf_op jit(solution)/shard_map/ppermute | solution.py:266
  51.1 40.7 %copy-start.2 = (bf16[8,288,128]{2,1,0:T(8,128)(2,1)}, bf16[8,288,128]{2,1,0:T(8,128)(2,1)S(1)}, u32[]{:S(2)}) copy-start(bf16[8,288,128]{2,1,0:T(8,128)(2,1)S(1)} %maximum_bitcast_fusion.3) | copy-start | bytes 1769476
  51.1 7.2 %copy-start.7 = (s32[2]{0:T(128)S(1)}, s32[2]{0:T(128)}, u32[]{:S(2)}) copy-start(s32[2]{0:T(128)} %param.11) | copy-start | bytes 28
  51.1 56.9 %all-to-all-start = ((bf16[8,2,512,128]{3,2,1,0:T(8,128)(2,1)}), bf16[8,2,512,128]{3,2,1,0:T(8,128)(2,1)}, u32[]{:S(2)}, u32[]{:S(2)}) async-start(bf16[8,2,512,128]{3,2,1,0:T(8,128)(2,1)} %maximum_bitcast_fusion), calls=%async_computation | async-start | bytes 4194304 | tf_op jit(solution)/shard_map/all_to_all | solution.py:286
  55.6 36.1 %collective-permute-start.3 = (bf16[8,288,128]{2,1,0:T(8,128)(2,1)S(1)}, bf16[8,288,128]{2,1,0:T(8,128)(2,1)S(1)}, u32[]{:S(2)}, u32[]{:S(2)}) collective-permute-start(bf16[8,288,128]{2,1,0:T(8,128)(2,1)S(1)} %maximum_bitcast_fusion.3), channel_id=1, source_target_pairs={{0,8},{1,9},{2,10},{3,11},{4,12},{5,13},{6,14},{7,15},{8,0},{9,1},... | collective-permute-start | bytes 1769480 | tf_op jit(solution)/shard_map/ppermute | solution.py:272
  91.7 0.8 copy-start.4
  107.1 0.8 copy-start
  108.0 21.8 %all-to-all-start.3 = ((bf16[16,136,128]{2,1,0:T(8,128)(2,1)}), bf16[16,136,128]{2,1,0:T(8,128)(2,1)S(1)}, u32[]{:S(2)}, u32[]{:S(2)}) async-start(bf16[16,136,128]{2,1,0:T(8,128)(2,1)} %copy-done), calls=%async_computation.3 | async-start | bytes 1114112 | tf_op jit(solution)/shard_map/all_to_all | solution.py:294
  129.8 19.1 %all-to-all-start.1 = ((bf16[16,136,128]{2,1,0:T(8,128)(2,1)}), bf16[16,136,128]{2,1,0:T(8,128)(2,1)S(1)}, u32[]{:S(2)}, u32[]{:S(2)}) async-start(bf16[16,136,128]{2,1,0:T(8,128)(2,1)} %shard_map.65), calls=%async_computation.1 | async-start | bytes 1114112 | tf_op jit(solution)/shard_map/all_to_all | solution.py:294

commit v4 on v3

v4 whole, which is shorter than its diff:
```python
import functools
import math

import jax
import jax.numpy as jnp
from jax import lax
from jax.experimental import pallas as pl
from jax.experimental.pallas import tpu as pltpu
from jax.sharding import PartitionSpec as P


NEG = -1e30
STAT_ROWS = 8
SMALL_VMEM = 12 * 2**20


VMEM_SPEC = pl.BlockSpec(memory_space=pltpu.VMEM)
HBM_SPEC = pl.BlockSpec(memory_space=pltpu.HBM)
SMEM_SPEC = pl.BlockSpec(memory_space=pltpu.SMEM)


def attend_kernel(*refs, blocks, chunk, tile, group_size, row_start, row_count):
    info_ref, q_hbm = refs[:2]
    kv_refs = refs[2 : 2 + blocks]
    fk_ref, fv_ref, out_hbm, q_ref, out_ref, keys, vals, fvals, s0, s1, m0, m1, in_sems, q_sem, out_sem = refs[
        2 + blocks :
    ]
    per_source, dim = row_count, q_ref.shape[2]
    block_slots = kv_refs[0].shape[1]
    slots = blocks * block_slots
    fresh = fk_ref.shape[0]
    rows = q_ref.shape[0] * per_source
    tiles = rows // tile
    span = tile // per_source
    scale = math.log2(math.e) / math.sqrt(dim)
    valid = info_ref[0]
    fresh_shift = info_ref[1]
    own = info_ref[2]

    copies = [
        pltpu.make_async_copy(q_hbm.at[:, row_start : row_start + row_count, :], q_ref, q_sem),
    ]
    for k, kv_ref in enumerate(kv_refs):
        at = pl.ds(pl.multiple_of((own ^ k) * block_slots, block_slots), block_slots)
        copies.append(pltpu.make_async_copy(kv_ref.at[0], keys.at[at, :], in_sems.at[k, 0]))
        copies.append(pltpu.make_async_copy(kv_ref.at[1], vals.at[at, :dim], in_sems.at[k, 1]))
    for copy in copies:
        copy.start()
    vals[:, dim:] = jnp.ones((slots, dim), jnp.bfloat16)
    fvals[:, :dim] = fv_ref[...]
    fvals[:, dim:] = jnp.ones((fresh, dim), jnp.bfloat16)
    for copy in copies:
        copy.wait()

    def product(a, b):
        return lax.dot_general(a, b, (((1,), (1,)), ((), ())), preferred_element_type=jnp.float32)

    def lane_max(scores, best):
        for lane in range(scores.shape[1] // dim):
            part = scores[:, lane * dim : (lane + 1) * dim]
            best = part if best is None else jnp.maximum(best, part)
        return best

    def score_chunk(t, j, count, s_ref, best):
        q = q_ref[pl.ds(t * span, span)].reshape(tile, dim)
        if j < count:
            scores = product(q, keys[j * chunk : (j + 1) * chunk, :])
            if j == count - 1:
                pos = j * chunk + lax.broadcasted_iota(jnp.int32, (1, chunk), 1)
                scores = scores + jnp.where(pos < valid, 0.0, NEG)
            s_ref[:, j * chunk : (j + 1) * chunk] = scores
            return lane_max(scores, best)
        scores = product(q, fk_ref[...])
        token = (t * tile + lax.broadcasted_iota(jnp.int32, (tile, 1), 0)) // group_size
        unit = lax.broadcasted_iota(jnp.int32, (1, fresh), 1)
        scores = jnp.where(unit <= token + fresh_shift, scores, NEG)
        s_ref[:, slots : slots + fresh] = scores
        return lane_max(scores, best)

    def value_chunk(j, count, s_ref, top, acc):
        if j < count:
            scores = s_ref[:, j * chunk : (j + 1) * chunk]
            values = vals[j * chunk : (j + 1) * chunk, :]
        else:
            scores = s_ref[:, slots : slots + fresh]
            values = fvals[...]
        weights = jnp.exp2((scores - top) * scale).astype(jnp.bfloat16)
        part = jnp.dot(weights, values, preferred_element_type=jnp.float32)
        return part if acc is None else acc + part

    def stage(t_next, s_next, m_next, t_now, s_now, m_now, count):
        best = None
        acc = None
        if t_now is not None:
            top = jnp.max(m_now[...], axis=1, keepdims=True)
        for j in range(count + 1):
            if t_next is not None:
                best = score_chunk(t_next, j, count, s_next, best)
            if t_now is not None:
                acc = value_chunk(j, count, s_now, top, acc)
        if t_next is not None:
            m_next[...] = best
        if t_now is not None:
            total = acc[:, dim:]
            out = (acc[:, :dim] / total).astype(jnp.bfloat16)
            out_ref[pl.ds(t_now * span, span), :per_source, :] = out.reshape(span, per_source, dim)
            level = top * scale + jnp.log2(total)
            for first in range(0, tile, dim):
                flat = jnp.transpose(level[first : first + dim, :STAT_ROWS])
                high = flat.astype(jnp.bfloat16).astype(jnp.float32)
                mid = (flat - high).astype(jnp.bfloat16).astype(jnp.float32)
                low = flat - high - mid
                which = lax.broadcasted_iota(jnp.int32, flat.shape, 0)
                stats = jnp.where(which == 0, high, jnp.where(which == 1, mid, low)).astype(jnp.bfloat16)
                width = min(per_source, dim)
                for part in range(dim // width):
                    row = first + part * width
                    out_ref[t_now * span + row // per_source, per_source:, :width] = stats[
                        :, part * width : (part + 1) * width
                    ]

    for count in range(slots // chunk + 1):

        @pl.when((valid > (count - 1) * chunk) & (valid <= count * chunk))
        def _(count=count):
            stage(0, s0, m0, None, None, None, count)

            def pair(i, carry):
                stage(2 * i + 1, s1, m1, 2 * i, s0, m0, count)
                stage(jnp.minimum(2 * i + 2, tiles - 1), s0, m0, 2 * i + 1, s1, m1, count)
                return carry

            lax.fori_loop(0, tiles // 2, pair, 0)

    result = pltpu.make_async_copy(out_ref, out_hbm, out_sem)
    result.start()
    result.wait()


def attend(info, head_q, kv_blocks, fresh_k, fresh_v, row_start, row_count, group_size):
    sources, _, dim = head_q.shape
    slots = len(kv_blocks) * kv_blocks[0].shape[1]
    rows = sources * row_count
    fresh = fresh_k.shape[0]
    tile = min(256, rows // 2)
    chunk = min(1024, slots)
    grant = 4 * (2 * tile * (slots + fresh) + 4 * slots * dim + 2 * rows * dim) + SMALL_VMEM
    return pl.pallas_call(
        functools.partial(
            attend_kernel,
            blocks=len(kv_blocks),
            chunk=chunk,
            tile=tile,
            group_size=group_size,
            row_start=row_start,
            row_count=row_count,
        ),
        in_specs=[SMEM_SPEC] + [HBM_SPEC] * (1 + len(kv_blocks)) + [VMEM_SPEC] * 2,
        out_specs=HBM_SPEC,
        scratch_shapes=[
            pltpu.VMEM((sources, row_count, dim), jnp.bfloat16),
            pltpu.VMEM((sources, row_count + STAT_ROWS, dim), jnp.bfloat16),
            pltpu.VMEM((slots, dim), jnp.bfloat16),
            pltpu.VMEM((slots, 2 * dim), jnp.bfloat16),
            pltpu.VMEM((fresh, 2 * dim), jnp.bfloat16),
            pltpu.VMEM((tile, slots + fresh), jnp.float32),
            pltpu.VMEM((tile, slots + fresh), jnp.float32),
            pltpu.VMEM((tile, dim), jnp.float32),
            pltpu.VMEM((tile, dim), jnp.float32),
            pltpu.SemaphoreType.DMA((len(kv_blocks), 2)),
            pltpu.SemaphoreType.DMA,
            pltpu.SemaphoreType.DMA,
        ],
        out_shape=jax.ShapeDtypeStruct((sources, row_count + STAT_ROWS, dim), jnp.bfloat16),
        compiler_params=pltpu.CompilerParams(vmem_limit_bytes=grant),
        cost_estimate=pl.CostEstimate(
            flops=4 * rows * slots * dim,
            bytes_accessed=4 * slots * dim + 4 * rows * dim,
            transcendentals=rows * slots,
        ),
    )(info, head_q, *kv_blocks, fresh_k, fresh_v)


def merge_kernel(part_ref, *refs, group_size):
    out_ref = refs[-1]
    spread, heads, _, dim = part_ref.shape
    local_rows = out_ref.shape[1]
    per_source = local_rows * group_size
    levels = []
    for b in range(spread):
        stats = [
            part_ref[b, h, per_source : per_source + STAT_ROWS, :].astype(jnp.float32) for h in range(heads)
        ]
        levels.append(jnp.concatenate([x[0:1] + x[1:2] + x[2:3] for x in stats], axis=0))
    top = functools.reduce(jnp.maximum, levels)
    weights = [jnp.exp2(level - top) for level in levels]
    total = functools.reduce(jnp.add, weights)
    weights = [jnp.transpose(w / total) for w in weights]
    for h in range(heads):
        mixed = functools.reduce(
            jnp.add,
            [
                w[:per_source, h : h + 1] * part_ref[b, h, :per_source, :].astype(jnp.float32)
                for b, w in enumerate(weights)
            ],
        ).astype(jnp.bfloat16)
        out_ref[0, :, h * group_size : (h + 1) * group_size, :] = mixed.reshape(local_rows, group_size, dim)


def merge(parts, request, requests, local_rows, group_size, earlier):
    heads, dim = parts.shape[1], parts.shape[3]
    rest = [] if earlier is None else [earlier]
    return pl.pallas_call(
        functools.partial(merge_kernel, group_size=group_size),
        grid=(1,),
        in_specs=[pl.BlockSpec(parts.shape, lambda i: (0, 0, 0, 0))]
        + [pl.BlockSpec(memory_space=pl.ANY) for _ in rest],
        out_specs=pl.BlockSpec((1, local_rows, heads * group_size, dim), lambda i: (request, 0, 0, 0)),
        out_shape=jax.ShapeDtypeStruct((requests, local_rows, heads * group_size, dim), jnp.bfloat16),
        input_output_aliases={1: 0} if rest else {},
        compiler_params=pltpu.CompilerParams(vmem_limit_bytes=SMALL_VMEM),
    )(parts, *rest)


def pack_kernel(q_ref, fresh_ref, out_ref):
    requests, local_rows, heads, dim = q_ref.shape
    kv_heads = fresh_ref.shape[0]
    group_size = heads // kv_heads
    rows = requests * local_rows * group_size
    for d in range(out_ref.shape[0]):
        head = d % kv_heads
        out_ref[d, :rows, :] = q_ref[:, :, head * group_size : (head + 1) * group_size, :].reshape(rows, dim)
        out_ref[d, rows:, :] = fresh_ref[head]


def pack(queries, fresh, devices):
    requests, local_rows, heads, dim = queries.shape
    rows = requests * local_rows * (heads // fresh.shape[0]) + fresh.shape[1]
    return pl.pallas_call(
        pack_kernel,
        in_specs=[VMEM_SPEC, VMEM_SPEC],
        out_specs=VMEM_SPEC,
        out_shape=jax.ShapeDtypeStruct((devices, rows, dim), jnp.bfloat16),
        compiler_params=pltpu.CompilerParams(vmem_limit_bytes=SMALL_VMEM),
    )(queries, fresh)


def split_kernel(own_ref, k_ref, v_ref, *refs):
    held = refs[-1]
    held[:, 0] = jnp.swapaxes(k_ref[0], 0, 1)
    held[:, 1] = jnp.swapaxes(v_ref[0], 0, 1)
    for k, out_ref in enumerate(refs[:-1]):
        out_ref[...] = held[own_ref[0] ^ k]


def split_heads(own, cache_k, cache_v, request):
    _, slots, kv_heads, dim = cache_k.shape
    return pl.pallas_call(
        split_kernel,
        grid=(1,),
        in_specs=[SMEM_SPEC] + [pl.BlockSpec((1, slots, kv_heads, dim), lambda i: (request, 0, 0, 0))] * 2,
        out_specs=[pl.BlockSpec((2, slots, dim), lambda i: (0, 0, 0))] * kv_heads,
        out_shape=[jax.ShapeDtypeStruct((2, slots, dim), jnp.bfloat16)] * kv_heads,
        scratch_shapes=[pltpu.VMEM((kv_heads, 2, slots, dim), jnp.bfloat16)],
        compiler_params=pltpu.CompilerParams(vmem_limit_bytes=2 * SMALL_VMEM),
    )(own, cache_k, cache_v)


def attention(queries, new_k, new_v, cache_k, cache_v, cache_len):
    requests, local_rows, heads, head_dim = queries.shape
    slots = cache_k.shape[1]
    kv_heads = cache_k.shape[2]
    group_size = heads // kv_heads
    devices_seq = lax.axis_size("seq")
    seq_index = lax.axis_index("seq")
    spread = devices_seq // kv_heads
    block = seq_index // kv_heads
    own = (seq_index % kv_heads).astype(jnp.int32)
    per_source = local_rows * group_size

    fresh = jnp.transpose(jnp.stack([new_k, new_v]), (3, 0, 1, 2, 4)).reshape(
        kv_heads, 2 * requests * local_rows, head_dim
    )
    head_q = lax.all_to_all(
        pack(queries, fresh, devices_seq), "seq", split_axis=0, concat_axis=0, tiled=True
    )
    head_fresh = head_q[:, requests * per_source :, :].reshape(
        devices_seq, 2, requests, local_rows, head_dim
    )
    head_fresh = jnp.transpose(head_fresh, (1, 2, 0, 3, 4)).reshape(
        2, requests, devices_seq * local_rows, head_dim
    )

    kv_blocks = []
    for r in range(requests):
        parts = split_heads(own[None], cache_k, cache_v, r)
        moved = [lax.ppermute(parts[k], "seq", [(i, i ^ k) for i in range(devices_seq)]) for k in range(1, kv_heads)]
        kv_blocks.append([parts[0]] + moved)

    out = None
    for r in range(requests):
        held = kv_heads * slots
        valid = jnp.clip(cache_len[r] - block * held, 0, held)
        fresh_shift = jnp.where(block == spread - 1, 0, -devices_seq * local_rows)
        info = jnp.stack([valid, fresh_shift, own]).astype(jnp.int32)
        part = attend(
            info, head_q, kv_blocks[r], head_fresh[0, r], head_fresh[1, r], r * per_source, per_source, group_size
        )
        part = lax.all_to_all(part, "seq", split_axis=0, concat_axis=0, tiled=True)
        part = part.reshape(spread, kv_heads, per_source + STAT_ROWS, head_dim)
        out = merge(part, r, requests, local_rows, group_size, out)
    return out


def solution(mesh):
    in_specs = (
        P("groups", "seq", None, None),
        P("groups", "seq", None, None),
        P("groups", "seq", None, None),
        P("groups", "seq", None, None),
        P("groups", "seq", None, None),
        P("groups"),
    )
    out_specs = P("groups", "seq", None, None)
    return jax.shard_map(attention, mesh=mesh, in_specs=in_specs, out_specs=out_specs, check_vma=False)
```

time: 153 us -> 149 us (0.974)
  the two profiles are of different devices: /device:TPU:0 before, /device:TPU:13 now
where the time goes in v4:
time: 149 us
  waiting for transfers between devices  63.5 us (43%)
  Pallas kernels  35.9 us (24%)
  starting transfers between devices  33.4 us (22%)
  local copies, waits for them, and re-layouts  13.5 us (9%)
    ppermute x14, waiting for transfers between devices, attention(): lax.ppermute(parts[k], 'seq', [(i, i ^ k) for i in range(devices_seq)])  44.4 us
    pallas_call x2, Pallas kernels, attend(): pl.pallas_call(functools.partial(attend_kernel, blocks=len(kv_blocks), ch...  28.8 us
    ppermute x14, starting transfers between devices, attention(): lax.ppermute(parts[k], 'seq', [(i, i ^ k) for i in range(devices_seq)])  15.5 us
    all_to_all x2, waiting for transfers between devices, attention(): part = lax.all_to_all(part, 'seq', split_axis=0, concat_axis=0, tiled=True)  13.6 us
    unnamed x32, local copies, waits for them, and re-layouts  12.8 us
    all_to_all x2, starting transfers between devices, attention(): part = lax.all_to_all(part, 'seq', split_axis=0, concat_axis=0, tiled=True)  11.3 us
    all_to_all x1, starting transfers between devices, attention(): lax.all_to_all(pack(queries, fresh, devices_seq), 'seq', split_axis=0, co...  6.55 us
    all_to_all x1, waiting for transfers between devices, attention(): lax.all_to_all(pack(queries, fresh, devices_seq), 'seq', split_axis=0, co...  5.59 us
  transfers between devices with their start and end apart: 17, of which 12 were waited for; matrix products, arithmetic and copies ran while one was open for 1% of the time, Pallas kernels for 13%

profile of v4, /device:TPU:13, one launch (start us, length us, event | category | flops | bytes accessed | tf_op | source)
XLA Modules:
  0.0 148.6 jit_solution(5432630498742946140)
XLA Ops:
  3.1 6.5 %all-to-all-start = ((bf16[16,288,128]{2,1,0:T(8,128)(2,1)}), bf16[16,288,128]{2,1,0:T(8,128)(2,1)S(1)}, u32[]{:S(2)}, u32[]{:S(2)}) async-start(bf16[16,288,128]{2,1,0:T(8,128)(2,1)} %shard_map.64), calls=%async_computation | async-start | bytes 2359296 | tf_op jit(solution)/shard_map/all_to_all | solution.py:284
  9.7 1.6 %copy-done.1 = bf16[2,512,8,128]{3,2,1,0:T(8,128)(2,1)S(1)} copy-done((bf16[2,512,8,128]{3,2,1,0:T(8,128)(2,1)S(1)}, bf16[2,512,8,128]{3,2,1,0:T(8,128)(2,1)}, u32[]{:S(2)}) %copy-start.1) | copy-done | bytes 2097176
  11.3 1.8 %shard_map.67 = (bf16[2,512,128]{2,1,0:T(8,128)(2,1)S(1)}, bf16[2,512,128]{2,1,0:T(8,128)(2,1)}, bf16[2,512,128]{2,1,0:T(8,128)(2,1)}, bf16[2,512,128]{2,1,0:T(8...) custom-call(s32[1]{0:T(128)} %bitcast.3.own_ref, ...), custom_call_target="tpu_custom_call" | custom-call | tf_op jit(solution)/shard_map/pallas_call | solution.py:258
  17.4 1.6 %collective-permute-start.11 = (bf16[2,512,128]{2,1,0:T(8,128)(2,1)}, bf16[2,512,128]{2,1,0:T(8,128)(2,1)}, u32[]{:S(2)}, u32[]{:S(2)}) collective-permute-start(bf16[2,512,128]{2,1,0:T(8,128)(2,1)} %get-tuple-element.34), channel_id=1, source_target_pairs={{0,5},{1,4},{2,7},{3,6},{4,1},{5,0},{6,3},{7,2},{8,13},{9,12},{10,... | collective-permute-start | bytes 786440 | tf_op jit(solution)/shard_map/ppermute | solution.py:297
  22.1 5.6 %collective-permute-done.8.refs_4_ = bf16[2,512,128]{2,1,0:T(8,128)(2,1)} collective-permute-done((bf16[2,512,128]{2,1,0:T(8,128)(2,1)}, bf16[2,512,128]{2,1,0:T(8,128)(2,1)}, u32[]{:S(2)}, u32[]{:S(2)}) %collective-permute-start.8) | collective-permute-done | bytes 262176 | tf_op jit(solution)/shard_map/ppermute | solution.py:297
  27.8 3.9 %collective-permute-start.13 = (bf16[2,512,128]{2,1,0:T(8,128)(2,1)}, bf16[2,512,128]{2,1,0:T(8,128)(2,1)}, u32[]{:S(2)}, u32[]{:S(2)}) collective-permute-start(bf16[2,512,128]{2,1,0:T(8,128)(2,1)} %copy-done.11), channel_id=1, source_target_pairs={{0,7},{1,6},{2,5},{3,4},{4,3},{5,2},{6,1},{7,0},{8,15},{9,14},{10,... | collective-permute-start | bytes 786440 | tf_op jit(solution)/shard_map/ppermute | solution.py:297
  31.7 5.6 %all-to-all-done.refs_1_ = bf16[16,288,128]{2,1,0:T(8,128)(2,1)S(1)} async-done(((bf16[16,288,128]{2,1,0:T(8,128)(2,1)}), bf16[16,288,128]{2,1,0:T(8,128)(2,1)S(1)}, u32[]{:S(2)}, u32[]{:S(2)}) %all-to-all-start) | async-done | bytes 1179680 | tf_op jit(solution)/shard_map/all_to_all | solution.py:284
  37.7 4.1 %collective-permute-done.11.refs_7_ = bf16[2,512,128]{2,1,0:T(8,128)(2,1)} collective-permute-done((bf16[2,512,128]{2,1,0:T(8,128)(2,1)}, bf16[2,512,128]{2,1,0:T(8,128)(2,1)}, u32[]{:S(2)}, u32[]{:S(2)}) %collective-permute-start.11) | collective-permute-done | bytes 262176 | tf_op jit(solution)/shard_map/ppermute | solution.py:297
  41.8 6.1 %collective-permute-done.12.refs_8_ = bf16[2,512,128]{2,1,0:T(8,128)(2,1)} collective-permute-done((bf16[2,512,128]{2,1,0:T(8,128)(2,1)}, bf16[2,512,128]{2,1,0:T(8,128)(2,1)}, u32[]{:S(2)}, u32[]{:S(2)}) %collective-permute-start.12) | collective-permute-done | bytes 262176 | tf_op jit(solution)/shard_map/ppermute | solution.py:297
  47.8 5.9 %collective-permute-done.13.refs_9_ = bf16[2,512,128]{2,1,0:T(8,128)(2,1)} collective-permute-done((bf16[2,512,128]{2,1,0:T(8,128)(2,1)}, bf16[2,512,128]{2,1,0:T(8,128)(2,1)}, u32[]{:S(2)}, u32[]{:S(2)}) %collective-permute-start.13) | collective-permute-done | bytes 262176 | tf_op jit(solution)/shard_map/ppermute | solution.py:297
  55.6 13.9 %shard_map.68 = bf16[16,136,128]{2,1,0:T(8,128)(2,1)S(1)} custom-call(s32[3]{0:T(128)S(1)} %add_add_fusion.1.refs_0_, bf16[16,288,128]{2,1,0:T(8,128)(2,1)S(1)} %all-to-all-done.refs_1_, bf16[2,512,128]{2,1,0:T(8,128)(2,1)S(1)} %copy-done.8, bf16[2,512,128]{2,1,0:T(8,128)(2,1)S(1)} %copy-done.10, bf16[2,512,128]{2,1,0:T(8,128)(2,1)} %collective-permute-done.8.refs_4_, ...), custom_call_target="tpu_custom_call" | custom-call | flops 4294967296 | bytes 3145728 | tf_op jit(solution)/shard_map/pallas_call | solution.py:148
  70.4 4.5 %all-to-all-start.2 = ((bf16[16,136,128]{2,1,0:T(8,128)(2,1)}), bf16[16,136,128]{2,1,0:T(8,128)(2,1)S(1)}, u32[]{:S(2)}, u32[]{:S(2)}) async-start(bf16[16,136,128]{2,1,0:T(8,128)(2,1)} %copy-done.5), calls=%async_computation.2 | async-start | bytes 1114112 | tf_op jit(solution)/shard_map/all_to_all | solution.py:309
  74.9 1.6 %copy-done.2 = bf16[2,512,8,128]{3,2,1,0:T(8,128)(2,1)S(1)} copy-done((bf16[2,512,8,128]{3,2,1,0:T(8,128)(2,1)S(1)}, bf16[2,512,8,128]{3,2,1,0:T(8,128)(2,1)}, u32[]{:S(2)}) %copy-start.2) | copy-done | bytes 2097176
  76.5 1.8 %shard_map.65 = (bf16[2,512,128]{2,1,0:T(8,128)(2,1)S(1)}, bf16[2,512,128]{2,1,0:T(8,128)(2,1)S(1)}, bf16[2,512,128]{2,1,0:T(8,128)(2,1)S(1)}, bf16[2,512,128]{2...) custom-call(s32[1]{0:T(128)} %bitcast.3.own_ref, ...), custom_call_target="tpu_custom_call" | custom-call | tf_op jit(solution)/shard_map/pallas_call | solution.py:258
  81.2 1.6 %collective-permute-start.4 = (bf16[2,512,128]{2,1,0:T(8,128)(2,1)}, bf16[2,512,128]{2,1,0:T(8,128)(2,1)S(1)}, u32[]{:S(2)}, u32[]{:S(2)}) collective-permute-start(bf16[2,512,128]{2,1,0:T(8,128)(2,1)} %get-tuple-element.26), channel_id=1, source_target_pairs={{0,5},{1,4},{2,7},{3,6},{4,1},{5,0},{6,3},{7,2},{8,13},{9,12},{10,... | collective-permute-start | bytes 786440 | tf_op jit(solution)/shard_map/ppermute | solution.py:297
  84.0 6.4 %collective-permute-done.1.refs_4_ = bf16[2,512,128]{2,1,0:T(8,128)(2,1)S(1)} collective-permute-done((bf16[2,512,128]{2,1,0:T(8,128)(2,1)S(1)}, bf16[2,512,128]{2,1,0:T(8,128)(2,1)S(1)}, u32[]{:S(2)}, u32[]{:S(2)}) %collective-permute-start.1) | collective-permute-done | bytes 262176 | tf_op jit(solution)/shard_map/ppermute | solution.py:297
  90.4 1.5 %collective-permute-start.6 = (bf16[2,512,128]{2,1,0:T(8,128)(2,1)}, bf16[2,512,128]{2,1,0:T(8,128)(2,1)S(1)}, u32[]{:S(2)}, u32[]{:S(2)}) collective-permute-start(bf16[2,512,128]{2,1,0:T(8,128)(2,1)} %get-tuple-element.28), channel_id=1, source_target_pairs={{0,7},{1,6},{2,5},{3,4},{4,3},{5,2},{6,1},{7,0},{8,15},{9,14},{10,... | collective-permute-start | bytes 786440 | tf_op jit(solution)/shard_map/ppermute | solution.py:297
  92.6 3.6 %collective-permute-done.2.refs_5_ = bf16[2,512,128]{2,1,0:T(8,128)(2,1)S(1)} collective-permute-done((bf16[2,512,128]{2,1,0:T(8,128)(2,1)}, bf16[2,512,128]{2,1,0:T(8,128)(2,1)S(1)}, u32[]{:S(2)}, u32[]{:S(2)}) %collective-permute-start.2) | collective-permute-done | bytes 262176 | tf_op jit(solution)/shard_map/ppermute | solution.py:297
  96.7 6.0 %collective-permute-done.5.refs_8_ = bf16[2,512,128]{2,1,0:T(8,128)(2,1)S(1)} collective-permute-done((bf16[2,512,128]{2,1,0:T(8,128)(2,1)}, bf16[2,512,128]{2,1,0:T(8,128)(2,1)S(1)}, u32[]{:S(2)}, u32[]{:S(2)}) %collective-permute-start.5) | collective-permute-done | bytes 262176 | tf_op jit(solution)/shard_map/ppermute | solution.py:297
  102.7 5.9 %collective-permute-done.6.refs_9_ = bf16[2,512,128]{2,1,0:T(8,128)(2,1)S(1)} collective-permute-done((bf16[2,512,128]{2,1,0:T(8,128)(2,1)}, bf16[2,512,128]{2,1,0:T(8,128)(2,1)S(1)}, u32[]{:S(2)}, u32[]{:S(2)}) %collective-permute-start.6) | collective-permute-done | bytes 262176 | tf_op jit(solution)/shard_map/ppermute | solution.py:297
  108.6 1.3 copy-done.4
  110.8 14.8 %shard_map.66 = bf16[16,136,128]{2,1,0:T(8,128)(2,1)} custom-call(s32[3]{0:T(128)S(1)} %add_add_fusion.refs_0_, bf16[16,288,128]{2,1,0:T(8,128)(2,1)S(1)} %copy-done.4, bf16[2,512,128]{2,1,0:T(8,128)(2,1)S(1)} %copy-done.14, bf16[2,512,128]{2,1,0:T(8,128)(2,1)S(1)} %collective-permute-done.refs_3_, bf16[2,512,128]{2,1,0:T(8,128)(2,1)S(1)} %collective-permute-done.1.refs_4_, ...), custom_call_target="tpu_custom_call" | custom-call | flops 4294967296 | bytes 3145728 | tf_op jit(solution)/shard_map/pallas_call | solution.py:148
  125.7 6.9 %all-to-all-start.1 = ((bf16[16,136,128]{2,1,0:T(8,128)(2,1)}), bf16[16,136,128]{2,1,0:T(8,128)(2,1)S(1)}, u32[]{:S(2)}, u32[]{:S(2)}) async-start(bf16[16,136,128]{2,1,0:T(8,128)(2,1)} %shard_map.66), calls=%async_computation.1 | async-start | bytes 1114112 | tf_op jit(solution)/shard_map/all_to_all | solution.py:309
  133.8 13.6 %all-to-all-done.1 = bf16[16,136,128]{2,1,0:T(8,128)(2,1)S(1)} async-done(((bf16[16,136,128]{2,1,0:T(8,128)(2,1)}), bf16[16,136,128]{2,1,0:T(8,128)(2,1)S(1)}, u32[]{:S(2)}, u32[]{:S(2)}) %all-to-all-start.1) | async-done | bytes 557088 | tf_op jit(solution)/shard_map/all_to_all | solution.py:309
  (57 shorter events, 21.2 us)
Async XLA Ops:
  0.8 8.9 %copy-start = (bf16[2,512,8,128]{3,2,1,0:T(8,128)(2,1)S(1)}, bf16[2,512,8,128]{3,2,1,0:T(8,128)(2,1)}, u32[]{:S(2)}) copy-start(bf16[2,512,8,128]{3,2,1,0:T(8,128)(2,1)} %k_ref.3) | copy-start | bytes 6291460
  0.8 1.2 copy-start.6
  3.1 34.2 %all-to-all-start = ((bf16[16,288,128]{2,1,0:T(8,128)(2,1)}), bf16[16,288,128]{2,1,0:T(8,128)(2,1)S(1)}, u32[]{:S(2)}, u32[]{:S(2)}) async-start(bf16[16,288,128]{2,1,0:T(8,128)(2,1)} %shard_map.64), calls=%async_computation | async-start | bytes 2359296 | tf_op jit(solution)/shard_map/all_to_all | solution.py:284
  9.7 1.6 %copy-start.1 = (bf16[2,512,8,128]{3,2,1,0:T(8,128)(2,1)S(1)}, bf16[2,512,8,128]{3,2,1,0:T(8,128)(2,1)}, u32[]{:S(2)}) copy-start(bf16[2,512,8,128]{3,2,1,0:T(8,128)(2,1)} %v_ref.3) | copy-start | bytes 6291460
  11.3 7.8 %copy-start.15 = (s32[2]{0:T(128)S(1)}, s32[2]{0:T(128)}, u32[]{:S(2)}) copy-start(s32[2]{0:T(128)} %param.11) | copy-start | bytes 28
  15.2 5.1 %collective-permute-start.7 = (bf16[2,512,128]{2,1,0:T(8,128)(2,1)}, bf16[2,512,128]{2,1,0:T(8,128)(2,1)S(1)}, u32[]{:S(2)}, u32[]{:S(2)}) collective-permute-start(bf16[2,512,128]{2,1,0:T(8,128)(2,1)} %get-tuple-element.30), channel_id=1, source_target_pairs={{0,1},{1,0},{2,3},{3,2},{4,5},{5,4},{6,7},{7,6},{8,9},{9,8},{10,11... | collective-permute-start | bytes 786440 | tf_op jit(solution)/shard_map/ppermute | solution.py:297
  15.6 12.2 %collective-permute-start.8 = (bf16[2,512,128]{2,1,0:T(8,128)(2,1)}, bf16[2,512,128]{2,1,0:T(8,128)(2,1)}, u32[]{:S(2)}, u32[]{:S(2)}) collective-permute-start(bf16[2,512,128]{2,1,0:T(8,128)(2,1)} %get-tuple-element.31), channel_id=1, source_target_pairs={{0,2},{1,3},{2,0},{3,1},{4,6},{5,7},{6,4},{7,5},{8,10},{9,11},{10,... | collective-permute-start | bytes 786440 | tf_op jit(solution)/shard_map/ppermute | solution.py:297
  16.7 20.9 %collective-permute-start.9 = (bf16[2,512,128]{2,1,0:T(8,128)(2,1)}, bf16[2,512,128]{2,1,0:T(8,128)(2,1)}, u32[]{:S(2)}, u32[]{:S(2)}) collective-permute-start(bf16[2,512,128]{2,1,0:T(8,128)(2,1)} %get-tuple-element.32), channel_id=1, source_target_pairs={{0,3},{1,2},{2,1},{3,0},{4,7},{5,6},{6,5},{7,4},{8,11},{9,10},{10,... | collective-permute-start | bytes 786440 | tf_op jit(solution)/shard_map/ppermute | solution.py:297
  17.3 20.4 %collective-permute-start.10 = (bf16[2,512,128]{2,1,0:T(8,128)(2,1)}, bf16[2,512,128]{2,1,0:T(8,128)(2,1)}, u32[]{:S(2)}, u32[]{:S(2)}) collective-permute-start(bf16[2,512,128]{2,1,0:T(8,128)(2,1)} %get-tuple-element.33), channel_id=1, source_target_pairs={{0,4},{1,5},{2,6},{3,7},{4,0},{5,1},{6,2},{7,3},{8,12},{9,13},{10,... | collective-permute-start | bytes 786440 | tf_op jit(solution)/shard_map/ppermute | solution.py:297
  17.4 24.3 %collective-permute-start.11 = (bf16[2,512,128]{2,1,0:T(8,128)(2,1)}, bf16[2,512,128]{2,1,0:T(8,128)(2,1)}, u32[]{:S(2)}, u32[]{:S(2)}) collective-permute-start(bf16[2,512,128]{2,1,0:T(8,128)(2,1)} %get-tuple-element.34), channel_id=1, source_target_pairs={{0,5},{1,4},{2,7},{3,6},{4,1},{5,0},{6,3},{7,2},{8,13},{9,12},{10,... | collective-permute-start | bytes 786440 | tf_op jit(solution)/shard_map/ppermute | solution.py:297
  21.0 26.9 %collective-permute-start.12 = (bf16[2,512,128]{2,1,0:T(8,128)(2,1)}, bf16[2,512,128]{2,1,0:T(8,128)(2,1)}, u32[]{:S(2)}, u32[]{:S(2)}) collective-permute-start(bf16[2,512,128]{2,1,0:T(8,128)(2,1)} %copy-done.12), channel_id=1, source_target_pairs={{0,6},{1,7},{2,4},{3,5},{4,2},{5,3},{6,0},{7,1},{8,14},{9,15},{10,... | collective-permute-start | bytes 786440 | tf_op jit(solution)/shard_map/ppermute | solution.py:297
  27.8 25.9 %collective-permute-start.13 = (bf16[2,512,128]{2,1,0:T(8,128)(2,1)}, bf16[2,512,128]{2,1,0:T(8,128)(2,1)}, u32[]{:S(2)}, u32[]{:S(2)}) collective-permute-start(bf16[2,512,128]{2,1,0:T(8,128)(2,1)} %copy-done.11), channel_id=1, source_target_pairs={{0,7},{1,6},{2,5},{3,4},{4,3},{5,2},{6,1},{7,0},{8,15},{9,14},{10,... | collective-permute-start | bytes 786440 | tf_op jit(solution)/shard_map/ppermute | solution.py:297
  37.3 32.3 %copy-start.3 = (bf16[16,288,128]{2,1,0:T(8,128)(2,1)}, bf16[16,288,128]{2,1,0:T(8,128)(2,1)S(1)}, u32[]{:S(2)}) copy-start(bf16[16,288,128]{2,1,0:T(8,128)(2,1)S(1)} %all-to-all-done.refs_1_) | copy-start | bytes 3538948
  70.4 55.3 %all-to-all-start.2 = ((bf16[16,136,128]{2,1,0:T(8,128)(2,1)}), bf16[16,136,128]{2,1,0:T(8,128)(2,1)S(1)}, u32[]{:S(2)}, u32[]{:S(2)}) async-start(bf16[16,136,128]{2,1,0:T(8,128)(2,1)} %copy-done.5), calls=%async_computation.2 | async-start | bytes 1114112 | tf_op jit(solution)/shard_map/all_to_all | solution.py:309
  74.9 1.6 %copy-start.2 = (bf16[2,512,8,128]{3,2,1,0:T(8,128)(2,1)S(1)}, bf16[2,512,8,128]{3,2,1,0:T(8,128)(2,1)}, u32[]{:S(2)}) copy-start(bf16[2,512,8,128]{3,2,1,0:T(8,128)(2,1)} %v_ref.3) | copy-start | bytes 6291460
  78.9 3.9 %collective-permute-start = (bf16[2,512,128]{2,1,0:T(8,128)(2,1)S(1)}, bf16[2,512,128]{2,1,0:T(8,128)(2,1)S(1)}, u32[]{:S(2)}, u32[]{:S(2)}) collective-permute-start(bf16[2,512,128]{2,1,0:T(8,128)(2,1)S(1)} %get-tuple-element.22), channel_id=1, source_target_pairs={{0,1},{1,0},{2,3},{3,2},{4,5},{5,4},{6,7},{7,6},{8,9},{9,8},{10,11... | collective-permute-start | bytes 786440 | tf_op jit(solution)/shard_map/ppermute | solution.py:297
  79.3 11.1 %collective-permute-start.1 = (bf16[2,512,128]{2,1,0:T(8,128)(2,1)S(1)}, bf16[2,512,128]{2,1,0:T(8,128)(2,1)S(1)}, u32[]{:S(2)}, u32[]{:S(2)}) collective-permute-start(bf16[2,512,128]{2,1,0:T(8,128)(2,1)S(1)} %get-tuple-element.23), channel_id=1, source_target_pairs={{0,2},{1,3},{2,0},{3,1},{4,6},{5,7},{6,4},{7,5},{8,10},{9,11},{10,... | collective-permute-start | bytes 786440 | tf_op jit(solution)/shard_map/ppermute | solution.py:297
  80.5 15.7 %collective-permute-start.2 = (bf16[2,512,128]{2,1,0:T(8,128)(2,1)}, bf16[2,512,128]{2,1,0:T(8,128)(2,1)S(1)}, u32[]{:S(2)}, u32[]{:S(2)}) collective-permute-start(bf16[2,512,128]{2,1,0:T(8,128)(2,1)} %get-tuple-element.24), channel_id=1, source_target_pairs={{0,3},{1,2},{2,1},{3,0},{4,7},{5,6},{6,5},{7,4},{8,11},{9,10},{10,... | collective-permute-start | bytes 786440 | tf_op jit(solution)/shard_map/ppermute | solution.py:297
  81.1 15.2 %collective-permute-start.3 = (bf16[2,512,128]{2,1,0:T(8,128)(2,1)}, bf16[2,512,128]{2,1,0:T(8,128)(2,1)S(1)}, u32[]{:S(2)}, u32[]{:S(2)}) collective-permute-start(bf16[2,512,128]{2,1,0:T(8,128)(2,1)} %get-tuple-element.25), channel_id=1, source_target_pairs={{0,4},{1,5},{2,6},{3,7},{4,0},{5,1},{6,2},{7,3},{8,12},{9,13},{10,... | collective-permute-start | bytes 786440 | tf_op jit(solution)/shard_map/ppermute | solution.py:297
  81.2 15.5 %collective-permute-start.4 = (bf16[2,512,128]{2,1,0:T(8,128)(2,1)}, bf16[2,512,128]{2,1,0:T(8,128)(2,1)S(1)}, u32[]{:S(2)}, u32[]{:S(2)}) collective-permute-start(bf16[2,512,128]{2,1,0:T(8,128)(2,1)} %get-tuple-element.26), channel_id=1, source_target_pairs={{0,5},{1,4},{2,7},{3,6},{4,1},{5,0},{6,3},{7,2},{8,13},{9,12},{10,... | collective-permute-start | bytes 786440 | tf_op jit(solution)/shard_map/ppermute | solution.py:297
  82.8 19.9 %collective-permute-start.5 = (bf16[2,512,128]{2,1,0:T(8,128)(2,1)}, bf16[2,512,128]{2,1,0:T(8,128)(2,1)S(1)}, u32[]{:S(2)}, u32[]{:S(2)}) collective-permute-start(bf16[2,512,128]{2,1,0:T(8,128)(2,1)} %get-tuple-element.27), channel_id=1, source_target_pairs={{0,6},{1,7},{2,4},{3,5},{4,2},{5,3},{6,0},{7,1},{8,14},{9,15},{10,... | collective-permute-start | bytes 786440 | tf_op jit(solution)/shard_map/ppermute | solution.py:297
  90.4 18.2 %collective-permute-start.6 = (bf16[2,512,128]{2,1,0:T(8,128)(2,1)}, bf16[2,512,128]{2,1,0:T(8,128)(2,1)S(1)}, u32[]{:S(2)}, u32[]{:S(2)}) collective-permute-start(bf16[2,512,128]{2,1,0:T(8,128)(2,1)} %get-tuple-element.28), channel_id=1, source_target_pairs={{0,7},{1,6},{2,5},{3,4},{4,3},{5,2},{6,1},{7,0},{8,15},{9,14},{10,... | collective-permute-start | bytes 786440 | tf_op jit(solution)/shard_map/ppermute | solution.py:297
  108.6 1.3 copy-start.4
  125.7 21.7 %all-to-all-start.1 = ((bf16[16,136,128]{2,1,0:T(8,128)(2,1)}), bf16[16,136,128]{2,1,0:T(8,128)(2,1)S(1)}, u32[]{:S(2)}, u32[]{:S(2)}) async-start(bf16[16,136,128]{2,1,0:T(8,128)(2,1)} %shard_map.66), calls=%async_computation.1 | async-start | bytes 1114112 | tf_op jit(solution)/shard_map/all_to_all | solution.py:309
  (9 other events, 7.2 us)

commit v5 on v4

--- a/solution.py
+++ b/solution.py
@@ -19,16 +19,28 @@
 SMEM_SPEC = pl.BlockSpec(memory_space=pltpu.SMEM)
 
 
-def attend_kernel(*refs, blocks, chunk, tile, group_size, row_start, row_count):
-    info_ref, q_hbm = refs[:2]
-    kv_refs = refs[2 : 2 + blocks]
-    fk_ref, fv_ref, out_hbm, q_ref, out_ref, keys, vals, fvals, s0, s1, m0, m1, in_sems, q_sem, out_sem = refs[
-        2 + blocks :
-    ]
-    per_source, dim = row_count, q_ref.shape[2]
+def attend_kernel(*refs, order, total_blocks, tile, group_size, row_start, with_fresh, with_state, final):
+    refs = list(refs)
+    info_ref, q_hbm = refs.pop(0), refs.pop(0)
+    kv_refs = [refs.pop(0) for _ in order]
+    if with_fresh:
+        fk_ref, fv_ref = refs.pop(0), refs.pop(0)
+    if with_state:
+        acc_in, top_in = refs.pop(0), refs.pop(0)
+    if final:
+        out_hbm = refs.pop(0)
+    else:
+        acc_out, top_out = refs.pop(0), refs.pop(0)
+    if final:
+        out_ref, out_sem = refs.pop(), refs.pop()
+    if with_fresh:
+        fvals = refs.pop()
+    q_ref, keys, vals, s0, s1, m0, m1, in_sems, q_sem = refs
+    per_source, dim = q_ref.shape[1:]
     block_slots = kv_refs[0].shape[1]
-    slots = blocks * block_slots
-    fresh = fk_ref.shape[0]
+    chunk = 2 * block_slots
+    chunks = len(order) // 2
+    slots = chunks * chunk
     rows = q_ref.shape[0] * per_source
     tiles = rows // tile
     span = tile // per_source
@@ -37,18 +49,36 @@
     fresh_shift = info_ref[1]
     own = info_ref[2]
 
-    copies = [
-        pltpu.make_async_copy(q_hbm.at[:, row_start : row_start + row_count, :], q_ref, q_sem),
-    ]
-    for k, kv_ref in enumerate(kv_refs):
-        at = pl.ds(pl.multiple_of((own ^ k) * block_slots, block_slots), block_slots)
-        copies.append(pltpu.make_async_copy(kv_ref.at[0], keys.at[at, :], in_sems.at[k, 0]))
-        copies.append(pltpu.make_async_copy(kv_ref.at[1], vals.at[at, :dim], in_sems.at[k, 1]))
+    held = sorted({k // 2 for k in order})
+    absent = [c for c in range(total_blocks // 2) if c not in held]
+
+    def rank_of(index):
+        rank = index
+        for c in absent:
+            rank = rank - jnp.where((own // 2) ^ c < index, 1, 0)
+        return rank
+
+    copies = [pltpu.make_async_copy(q_hbm.at[:, row_start : row_start + per_source, :], q_ref, q_sem)]
+    for i, k in enumerate(order):
+        first = rank_of((own // 2) ^ (k // 2)) * chunk + ((own % 2) ^ (k % 2)) * block_slots
+        at = pl.ds(pl.multiple_of(first, block_slots), block_slots)
+        copies.append(pltpu.make_async_copy(kv_refs[i].at[0], keys.at[at, :], in_sems.at[i, 0]))
+        copies.append(pltpu.make_async_copy(kv_refs[i].at[1], vals.at[at, :dim], in_sems.at[i, 1]))
     for copy in copies:
         copy.start()
     vals[:, dim:] = jnp.ones((slots, dim), jnp.bfloat16)
-    fvals[:, :dim] = fv_ref[...]
-    fvals[:, dim:] = jnp.ones((fresh, dim), jnp.bfloat16)
+    if with_fresh:
+        fresh = fk_ref.shape[0]
+        fvals[:, :dim] = fv_ref[...]
+        fvals[:, dim:] = jnp.ones((fresh, dim), jnp.bfloat16)
+
+    filled = jnp.int32(0)
+    last_valid = jnp.int32(0)
+    for c in held:
+        left = valid - ((own // 2) ^ c) * chunk
+        filled = filled + jnp.where(left > 0, 1, 0)
+        last_valid = jnp.where((left > 0) & (left < chunk), left, last_valid)
+    last_valid = jnp.where(last_valid == 0, chunk, last_valid)
     for copy in copies:
         copy.wait()
 
@@ -66,8 +96,8 @@
         if j < count:
             scores = product(q, keys[j * chunk : (j + 1) * chunk, :])
             if j == count - 1:
-                pos = j * chunk + lax.broadcasted_iota(jnp.int32, (1, chunk), 1)
-                scores = scores + jnp.where(pos < valid, 0.0, NEG)
+                pos = lax.broadcasted_iota(jnp.int32, (1, chunk), 1)
+                scores = scores + jnp.where(pos < last_valid, 0.0, NEG)
             s_ref[:, j * chunk : (j + 1) * chunk] = scores
             return lane_max(scores, best)
         scores = product(q, fk_ref[...])
@@ -88,40 +118,53 @@
         part = jnp.dot(weights, values, preferred_element_type=jnp.float32)
         return part if acc is None else acc + part
 
+    def finish(t, top, acc):
+        total = acc[:, dim:]
+        out = (acc[:, :dim] / total).astype(jnp.bfloat16)
+        out_ref[pl.ds(t * span, span), :per_source, :] = out.reshape(span, per_source, dim)
+        level = top * scale + jnp.log2(total)
+        for first in range(0, tile, dim):
+            flat = jnp.transpose(level[first : first + dim, :STAT_ROWS])
+            high = flat.astype(jnp.bfloat16).astype(jnp.float32)
+            mid = (flat - high).astype(jnp.bfloat16).astype(jnp.float32)
+            low = flat - high - mid
+            which = lax.broadcasted_iota(jnp.int32, flat.shape, 0)
+            stats = jnp.where(which == 0, high, jnp.where(which == 1, mid, low)).astype(jnp.bfloat16)
+            width = min(per_source, dim)
+            for part in range(dim // width):
+                row = first + part * width
+                out_ref[t * span + row // per_source, per_source:, :width] = stats[
+                    :, part * width : (part + 1) * width
+                ]
+
     def stage(t_next, s_next, m_next, t_now, s_now, m_now, count):
+        pieces = count + (1 if with_fresh else 0)
         best = None
         acc = None
         if t_now is not None:
-            top = jnp.max(m_now[...], axis=1, keepdims=True)
-        for j in range(count + 1):
+            at = pl.ds(pl.multiple_of(t_now * tile, tile), tile)
+            top = jnp.max(m_now[...], axis=1, keepdims=True) if pieces else None
+            if with_state:
+                before = top_in[at, :1]
+                top = before if top is None else jnp.maximum(top, before)
+                acc = acc_in[at, :] * jnp.exp2((before - top) * scale)
+        for j in range(pieces):
             if t_next is not None:
                 best = score_chunk(t_next, j, count, s_next, best)
             if t_now is not None:
                 acc = value_chunk(j, count, s_now, top, acc)
-        if t_next is not None:
+        if t_next is not None and pieces:
             m_next[...] = best
         if t_now is not None:
-            total = acc[:, dim:]
-            out = (acc[:, :dim] / total).astype(jnp.bfloat16)
-            out_ref[pl.ds(t_now * span, span), :per_source, :] = out.reshape(span, per_source, dim)
-            level = top * scale + jnp.log2(total)
-            for first in range(0, tile, dim):
-                flat = jnp.transpose(level[first : first + dim, :STAT_ROWS])
-                high = flat.astype(jnp.bfloat16).astype(jnp.float32)
-                mid = (flat - high).astype(jnp.bfloat16).astype(jnp.float32)
-                low = flat - high - mid
-                which = lax.broadcasted_iota(jnp.int32, flat.shape, 0)
-                stats = jnp.where(which == 0, high, jnp.where(which == 1, mid, low)).astype(jnp.bfloat16)
-                width = min(per_source, dim)
-                for part in range(dim // width):
-                    row = first + part * width
-                    out_ref[t_now * span + row // per_source, per_source:, :width] = stats[
-                        :, part * width : (part + 1) * width
-                    ]
-
-    for count in range(slots // chunk + 1):
-
-        @pl.when((valid > (count - 1) * chunk) & (valid <= count * chunk))
+            if final:
+                finish(t_now, top, acc)
+            else:
+                acc_out[at, :] = acc
+                top_out[at, :] = jnp.broadcast_to(top, (tile, dim))
+
+    for count in range(chunks + 1):
+
+        @pl.when(filled == count)
         def _(count=count):
             stage(0, s0, m0, None, None, None, count)
 
@@ -132,53 +175,72 @@
 
             lax.fori_loop(0, tiles // 2, pair, 0)
 
-    result = pltpu.make_async_copy(out_ref, out_hbm, out_sem)
-    result.start()
-    result.wait()
-
-
-def attend(info, head_q, kv_blocks, fresh_k, fresh_v, row_start, row_count, group_size):
+    if final:
+        result = pltpu.make_async_copy(out_ref, out_hbm, out_sem)
+        result.start()
+        result.wait()
+
+
+def attend(info, head_q, kv_blocks, order, fresh, state, final, row_start, row_count, group_size):
     sources, _, dim = head_q.shape
-    slots = len(kv_blocks) * kv_blocks[0].shape[1]
+    slots = len(order) * kv_blocks[0].shape[1]
     rows = sources * row_count
-    fresh = fresh_k.shape[0]
+    units = 0 if fresh is None else fresh[0].shape[0]
     tile = min(256, rows // 2)
-    chunk = min(1024, slots)
-    grant = 4 * (2 * tile * (slots + fresh) + 4 * slots * dim + 2 * rows * dim) + SMALL_VMEM
+    operands = [info, head_q] + [kv_blocks[k] for k in order]
+    in_specs = [SMEM_SPEC] + [HBM_SPEC] * (1 + len(order))
+    scratch = [
+        pltpu.VMEM((sources, row_count, dim), jnp.bfloat16),
+        pltpu.VMEM((slots, dim), jnp.bfloat16),
+        pltpu.VMEM((slots, 2 * dim), jnp.bfloat16),
+        pltpu.VMEM((tile, slots + units), jnp.float32),
+        pltpu.VMEM((tile, slots + units), jnp.float32),
+        pltpu.VMEM((tile, dim), jnp.float32),
+        pltpu.VMEM((tile, dim), jnp.float32),
+        pltpu.SemaphoreType.DMA((len(order), 2)),
+        pltpu.SemaphoreType.DMA,
+    ]
+    if fresh is not None:
+        operands += list(fresh)
+        in_specs += [VMEM_SPEC] * 2
+        scratch.append(pltpu.VMEM((units, 2 * dim), jnp.bfloat16))
+    if state is not None:
+        operands += list(state)
+        in_specs += [VMEM_SPEC] * 2
+    if final:
+        out_shape = jax.ShapeDtypeStruct((sources, row_count + STAT_ROWS, dim), jnp.bfloat16)
+        out_specs = HBM_SPEC
+        scratch += [pltpu.SemaphoreType.DMA, pltpu.VMEM(out_shape.shape, jnp.bfloat16)]
+    else:
+        out_shape = [
+            jax.ShapeDtypeStruct((rows, 2 * dim), jnp.float32),
+            jax.ShapeDtypeStruct((rows, dim), jnp.float32),
+        ]
+        out_specs = [VMEM_SPEC] * 2
+    grant = 8 * tile * (slots + units) + 6 * slots * dim + 24 * rows * dim + SMALL_VMEM
     return pl.pallas_call(
         functools.partial(
             attend_kernel,
-            blocks=len(kv_blocks),
-            chunk=chunk,
+            order=order,
+            total_blocks=len(kv_blocks),
             tile=tile,
             group_size=group_size,
             row_start=row_start,
-            row_count=row_count,
+            with_fresh=fresh is not None,
+            with_state=state is not None,
+            final=final,
         ),
-        in_specs=[SMEM_SPEC] + [HBM_SPEC] * (1 + len(kv_blocks)) + [VMEM_SPEC] * 2,
-        out_specs=HBM_SPEC,
-        scratch_shapes=[
-            pltpu.VMEM((sources, row_count, dim), jnp.bfloat16),
-            pltpu.VMEM((sources, row_count + STAT_ROWS, dim), jnp.bfloat16),
-            pltpu.VMEM((slots, dim), jnp.bfloat16),
-            pltpu.VMEM((slots, 2 * dim), jnp.bfloat16),
-            pltpu.VMEM((fresh, 2 * dim), jnp.bfloat16),
-            pltpu.VMEM((tile, slots + fresh), jnp.float32),
-            pltpu.VMEM((tile, slots + fresh), jnp.float32),
-            pltpu.VMEM((tile, dim), jnp.float32),
-            pltpu.VMEM((tile, dim), jnp.float32),
-            pltpu.SemaphoreType.DMA((len(kv_blocks), 2)),
-            pltpu.SemaphoreType.DMA,
-            pltpu.SemaphoreType.DMA,
-        ],
-        out_shape=jax.ShapeDtypeStruct((sources, row_count + STAT_ROWS, dim), jnp.bfloat16),
+        in_specs=in_specs,
+        out_specs=out_specs,
+        scratch_shapes=scratch,
+        out_shape=out_shape,
         compiler_params=pltpu.CompilerParams(vmem_limit_bytes=grant),
         cost_estimate=pl.CostEstimate(
             flops=4 * rows * slots * dim,
             bytes_accessed=4 * slots * dim + 4 * rows * dim,
             transcendentals=rows * slots,
         ),
-    )(info, head_q, *kv_blocks, fresh_k, fresh_v)
+    )(*operands)
 
 
 def merge_kernel(part_ref, *refs, group_size):
@@ -245,23 +307,32 @@
     )(queries, fresh)
 
 
-def split_kernel(own_ref, k_ref, v_ref, *refs):
-    held = refs[-1]
-    held[:, 0] = jnp.swapaxes(k_ref[0], 0, 1)
-    held[:, 1] = jnp.swapaxes(v_ref[0], 0, 1)
-    for k, out_ref in enumerate(refs[:-1]):
+def split_kernel(own_ref, k_hbm, v_hbm, *refs, request):
+    loaded, held, sems = refs[-3:]
+    copies = [
+        pltpu.make_async_copy(hbm.at[request], loaded.at[i], sems.at[i]) for i, hbm in enumerate((k_hbm, v_hbm))
+    ]
+    for copy in copies:
+        copy.start()
+    for i, copy in enumerate(copies):
+        copy.wait()
+        held[:, i] = jnp.swapaxes(loaded[i], 0, 1)
+    for k, out_ref in enumerate(refs[:-3]):
         out_ref[...] = held[own_ref[0] ^ k]
 
 
 def split_heads(own, cache_k, cache_v, request):
     _, slots, kv_heads, dim = cache_k.shape
     return pl.pallas_call(
-        split_kernel,
-        grid=(1,),
-        in_specs=[SMEM_SPEC] + [pl.BlockSpec((1, slots, kv_heads, dim), lambda i: (request, 0, 0, 0))] * 2,
-        out_specs=[pl.BlockSpec((2, slots, dim), lambda i: (0, 0, 0))] * kv_heads,
+        functools.partial(split_kernel, request=request),
+        in_specs=[SMEM_SPEC, HBM_SPEC, HBM_SPEC],
+        out_specs=[VMEM_SPEC] * kv_heads,
         out_shape=[jax.ShapeDtypeStruct((2, slots, dim), jnp.bfloat16)] * kv_heads,
-        scratch_shapes=[pltpu.VMEM((kv_heads, 2, slots, dim), jnp.bfloat16)],
+        scratch_shapes=[
+            pltpu.VMEM((2, slots, kv_heads, dim), jnp.bfloat16),
+            pltpu.VMEM((kv_heads, 2, slots, dim), jnp.bfloat16),
+            pltpu.SemaphoreType.DMA((2,)),
+        ],
         compiler_params=pltpu.CompilerParams(vmem_limit_bytes=2 * SMALL_VMEM),
     )(own, cache_k, cache_v)
 
@@ -291,11 +362,14 @@
         2, requests, devices_seq * local_rows, head_dim
     )
 
+    early = kv_heads - 2
     kv_blocks = []
     for r in range(requests):
         parts = split_heads(own[None], cache_k, cache_v, r)
-        moved = [lax.ppermute(parts[k], "seq", [(i, i ^ k) for i in range(devices_seq)]) for k in range(1, kv_heads)]
-        kv_blocks.append([parts[0]] + moved)
+        moved = [parts[0]]
+        for k in range(1, kv_heads):
+            moved.append(lax.ppermute(parts[k], "seq", [(i, i ^ k) for i in range(devices_seq)]))
+        kv_blocks.append(moved)
 
     out = None
     for r in range(requests):
@@ -303,9 +377,11 @@
         valid = jnp.clip(cache_len[r] - block * held, 0, held)
         fresh_shift = jnp.where(block == spread - 1, 0, -devices_seq * local_rows)
         info = jnp.stack([valid, fresh_shift, own]).astype(jnp.int32)
-        part = attend(
-            info, head_q, kv_blocks[r], head_fresh[0, r], head_fresh[1, r], r * per_source, per_source, group_size
+        rows = (r * per_source, per_source, group_size)
+        state = attend(
+            info, head_q, kv_blocks[r], tuple(range(early)), (head_fresh[0, r], head_fresh[1, r]), None, False, *rows
         )
+        part = attend(info, head_q, kv_blocks[r], tuple(range(early, kv_heads)), None, state, True, *rows)
         part = lax.all_to_all(part, "seq", split_axis=0, concat_axis=0, tiled=True)
         part = part.reshape(spread, kv_heads, per_source + STAT_ROWS, head_dim)
         out = merge(part, r, requests, local_rows, group_size, out)

time: 149 us -> 136 us (0.913)
  waiting for transfers between devices: 63.5 us -> 39.3 us
  local copies, waits for them, and re-layouts: 13.5 us -> 22.1 us
  Pallas kernels: 35.9 us -> 41.2 us
  starting transfers between devices: 33.4 us -> 30 us
    ppermute x14, waiting for transfers between devices: 44.4 us -> 10.2 us  [attention(): lax.ppermute(parts[k], 'seq', [(i, i ^ k) for i in range(devices_seq)])]
    all_to_all x1, waiting for transfers between devices: 5.59 us -> 16.7 us  [attention(): lax.all_to_all(pack(queries, fresh, devices_seq), 'seq', split_axis=0, co...]
    unnamed x32 -> x52, local copies, waits for them, and re-layouts: 12.8 us -> 21.4 us
    pallas_call x4 -> x6, Pallas kernels: 32.3 us -> 37.5 us  [the longest x4 33.6 us: attend(): pl.pallas_call(functools.partial(attend_kernel, order=order, total_blocks...]
    ppermute x14, starting transfers between devices: 15.5 us -> 12.8 us  [attention(): lax.ppermute(parts[k], 'seq', [(i, i ^ k) for i in range(devices_seq)])]
  transfers between devices with their start and end apart: 17 -> 17, of which waited for: 12 -> 6; matrix products, arithmetic and copies ran while one was open for 1% -> 1% of each run, Pallas kernels for 13% -> 25%
where the time goes in v5:
time: 136 us; the launch traced here: 135 us
  Pallas kernels  41.2 us (30%)
  waiting for transfers between devices  39.3 us (29%)
  starting transfers between devices  30 us (22%)
  local copies, waits for them, and re-layouts  22.1 us (16%)
  between operations  1.53 us (1%)
    pallas_call x4, Pallas kernels, attend(): pl.pallas_call(functools.partial(attend_kernel, order=order, total_blocks...  33.6 us
    unnamed x52, local copies, waits for them, and re-layouts  21.4 us
    all_to_all x1, waiting for transfers between devices, attention(): lax.all_to_all(pack(queries, fresh, devices_seq), 'seq', split_axis=0, co...  16.7 us
    ppermute x14, starting transfers between devices, attention(): lax.ppermute(parts[k], 'seq', [(i, i ^ k) for i in range(devices_seq)])  12.8 us
    all_to_all x2, waiting for transfers between devices, attention(): part = lax.all_to_all(part, 'seq', split_axis=0, concat_axis=0, tiled=True)  12.5 us
    all_to_all x2, starting transfers between devices, attention(): part = lax.all_to_all(part, 'seq', split_axis=0, concat_axis=0, tiled=True)  10.6 us
    ppermute x14, waiting for transfers between devices, attention(): lax.ppermute(parts[k], 'seq', [(i, i ^ k) for i in range(devices_seq)])  10.2 us
    all_to_all x1, starting transfers between devices, attention(): lax.all_to_all(pack(queries, fresh, devices_seq), 'seq', split_axis=0, co...  6.55 us
  transfers between devices with their start and end apart: 17, of which 6 were waited for; matrix products, arithmetic and copies ran while one was open for 1% of the time, Pallas kernels for 25%

profile of v5, /device:TPU:13, one launch (start us, length us, event | category | flops | bytes accessed | tf_op | source)
XLA Modules:
  0.0 135.1 jit_solution(17760539877771680354)
XLA Ops:
  3.1 6.5 %all-to-all-start = ((bf16[16,288,128]{2,1,0:T(8,128)(2,1)}), bf16[16,288,128]{2,1,0:T(8,128)(2,1)S(1)}, u32[]{:S(2)}, u32[]{:S(2)}) async-start(bf16[16,288,128]{2,1,0:T(8,128)(2,1)} %copy-done.3), calls=%async_computation | async-start | bytes 2359296 | tf_op jit(solution)/shard_map/all_to_all | solution.py:355
  9.7 1.6 %copy-done.1 = bf16[2,512,8,128]{3,2,1,0:T(8,128)(2,1)S(1)} copy-done((bf16[2,512,8,128]{3,2,1,0:T(8,128)(2,1)S(1)}, bf16[2,512,8,128]{3,2,1,0:T(8,128)(2,1)}, u32[]{:S(2)}) %copy-start.1) | copy-done | bytes 2097176
  11.3 2.0 %shard_map.68 = (bf16[2,512,128]{2,1,0:T(8,128)(2,1)S(1)}, bf16[2,512,128]{2,1,0:T(8,128)(2,1)}, bf16[2,512,128]{2,1,0:T(8,128)(2,1)}, bf16[2,512,128]{2,1,0:T(8...) custom-call(s32[1]{0:T(128)} %bitcast.3.own_ref, ...), custom_call_target="tpu_custom_call" | custom-call | tf_op jit(solution)/shard_map/pallas_call | solution.py:326
  15.8 1.2 collective-permute-start.10
  17.7 1.6 %collective-permute-start.13 = (bf16[2,512,128]{2,1,0:T(8,128)(2,1)}, bf16[2,512,128]{2,1,0:T(8,128)(2,1)}, u32[]{:S(2)}, u32[]{:S(2)}) collective-permute-start(bf16[2,512,128]{2,1,0:T(8,128)(2,1)} %get-tuple-element.42), channel_id=1, source_target_pairs={{0,5},{1,4},{2,7},{3,6},{4,1},{5,0},{6,3},{7,2},{8,13},{9,12},{10,... | collective-permute-start | bytes 786440 | tf_op jit(solution)/shard_map/ppermute | solution.py:371
  20.7 16.7 %all-to-all-done.refs_1_ = bf16[16,288,128]{2,1,0:T(8,128)(2,1)S(1)} async-done(((bf16[16,288,128]{2,1,0:T(8,128)(2,1)}), bf16[16,288,128]{2,1,0:T(8,128)(2,1)S(1)}, u32[]{:S(2)}, u32[]{:S(2)}) %all-to-all-start) | async-done | bytes 1179680 | tf_op jit(solution)/shard_map/all_to_all | solution.py:355
  37.5 2.2 %collective-permute-start.8 = (bf16[2,512,128]{2,1,0:T(8,128)(2,1)}, bf16[2,512,128]{2,1,0:T(8,128)(2,1)S(1)}, u32[]{:S(2)}, u32[]{:S(2)}) collective-permute-start(bf16[2,512,128]{2,1,0:T(8,128)(2,1)} %copy-done.7), channel_id=1, source_target_pairs={{0,7},{1,6},{2,5},{3,4},{4,3},{5,2},{6,1},{7,0},{8,15},{9,14},{10,... | collective-permute-start | bytes 786440 | tf_op jit(solution)/shard_map/ppermute | solution.py:371
  39.7 2.0 %collective-permute-done.13.refs_7_ = bf16[2,512,128]{2,1,0:T(8,128)(2,1)} collective-permute-done((bf16[2,512,128]{2,1,0:T(8,128)(2,1)}, bf16[2,512,128]{2,1,0:T(8,128)(2,1)}, u32[]{:S(2)}, u32[]{:S(2)}) %collective-permute-start.13) | collective-permute-done | bytes 262176 | tf_op jit(solution)/shard_map/ppermute | solution.py:371
  42.6 10.7 %shard_map.69 = (f32[2048,256]{1,0:T(8,128)S(1)}, f32[2048,128]{1,0:T(8,128)S(1)}) custom-call(s32[3]{0:T(128)S(1)} %add_add_fusion.1.refs_0_, bf16[16,288,128]{2,1,0:T(8,128)(2,1)S(1)} %all-to-all-done.refs_1_, bf16[2,512,128]{2,1,0:T(8,128)(2,1)S(1)} %copy-done.10, bf16[2,512,128]{2,1,0:T(8,128)(2,1)} %collective-permute-done.9.refs_3_, ...), custom_call_target="tpu_custom_call" | custom-call | flops 3221225472 | bytes 2621440 | tf_op jit(solution)/shard_map/pallas_call | solution.py:221
  53.6 5.9 %shard_map.70 = bf16[16,136,128]{2,1,0:T(8,128)(2,1)S(1)} custom-call(s32[3]{0:T(128)S(1)} %add_add_fusion.1.refs_0_, bf16[16,288,128]{2,1,0:T(8,128)(2,1)S(1)} %all-to-all-done.refs_1_, bf16[2,512,128]{2,1,0:T(8,128)(2,1)S(1)} %collective-permute-done.7.refs_2_, bf16[2,512,128]{2,1,0:T(8,128)(2,1)S(1)} %collective-permute-done.8.refs_3_, ...), custom_call_target="tpu_custom_call" | custom-call | flops 1073741824 | bytes 1572864 | tf_op jit(solution)/shard_map/pallas_call | solution.py:221
  60.4 5.1 %all-to-all-start.2 = ((bf16[16,136,128]{2,1,0:T(8,128)(2,1)}), bf16[16,136,128]{2,1,0:T(8,128)(2,1)}, u32[]{:S(2)}, u32[]{:S(2)}) async-start(bf16[16,136,128]{2,1,0:T(8,128)(2,1)} %copy-done.4), calls=%async_computation.2 | async-start | bytes 1114112 | tf_op jit(solution)/shard_map/all_to_all | solution.py:385
  65.5 1.6 %copy-done.2 = bf16[2,512,8,128]{3,2,1,0:T(8,128)(2,1)S(1)} copy-done((bf16[2,512,8,128]{3,2,1,0:T(8,128)(2,1)S(1)}, bf16[2,512,8,128]{3,2,1,0:T(8,128)(2,1)}, u32[]{:S(2)}) %copy-start.2) | copy-done | bytes 2097176
  67.0 1.9 %shard_map.65 = (bf16[2,512,128]{2,1,0:T(8,128)(2,1)S(1)}, bf16[2,512,128]{2,1,0:T(8,128)(2,1)}, bf16[2,512,128]{2,1,0:T(8,128)(2,1)}, bf16[2,512,128]{2,1,0:T(8...) custom-call(s32[1]{0:T(128)} %bitcast.3.own_ref, ...), custom_call_target="tpu_custom_call" | custom-call | tf_op jit(solution)/shard_map/pallas_call | solution.py:326
  73.7 1.3 collective-permute-start.6
  76.4 1.2 collective-permute-start
  77.7 4.4 %collective-permute-done.3.refs_4_ = bf16[2,512,128]{2,1,0:T(8,128)(2,1)S(1)} collective-permute-done((bf16[2,512,128]{2,1,0:T(8,128)(2,1)}, bf16[2,512,128]{2,1,0:T(8,128)(2,1)S(1)}, u32[]{:S(2)}, u32[]{:S(2)}) %collective-permute-start.3) | collective-permute-done | bytes 262176 | tf_op jit(solution)/shard_map/ppermute | solution.py:371
  82.7 1.6 %collective-permute-start.1 = (bf16[2,512,128]{2,1,0:T(8,128)(2,1)}, bf16[2,512,128]{2,1,0:T(8,128)(2,1)S(1)}, u32[]{:S(2)}, u32[]{:S(2)}) collective-permute-start(bf16[2,512,128]{2,1,0:T(8,128)(2,1)} %copy-done.11), channel_id=1, source_target_pairs={{0,7},{1,6},{2,5},{3,4},{4,3},{5,2},{6,1},{7,0},{8,15},{9,14},{10,... | collective-permute-start | bytes 786440 | tf_op jit(solution)/shard_map/ppermute | solution.py:371
  84.3 3.5 %collective-permute-done.4.refs_5_ = bf16[2,512,128]{2,1,0:T(8,128)(2,1)S(1)} collective-permute-done((bf16[2,512,128]{2,1,0:T(8,128)(2,1)}, bf16[2,512,128]{2,1,0:T(8,128)(2,1)S(1)}, u32[]{:S(2)}, u32[]{:S(2)}) %collective-permute-start.4) | collective-permute-done | bytes 262176 | tf_op jit(solution)/shard_map/ppermute | solution.py:371
  95.6 11.1 %shard_map.66 = (f32[2048,256]{1,0:T(8,128)S(1)}, f32[2048,128]{1,0:T(8,128)S(1)}) custom-call(s32[3]{0:T(128)S(1)} %add_add_fusion.refs_0_, bf16[16,288,128]{2,1,0:T(8,128)(2,1)S(1)} %all-to-all-done.refs_1_, bf16[2,512,128]{2,1,0:T(8,128)(2,1)S(1)} %copy-done.14, bf16[2,512,128]{2,1,0:T(8,128)(2,1)S(1)} %copy-done.16, bf16[2,512,128]{2,1,0:T(8,128)(2,1)S(1)} %copy-done.18, ...), custom_call_target="tpu_custom_call" | custom-call | flops 3221225472 | bytes 2621440 | tf_op jit(solution)/shard_map/pallas_call | solution.py:221
  106.7 5.9 %shard_map.67 = bf16[16,136,128]{2,1,0:T(8,128)(2,1)S(1)} custom-call(s32[3]{0:T(128)S(1)} %add_add_fusion.refs_0_, bf16[16,288,128]{2,1,0:T(8,128)(2,1)S(1)} %all-to-all-done.refs_1_, bf16[2,512,128]{2,1,0:T(8,128)(2,1)S(1)} %collective-permute-done.refs_2_, bf16[2,512,128]{2,1,0:T(8,128)(2,1)S(1)} %collective-permute-done.1.refs_3_, ...), custom_call_target="tpu_custom_call" | custom-call | flops 1073741824 | bytes 1572864 | tf_op jit(solution)/shard_map/pallas_call | solution.py:221
  113.5 5.6 %all-to-all-start.1 = ((bf16[16,136,128]{2,1,0:T(8,128)(2,1)}), bf16[16,136,128]{2,1,0:T(8,128)(2,1)S(1)}, u32[]{:S(2)}, u32[]{:S(2)}) async-start(bf16[16,136,128]{2,1,0:T(8,128)(2,1)} %copy-done.5), calls=%async_computation.1 | async-start | bytes 1114112 | tf_op jit(solution)/shard_map/all_to_all | solution.py:385
  119.0 2.3 %shard_map.71.refs_0_ = bf16[2,8,128,128]{3,2,1,0:T(8,128)(2,1)} custom-call(bf16[2,8,136,128]{3,2,1,0:T(8,128)(2,1)} %bitcast.18.part_ref), custom_call_target="tpu_custom_call" | custom-call | tf_op jit(solution)/shard_map/pallas_call | solution.py:275
  121.3 12.5 %all-to-all-done.1 = bf16[16,136,128]{2,1,0:T(8,128)(2,1)S(1)} async-done(((bf16[16,136,128]{2,1,0:T(8,128)(2,1)}), bf16[16,136,128]{2,1,0:T(8,128)(2,1)S(1)}, u32[]{:S(2)}, u32[]{:S(2)}) %all-to-all-start.1) | async-done | bytes 557088 | tf_op jit(solution)/shard_map/all_to_all | solution.py:385
  133.8 1.3 shard_map.72
  (79 shorter events, 24.0 us)
Async XLA Ops:
  0.8 8.9 %copy-start = (bf16[2,512,8,128]{3,2,1,0:T(8,128)(2,1)S(1)}, bf16[2,512,8,128]{3,2,1,0:T(8,128)(2,1)}, u32[]{:S(2)}) copy-start(bf16[2,512,8,128]{3,2,1,0:T(8,128)(2,1)} %k_hbm.3) | copy-start | bytes 6291460
  0.8 1.2 copy-start.6
  2.1 1.1 copy-start.3
  3.1 34.2 %all-to-all-start = ((bf16[16,288,128]{2,1,0:T(8,128)(2,1)}), bf16[16,288,128]{2,1,0:T(8,128)(2,1)S(1)}, u32[]{:S(2)}, u32[]{:S(2)}) async-start(bf16[16,288,128]{2,1,0:T(8,128)(2,1)} %copy-done.3), calls=%async_computation | async-start | bytes 2359296 | tf_op jit(solution)/shard_map/all_to_all | solution.py:355
  9.7 1.6 %copy-start.1 = (bf16[2,512,8,128]{3,2,1,0:T(8,128)(2,1)S(1)}, bf16[2,512,8,128]{3,2,1,0:T(8,128)(2,1)}, u32[]{:S(2)}) copy-start(bf16[2,512,8,128]{3,2,1,0:T(8,128)(2,1)} %v_hbm.3) | copy-start | bytes 6291460
  11.3 8.0 %copy-start.25 = (s32[2]{0:T(128)S(1)}, s32[2]{0:T(128)}, u32[]{:S(2)}) copy-start(s32[2]{0:T(128)} %param.11) | copy-start | bytes 28
  15.4 22.0 %collective-permute-start.9 = (bf16[2,512,128]{2,1,0:T(8,128)(2,1)}, bf16[2,512,128]{2,1,0:T(8,128)(2,1)}, u32[]{:S(2)}, u32[]{:S(2)}) collective-permute-start(bf16[2,512,128]{2,1,0:T(8,128)(2,1)} %get-tuple-element.38), channel_id=1, source_target_pairs={{0,1},{1,0},{2,3},{3,2},{4,5},{5,4},{6,7},{7,6},{8,9},{9,8},{10,11... | collective-permute-start | bytes 786440 | tf_op jit(solution)/shard_map/ppermute | solution.py:371
  15.8 21.7 %collective-permute-start.10 = (bf16[2,512,128]{2,1,0:T(8,128)(2,1)}, bf16[2,512,128]{2,1,0:T(8,128)(2,1)}, u32[]{:S(2)}, u32[]{:S(2)}) collective-permute-start(bf16[2,512,128]{2,1,0:T(8,128)(2,1)} %get-tuple-element.39), channel_id=1, source_target_pairs={{0,2},{1,3},{2,0},{3,1},{4,6},{5,7},{6,4},{7,5},{8,10},{9,11},{10,... | collective-permute-start | bytes 786440 | tf_op jit(solution)/shard_map/ppermute | solution.py:371
  17.0 22.7 %collective-permute-start.11 = (bf16[2,512,128]{2,1,0:T(8,128)(2,1)}, bf16[2,512,128]{2,1,0:T(8,128)(2,1)}, u32[]{:S(2)}, u32[]{:S(2)}) collective-permute-start(bf16[2,512,128]{2,1,0:T(8,128)(2,1)} %get-tuple-element.40), channel_id=1, source_target_pairs={{0,3},{1,2},{2,1},{3,0},{4,7},{5,6},{6,5},{7,4},{8,11},{9,10},{10,... | collective-permute-start | bytes 786440 | tf_op jit(solution)/shard_map/ppermute | solution.py:371
  17.5 22.1 %collective-permute-start.12 = (bf16[2,512,128]{2,1,0:T(8,128)(2,1)}, bf16[2,512,128]{2,1,0:T(8,128)(2,1)}, u32[]{:S(2)}, u32[]{:S(2)}) collective-permute-start(bf16[2,512,128]{2,1,0:T(8,128)(2,1)} %get-tuple-element.41), channel_id=1, source_target_pairs={{0,4},{1,5},{2,6},{3,7},{4,0},{5,1},{6,2},{7,3},{8,12},{9,13},{10,... | collective-permute-start | bytes 786440 | tf_op jit(solution)/shard_map/ppermute | solution.py:371
  17.7 24.0 %collective-permute-start.13 = (bf16[2,512,128]{2,1,0:T(8,128)(2,1)}, bf16[2,512,128]{2,1,0:T(8,128)(2,1)}, u32[]{:S(2)}, u32[]{:S(2)}) collective-permute-start(bf16[2,512,128]{2,1,0:T(8,128)(2,1)} %get-tuple-element.42), channel_id=1, source_target_pairs={{0,5},{1,4},{2,7},{3,6},{4,1},{5,0},{6,3},{7,2},{8,13},{9,12},{10,... | collective-permute-start | bytes 786440 | tf_op jit(solution)/shard_map/ppermute | solution.py:371
  37.4 15.9 %collective-permute-start.7 = (bf16[2,512,128]{2,1,0:T(8,128)(2,1)}, bf16[2,512,128]{2,1,0:T(8,128)(2,1)S(1)}, u32[]{:S(2)}, u32[]{:S(2)}) collective-permute-start(bf16[2,512,128]{2,1,0:T(8,128)(2,1)} %copy-done.8), channel_id=1, source_target_pairs={{0,6},{1,7},{2,4},{3,5},{4,2},{5,3},{6,0},{7,1},{8,14},{9,15},{10,... | collective-permute-start | bytes 786440 | tf_op jit(solution)/shard_map/ppermute | solution.py:371
  37.5 16.1 %collective-permute-start.8 = (bf16[2,512,128]{2,1,0:T(8,128)(2,1)}, bf16[2,512,128]{2,1,0:T(8,128)(2,1)S(1)}, u32[]{:S(2)}, u32[]{:S(2)}) collective-permute-start(bf16[2,512,128]{2,1,0:T(8,128)(2,1)} %copy-done.7), channel_id=1, source_target_pairs={{0,7},{1,6},{2,5},{3,4},{4,3},{5,2},{6,1},{7,0},{8,15},{9,14},{10,... | collective-permute-start | bytes 786440 | tf_op jit(solution)/shard_map/ppermute | solution.py:371
  41.7 1.0 copy-start.10
  60.4 53.1 %all-to-all-start.2 = ((bf16[16,136,128]{2,1,0:T(8,128)(2,1)}), bf16[16,136,128]{2,1,0:T(8,128)(2,1)}, u32[]{:S(2)}, u32[]{:S(2)}) async-start(bf16[16,136,128]{2,1,0:T(8,128)(2,1)} %copy-done.4), calls=%async_computation.2 | async-start | bytes 1114112 | tf_op jit(solution)/shard_map/all_to_all | solution.py:385
  65.4 1.6 %copy-start.2 = (bf16[2,512,8,128]{3,2,1,0:T(8,128)(2,1)S(1)}, bf16[2,512,8,128]{3,2,1,0:T(8,128)(2,1)}, u32[]{:S(2)}) copy-start(bf16[2,512,8,128]{3,2,1,0:T(8,128)(2,1)} %v_hbm.3) | copy-start | bytes 6291460
  71.1 4.6 %collective-permute-start.2 = (bf16[2,512,128]{2,1,0:T(8,128)(2,1)}, bf16[2,512,128]{2,1,0:T(8,128)(2,1)S(1)}, u32[]{:S(2)}, u32[]{:S(2)}) collective-permute-start(bf16[2,512,128]{2,1,0:T(8,128)(2,1)} %get-tuple-element.28), channel_id=1, source_target_pairs={{0,1},{1,0},{2,3},{3,2},{4,5},{5,4},{6,7},{7,6},{8,9},{9,8},{10,11... | collective-permute-start | bytes 786440 | tf_op jit(solution)/shard_map/ppermute | solution.py:371
  71.5 10.5 %collective-permute-start.3 = (bf16[2,512,128]{2,1,0:T(8,128)(2,1)}, bf16[2,512,128]{2,1,0:T(8,128)(2,1)S(1)}, u32[]{:S(2)}, u32[]{:S(2)}) collective-permute-start(bf16[2,512,128]{2,1,0:T(8,128)(2,1)} %get-tuple-element.29), channel_id=1, source_target_pairs={{0,2},{1,3},{2,0},{3,1},{4,6},{5,7},{6,4},{7,5},{8,10},{9,11},{10,... | collective-permute-start | bytes 786440 | tf_op jit(solution)/shard_map/ppermute | solution.py:371
  72.7 15.1 %collective-permute-start.4 = (bf16[2,512,128]{2,1,0:T(8,128)(2,1)}, bf16[2,512,128]{2,1,0:T(8,128)(2,1)S(1)}, u32[]{:S(2)}, u32[]{:S(2)}) collective-permute-start(bf16[2,512,128]{2,1,0:T(8,128)(2,1)} %get-tuple-element.30), channel_id=1, source_target_pairs={{0,3},{1,2},{2,1},{3,0},{4,7},{5,6},{6,5},{7,4},{8,11},{9,10},{10,... | collective-permute-start | bytes 786440 | tf_op jit(solution)/shard_map/ppermute | solution.py:371
  73.2 15.2 %collective-permute-start.5 = (bf16[2,512,128]{2,1,0:T(8,128)(2,1)}, bf16[2,512,128]{2,1,0:T(8,128)(2,1)S(1)}, u32[]{:S(2)}, u32[]{:S(2)}) collective-permute-start(bf16[2,512,128]{2,1,0:T(8,128)(2,1)} %get-tuple-element.31), channel_id=1, source_target_pairs={{0,4},{1,5},{2,6},{3,7},{4,0},{5,1},{6,2},{7,3},{8,12},{9,13},{10,... | collective-permute-start | bytes 786440 | tf_op jit(solution)/shard_map/ppermute | solution.py:371
  73.7 15.4 %collective-permute-start.6 = (bf16[2,512,128]{2,1,0:T(8,128)(2,1)}, bf16[2,512,128]{2,1,0:T(8,128)(2,1)S(1)}, u32[]{:S(2)}, u32[]{:S(2)}) collective-permute-start(bf16[2,512,128]{2,1,0:T(8,128)(2,1)} %get-tuple-element.32), channel_id=1, source_target_pairs={{0,5},{1,4},{2,7},{3,6},{4,1},{5,0},{6,3},{7,2},{8,13},{9,12},{10,... | collective-permute-start | bytes 786440 | tf_op jit(solution)/shard_map/ppermute | solution.py:371
  76.4 30.3 %collective-permute-start = (bf16[2,512,128]{2,1,0:T(8,128)(2,1)}, bf16[2,512,128]{2,1,0:T(8,128)(2,1)S(1)}, u32[]{:S(2)}, u32[]{:S(2)}) collective-permute-start(bf16[2,512,128]{2,1,0:T(8,128)(2,1)} %copy-done.12), channel_id=1, source_target_pairs={{0,6},{1,7},{2,4},{3,5},{4,2},{5,3},{6,0},{7,1},{8,14},{9,15},{10,... | collective-permute-start | bytes 786440 | tf_op jit(solution)/shard_map/ppermute | solution.py:371
  82.7 24.0 %collective-permute-start.1 = (bf16[2,512,128]{2,1,0:T(8,128)(2,1)}, bf16[2,512,128]{2,1,0:T(8,128)(2,1)S(1)}, u32[]{:S(2)}, u32[]{:S(2)}) collective-permute-start(bf16[2,512,128]{2,1,0:T(8,128)(2,1)} %copy-done.11), channel_id=1, source_target_pairs={{0,7},{1,6},{2,5},{3,4},{4,3},{5,2},{6,1},{7,0},{8,15},{9,14},{10,... | collective-permute-start | bytes 786440 | tf_op jit(solution)/shard_map/ppermute | solution.py:371
  113.5 20.4 %all-to-all-start.1 = ((bf16[16,136,128]{2,1,0:T(8,128)(2,1)}), bf16[16,136,128]{2,1,0:T(8,128)(2,1)S(1)}, u32[]{:S(2)}, u32[]{:S(2)}) async-start(bf16[16,136,128]{2,1,0:T(8,128)(2,1)} %copy-done.5), calls=%async_computation.1 | async-start | bytes 1114112 | tf_op jit(solution)/shard_map/all_to_all | solution.py:385
  (19 other events, 15.1 us)

commit v6 on v5

--- a/solution.py
+++ b/solution.py
@@ -12,6 +12,7 @@
 NEG = -1e30
 STAT_ROWS = 8
 SMALL_VMEM = 12 * 2**20
+LARGE_VMEM = 56 * 2**20
 
 
 VMEM_SPEC = pl.BlockSpec(memory_space=pltpu.VMEM)
@@ -19,23 +20,26 @@
 SMEM_SPEC = pl.BlockSpec(memory_space=pltpu.SMEM)
 
 
-def attend_kernel(*refs, order, total_blocks, tile, group_size, row_start, with_fresh, with_state, final):
+def attend_kernel(
+    *refs, q_count, order, total_blocks, tile, group_size, row_start, with_fresh, with_state, final, out_count
+):
     refs = list(refs)
-    info_ref, q_hbm = refs.pop(0), refs.pop(0)
+    info_ref = refs.pop(0)
+    q_hbm = [refs.pop(0) for _ in range(q_count)]
     kv_refs = [refs.pop(0) for _ in order]
     if with_fresh:
         fk_ref, fv_ref = refs.pop(0), refs.pop(0)
     if with_state:
         acc_in, top_in = refs.pop(0), refs.pop(0)
     if final:
-        out_hbm = refs.pop(0)
+        out_hbm = [refs.pop(0) for _ in range(out_count)]
     else:
         acc_out, top_out = refs.pop(0), refs.pop(0)
     if final:
-        out_ref, out_sem = refs.pop(), refs.pop()
+        out_ref, out_sems = refs.pop(), refs.pop()
     if with_fresh:
         fvals = refs.pop()
-    q_ref, keys, vals, s0, s1, m0, m1, in_sems, q_sem = refs
+    q_ref, keys, vals, s0, s1, m0, m1, in_sems, q_sems = refs
     per_source, dim = q_ref.shape[1:]
     block_slots = kv_refs[0].shape[1]
     chunk = 2 * block_slots
@@ -48,6 +52,7 @@
     valid = info_ref[0]
     fresh_shift = info_ref[1]
     own = info_ref[2]
+    me = info_ref[3]
 
     held = sorted({k // 2 for k in order})
     absent = [c for c in range(total_blocks // 2) if c not in held]
@@ -58,7 +63,13 @@
             rank = rank - jnp.where((own // 2) ^ c < index, 1, 0)
         return rank
 
-    copies = [pltpu.make_async_copy(q_hbm.at[:, row_start : row_start + per_source, :], q_ref, q_sem)]
+    q_rows = pl.ds(row_start, per_source)
+    if q_count == 1:
+        copies = [pltpu.make_async_copy(q_hbm[0].at[:, q_rows, :], q_ref, q_sems.at[0])]
+    else:
+        copies = [
+            pltpu.make_async_copy(hbm.at[q_rows, :], q_ref.at[me ^ k], q_sems.at[k]) for k, hbm in enumerate(q_hbm)
+        ]
     for i, k in enumerate(order):
         first = rank_of((own // 2) ^ (k // 2)) * chunk + ((own % 2) ^ (k % 2)) * block_slots
         at = pl.ds(pl.multiple_of(first, block_slots), block_slots)
@@ -103,6 +114,9 @@
         scores = product(q, fk_ref[...])
         token = (t * tile + lax.broadcasted_iota(jnp.int32, (tile, 1), 0)) // group_size
         unit = lax.broadcasted_iota(jnp.int32, (1, fresh), 1)
+        if q_count > 1:
+            local_rows = per_source // group_size
+            unit = ((unit // local_rows) ^ me) * local_rows + unit % local_rows
         scores = jnp.where(unit <= token + fresh_shift, scores, NEG)
         s_ref[:, slots : slots + fresh] = scores
         return lane_max(scores, best)
@@ -176,19 +190,26 @@
             lax.fori_loop(0, tiles // 2, pair, 0)
 
     if final:
-        result = pltpu.make_async_copy(out_ref, out_hbm, out_sem)
-        result.start()
-        result.wait()
-
-
-def attend(info, head_q, kv_blocks, order, fresh, state, final, row_start, row_count, group_size):
-    sources, _, dim = head_q.shape
+        if out_count == 1:
+            results = [pltpu.make_async_copy(out_ref, out_hbm[0], out_sems.at[0])]
+        else:
+            results = [
+                pltpu.make_async_copy(out_ref.at[me ^ k], hbm, out_sems.at[k]) for k, hbm in enumerate(out_hbm)
+            ]
+        for result in results:
+            result.start()
+        for result in results:
+            result.wait()
+
+
+def attend(info, head_q, kv_blocks, order, fresh, state, final, out_count, sources, row_start, row_count, group_size):
+    dim = head_q[0].shape[-1]
     slots = len(order) * kv_blocks[0].shape[1]
     rows = sources * row_count
     units = 0 if fresh is None else fresh[0].shape[0]
     tile = min(256, rows // 2)
-    operands = [info, head_q] + [kv_blocks[k] for k in order]
-    in_specs = [SMEM_SPEC] + [HBM_SPEC] * (1 + len(order))
+    operands = [info] + head_q + [kv_blocks[k] for k in order]
+    in_specs = [SMEM_SPEC] + [HBM_SPEC] * (len(head_q) + len(order))
     scratch = [
         pltpu.VMEM((sources, row_count, dim), jnp.bfloat16),
         pltpu.VMEM((slots, dim), jnp.bfloat16),
@@ -198,7 +219,7 @@
         pltpu.VMEM((tile, dim), jnp.float32),
         pltpu.VMEM((tile, dim), jnp.float32),
         pltpu.SemaphoreType.DMA((len(order), 2)),
-        pltpu.SemaphoreType.DMA,
+        pltpu.SemaphoreType.DMA((len(head_q),)),
     ]
     if fresh is not None:
         operands += list(fresh)
@@ -208,9 +229,11 @@
         operands += list(state)
         in_specs += [VMEM_SPEC] * 2
     if final:
-        out_shape = jax.ShapeDtypeStruct((sources, row_count + STAT_ROWS, dim), jnp.bfloat16)
-        out_specs = HBM_SPEC
-        scratch += [pltpu.SemaphoreType.DMA, pltpu.VMEM(out_shape.shape, jnp.bfloat16)]
+        whole = (sources, row_count + STAT_ROWS, dim)
+        each = whole if out_count == 1 else whole[1:]
+        out_shape = [jax.ShapeDtypeStruct(each, jnp.bfloat16)] * out_count
+        out_specs = [HBM_SPEC] * out_count
+        scratch += [pltpu.SemaphoreType.DMA((out_count,)), pltpu.VMEM(whole, jnp.bfloat16)]
     else:
         out_shape = [
             jax.ShapeDtypeStruct((rows, 2 * dim), jnp.float32),
@@ -221,6 +244,8 @@
     return pl.pallas_call(
         functools.partial(
             attend_kernel,
+            q_count=len(head_q),
+            out_count=out_count,
             order=order,
             total_blocks=len(kv_blocks),
             tile=tile,
@@ -243,16 +268,17 @@
     )(*operands)
 
 
-def merge_kernel(part_ref, *refs, group_size):
-    out_ref = refs[-1]
-    spread, heads, _, dim = part_ref.shape
-    local_rows = out_ref.shape[1]
+def merge_kernel(own_ref, *refs, count, spread, heads, group_size):
+    parts, out_ref = refs[:count], refs[-1]
+    _, local_rows, _, dim = out_ref.shape
     per_source = local_rows * group_size
+
+    def part(b, h):
+        return parts[0].at[b * heads + h] if count == 1 else parts[b * heads + h]
+
     levels = []
     for b in range(spread):
-        stats = [
-            part_ref[b, h, per_source : per_source + STAT_ROWS, :].astype(jnp.float32) for h in range(heads)
-        ]
+        stats = [part(b, h)[per_source : per_source + STAT_ROWS, :].astype(jnp.float32) for h in range(heads)]
         levels.append(jnp.concatenate([x[0:1] + x[1:2] + x[2:3] for x in stats], axis=0))
     top = functools.reduce(jnp.maximum, levels)
     weights = [jnp.exp2(level - top) for level in levels]
@@ -262,49 +288,55 @@
         mixed = functools.reduce(
             jnp.add,
             [
-                w[:per_source, h : h + 1] * part_ref[b, h, :per_source, :].astype(jnp.float32)
+                w[:per_source, h : h + 1] * part(b, h)[:per_source, :].astype(jnp.float32)
                 for b, w in enumerate(weights)
             ],
         ).astype(jnp.bfloat16)
-        out_ref[0, :, h * group_size : (h + 1) * group_size, :] = mixed.reshape(local_rows, group_size, dim)
-
-
-def merge(parts, request, requests, local_rows, group_size, earlier):
-    heads, dim = parts.shape[1], parts.shape[3]
+        first = h * group_size if count == 1 else pl.multiple_of((own_ref[0] ^ h) * group_size, group_size)
+        out_ref[0, :, pl.ds(first, group_size), :] = mixed.reshape(local_rows, group_size, dim)
+
+
+def merge(own, parts, kv_heads, spread, request, requests, local_rows, group_size, earlier):
+    dim = parts[0].shape[-1]
     rest = [] if earlier is None else [earlier]
+
+    def whole(array):
+        return pl.BlockSpec(array.shape, lambda i: (0,) * array.ndim)
+
     return pl.pallas_call(
-        functools.partial(merge_kernel, group_size=group_size),
+        functools.partial(merge_kernel, count=len(parts), spread=spread, heads=kv_heads, group_size=group_size),
         grid=(1,),
-        in_specs=[pl.BlockSpec(parts.shape, lambda i: (0, 0, 0, 0))]
-        + [pl.BlockSpec(memory_space=pl.ANY) for _ in rest],
-        out_specs=pl.BlockSpec((1, local_rows, heads * group_size, dim), lambda i: (request, 0, 0, 0)),
-        out_shape=jax.ShapeDtypeStruct((requests, local_rows, heads * group_size, dim), jnp.bfloat16),
-        input_output_aliases={1: 0} if rest else {},
+        in_specs=[SMEM_SPEC] + [whole(x) for x in parts] + [pl.BlockSpec(memory_space=pl.ANY) for _ in rest],
+        out_specs=pl.BlockSpec((1, local_rows, kv_heads * group_size, dim), lambda i: (request, 0, 0, 0)),
+        out_shape=jax.ShapeDtypeStruct((requests, local_rows, kv_heads * group_size, dim), jnp.bfloat16),
+        input_output_aliases={1 + len(parts): 0} if rest else {},
         compiler_params=pltpu.CompilerParams(vmem_limit_bytes=SMALL_VMEM),
-    )(parts, *rest)
-
-
-def pack_kernel(q_ref, fresh_ref, out_ref):
+    )(own, *parts, *rest)
+
+
+def pack_kernel(own_ref, q_ref, fresh_ref, *out_refs):
     requests, local_rows, heads, dim = q_ref.shape
     kv_heads = fresh_ref.shape[0]
     group_size = heads // kv_heads
     rows = requests * local_rows * group_size
-    for d in range(out_ref.shape[0]):
-        head = d % kv_heads
-        out_ref[d, :rows, :] = q_ref[:, :, head * group_size : (head + 1) * group_size, :].reshape(rows, dim)
-        out_ref[d, rows:, :] = fresh_ref[head]
-
-
-def pack(queries, fresh, devices):
+    for d, out_ref in enumerate(out_refs):
+        head = own_ref[0] ^ d
+        first = pl.multiple_of(head * group_size, group_size)
+        out_ref[:rows, :] = q_ref[:, :, pl.ds(first, group_size), :].reshape(rows, dim)
+        out_ref[rows:, :] = fresh_ref[head]
+
+
+def pack(own, queries, fresh):
     requests, local_rows, heads, dim = queries.shape
-    rows = requests * local_rows * (heads // fresh.shape[0]) + fresh.shape[1]
+    kv_heads = fresh.shape[0]
+    rows = requests * local_rows * (heads // kv_heads) + fresh.shape[1]
     return pl.pallas_call(
         pack_kernel,
-        in_specs=[VMEM_SPEC, VMEM_SPEC],
-        out_specs=VMEM_SPEC,
-        out_shape=jax.ShapeDtypeStruct((devices, rows, dim), jnp.bfloat16),
+        in_specs=[SMEM_SPEC, VMEM_SPEC, VMEM_SPEC],
+        out_specs=[VMEM_SPEC] * kv_heads,
+        out_shape=[jax.ShapeDtypeStruct((rows, dim), jnp.bfloat16)] * kv_heads,
         compiler_params=pltpu.CompilerParams(vmem_limit_bytes=SMALL_VMEM),
-    )(queries, fresh)
+    )(own, queries, fresh)
 
 
 def split_kernel(own_ref, k_hbm, v_hbm, *refs, request):
@@ -333,7 +365,7 @@
             pltpu.VMEM((kv_heads, 2, slots, dim), jnp.bfloat16),
             pltpu.SemaphoreType.DMA((2,)),
         ],
-        compiler_params=pltpu.CompilerParams(vmem_limit_bytes=2 * SMALL_VMEM),
+        compiler_params=pltpu.CompilerParams(vmem_limit_bytes=LARGE_VMEM),
     )(own, cache_k, cache_v)
 
 
@@ -349,15 +381,28 @@
     own = (seq_index % kv_heads).astype(jnp.int32)
     per_source = local_rows * group_size
 
+    devices = range(devices_seq)
+    direct = spread <= 2
     fresh = jnp.transpose(jnp.stack([new_k, new_v]), (3, 0, 1, 2, 4)).reshape(
         kv_heads, 2 * requests * local_rows, head_dim
     )
-    head_q = lax.all_to_all(
-        pack(queries, fresh, devices_seq), "seq", split_axis=0, concat_axis=0, tiled=True
-    )
-    head_fresh = head_q[:, requests * per_source :, :].reshape(
-        devices_seq, 2, requests, local_rows, head_dim
-    )
+
+    def to_partner(array, k):
+        return lax.ppermute(array, "seq", [(i, i ^ k) for i in devices])
+
+    if direct:
+        packed = pack(own[None], queries, fresh)
+        head_q = [packed[0]]
+        for k in range(1, devices_seq):
+            head_q.append(to_partner(packed[k % kv_heads], k))
+        head_fresh = jnp.stack([x[requests * per_source :, :] for x in head_q])
+    else:
+        packed = jnp.stack(pack(jnp.zeros((1,), jnp.int32), queries, fresh))
+        packed = jnp.broadcast_to(packed[None], (spread,) + packed.shape).reshape((devices_seq,) + packed.shape[1:])
+        head_q = lax.all_to_all(packed, "seq", split_axis=0, concat_axis=0, tiled=True)
+        head_fresh = head_q[:, requests * per_source :, :]
+        head_q = [head_q]
+    head_fresh = head_fresh.reshape(devices_seq, 2, requests, local_rows, head_dim)
     head_fresh = jnp.transpose(head_fresh, (1, 2, 0, 3, 4)).reshape(
         2, requests, devices_seq * local_rows, head_dim
     )
@@ -368,7 +413,7 @@
         parts = split_heads(own[None], cache_k, cache_v, r)
         moved = [parts[0]]
         for k in range(1, kv_heads):
-            moved.append(lax.ppermute(parts[k], "seq", [(i, i ^ k) for i in range(devices_seq)]))
+            moved.append(to_partner(parts[k], k))
         kv_blocks.append(moved)
 
     out = None
@@ -376,15 +421,27 @@
         held = kv_heads * slots
         valid = jnp.clip(cache_len[r] - block * held, 0, held)
         fresh_shift = jnp.where(block == spread - 1, 0, -devices_seq * local_rows)
-        info = jnp.stack([valid, fresh_shift, own]).astype(jnp.int32)
-        rows = (r * per_source, per_source, group_size)
+        info = jnp.stack([valid, fresh_shift, own, seq_index]).astype(jnp.int32)
+        rows = (devices_seq, r * per_source, per_source, group_size)
+        separate = direct and r == requests - 1
+        out_count = devices_seq if separate else 1
         state = attend(
-            info, head_q, kv_blocks[r], tuple(range(early)), (head_fresh[0, r], head_fresh[1, r]), None, False, *rows
+            info,
+            head_q,
+            kv_blocks[r],
+            tuple(range(early)),
+            (head_fresh[0, r], head_fresh[1, r]),
+            None,
+            False,
+            1,
+            *rows,
         )
-        part = attend(info, head_q, kv_blocks[r], tuple(range(early, kv_heads)), None, state, True, *rows)
-        part = lax.all_to_all(part, "seq", split_axis=0, concat_axis=0, tiled=True)
-        part = part.reshape(spread, kv_heads, per_source + STAT_ROWS, head_dim)
-        out = merge(part, r, requests, local_rows, group_size, out)
+        parts = attend(info, head_q, kv_blocks[r], tuple(range(early, kv_heads)), None, state, True, out_count, *rows)
+        if separate:
+            parts = [parts[0]] + [to_partner(parts[k], k) for k in range(1, devices_seq)]
+        else:
+            parts = [lax.all_to_all(parts[0], "seq", split_axis=0, concat_axis=0, tiled=True)]
+        out = merge(own[None], parts, kv_heads, spread, r, requests, local_rows, group_size, out)
     return out
 
 

time: 136 us -> 164 us (1.21)
  the two profiles are of different devices: /device:TPU:13 before, /device:TPU:5 now
where the time goes in v6:
time: 164 us
  starting transfers between devices  67.2 us (41%)
  Pallas kernels  49.1 us (30%)
  waiting for transfers between devices  40.3 us (25%)
  local copies, waits for them, and re-layouts  4.5 us (3%)
    ppermute x44, starting transfers between devices, to_partner(): return lax.ppermute(array, 'seq', [(i, i ^ k) for i in devices])  63.5 us
    ppermute x44, waiting for transfers between devices, to_partner(): return lax.ppermute(array, 'seq', [(i, i ^ k) for i in devices])  40.3 us
    pallas_call x4, Pallas kernels, attend(): pl.pallas_call(functools.partial(attend_kernel, q_count=len(head_q), out_...  39.9 us
    pallas_call x2, Pallas kernels, split_heads(): pl.pallas_call(functools.partial(split_kernel, request=request), in_specs...  6.58 us
    all_to_all x1, starting transfers between devices, attention(): lax.all_to_all(parts[0], 'seq', split_axis=0, concat_axis=0, tiled=True)  3.67 us
  transfers between devices with their start and end apart: 45, of which 14 were waited for; matrix products, arithmetic and copies ran while one was open for 1% of the time, Pallas kernels for 24%

profile of v6, /device:TPU:5, one launch (start us, length us, event | category | flops | bytes accessed | tf_op | source)
XLA Modules:
  0.0 163.6 jit_solution(15183631671180209709)
XLA Ops:
  1.9 2.9 %collective-permute-start.8 = (bf16[288,128]{1,0:T(8,128)(2,1)S(1)}, bf16[288,128]{1,0:T(8,128)(2,1)S(1)}, u32[]{:S(2)}, u32[]{:S(2)}) collective-permute-start(bf16[288,128]{1,0:T(8,128)(2,1)S(1)} %get-tuple-element.50), channel_id=1, source_target_pairs={{0,9},{1,8},{2,11},{3,10},{4,13},{5,12},{6,15},{7,14},{8,1},{9,0},... | collective-permute-start | bytes 221192 | tf_op jit(solution)/shard_map/ppermute | solution.py:391
  6.2 4.1 %collective-permute-start.10 = (bf16[288,128]{1,0:T(8,128)(2,1)S(1)}, bf16[288,128]{1,0:T(8,128)(2,1)S(1)}, u32[]{:S(2)}, u32[]{:S(2)}) collective-permute-start(bf16[288,128]{1,0:T(8,128)(2,1)S(1)} %get-tuple-element.52), channel_id=1, source_target_pairs={{0,11},{1,10},{2,9},{3,8},{4,15},{5,14},{6,13},{7,12},{8,3},{9,2},... | collective-permute-start | bytes 221192 | tf_op jit(solution)/shard_map/ppermute | solution.py:391
  12.3 3.3 %shard_map.68 = (bf16[2,512,128]{2,1,0:T(8,128)(2,1)}, bf16[2,512,128]{2,1,0:T(8,128)(2,1)}, bf16[2,512,128]{2,1,0:T(8,128)(2,1)}, bf16[2,512,128]{2,1,0:T(8,128...) custom-call(s32[1]{0:T(128)} %bitcast.own_ref, ...), custom_call_target="tpu_custom_call" | custom-call | tf_op jit(solution)/shard_map/pallas_call | solution.py:358
  21.1 2.6 %collective-permute-done.3.refs_5_ = bf16[288,128]{1,0:T(8,128)(2,1)S(1)} collective-permute-done((bf16[288,128]{1,0:T(8,128)(2,1)S(1)}, bf16[288,128]{1,0:T(8,128)(2,1)S(1)}, u32[]{:S(2)}, u32[]{:S(2)}) %collective-permute-start.3) | collective-permute-done | bytes 73760 | tf_op jit(solution)/shard_map/ppermute | solution.py:391
  24.9 3.0 %collective-permute-done.4.refs_6_ = bf16[288,128]{1,0:T(8,128)(2,1)S(1)} collective-permute-done((bf16[288,128]{1,0:T(8,128)(2,1)S(1)}, bf16[288,128]{1,0:T(8,128)(2,1)S(1)}, u32[]{:S(2)}, u32[]{:S(2)}) %collective-permute-start.4) | collective-permute-done | bytes 73760 | tf_op jit(solution)/shard_map/ppermute | solution.py:391
  32.0 3.1 %collective-permute-start.6 = (bf16[288,128]{1,0:T(8,128)(2,1)S(1)}, bf16[288,128]{1,0:T(8,128)(2,1)S(1)}, u32[]{:S(2)}, u32[]{:S(2)}) collective-permute-start(bf16[288,128]{1,0:T(8,128)(2,1)S(1)} %get-tuple-element.56), channel_id=1, source_target_pairs={{0,7},{1,6},{2,5},{3,4},{4,3},{5,2},{6,1},{7,0},{8,15},{9,14},{10,... | collective-permute-start | bytes 221192 | tf_op jit(solution)/shard_map/ppermute | solution.py:391
  35.1 2.7 %collective-permute-done.6.refs_8_ = bf16[288,128]{1,0:T(8,128)(2,1)S(1)} collective-permute-done((bf16[288,128]{1,0:T(8,128)(2,1)S(1)}, bf16[288,128]{1,0:T(8,128)(2,1)S(1)}, u32[]{:S(2)}, u32[]{:S(2)}) %collective-permute-start.6) | collective-permute-done | bytes 73760 | tf_op jit(solution)/shard_map/ppermute | solution.py:391
  39.0 3.0 %collective-permute-done.7.refs_9_ = bf16[288,128]{1,0:T(8,128)(2,1)S(1)} collective-permute-done((bf16[288,128]{1,0:T(8,128)(2,1)S(1)}, bf16[288,128]{1,0:T(8,128)(2,1)S(1)}, u32[]{:S(2)}, u32[]{:S(2)}) %collective-permute-start.7) | collective-permute-done | bytes 73760 | tf_op jit(solution)/shard_map/ppermute | solution.py:391
  41.9 4.2 %collective-permute-start.12 = (bf16[288,128]{1,0:T(8,128)(2,1)S(1)}, bf16[288,128]{1,0:T(8,128)(2,1)S(1)}, u32[]{:S(2)}, u32[]{:S(2)}) collective-permute-start(bf16[288,128]{1,0:T(8,128)(2,1)S(1)} %get-tuple-element.54), channel_id=1, source_target_pairs={{0,13},{1,12},{2,15},{3,14},{4,9},{5,8},{6,11},{7,10},{8,5},{9,4},... | collective-permute-start | bytes 221192 | tf_op jit(solution)/shard_map/ppermute | solution.py:391
  57.1 2.7 %collective-permute-done.40.refs_19_ = bf16[2,512,128]{2,1,0:T(8,128)(2,1)S(1)} collective-permute-done((bf16[2,512,128]{2,1,0:T(8,128)(2,1)}, bf16[2,512,128]{2,1,0:T(8,128)(2,1)S(1)}, u32[]{:S(2)}, u32[]{:S(2)}) %collective-permute-start.40) | collective-permute-done | bytes 262176 | tf_op jit(solution)/shard_map/ppermute | solution.py:391
  60.1 5.8 %collective-permute-done.41.refs_20_ = bf16[2,512,128]{2,1,0:T(8,128)(2,1)S(1)} collective-permute-done((bf16[2,512,128]{2,1,0:T(8,128)(2,1)}, bf16[2,512,128]{2,1,0:T(8,128)(2,1)S(1)}, u32[]{:S(2)}, u32[]{:S(2)}) %collective-permute-start.41) | collective-permute-done | bytes 262176 | tf_op jit(solution)/shard_map/ppermute | solution.py:391
  68.2 12.1 %shard_map.69 = (f32[2048,256]{1,0:T(8,128)S(1)}, f32[2048,128]{1,0:T(8,128)S(1)}) custom-call(s32[4]{0:T(128)S(1)} %add_add_fusion.1.refs_0_, bf16[288,128]{1,0:T(8,128)(2,1)S(1)} %get-tuple-element.49.refs_1_, bf16[288,128]{1,0:T(8,128)(2,1)S(1)} %collective-permute-done.refs_2_, bf16[288,128]{1,0:T(8,128)(2,1)S(1)} %collective-permute-done.1.refs_3_, ...), custom_call_target="tpu_custom_call" | custom-call | flops 3221225472 | bytes 2621440 | tf_op jit(solution)/shard_map/pallas_call | solution.py:244
  80.4 7.7 %shard_map.70 = bf16[16,136,128]{2,1,0:T(8,128)(2,1)} custom-call(s32[4]{0:T(128)S(1)} %add_add_fusion.1.refs_0_, bf16[288,128]{1,0:T(8,128)(2,1)S(1)} %get-tuple-element.49.refs_1_, bf16[288,128]{1,0:T(8,128)(2,1)S(1)} %collective-permute-done.refs_2_, bf16[288,128]{1,0:T(8,128)(2,1)S(1)} %collective-permute-done.1.refs_3_, ...), custom_call_target="tpu_custom_call" | custom-call | flops 1073741824 | bytes 1572864 | tf_op jit(solution)/shard_map/pallas_call | solution.py:244
  88.1 3.7 %all-to-all-start = ((bf16[16,136,128]{2,1,0:T(8,128)(2,1)}), bf16[16,136,128]{2,1,0:T(8,128)(2,1)S(1)}, u32[]{:S(2)}, u32[]{:S(2)}) async-start(bf16[16,136,128]{2,1,0:T(8,128)(2,1)} %shard_map.70), calls=%async_computation | async-start | bytes 1114112 | tf_op jit(solution)/shard_map/all_to_all | solution.py:443
  91.8 3.3 %shard_map.65 = (bf16[2,512,128]{2,1,0:T(8,128)(2,1)}, bf16[2,512,128]{2,1,0:T(8,128)(2,1)}, bf16[2,512,128]{2,1,0:T(8,128)(2,1)}, bf16[2,512,128]{2,1,0:T(8,128...) custom-call(s32[1]{0:T(128)} %bitcast.own_ref, ...), custom_call_target="tpu_custom_call" | custom-call | tf_op jit(solution)/shard_map/pallas_call | solution.py:358
  102.0 3.6 %collective-permute-done.18.refs_19_ = bf16[2,512,128]{2,1,0:T(8,128)(2,1)S(1)} collective-permute-done((bf16[2,512,128]{2,1,0:T(8,128)(2,1)}, bf16[2,512,128]{2,1,0:T(8,128)(2,1)S(1)}, u32[]{:S(2)}, u32[]{:S(2)}) %collective-permute-start.18) | collective-permute-done | bytes 262176 | tf_op jit(solution)/shard_map/ppermute | solution.py:391
  105.6 4.2 %collective-permute-start.16 = (bf16[2,512,128]{2,1,0:T(8,128)(2,1)}, bf16[2,512,128]{2,1,0:T(8,128)(2,1)S(1)}, u32[]{:S(2)}, u32[]{:S(2)}) collective-permute-start(bf16[2,512,128]{2,1,0:T(8,128)(2,1)} %get-tuple-element.58), channel_id=1, source_target_pairs={{0,7},{1,6},{2,5},{3,4},{4,3},{5,2},{6,1},{7,0},{8,15},{9,14},{10,... | collective-permute-start | bytes 786440 | tf_op jit(solution)/shard_map/ppermute | solution.py:391
  109.7 2.8 %collective-permute-done.19.refs_20_ = bf16[2,512,128]{2,1,0:T(8,128)(2,1)S(1)} collective-permute-done((bf16[2,512,128]{2,1,0:T(8,128)(2,1)}, bf16[2,512,128]{2,1,0:T(8,128)(2,1)S(1)}, u32[]{:S(2)}, u32[]{:S(2)}) %collective-permute-start.19) | collective-permute-done | bytes 262176 | tf_op jit(solution)/shard_map/ppermute | solution.py:391
  115.8 12.1 %shard_map.66 = (f32[2048,256]{1,0:T(8,128)S(1)}, f32[2048,128]{1,0:T(8,128)S(1)}) custom-call(s32[4]{0:T(128)S(1)} %add_add_fusion.refs_0_, bf16[288,128]{1,0:T(8,128)(2,1)S(1)} %get-tuple-element.49.refs_1_, bf16[288,128]{1,0:T(8,128)(2,1)S(1)} %collective-permute-done.refs_2_, bf16[288,128]{1,0:T(8,128)(2,1)S(1)} %collective-permute-done.1.refs_3_, ...), custom_call_target="tpu_custom_call" | custom-call | flops 3221225472 | bytes 2621440 | tf_op jit(solution)/shard_map/pallas_call | solution.py:244
  128.0 8.0 %shard_map.67 = (bf16[136,128]{1,0:T(8,128)(2,1)S(1)}, bf16[136,128]{1,0:T(8,128)(2,1)S(1)}, bf16[136,128]{1,0:T(8,128)(2,1)S(1)}, bf16[136,128]{1,0:T(8,128)(2,...) custom-call(s32[4]{0:T(128)S(1)} %add_add_fusion.refs_0_, ...), custom_call_target="tpu_custom_call" | custom-call | flops 1073741824 | bytes 1572864 | tf_op jit(solution)/shard_map/pallas_call | solution.py:244
  145.0 3.1 %collective-permute-start.31 = (bf16[136,128]{1,0:T(8,128)(2,1)S(1)}, bf16[136,128]{1,0:T(8,128)(2,1)S(1)}, u32[]{:S(2)}, u32[]{:S(2)}) collective-permute-start(bf16[136,128]{1,0:T(8,128)(2,1)S(1)} %get-tuple-element.77), channel_id=1, source_target_pairs={{0,10},{1,11},{2,8},{3,9},{4,14},{5,15},{6,12},{7,13},{8,2},{9,3},... | collective-permute-start | bytes 104456 | tf_op jit(solution)/shard_map/ppermute | solution.py:391
  148.8 3.1 %collective-permute-start.33 = (bf16[136,128]{1,0:T(8,128)(2,1)S(1)}, bf16[136,128]{1,0:T(8,128)(2,1)S(1)}, u32[]{:S(2)}, u32[]{:S(2)}) collective-permute-start(bf16[136,128]{1,0:T(8,128)(2,1)S(1)} %get-tuple-element.79), channel_id=1, source_target_pairs={{0,12},{1,13},{2,14},{3,15},{4,8},{5,9},{6,10},{7,11},{8,4},{9,5},... | collective-permute-start | bytes 104456 | tf_op jit(solution)/shard_map/ppermute | solution.py:391
  152.4 3.2 %collective-permute-start.35 = (bf16[136,128]{1,0:T(8,128)(2,1)S(1)}, bf16[136,128]{1,0:T(8,128)(2,1)S(1)}, u32[]{:S(2)}, u32[]{:S(2)}) collective-permute-start(bf16[136,128]{1,0:T(8,128)(2,1)S(1)} %get-tuple-element.81), channel_id=1, source_target_pairs={{0,14},{1,15},{2,12},{3,13},{4,10},{5,11},{6,8},{7,9},{8,6},{9,7},... | collective-permute-start | bytes 104456 | tf_op jit(solution)/shard_map/ppermute | solution.py:391
  158.1 4.2 %collective-permute-done.36.refs_15_ = bf16[136,128]{1,0:T(8,128)(2,1)S(1)} collective-permute-done((bf16[136,128]{1,0:T(8,128)(2,1)S(1)}, bf16[136,128]{1,0:T(8,128)(2,1)S(1)}, u32[]{:S(2)}, u32[]{:S(2)}) %collective-permute-start.36) | collective-permute-done | bytes 34848 | tf_op jit(solution)/shard_map/ppermute | solution.py:391
  (120 shorter events, 53.6 us)
Async XLA Ops:
  1.9 44.2 %collective-permute-start.8 = (bf16[288,128]{1,0:T(8,128)(2,1)S(1)}, bf16[288,128]{1,0:T(8,128)(2,1)S(1)}, u32[]{:S(2)}, u32[]{:S(2)}) collective-permute-start(bf16[288,128]{1,0:T(8,128)(2,1)S(1)} %get-tuple-element.50), channel_id=1, source_target_pairs={{0,9},{1,8},{2,11},{3,10},{4,13},{5,12},{6,15},{7,14},{8,1},{9,0},... | collective-permute-start | bytes 221192 | tf_op jit(solution)/shard_map/ppermute | solution.py:391
  4.9 10.8 %collective-permute-start = (bf16[288,128]{1,0:T(8,128)(2,1)S(1)}, bf16[288,128]{1,0:T(8,128)(2,1)S(1)}, u32[]{:S(2)}, u32[]{:S(2)}) collective-permute-start(bf16[288,128]{1,0:T(8,128)(2,1)S(1)} %get-tuple-element.50), channel_id=1, source_target_pairs={{0,1},{1,0},{2,3},{3,2},{4,5},{5,4},{6,7},{7,6},{8,9},{9,8},{10,11... | collective-permute-start | bytes 221192 | tf_op jit(solution)/shard_map/ppermute | solution.py:391
  4.9 43.8 %collective-permute-start.9 = (bf16[288,128]{1,0:T(8,128)(2,1)S(1)}, bf16[288,128]{1,0:T(8,128)(2,1)S(1)}, u32[]{:S(2)}, u32[]{:S(2)}) collective-permute-start(bf16[288,128]{1,0:T(8,128)(2,1)S(1)} %get-tuple-element.51), channel_id=1, source_target_pairs={{0,10},{1,11},{2,8},{3,9},{4,14},{5,15},{6,12},{7,13},{8,2},{9,3},... | collective-permute-start | bytes 221192 | tf_op jit(solution)/shard_map/ppermute | solution.py:391
  6.0 9.7 %collective-permute-start.1 = (bf16[288,128]{1,0:T(8,128)(2,1)S(1)}, bf16[288,128]{1,0:T(8,128)(2,1)S(1)}, u32[]{:S(2)}, u32[]{:S(2)}) collective-permute-start(bf16[288,128]{1,0:T(8,128)(2,1)S(1)} %get-tuple-element.51), channel_id=1, source_target_pairs={{0,2},{1,3},{2,0},{3,1},{4,6},{5,7},{6,4},{7,5},{8,10},{9,11},{10,... | collective-permute-start | bytes 221192 | tf_op jit(solution)/shard_map/ppermute | solution.py:391
  6.2 43.2 %collective-permute-start.10 = (bf16[288,128]{1,0:T(8,128)(2,1)S(1)}, bf16[288,128]{1,0:T(8,128)(2,1)S(1)}, u32[]{:S(2)}, u32[]{:S(2)}) collective-permute-start(bf16[288,128]{1,0:T(8,128)(2,1)S(1)} %get-tuple-element.52), channel_id=1, source_target_pairs={{0,11},{1,10},{2,9},{3,8},{4,15},{5,14},{6,13},{7,12},{8,3},{9,2},... | collective-permute-start | bytes 221192 | tf_op jit(solution)/shard_map/ppermute | solution.py:391
  15.7 35.2 %collective-permute-start.11 = (bf16[288,128]{1,0:T(8,128)(2,1)S(1)}, bf16[288,128]{1,0:T(8,128)(2,1)S(1)}, u32[]{:S(2)}, u32[]{:S(2)}) collective-permute-start(bf16[288,128]{1,0:T(8,128)(2,1)S(1)} %get-tuple-element.53), channel_id=1, source_target_pairs={{0,12},{1,13},{2,14},{3,15},{4,8},{5,9},{6,10},{7,11},{8,4},{9,5},... | collective-permute-start | bytes 221192 | tf_op jit(solution)/shard_map/ppermute | solution.py:391
  41.9 9.9 %collective-permute-start.12 = (bf16[288,128]{1,0:T(8,128)(2,1)S(1)}, bf16[288,128]{1,0:T(8,128)(2,1)S(1)}, u32[]{:S(2)}, u32[]{:S(2)}) collective-permute-start(bf16[288,128]{1,0:T(8,128)(2,1)S(1)} %get-tuple-element.54), channel_id=1, source_target_pairs={{0,13},{1,12},{2,15},{3,14},{4,9},{5,8},{6,11},{7,10},{8,5},{9,4},... | collective-permute-start | bytes 221192 | tf_op jit(solution)/shard_map/ppermute | solution.py:391
  50.9 8.9 %collective-permute-start.40 = (bf16[2,512,128]{2,1,0:T(8,128)(2,1)}, bf16[2,512,128]{2,1,0:T(8,128)(2,1)S(1)}, u32[]{:S(2)}, u32[]{:S(2)}) collective-permute-start(bf16[2,512,128]{2,1,0:T(8,128)(2,1)} %get-tuple-element.87), channel_id=1, source_target_pairs={{0,2},{1,3},{2,0},{3,1},{4,6},{5,7},{6,4},{7,5},{8,10},{9,11},{10,... | collective-permute-start | bytes 786440 | tf_op jit(solution)/shard_map/ppermute | solution.py:391
  51.8 14.1 %collective-permute-start.41 = (bf16[2,512,128]{2,1,0:T(8,128)(2,1)}, bf16[2,512,128]{2,1,0:T(8,128)(2,1)S(1)}, u32[]{:S(2)}, u32[]{:S(2)}) collective-permute-start(bf16[2,512,128]{2,1,0:T(8,128)(2,1)} %get-tuple-element.88), channel_id=1, source_target_pairs={{0,3},{1,2},{2,1},{3,0},{4,7},{5,6},{6,5},{7,4},{8,11},{9,10},{10,... | collective-permute-start | bytes 786440 | tf_op jit(solution)/shard_map/ppermute | solution.py:391
  52.7 13.2 %collective-permute-start.42 = (bf16[2,512,128]{2,1,0:T(8,128)(2,1)}, bf16[2,512,128]{2,1,0:T(8,128)(2,1)S(1)}, u32[]{:S(2)}, u32[]{:S(2)}) collective-permute-start(bf16[2,512,128]{2,1,0:T(8,128)(2,1)} %get-tuple-element.89), channel_id=1, source_target_pairs={{0,4},{1,5},{2,6},{3,7},{4,0},{5,1},{6,2},{7,3},{8,12},{9,13},{10,... | collective-permute-start | bytes 786440 | tf_op jit(solution)/shard_map/ppermute | solution.py:391
  55.3 12.0 %collective-permute-start.43 = (bf16[2,512,128]{2,1,0:T(8,128)(2,1)}, bf16[2,512,128]{2,1,0:T(8,128)(2,1)S(1)}, u32[]{:S(2)}, u32[]{:S(2)}) collective-permute-start(bf16[2,512,128]{2,1,0:T(8,128)(2,1)} %get-tuple-element.90), channel_id=1, source_target_pairs={{0,5},{1,4},{2,7},{3,6},{4,1},{5,0},{6,3},{7,2},{8,13},{9,12},{10,... | collective-permute-start | bytes 786440 | tf_op jit(solution)/shard_map/ppermute | solution.py:391
  57.0 23.3 %collective-permute-start.37 = (bf16[2,512,128]{2,1,0:T(8,128)(2,1)}, bf16[2,512,128]{2,1,0:T(8,128)(2,1)S(1)}, u32[]{:S(2)}, u32[]{:S(2)}) collective-permute-start(bf16[2,512,128]{2,1,0:T(8,128)(2,1)} %get-tuple-element.83), channel_id=1, source_target_pairs={{0,6},{1,7},{2,4},{3,5},{4,2},{5,3},{6,0},{7,1},{8,14},{9,15},{10,... | collective-permute-start | bytes 786440 | tf_op jit(solution)/shard_map/ppermute | solution.py:391
  59.8 20.6 %collective-permute-start.38 = (bf16[2,512,128]{2,1,0:T(8,128)(2,1)}, bf16[2,512,128]{2,1,0:T(8,128)(2,1)S(1)}, u32[]{:S(2)}, u32[]{:S(2)}) collective-permute-start(bf16[2,512,128]{2,1,0:T(8,128)(2,1)} %get-tuple-element.84), channel_id=1, source_target_pairs={{0,7},{1,6},{2,5},{3,4},{4,3},{5,2},{6,1},{7,0},{8,15},{9,14},{10,... | collective-permute-start | bytes 786440 | tf_op jit(solution)/shard_map/ppermute | solution.py:391
  88.1 68.7 %all-to-all-start = ((bf16[16,136,128]{2,1,0:T(8,128)(2,1)}), bf16[16,136,128]{2,1,0:T(8,128)(2,1)S(1)}, u32[]{:S(2)}, u32[]{:S(2)}) async-start(bf16[16,136,128]{2,1,0:T(8,128)(2,1)} %shard_map.70), calls=%async_computation | async-start | bytes 1114112 | tf_op jit(solution)/shard_map/all_to_all | solution.py:443
  95.4 10.2 %collective-permute-start.18 = (bf16[2,512,128]{2,1,0:T(8,128)(2,1)}, bf16[2,512,128]{2,1,0:T(8,128)(2,1)S(1)}, u32[]{:S(2)}, u32[]{:S(2)}) collective-permute-start(bf16[2,512,128]{2,1,0:T(8,128)(2,1)} %get-tuple-element.61), channel_id=1, source_target_pairs={{0,2},{1,3},{2,0},{3,1},{4,6},{5,7},{6,4},{7,5},{8,10},{9,11},{10,... | collective-permute-start | bytes 786440 | tf_op jit(solution)/shard_map/ppermute | solution.py:391
  96.9 15.6 %collective-permute-start.19 = (bf16[2,512,128]{2,1,0:T(8,128)(2,1)}, bf16[2,512,128]{2,1,0:T(8,128)(2,1)S(1)}, u32[]{:S(2)}, u32[]{:S(2)}) collective-permute-start(bf16[2,512,128]{2,1,0:T(8,128)(2,1)} %get-tuple-element.62), channel_id=1, source_target_pairs={{0,3},{1,2},{2,1},{3,0},{4,7},{5,6},{6,5},{7,4},{8,11},{9,10},{10,... | collective-permute-start | bytes 786440 | tf_op jit(solution)/shard_map/ppermute | solution.py:391
  97.3 15.2 %collective-permute-start.20 = (bf16[2,512,128]{2,1,0:T(8,128)(2,1)}, bf16[2,512,128]{2,1,0:T(8,128)(2,1)S(1)}, u32[]{:S(2)}, u32[]{:S(2)}) collective-permute-start(bf16[2,512,128]{2,1,0:T(8,128)(2,1)} %get-tuple-element.63), channel_id=1, source_target_pairs={{0,4},{1,5},{2,6},{3,7},{4,0},{5,1},{6,2},{7,3},{8,12},{9,13},{10,... | collective-permute-start | bytes 786440 | tf_op jit(solution)/shard_map/ppermute | solution.py:391
  98.9 16.0 %collective-permute-start.21 = (bf16[2,512,128]{2,1,0:T(8,128)(2,1)}, bf16[2,512,128]{2,1,0:T(8,128)(2,1)S(1)}, u32[]{:S(2)}, u32[]{:S(2)}) collective-permute-start(bf16[2,512,128]{2,1,0:T(8,128)(2,1)} %get-tuple-element.64), channel_id=1, source_target_pairs={{0,5},{1,4},{2,7},{3,6},{4,1},{5,0},{6,3},{7,2},{8,13},{9,12},{10,... | collective-permute-start | bytes 786440 | tf_op jit(solution)/shard_map/ppermute | solution.py:391
  99.6 28.4 %collective-permute-start.15 = (bf16[2,512,128]{2,1,0:T(8,128)(2,1)}, bf16[2,512,128]{2,1,0:T(8,128)(2,1)S(1)}, u32[]{:S(2)}, u32[]{:S(2)}) collective-permute-start(bf16[2,512,128]{2,1,0:T(8,128)(2,1)} %get-tuple-element.57), channel_id=1, source_target_pairs={{0,6},{1,7},{2,4},{3,5},{4,2},{5,3},{6,0},{7,1},{8,14},{9,15},{10,... | collective-permute-start | bytes 786440 | tf_op jit(solution)/shard_map/ppermute | solution.py:391
  105.6 22.4 %collective-permute-start.16 = (bf16[2,512,128]{2,1,0:T(8,128)(2,1)}, bf16[2,512,128]{2,1,0:T(8,128)(2,1)S(1)}, u32[]{:S(2)}, u32[]{:S(2)}) collective-permute-start(bf16[2,512,128]{2,1,0:T(8,128)(2,1)} %get-tuple-element.58), channel_id=1, source_target_pairs={{0,7},{1,6},{2,5},{3,4},{4,3},{5,2},{6,1},{7,0},{8,15},{9,14},{10,... | collective-permute-start | bytes 786440 | tf_op jit(solution)/shard_map/ppermute | solution.py:391
  142.6 9.3 %collective-permute-start.29 = (bf16[136,128]{1,0:T(8,128)(2,1)S(1)}, bf16[136,128]{1,0:T(8,128)(2,1)S(1)}, u32[]{:S(2)}, u32[]{:S(2)}) collective-permute-start(bf16[136,128]{1,0:T(8,128)(2,1)S(1)} %get-tuple-element.75), channel_id=1, source_target_pairs={{0,8},{1,9},{2,10},{3,11},{4,12},{5,13},{6,14},{7,15},{8,0},{9,1},... | collective-permute-start | bytes 104456 | tf_op jit(solution)/shard_map/ppermute | solution.py:391
  145.0 10.6 %collective-permute-start.31 = (bf16[136,128]{1,0:T(8,128)(2,1)S(1)}, bf16[136,128]{1,0:T(8,128)(2,1)S(1)}, u32[]{:S(2)}, u32[]{:S(2)}) collective-permute-start(bf16[136,128]{1,0:T(8,128)(2,1)S(1)} %get-tuple-element.77), channel_id=1, source_target_pairs={{0,10},{1,11},{2,8},{3,9},{4,14},{5,15},{6,12},{7,13},{8,2},{9,3},... | collective-permute-start | bytes 104456 | tf_op jit(solution)/shard_map/ppermute | solution.py:391
  148.1 10.0 %collective-permute-start.32 = (bf16[136,128]{1,0:T(8,128)(2,1)S(1)}, bf16[136,128]{1,0:T(8,128)(2,1)S(1)}, u32[]{:S(2)}, u32[]{:S(2)}) collective-permute-start(bf16[136,128]{1,0:T(8,128)(2,1)S(1)} %get-tuple-element.78), channel_id=1, source_target_pairs={{0,11},{1,10},{2,9},{3,8},{4,15},{5,14},{6,13},{7,12},{8,3},{9,2},... | collective-permute-start | bytes 104456 | tf_op jit(solution)/shard_map/ppermute | solution.py:391
  148.8 9.3 %collective-permute-start.33 = (bf16[136,128]{1,0:T(8,128)(2,1)S(1)}, bf16[136,128]{1,0:T(8,128)(2,1)S(1)}, u32[]{:S(2)}, u32[]{:S(2)}) collective-permute-start(bf16[136,128]{1,0:T(8,128)(2,1)S(1)} %get-tuple-element.79), channel_id=1, source_target_pairs={{0,12},{1,13},{2,14},{3,15},{4,8},{5,9},{6,10},{7,11},{8,4},{9,5},... | collective-permute-start | bytes 104456 | tf_op jit(solution)/shard_map/ppermute | solution.py:391
  (24 other events, 123.8 us)

commit v7 on v5

--- a/solution.py
+++ b/solution.py
@@ -12,6 +12,7 @@
 NEG = -1e30
 STAT_ROWS = 8
 SMALL_VMEM = 12 * 2**20
+LARGE_VMEM = 56 * 2**20
 
 
 VMEM_SPEC = pl.BlockSpec(memory_space=pltpu.VMEM)
@@ -321,7 +322,7 @@
         out_ref[...] = held[own_ref[0] ^ k]
 
 
-def split_heads(own, cache_k, cache_v, request):
+def split_heads(own, cache_k, cache_v, request, grant):
     _, slots, kv_heads, dim = cache_k.shape
     return pl.pallas_call(
         functools.partial(split_kernel, request=request),
@@ -333,7 +334,7 @@
             pltpu.VMEM((kv_heads, 2, slots, dim), jnp.bfloat16),
             pltpu.SemaphoreType.DMA((2,)),
         ],
-        compiler_params=pltpu.CompilerParams(vmem_limit_bytes=2 * SMALL_VMEM),
+        compiler_params=pltpu.CompilerParams(vmem_limit_bytes=grant),
     )(own, cache_k, cache_v)
 
 
@@ -362,10 +363,9 @@
         2, requests, devices_seq * local_rows, head_dim
     )
 
-    early = kv_heads - 2
     kv_blocks = []
     for r in range(requests):
-        parts = split_heads(own[None], cache_k, cache_v, r)
+        parts = split_heads(own[None], cache_k, cache_v, r, LARGE_VMEM if r == 0 else 2 * SMALL_VMEM)
         moved = [parts[0]]
         for k in range(1, kv_heads):
             moved.append(lax.ppermute(parts[k], "seq", [(i, i ^ k) for i in range(devices_seq)]))
@@ -378,10 +378,9 @@
         fresh_shift = jnp.where(block == spread - 1, 0, -devices_seq * local_rows)
         info = jnp.stack([valid, fresh_shift, own]).astype(jnp.int32)
         rows = (r * per_source, per_source, group_size)
-        state = attend(
-            info, head_q, kv_blocks[r], tuple(range(early)), (head_fresh[0, r], head_fresh[1, r]), None, False, *rows
+        part = attend(
+            info, head_q, kv_blocks[r], tuple(range(kv_heads)), (head_fresh[0, r], head_fresh[1, r]), None, True, *rows
         )
-        part = attend(info, head_q, kv_blocks[r], tuple(range(early, kv_heads)), None, state, True, *rows)
         part = lax.all_to_all(part, "seq", split_axis=0, concat_axis=0, tiled=True)
         part = part.reshape(spread, kv_heads, per_source + STAT_ROWS, head_dim)
         out = merge(part, r, requests, local_rows, group_size, out)

time: 136 us -> 156 us (1.15)
  waiting for transfers between devices: 39.3 us -> 61.9 us
  starting transfers between devices: 30 us -> 34.9 us
  local copies, waits for them, and re-layouts: 22.1 us -> 18.2 us
  Pallas kernels: 41.2 us -> 37.7 us
    ppermute x14, waiting for transfers between devices: 10.2 us -> 42 us  [attention(): lax.ppermute(parts[k], 'seq', [(i, i ^ k) for i in range(devices_seq)])]
    all_to_all x1, waiting for transfers between devices: 16.7 us -> 6.28 us  [attention(): lax.all_to_all(pack(queries, fresh, devices_seq), 'seq', split_axis=0, co...]
    pallas_call x4 -> x2, Pallas kernels: 33.6 us -> 28.8 us  [attend(): pl.pallas_call(functools.partial(attend_kernel, order=order, total_blocks...]
    ppermute x14, starting transfers between devices: 12.8 us -> 16.9 us  [attention(): lax.ppermute(parts[k], 'seq', [(i, i ^ k) for i in range(devices_seq)])]
    unnamed x52 -> x48, local copies, waits for them, and re-layouts: 21.4 us -> 17.5 us
  transfers between devices with their start and end apart: 17 -> 17, of which waited for: 6 -> 11; matrix products, arithmetic and copies ran while one was open for 1% -> 1% of each run, Pallas kernels for 25% -> 14%
where the time goes in v7:
time: 156 us; the launch traced here: 155 us
  waiting for transfers between devices  61.9 us (40%)
  Pallas kernels  37.7 us (24%)
  starting transfers between devices  34.9 us (22%)
  local copies, waits for them, and re-layouts  18.2 us (12%)
    ppermute x14, waiting for transfers between devices, attention(): lax.ppermute(parts[k], 'seq', [(i, i ^ k) for i in range(devices_seq)])  42 us
    pallas_call x2, Pallas kernels, attend(): pl.pallas_call(functools.partial(attend_kernel, order=order, total_blocks...  28.8 us
    unnamed x48, local copies, waits for them, and re-layouts  17.5 us
    ppermute x14, starting transfers between devices, attention(): lax.ppermute(parts[k], 'seq', [(i, i ^ k) for i in range(devices_seq)])  16.9 us
    all_to_all x2, waiting for transfers between devices, attention(): part = lax.all_to_all(part, 'seq', split_axis=0, concat_axis=0, tiled=True)  13.6 us
    all_to_all x2, starting transfers between devices, attention(): part = lax.all_to_all(part, 'seq', split_axis=0, concat_axis=0, tiled=True)  11.5 us
    all_to_all x1, starting transfers between devices, attention(): lax.all_to_all(pack(queries, fresh, devices_seq), 'seq', split_axis=0, co...  6.55 us
    all_to_all x1, waiting for transfers between devices, attention(): lax.all_to_all(pack(queries, fresh, devices_seq), 'seq', split_axis=0, co...  6.28 us
  transfers between devices with their start and end apart: 17, of which 11 were waited for; matrix products, arithmetic and copies ran while one was open for 1% of the time, Pallas kernels for 14%

profile of v7, /device:TPU:13, one launch (start us, length us, event | category | flops | bytes accessed | tf_op | source)
XLA Modules:
  0.0 155.0 jit_solution(3143696487429964775)
XLA Ops:
  3.0 6.5 %all-to-all-start = ((bf16[16,288,128]{2,1,0:T(8,128)(2,1)}), bf16[16,288,128]{2,1,0:T(8,128)(2,1)S(1)}, u32[]{:S(2)}, u32[]{:S(2)}) async-start(bf16[16,288,128]{2,1,0:T(8,128)(2,1)} %shard_map.64), calls=%async_computation | async-start | bytes 2359296 | tf_op jit(solution)/shard_map/all_to_all | solution.py:356
  9.5 3.3 %shard_map.67 = (bf16[2,512,128]{2,1,0:T(8,128)(2,1)}, bf16[2,512,128]{2,1,0:T(8,128)(2,1)}, bf16[2,512,128]{2,1,0:T(8,128)(2,1)}, bf16[2,512,128]{2,1,0:T(8,128...) custom-call(s32[1]{0:T(128)} %bitcast.3.own_ref, ...), custom_call_target="tpu_custom_call" | custom-call | tf_op jit(solution)/shard_map/pallas_call | solution.py:327
  15.1 1.6 %collective-permute-start.11 = (bf16[2,512,128]{2,1,0:T(8,128)(2,1)}, bf16[2,512,128]{2,1,0:T(8,128)(2,1)S(1)}, u32[]{:S(2)}, u32[]{:S(2)}) collective-permute-start(bf16[2,512,128]{2,1,0:T(8,128)(2,1)} %get-tuple-element.34), channel_id=1, source_target_pairs={{0,5},{1,4},{2,7},{3,6},{4,1},{5,0},{6,3},{7,2},{8,13},{9,12},{10,... | collective-permute-start | bytes 786440 | tf_op jit(solution)/shard_map/ppermute | solution.py:371
  19.3 6.6 %collective-permute-done.8.refs_4_ = bf16[2,512,128]{2,1,0:T(8,128)(2,1)S(1)} collective-permute-done((bf16[2,512,128]{2,1,0:T(8,128)(2,1)}, bf16[2,512,128]{2,1,0:T(8,128)(2,1)S(1)}, u32[]{:S(2)}, u32[]{:S(2)}) %collective-permute-start.8) | collective-permute-done | bytes 262176 | tf_op jit(solution)/shard_map/ppermute | solution.py:371
  25.9 4.9 %collective-permute-start.13 = (bf16[2,512,128]{2,1,0:T(8,128)(2,1)}, bf16[2,512,128]{2,1,0:T(8,128)(2,1)S(1)}, u32[]{:S(2)}, u32[]{:S(2)}) collective-permute-start(bf16[2,512,128]{2,1,0:T(8,128)(2,1)} %get-tuple-element.36), channel_id=1, source_target_pairs={{0,7},{1,6},{2,5},{3,4},{4,3},{5,2},{6,1},{7,0},{8,15},{9,14},{10,... | collective-permute-start | bytes 786440 | tf_op jit(solution)/shard_map/ppermute | solution.py:371
  30.9 6.3 %all-to-all-done.refs_1_ = bf16[16,288,128]{2,1,0:T(8,128)(2,1)S(1)} async-done(((bf16[16,288,128]{2,1,0:T(8,128)(2,1)}), bf16[16,288,128]{2,1,0:T(8,128)(2,1)S(1)}, u32[]{:S(2)}, u32[]{:S(2)}) %all-to-all-start) | async-done | bytes 1179680 | tf_op jit(solution)/shard_map/all_to_all | solution.py:356
  38.7 2.8 %collective-permute-done.11.refs_7_ = bf16[2,512,128]{2,1,0:T(8,128)(2,1)S(1)} collective-permute-done((bf16[2,512,128]{2,1,0:T(8,128)(2,1)}, bf16[2,512,128]{2,1,0:T(8,128)(2,1)S(1)}, u32[]{:S(2)}, u32[]{:S(2)}) %collective-permute-start.11) | collective-permute-done | bytes 262176 | tf_op jit(solution)/shard_map/ppermute | solution.py:371
  42.2 5.4 %collective-permute-done.12.refs_8_ = bf16[2,512,128]{2,1,0:T(8,128)(2,1)S(1)} collective-permute-done((bf16[2,512,128]{2,1,0:T(8,128)(2,1)}, bf16[2,512,128]{2,1,0:T(8,128)(2,1)S(1)}, u32[]{:S(2)}, u32[]{:S(2)}) %collective-permute-start.12) | collective-permute-done | bytes 262176 | tf_op jit(solution)/shard_map/ppermute | solution.py:371
  48.3 5.2 %collective-permute-done.13.refs_9_ = bf16[2,512,128]{2,1,0:T(8,128)(2,1)S(1)} collective-permute-done((bf16[2,512,128]{2,1,0:T(8,128)(2,1)}, bf16[2,512,128]{2,1,0:T(8,128)(2,1)S(1)}, u32[]{:S(2)}, u32[]{:S(2)}) %collective-permute-start.13) | collective-permute-done | bytes 262176 | tf_op jit(solution)/shard_map/ppermute | solution.py:371
  61.8 14.0 %shard_map.68 = bf16[16,136,128]{2,1,0:T(8,128)(2,1)S(1)} custom-call(s32[3]{0:T(128)S(1)} %add_add_fusion.1.refs_0_, bf16[16,288,128]{2,1,0:T(8,128)(2,1)S(1)} %all-to-all-done.refs_1_, bf16[2,512,128]{2,1,0:T(8,128)(2,1)S(1)} %copy-done.6, bf16[2,512,128]{2,1,0:T(8,128)(2,1)S(1)} %copy-done.8, bf16[2,512,128]{2,1,0:T(8,128)(2,1)S(1)} %copy-done.10, ...), custom_call_target="tpu_custom_call" | custom-call | flops 4294967296 | bytes 3145728 | tf_op jit(solution)/shard_map/pallas_call | solution.py:222
  76.6 4.4 %all-to-all-start.2 = ((bf16[16,136,128]{2,1,0:T(8,128)(2,1)}), bf16[16,136,128]{2,1,0:T(8,128)(2,1)S(1)}, u32[]{:S(2)}, u32[]{:S(2)}) async-start(bf16[16,136,128]{2,1,0:T(8,128)(2,1)} %copy-done.4), calls=%async_computation.2 | async-start | bytes 1114112 | tf_op jit(solution)/shard_map/all_to_all | solution.py:384
  81.1 1.6 %copy-done.1 = bf16[2,512,8,128]{3,2,1,0:T(8,128)(2,1)S(1)} copy-done((bf16[2,512,8,128]{3,2,1,0:T(8,128)(2,1)S(1)}, bf16[2,512,8,128]{3,2,1,0:T(8,128)(2,1)}, u32[]{:S(2)}) %copy-start.1) | copy-done | bytes 2097176
  82.7 1.9 %shard_map.65 = (bf16[2,512,128]{2,1,0:T(8,128)(2,1)S(1)}, bf16[2,512,128]{2,1,0:T(8,128)(2,1)S(1)}, bf16[2,512,128]{2,1,0:T(8,128)(2,1)S(1)}, bf16[2,512,128]{2...) custom-call(s32[1]{0:T(128)} %bitcast.3.own_ref, ...), custom_call_target="tpu_custom_call" | custom-call | tf_op jit(solution)/shard_map/pallas_call | solution.py:327
  87.5 1.6 %collective-permute-start.4 = (bf16[2,512,128]{2,1,0:T(8,128)(2,1)}, bf16[2,512,128]{2,1,0:T(8,128)(2,1)S(1)}, u32[]{:S(2)}, u32[]{:S(2)}) collective-permute-start(bf16[2,512,128]{2,1,0:T(8,128)(2,1)} %get-tuple-element.26), channel_id=1, source_target_pairs={{0,5},{1,4},{2,7},{3,6},{4,1},{5,0},{6,3},{7,2},{8,13},{9,12},{10,... | collective-permute-start | bytes 786440 | tf_op jit(solution)/shard_map/ppermute | solution.py:371
  90.4 6.2 %collective-permute-done.1.refs_4_ = bf16[2,512,128]{2,1,0:T(8,128)(2,1)S(1)} collective-permute-done((bf16[2,512,128]{2,1,0:T(8,128)(2,1)S(1)}, bf16[2,512,128]{2,1,0:T(8,128)(2,1)S(1)}, u32[]{:S(2)}, u32[]{:S(2)}) %collective-permute-start.1) | collective-permute-done | bytes 262176 | tf_op jit(solution)/shard_map/ppermute | solution.py:371
  96.5 1.7 %collective-permute-start.6 = (bf16[2,512,128]{2,1,0:T(8,128)(2,1)}, bf16[2,512,128]{2,1,0:T(8,128)(2,1)S(1)}, u32[]{:S(2)}, u32[]{:S(2)}) collective-permute-start(bf16[2,512,128]{2,1,0:T(8,128)(2,1)} %get-tuple-element.28), channel_id=1, source_target_pairs={{0,7},{1,6},{2,5},{3,4},{4,3},{5,2},{6,1},{7,0},{8,15},{9,14},{10,... | collective-permute-start | bytes 786440 | tf_op jit(solution)/shard_map/ppermute | solution.py:371
  98.9 3.6 %collective-permute-done.2.refs_5_ = bf16[2,512,128]{2,1,0:T(8,128)(2,1)S(1)} collective-permute-done((bf16[2,512,128]{2,1,0:T(8,128)(2,1)}, bf16[2,512,128]{2,1,0:T(8,128)(2,1)S(1)}, u32[]{:S(2)}, u32[]{:S(2)}) %collective-permute-start.2) | collective-permute-done | bytes 262176 | tf_op jit(solution)/shard_map/ppermute | solution.py:371
  102.9 6.0 %collective-permute-done.5.refs_8_ = bf16[2,512,128]{2,1,0:T(8,128)(2,1)S(1)} collective-permute-done((bf16[2,512,128]{2,1,0:T(8,128)(2,1)}, bf16[2,512,128]{2,1,0:T(8,128)(2,1)S(1)}, u32[]{:S(2)}, u32[]{:S(2)}) %collective-permute-start.5) | collective-permute-done | bytes 262176 | tf_op jit(solution)/shard_map/ppermute | solution.py:371
  108.9 5.9 %collective-permute-done.6.refs_9_ = bf16[2,512,128]{2,1,0:T(8,128)(2,1)S(1)} collective-permute-done((bf16[2,512,128]{2,1,0:T(8,128)(2,1)}, bf16[2,512,128]{2,1,0:T(8,128)(2,1)S(1)}, u32[]{:S(2)}, u32[]{:S(2)}) %collective-permute-start.6) | collective-permute-done | bytes 262176 | tf_op jit(solution)/shard_map/ppermute | solution.py:371
  114.8 1.3 copy-done.3
  117.0 14.8 %shard_map.66 = bf16[16,136,128]{2,1,0:T(8,128)(2,1)} custom-call(s32[3]{0:T(128)S(1)} %add_add_fusion.refs_0_, bf16[16,288,128]{2,1,0:T(8,128)(2,1)S(1)} %copy-done.3, bf16[2,512,128]{2,1,0:T(8,128)(2,1)S(1)} %copy-done.18, bf16[2,512,128]{2,1,0:T(8,128)(2,1)S(1)} %collective-permute-done.refs_3_, bf16[2,512,128]{2,1,0:T(8,128)(2,1)S(1)} %collective-permute-done.1.refs_4_, ...), custom_call_target="tpu_custom_call" | custom-call | flops 4294967296 | bytes 3145728 | tf_op jit(solution)/shard_map/pallas_call | solution.py:222
  131.9 7.0 %all-to-all-start.1 = ((bf16[16,136,128]{2,1,0:T(8,128)(2,1)}), bf16[16,136,128]{2,1,0:T(8,128)(2,1)S(1)}, u32[]{:S(2)}, u32[]{:S(2)}) async-start(bf16[16,136,128]{2,1,0:T(8,128)(2,1)} %shard_map.66), calls=%async_computation.1 | async-start | bytes 1114112 | tf_op jit(solution)/shard_map/all_to_all | solution.py:384
  140.1 13.6 %all-to-all-done.1 = bf16[16,136,128]{2,1,0:T(8,128)(2,1)S(1)} async-done(((bf16[16,136,128]{2,1,0:T(8,128)(2,1)}), bf16[16,136,128]{2,1,0:T(8,128)(2,1)S(1)}, u32[]{:S(2)}, u32[]{:S(2)}) %all-to-all-start.1) | async-done | bytes 557088 | tf_op jit(solution)/shard_map/all_to_all | solution.py:384
  153.7 1.3 shard_map.70
  (73 shorter events, 26.0 us)
Async XLA Ops:
  3.0 34.2 %all-to-all-start = ((bf16[16,288,128]{2,1,0:T(8,128)(2,1)}), bf16[16,288,128]{2,1,0:T(8,128)(2,1)S(1)}, u32[]{:S(2)}, u32[]{:S(2)}) async-start(bf16[16,288,128]{2,1,0:T(8,128)(2,1)} %shard_map.64), calls=%async_computation | async-start | bytes 2359296 | tf_op jit(solution)/shard_map/all_to_all | solution.py:356
  9.5 7.3 %copy-start.23 = (s32[2]{0:T(128)S(1)}, s32[2]{0:T(128)}, u32[]{:S(2)}) copy-start(s32[2]{0:T(128)} %param.11) | copy-start | bytes 28
  12.8 5.2 %collective-permute-start.7 = (bf16[2,512,128]{2,1,0:T(8,128)(2,1)}, bf16[2,512,128]{2,1,0:T(8,128)(2,1)S(1)}, u32[]{:S(2)}, u32[]{:S(2)}) collective-permute-start(bf16[2,512,128]{2,1,0:T(8,128)(2,1)} %get-tuple-element.30), channel_id=1, source_target_pairs={{0,1},{1,0},{2,3},{3,2},{4,5},{5,4},{6,7},{7,6},{8,9},{9,8},{10,11... | collective-permute-start | bytes 786440 | tf_op jit(solution)/shard_map/ppermute | solution.py:371
  13.3 12.6 %collective-permute-start.8 = (bf16[2,512,128]{2,1,0:T(8,128)(2,1)}, bf16[2,512,128]{2,1,0:T(8,128)(2,1)S(1)}, u32[]{:S(2)}, u32[]{:S(2)}) collective-permute-start(bf16[2,512,128]{2,1,0:T(8,128)(2,1)} %get-tuple-element.31), channel_id=1, source_target_pairs={{0,2},{1,3},{2,0},{3,1},{4,6},{5,7},{6,4},{7,5},{8,10},{9,11},{10,... | collective-permute-start | bytes 786440 | tf_op jit(solution)/shard_map/ppermute | solution.py:371
  14.5 22.8 %collective-permute-start.9 = (bf16[2,512,128]{2,1,0:T(8,128)(2,1)}, bf16[2,512,128]{2,1,0:T(8,128)(2,1)S(1)}, u32[]{:S(2)}, u32[]{:S(2)}) collective-permute-start(bf16[2,512,128]{2,1,0:T(8,128)(2,1)} %get-tuple-element.32), channel_id=1, source_target_pairs={{0,3},{1,2},{2,1},{3,0},{4,7},{5,6},{6,5},{7,4},{8,11},{9,10},{10,... | collective-permute-start | bytes 786440 | tf_op jit(solution)/shard_map/ppermute | solution.py:371
  15.0 23.0 %collective-permute-start.10 = (bf16[2,512,128]{2,1,0:T(8,128)(2,1)}, bf16[2,512,128]{2,1,0:T(8,128)(2,1)S(1)}, u32[]{:S(2)}, u32[]{:S(2)}) collective-permute-start(bf16[2,512,128]{2,1,0:T(8,128)(2,1)} %get-tuple-element.33), channel_id=1, source_target_pairs={{0,4},{1,5},{2,6},{3,7},{4,0},{5,1},{6,2},{7,3},{8,12},{9,13},{10,... | collective-permute-start | bytes 786440 | tf_op jit(solution)/shard_map/ppermute | solution.py:371
  15.1 26.4 %collective-permute-start.11 = (bf16[2,512,128]{2,1,0:T(8,128)(2,1)}, bf16[2,512,128]{2,1,0:T(8,128)(2,1)S(1)}, u32[]{:S(2)}, u32[]{:S(2)}) collective-permute-start(bf16[2,512,128]{2,1,0:T(8,128)(2,1)} %get-tuple-element.34), channel_id=1, source_target_pairs={{0,5},{1,4},{2,7},{3,6},{4,1},{5,0},{6,3},{7,2},{8,13},{9,12},{10,... | collective-permute-start | bytes 786440 | tf_op jit(solution)/shard_map/ppermute | solution.py:371
  18.0 36.2 %copy-start.7 = (bf16[2,512,128]{2,1,0:T(8,128)(2,1)}, bf16[2,512,128]{2,1,0:T(8,128)(2,1)S(1)}, u32[]{:S(2)}) copy-start(bf16[2,512,128]{2,1,0:T(8,128)(2,1)S(1)} %collective-permute-done.7.refs_3_) | copy-start | bytes 786436
  18.0 29.5 %collective-permute-start.12 = (bf16[2,512,128]{2,1,0:T(8,128)(2,1)}, bf16[2,512,128]{2,1,0:T(8,128)(2,1)S(1)}, u32[]{:S(2)}, u32[]{:S(2)}) collective-permute-start(bf16[2,512,128]{2,1,0:T(8,128)(2,1)} %get-tuple-element.35), channel_id=1, source_target_pairs={{0,6},{1,7},{2,4},{3,5},{4,2},{5,3},{6,0},{7,1},{8,14},{9,15},{10,... | collective-permute-start | bytes 786440 | tf_op jit(solution)/shard_map/ppermute | solution.py:371
  25.9 28.3 %copy-start.9 = (bf16[2,512,128]{2,1,0:T(8,128)(2,1)}, bf16[2,512,128]{2,1,0:T(8,128)(2,1)S(1)}, u32[]{:S(2)}) copy-start(bf16[2,512,128]{2,1,0:T(8,128)(2,1)S(1)} %collective-permute-done.8.refs_4_) | copy-start | bytes 786436
  25.9 27.6 %collective-permute-start.13 = (bf16[2,512,128]{2,1,0:T(8,128)(2,1)}, bf16[2,512,128]{2,1,0:T(8,128)(2,1)S(1)}, u32[]{:S(2)}, u32[]{:S(2)}) collective-permute-start(bf16[2,512,128]{2,1,0:T(8,128)(2,1)} %get-tuple-element.36), channel_id=1, source_target_pairs={{0,7},{1,6},{2,5},{3,4},{4,3},{5,2},{6,1},{7,0},{8,15},{9,14},{10,... | collective-permute-start | bytes 786440 | tf_op jit(solution)/shard_map/ppermute | solution.py:371
  37.2 38.6 %copy-start.2 = (bf16[16,288,128]{2,1,0:T(8,128)(2,1)}, bf16[16,288,128]{2,1,0:T(8,128)(2,1)S(1)}, u32[]{:S(2)}) copy-start(bf16[16,288,128]{2,1,0:T(8,128)(2,1)S(1)} %all-to-all-done.refs_1_) | copy-start | bytes 3538948
  61.8 19.3 %copy-start = (bf16[2,512,8,128]{3,2,1,0:T(8,128)(2,1)S(1)}, bf16[2,512,8,128]{3,2,1,0:T(8,128)(2,1)}, u32[]{:S(2)}) copy-start(bf16[2,512,8,128]{3,2,1,0:T(8,128)(2,1)} %k_hbm.3) | copy-start | bytes 6291460
  76.6 55.2 %all-to-all-start.2 = ((bf16[16,136,128]{2,1,0:T(8,128)(2,1)}), bf16[16,136,128]{2,1,0:T(8,128)(2,1)S(1)}, u32[]{:S(2)}, u32[]{:S(2)}) async-start(bf16[16,136,128]{2,1,0:T(8,128)(2,1)} %copy-done.4), calls=%async_computation.2 | async-start | bytes 1114112 | tf_op jit(solution)/shard_map/all_to_all | solution.py:384
  81.1 1.6 %copy-start.1 = (bf16[2,512,8,128]{3,2,1,0:T(8,128)(2,1)S(1)}, bf16[2,512,8,128]{3,2,1,0:T(8,128)(2,1)}, u32[]{:S(2)}) copy-start(bf16[2,512,8,128]{3,2,1,0:T(8,128)(2,1)} %v_hbm.3) | copy-start | bytes 6291460
  85.3 3.9 %collective-permute-start = (bf16[2,512,128]{2,1,0:T(8,128)(2,1)S(1)}, bf16[2,512,128]{2,1,0:T(8,128)(2,1)S(1)}, u32[]{:S(2)}, u32[]{:S(2)}) collective-permute-start(bf16[2,512,128]{2,1,0:T(8,128)(2,1)S(1)} %get-tuple-element.22), channel_id=1, source_target_pairs={{0,1},{1,0},{2,3},{3,2},{4,5},{5,4},{6,7},{7,6},{8,9},{9,8},{10,11... | collective-permute-start | bytes 786440 | tf_op jit(solution)/shard_map/ppermute | solution.py:371
  85.7 10.8 %collective-permute-start.1 = (bf16[2,512,128]{2,1,0:T(8,128)(2,1)S(1)}, bf16[2,512,128]{2,1,0:T(8,128)(2,1)S(1)}, u32[]{:S(2)}, u32[]{:S(2)}) collective-permute-start(bf16[2,512,128]{2,1,0:T(8,128)(2,1)S(1)} %get-tuple-element.23), channel_id=1, source_target_pairs={{0,2},{1,3},{2,0},{3,1},{4,6},{5,7},{6,4},{7,5},{8,10},{9,11},{10,... | collective-permute-start | bytes 786440 | tf_op jit(solution)/shard_map/ppermute | solution.py:371
  86.9 15.6 %collective-permute-start.2 = (bf16[2,512,128]{2,1,0:T(8,128)(2,1)}, bf16[2,512,128]{2,1,0:T(8,128)(2,1)S(1)}, u32[]{:S(2)}, u32[]{:S(2)}) collective-permute-start(bf16[2,512,128]{2,1,0:T(8,128)(2,1)} %get-tuple-element.24), channel_id=1, source_target_pairs={{0,3},{1,2},{2,1},{3,0},{4,7},{5,6},{6,5},{7,4},{8,11},{9,10},{10,... | collective-permute-start | bytes 786440 | tf_op jit(solution)/shard_map/ppermute | solution.py:371
  87.5 15.0 %collective-permute-start.3 = (bf16[2,512,128]{2,1,0:T(8,128)(2,1)}, bf16[2,512,128]{2,1,0:T(8,128)(2,1)S(1)}, u32[]{:S(2)}, u32[]{:S(2)}) collective-permute-start(bf16[2,512,128]{2,1,0:T(8,128)(2,1)} %get-tuple-element.25), channel_id=1, source_target_pairs={{0,4},{1,5},{2,6},{3,7},{4,0},{5,1},{6,2},{7,3},{8,12},{9,13},{10,... | collective-permute-start | bytes 786440 | tf_op jit(solution)/shard_map/ppermute | solution.py:371
  87.5 15.3 %collective-permute-start.4 = (bf16[2,512,128]{2,1,0:T(8,128)(2,1)}, bf16[2,512,128]{2,1,0:T(8,128)(2,1)S(1)}, u32[]{:S(2)}, u32[]{:S(2)}) collective-permute-start(bf16[2,512,128]{2,1,0:T(8,128)(2,1)} %get-tuple-element.26), channel_id=1, source_target_pairs={{0,5},{1,4},{2,7},{3,6},{4,1},{5,0},{6,3},{7,2},{8,13},{9,12},{10,... | collective-permute-start | bytes 786440 | tf_op jit(solution)/shard_map/ppermute | solution.py:371
  89.2 19.7 %collective-permute-start.5 = (bf16[2,512,128]{2,1,0:T(8,128)(2,1)}, bf16[2,512,128]{2,1,0:T(8,128)(2,1)S(1)}, u32[]{:S(2)}, u32[]{:S(2)}) collective-permute-start(bf16[2,512,128]{2,1,0:T(8,128)(2,1)} %get-tuple-element.27), channel_id=1, source_target_pairs={{0,6},{1,7},{2,4},{3,5},{4,2},{5,3},{6,0},{7,1},{8,14},{9,15},{10,... | collective-permute-start | bytes 786440 | tf_op jit(solution)/shard_map/ppermute | solution.py:371
  96.5 18.3 %collective-permute-start.6 = (bf16[2,512,128]{2,1,0:T(8,128)(2,1)}, bf16[2,512,128]{2,1,0:T(8,128)(2,1)S(1)}, u32[]{:S(2)}, u32[]{:S(2)}) collective-permute-start(bf16[2,512,128]{2,1,0:T(8,128)(2,1)} %get-tuple-element.28), channel_id=1, source_target_pairs={{0,7},{1,6},{2,5},{3,4},{4,3},{5,2},{6,1},{7,0},{8,15},{9,14},{10,... | collective-permute-start | bytes 786440 | tf_op jit(solution)/shard_map/ppermute | solution.py:371
  114.8 1.3 copy-start.3
  131.9 21.8 %all-to-all-start.1 = ((bf16[16,136,128]{2,1,0:T(8,128)(2,1)}), bf16[16,136,128]{2,1,0:T(8,128)(2,1)S(1)}, u32[]{:S(2)}, u32[]{:S(2)}) async-start(bf16[16,136,128]{2,1,0:T(8,128)(2,1)} %shard_map.66), calls=%async_computation.1 | async-start | bytes 1114112 | tf_op jit(solution)/shard_map/all_to_all | solution.py:384
  (17 other events, 14.7 us)

commit v8 on v6

--- a/solution.py
+++ b/solution.py
@@ -24,7 +24,7 @@
     *refs, q_count, order, total_blocks, tile, group_size, row_start, with_fresh, with_state, final, out_count
 ):
     refs = list(refs)
-    info_ref = refs.pop(0)
+    length_ref, place_ref = refs.pop(0), refs.pop(0)
     q_hbm = [refs.pop(0) for _ in range(q_count)]
     kv_refs = [refs.pop(0) for _ in order]
     if with_fresh:
@@ -49,10 +49,9 @@
     tiles = rows // tile
     span = tile // per_source
     scale = math.log2(math.e) / math.sqrt(dim)
-    valid = info_ref[0]
-    fresh_shift = info_ref[1]
-    own = info_ref[2]
-    me = info_ref[3]
+    own, device_block, me = place_ref[0], place_ref[1], place_ref[2]
+    valid = jnp.clip(length_ref[0] - device_block * total_blocks * block_slots, 0, total_blocks * block_slots)
+    fresh_shift = jnp.where(device_block == q_ref.shape[0] // total_blocks - 1, 0, -rows)
 
     held = sorted({k // 2 for k in order})
     absent = [c for c in range(total_blocks // 2) if c not in held]
@@ -202,14 +201,14 @@
             result.wait()
 
 
-def attend(info, head_q, kv_blocks, order, fresh, state, final, out_count, sources, row_start, row_count, group_size):
+def attend(length, place, head_q, kv_blocks, order, fresh, state, final, out_count, sources, row_start, row_count, group_size):
     dim = head_q[0].shape[-1]
     slots = len(order) * kv_blocks[0].shape[1]
     rows = sources * row_count
     units = 0 if fresh is None else fresh[0].shape[0]
     tile = min(256, rows // 2)
-    operands = [info] + head_q + [kv_blocks[k] for k in order]
-    in_specs = [SMEM_SPEC] + [HBM_SPEC] * (len(head_q) + len(order))
+    operands = [length, place] + head_q + [kv_blocks[k] for k in order]
+    in_specs = [SMEM_SPEC] * 2 + [HBM_SPEC] * (len(head_q) + len(order))
     scratch = [
         pltpu.VMEM((sources, row_count, dim), jnp.bfloat16),
         pltpu.VMEM((slots, dim), jnp.bfloat16),
@@ -353,7 +352,7 @@
         out_ref[...] = held[own_ref[0] ^ k]
 
 
-def split_heads(own, cache_k, cache_v, request):
+def split_heads(own, cache_k, cache_v, request, grant):
     _, slots, kv_heads, dim = cache_k.shape
     return pl.pallas_call(
         functools.partial(split_kernel, request=request),
@@ -365,13 +364,12 @@
             pltpu.VMEM((kv_heads, 2, slots, dim), jnp.bfloat16),
             pltpu.SemaphoreType.DMA((2,)),
         ],
-        compiler_params=pltpu.CompilerParams(vmem_limit_bytes=LARGE_VMEM),
+        compiler_params=pltpu.CompilerParams(vmem_limit_bytes=grant),
     )(own, cache_k, cache_v)
 
 
 def attention(queries, new_k, new_v, cache_k, cache_v, cache_len):
     requests, local_rows, heads, head_dim = queries.shape
-    slots = cache_k.shape[1]
     kv_heads = cache_k.shape[2]
     group_size = heads // kv_heads
     devices_seq = lax.axis_size("seq")
@@ -407,40 +405,31 @@
         2, requests, devices_seq * local_rows, head_dim
     )
 
-    early = kv_heads - 2
     kv_blocks = []
     for r in range(requests):
-        parts = split_heads(own[None], cache_k, cache_v, r)
+        parts = split_heads(own[None], cache_k, cache_v, r, LARGE_VMEM if r == 0 else 2 * SMALL_VMEM)
         moved = [parts[0]]
         for k in range(1, kv_heads):
             moved.append(to_partner(parts[k], k))
         kv_blocks.append(moved)
 
+    place = jnp.stack([own, block, seq_index]).astype(jnp.int32)
     out = None
     for r in range(requests):
-        held = kv_heads * slots
-        valid = jnp.clip(cache_len[r] - block * held, 0, held)
-        fresh_shift = jnp.where(block == spread - 1, 0, -devices_seq * local_rows)
-        info = jnp.stack([valid, fresh_shift, own, seq_index]).astype(jnp.int32)
         rows = (devices_seq, r * per_source, per_source, group_size)
-        separate = direct and r == requests - 1
-        out_count = devices_seq if separate else 1
-        state = attend(
-            info,
+        parts = attend(
+            cache_len[r : r + 1],
+            place,
             head_q,
             kv_blocks[r],
-            tuple(range(early)),
+            tuple(range(kv_heads)),
             (head_fresh[0, r], head_fresh[1, r]),
             None,
-            False,
+            True,
             1,
             *rows,
         )
-        parts = attend(info, head_q, kv_blocks[r], tuple(range(early, kv_heads)), None, state, True, out_count, *rows)
-        if separate:
-            parts = [parts[0]] + [to_partner(parts[k], k) for k in range(1, devices_seq)]
-        else:
-            parts = [lax.all_to_all(parts[0], "seq", split_axis=0, concat_axis=0, tiled=True)]
+        parts = [lax.all_to_all(parts[0], "seq", split_axis=0, concat_axis=0, tiled=True)]
         out = merge(own[None], parts, kv_heads, spread, r, requests, local_rows, group_size, out)
     return out
 

time: 164 us -> 172 us (1.049)
  the two profiles are of different devices: /device:TPU:5 before, /device:TPU:0 now
where the time goes in v8:
time: 172 us; the launch traced here: 169 us
  waiting for transfers between devices  79.7 us (46%)
  starting transfers between devices  45.4 us (26%)
  Pallas kernels  37.8 us (22%)
  local copies, waits for them, and re-layouts  5.21 us (3%)
    ppermute x29, waiting for transfers between devices, to_partner(): return lax.ppermute(array, 'seq', [(i, i ^ k) for i in devices])  66.2 us
    ppermute x29, starting transfers between devices, to_partner(): return lax.ppermute(array, 'seq', [(i, i ^ k) for i in devices])  38.2 us
    pallas_call x2, Pallas kernels, attend(): pl.pallas_call(functools.partial(attend_kernel, q_count=len(head_q), out_...  30.9 us
    all_to_all x2, waiting for transfers between devices, attention(): lax.all_to_all(parts[0], 'seq', split_axis=0, concat_axis=0, tiled=True)  13.5 us
    all_to_all x2, starting transfers between devices, attention(): lax.all_to_all(parts[0], 'seq', split_axis=0, concat_axis=0, tiled=True)  7.18 us
    pallas_call x2, Pallas kernels, split_heads(): pl.pallas_call(functools.partial(split_kernel, request=request), in_specs...  4.3 us
    unnamed x43, local copies, waits for them, and re-layouts  3.77 us
  transfers between devices with their start and end apart: 31, of which 17 were waited for; matrix products, arithmetic and copies ran while one was open for 1% of the time, Pallas kernels for 12%

profile of v8, /device:TPU:0, one launch (start us, length us, event | category | flops | bytes accessed | tf_op | source)
XLA Modules:
  0.0 169.2 jit_solution(6505147185407285590)
XLA Ops:
  1.9 3.6 %collective-permute-start.8 = (bf16[288,128]{1,0:T(8,128)(2,1)S(1)}, bf16[288,128]{1,0:T(8,128)(2,1)S(1)}, u32[]{:S(2)}, u32[]{:S(2)}) collective-permute-start(bf16[288,128]{1,0:T(8,128)(2,1)S(1)} %get-tuple-element.30), channel_id=1, source_target_pairs={{0,9},{1,8},{2,11},{3,10},{4,13},{5,12},{6,15},{7,14},{8,1},{9,0},... | collective-permute-start | bytes 221192 | tf_op jit(solution)/shard_map/ppermute | solution.py:389
  7.7 2.9 %collective-permute-start.10 = (bf16[288,128]{1,0:T(8,128)(2,1)S(1)}, bf16[288,128]{1,0:T(8,128)(2,1)S(1)}, u32[]{:S(2)}, u32[]{:S(2)}) collective-permute-start(bf16[288,128]{1,0:T(8,128)(2,1)S(1)} %get-tuple-element.32), channel_id=1, source_target_pairs={{0,11},{1,10},{2,9},{3,8},{4,15},{5,14},{6,13},{7,12},{8,3},{9,2},... | collective-permute-start | bytes 221192 | tf_op jit(solution)/shard_map/ppermute | solution.py:389
  11.9 3.3 %shard_map.67 = (bf16[2,512,128]{2,1,0:T(8,128)(2,1)}, bf16[2,512,128]{2,1,0:T(8,128)(2,1)}, bf16[2,512,128]{2,1,0:T(8,128)(2,1)}, bf16[2,512,128]{2,1,0:T(8,128...) custom-call(s32[1]{0:T(128)} %bitcast.own_ref, ...), custom_call_target="tpu_custom_call" | custom-call | tf_op jit(solution)/shard_map/pallas_call | solution.py:357
  20.7 3.5 %collective-permute-done.3.refs_6_ = bf16[288,128]{1,0:T(8,128)(2,1)S(1)} collective-permute-done((bf16[288,128]{1,0:T(8,128)(2,1)S(1)}, bf16[288,128]{1,0:T(8,128)(2,1)S(1)}, u32[]{:S(2)}, u32[]{:S(2)}) %collective-permute-start.3) | collective-permute-done | bytes 73760 | tf_op jit(solution)/shard_map/ppermute | solution.py:389
  25.3 3.2 %collective-permute-done.4.refs_7_ = bf16[288,128]{1,0:T(8,128)(2,1)S(1)} collective-permute-done((bf16[288,128]{1,0:T(8,128)(2,1)S(1)}, bf16[288,128]{1,0:T(8,128)(2,1)S(1)}, u32[]{:S(2)}, u32[]{:S(2)}) %collective-permute-start.4) | collective-permute-done | bytes 73760 | tf_op jit(solution)/shard_map/ppermute | solution.py:389
  30.4 3.3 %collective-permute-done.5.refs_8_ = bf16[288,128]{1,0:T(8,128)(2,1)S(1)} collective-permute-done((bf16[288,128]{1,0:T(8,128)(2,1)S(1)}, bf16[288,128]{1,0:T(8,128)(2,1)S(1)}, u32[]{:S(2)}, u32[]{:S(2)}) %collective-permute-start.5) | collective-permute-done | bytes 73760 | tf_op jit(solution)/shard_map/ppermute | solution.py:389
  34.2 4.6 %collective-permute-done.6.refs_9_ = bf16[288,128]{1,0:T(8,128)(2,1)S(1)} collective-permute-done((bf16[288,128]{1,0:T(8,128)(2,1)S(1)}, bf16[288,128]{1,0:T(8,128)(2,1)S(1)}, u32[]{:S(2)}, u32[]{:S(2)}) %collective-permute-start.6) | collective-permute-done | bytes 73760 | tf_op jit(solution)/shard_map/ppermute | solution.py:389
  40.0 5.2 %collective-permute-done.7.refs_10_ = bf16[288,128]{1,0:T(8,128)(2,1)S(1)} collective-permute-done((bf16[288,128]{1,0:T(8,128)(2,1)S(1)}, bf16[288,128]{1,0:T(8,128)(2,1)S(1)}, u32[]{:S(2)}, u32[]{:S(2)}) %collective-permute-start.7) | collective-permute-done | bytes 73760 | tf_op jit(solution)/shard_map/ppermute | solution.py:389
  47.6 3.6 %collective-permute-start.14 = (bf16[288,128]{1,0:T(8,128)(2,1)S(1)}, bf16[288,128]{1,0:T(8,128)(2,1)S(1)}, u32[]{:S(2)}, u32[]{:S(2)}) collective-permute-start(bf16[288,128]{1,0:T(8,128)(2,1)S(1)} %get-tuple-element.36), channel_id=1, source_target_pairs={{0,15},{1,14},{2,13},{3,12},{4,11},{5,10},{6,9},{7,8},{8,7},{9,6},... | collective-permute-start | bytes 221192 | tf_op jit(solution)/shard_map/ppermute | solution.py:389
  58.2 3.4 %collective-permute-done.23.refs_20_ = bf16[2,512,128]{2,1,0:T(8,128)(2,1)S(1)} collective-permute-done((bf16[2,512,128]{2,1,0:T(8,128)(2,1)}, bf16[2,512,128]{2,1,0:T(8,128)(2,1)S(1)}, u32[]{:S(2)}, u32[]{:S(2)}) %collective-permute-start.23) | collective-permute-done | bytes 262176 | tf_op jit(solution)/shard_map/ppermute | solution.py:389
  61.6 4.6 %collective-permute-done.24.refs_21_ = bf16[2,512,128]{2,1,0:T(8,128)(2,1)S(1)} collective-permute-done((bf16[2,512,128]{2,1,0:T(8,128)(2,1)}, bf16[2,512,128]{2,1,0:T(8,128)(2,1)S(1)}, u32[]{:S(2)}, u32[]{:S(2)}) %collective-permute-start.24) | collective-permute-done | bytes 262176 | tf_op jit(solution)/shard_map/ppermute | solution.py:389
  68.0 6.6 %collective-permute-done.27.refs_24_ = bf16[2,512,128]{2,1,0:T(8,128)(2,1)S(1)} collective-permute-done((bf16[2,512,128]{2,1,0:T(8,128)(2,1)}, bf16[2,512,128]{2,1,0:T(8,128)(2,1)S(1)}, u32[]{:S(2)}, u32[]{:S(2)}) %collective-permute-start.27) | collective-permute-done | bytes 262176 | tf_op jit(solution)/shard_map/ppermute | solution.py:389
  74.6 4.3 %collective-permute-done.28.refs_25_ = bf16[2,512,128]{2,1,0:T(8,128)(2,1)S(1)} collective-permute-done((bf16[2,512,128]{2,1,0:T(8,128)(2,1)}, bf16[2,512,128]{2,1,0:T(8,128)(2,1)S(1)}, u32[]{:S(2)}, u32[]{:S(2)}) %collective-permute-start.28) | collective-permute-done | bytes 262176 | tf_op jit(solution)/shard_map/ppermute | solution.py:389
  79.8 16.7 %shard_map.68 = bf16[16,136,128]{2,1,0:T(8,128)(2,1)} custom-call(s32[1]{0:T(128)} %get-tuple-element.57.refs_0_, s32[3]{0:T(128)S(1)} %pad_add_fusion.refs_1_, bf16[288,128]{1,0:T(8,128)(2,1)S(1)} %get-tuple-element.29.refs_2_, bf16[288,128]{1,0:T(8,128)(2,1)S(1)} %collective-permute-done.refs_3_, bf16[288,128]{1,0:T(8,128)(2,1)S(1)} %collective-permute-done.1.refs_4_, ...), custom_call_target="tpu_custom_call" | custom-call | flops 4294967296 | bytes 3145728 | tf_op jit(solution)/shard_map/pallas_call | solution.py:243
  96.6 3.6 %all-to-all-start.1 = ((bf16[16,136,128]{2,1,0:T(8,128)(2,1)}), bf16[16,136,128]{2,1,0:T(8,128)(2,1)S(1)}, u32[]{:S(2)}, u32[]{:S(2)}) async-start(bf16[16,136,128]{2,1,0:T(8,128)(2,1)} %shard_map.68), calls=%async_computation.1 | async-start | bytes 1114112 | tf_op jit(solution)/shard_map/all_to_all | solution.py:432
  106.7 2.5 %collective-permute-start.20 = (bf16[2,512,128]{2,1,0:T(8,128)(2,1)S(1)}, bf16[2,512,128]{2,1,0:T(8,128)(2,1)S(1)}, u32[]{:S(2)}, u32[]{:S(2)}) collective-permute-start(bf16[2,512,128]{2,1,0:T(8,128)(2,1)S(1)} %get-tuple-element.43), channel_id=1, source_target_pairs={{0,6},{1,7},{2,4},{3,5},{4,2},{5,3},{6,0},{7,1},{8,14},{9,15},{10,... | collective-permute-start | bytes 786440 | tf_op jit(solution)/shard_map/ppermute | solution.py:389
  109.2 6.0 %collective-permute-done.16.refs_20_ = bf16[2,512,128]{2,1,0:T(8,128)(2,1)S(1)} collective-permute-done((bf16[2,512,128]{2,1,0:T(8,128)(2,1)S(1)}, bf16[2,512,128]{2,1,0:T(8,128)(2,1)S(1)}, u32[]{:S(2)}, u32[]{:S(2)}) %collective-permute-start.16) | collective-permute-done | bytes 262176 | tf_op jit(solution)/shard_map/ppermute | solution.py:389
  116.7 3.3 %collective-permute-done.17.refs_21_ = bf16[2,512,128]{2,1,0:T(8,128)(2,1)S(1)} collective-permute-done((bf16[2,512,128]{2,1,0:T(8,128)(2,1)S(1)}, bf16[2,512,128]{2,1,0:T(8,128)(2,1)S(1)}, u32[]{:S(2)}, u32[]{:S(2)}) %collective-permute-start.17) | collective-permute-done | bytes 262176 | tf_op jit(solution)/shard_map/ppermute | solution.py:389
  120.1 2.7 %collective-permute-done.19.refs_23_ = bf16[2,512,128]{2,1,0:T(8,128)(2,1)S(1)} collective-permute-done((bf16[2,512,128]{2,1,0:T(8,128)(2,1)S(1)}, bf16[2,512,128]{2,1,0:T(8,128)(2,1)S(1)}, u32[]{:S(2)}, u32[]{:S(2)}) %collective-permute-start.19) | collective-permute-done | bytes 262176 | tf_op jit(solution)/shard_map/ppermute | solution.py:389
  122.8 7.2 %collective-permute-done.20.refs_24_ = bf16[2,512,128]{2,1,0:T(8,128)(2,1)S(1)} collective-permute-done((bf16[2,512,128]{2,1,0:T(8,128)(2,1)S(1)}, bf16[2,512,128]{2,1,0:T(8,128)(2,1)S(1)}, u32[]{:S(2)}, u32[]{:S(2)}) %collective-permute-start.20) | collective-permute-done | bytes 262176 | tf_op jit(solution)/shard_map/ppermute | solution.py:389
  130.0 5.3 %collective-permute-done.21.refs_25_ = bf16[2,512,128]{2,1,0:T(8,128)(2,1)S(1)} collective-permute-done((bf16[2,512,128]{2,1,0:T(8,128)(2,1)S(1)}, bf16[2,512,128]{2,1,0:T(8,128)(2,1)S(1)}, u32[]{:S(2)}, u32[]{:S(2)}) %collective-permute-start.21) | collective-permute-done | bytes 262176 | tf_op jit(solution)/shard_map/ppermute | solution.py:389
  135.4 14.2 %shard_map.66 = bf16[16,136,128]{2,1,0:T(8,128)(2,1)} custom-call(s32[1]{0:T(128)} %get-tuple-element.58.refs_0_, s32[3]{0:T(128)S(1)} %pad_add_fusion.refs_1_, bf16[288,128]{1,0:T(8,128)(2,1)S(1)} %get-tuple-element.29.refs_2_, bf16[288,128]{1,0:T(8,128)(2,1)S(1)} %collective-permute-done.refs_3_, bf16[288,128]{1,0:T(8,128)(2,1)S(1)} %collective-permute-done.1.refs_4_, ...), custom_call_target="tpu_custom_call" | custom-call | flops 4294967296 | bytes 3145728 | tf_op jit(solution)/shard_map/pallas_call | solution.py:243
  149.6 3.6 %all-to-all-start = ((bf16[16,136,128]{2,1,0:T(8,128)(2,1)}), bf16[16,136,128]{2,1,0:T(8,128)(2,1)S(1)}, u32[]{:S(2)}, u32[]{:S(2)}) async-start(bf16[16,136,128]{2,1,0:T(8,128)(2,1)} %shard_map.66), calls=%async_computation | async-start | bytes 1114112 | tf_op jit(solution)/shard_map/all_to_all | solution.py:432
  154.4 13.5 %all-to-all-done.refs_0_ = bf16[16,136,128]{2,1,0:T(8,128)(2,1)S(1)} async-done(((bf16[16,136,128]{2,1,0:T(8,128)(2,1)}), bf16[16,136,128]{2,1,0:T(8,128)(2,1)S(1)}, u32[]{:S(2)}, u32[]{:S(2)}) %all-to-all-start) | async-done | bytes 557088 | tf_op jit(solution)/shard_map/all_to_all | solution.py:432
  (110 shorter events, 38.4 us)
Async XLA Ops:
  1.9 43.2 %collective-permute-start.8 = (bf16[288,128]{1,0:T(8,128)(2,1)S(1)}, bf16[288,128]{1,0:T(8,128)(2,1)S(1)}, u32[]{:S(2)}, u32[]{:S(2)}) collective-permute-start(bf16[288,128]{1,0:T(8,128)(2,1)S(1)} %get-tuple-element.30), channel_id=1, source_target_pairs={{0,9},{1,8},{2,11},{3,10},{4,13},{5,12},{6,15},{7,14},{8,1},{9,0},... | collective-permute-start | bytes 221192 | tf_op jit(solution)/shard_map/ppermute | solution.py:389
  5.5 9.8 %collective-permute-start = (bf16[288,128]{1,0:T(8,128)(2,1)S(1)}, bf16[288,128]{1,0:T(8,128)(2,1)S(1)}, u32[]{:S(2)}, u32[]{:S(2)}) collective-permute-start(bf16[288,128]{1,0:T(8,128)(2,1)S(1)} %get-tuple-element.30), channel_id=1, source_target_pairs={{0,1},{1,0},{2,3},{3,2},{4,5},{5,4},{6,7},{7,6},{8,9},{9,8},{10,11... | collective-permute-start | bytes 221192 | tf_op jit(solution)/shard_map/ppermute | solution.py:389
  6.2 41.4 %collective-permute-start.9 = (bf16[288,128]{1,0:T(8,128)(2,1)S(1)}, bf16[288,128]{1,0:T(8,128)(2,1)S(1)}, u32[]{:S(2)}, u32[]{:S(2)}) collective-permute-start(bf16[288,128]{1,0:T(8,128)(2,1)S(1)} %get-tuple-element.31), channel_id=1, source_target_pairs={{0,10},{1,11},{2,8},{3,9},{4,14},{5,15},{6,12},{7,13},{8,2},{9,3},... | collective-permute-start | bytes 221192 | tf_op jit(solution)/shard_map/ppermute | solution.py:389
  7.4 9.1 %collective-permute-start.1 = (bf16[288,128]{1,0:T(8,128)(2,1)S(1)}, bf16[288,128]{1,0:T(8,128)(2,1)S(1)}, u32[]{:S(2)}, u32[]{:S(2)}) collective-permute-start(bf16[288,128]{1,0:T(8,128)(2,1)S(1)} %get-tuple-element.31), channel_id=1, source_target_pairs={{0,2},{1,3},{2,0},{3,1},{4,6},{5,7},{6,4},{7,5},{8,10},{9,11},{10,... | collective-permute-start | bytes 221192 | tf_op jit(solution)/shard_map/ppermute | solution.py:389
  7.7 43.5 %collective-permute-start.10 = (bf16[288,128]{1,0:T(8,128)(2,1)S(1)}, bf16[288,128]{1,0:T(8,128)(2,1)S(1)}, u32[]{:S(2)}, u32[]{:S(2)}) collective-permute-start(bf16[288,128]{1,0:T(8,128)(2,1)S(1)} %get-tuple-element.32), channel_id=1, source_target_pairs={{0,11},{1,10},{2,9},{3,8},{4,15},{5,14},{6,13},{7,12},{8,3},{9,2},... | collective-permute-start | bytes 221192 | tf_op jit(solution)/shard_map/ppermute | solution.py:389
  16.5 34.7 %collective-permute-start.11 = (bf16[288,128]{1,0:T(8,128)(2,1)S(1)}, bf16[288,128]{1,0:T(8,128)(2,1)S(1)}, u32[]{:S(2)}, u32[]{:S(2)}) collective-permute-start(bf16[288,128]{1,0:T(8,128)(2,1)S(1)} %get-tuple-element.33), channel_id=1, source_target_pairs={{0,12},{1,13},{2,14},{3,15},{4,8},{5,9},{6,10},{7,11},{8,4},{9,5},... | collective-permute-start | bytes 221192 | tf_op jit(solution)/shard_map/ppermute | solution.py:389
  38.8 6.4 %collective-permute-start.7 = (bf16[288,128]{1,0:T(8,128)(2,1)S(1)}, bf16[288,128]{1,0:T(8,128)(2,1)S(1)}, u32[]{:S(2)}, u32[]{:S(2)}) collective-permute-start(bf16[288,128]{1,0:T(8,128)(2,1)S(1)} %get-tuple-element.29.refs_2_), channel_id=1, source_target_pairs={{0,8},{1,9},{2,10},{3,11},{4,12},{5,13},{6,14},{7,15},{8,0},{9,1},... | collective-permute-start | bytes 221192 | tf_op jit(solution)/shard_map/ppermute | solution.py:389
  45.2 7.4 %collective-permute-start.12 = (bf16[288,128]{1,0:T(8,128)(2,1)S(1)}, bf16[288,128]{1,0:T(8,128)(2,1)S(1)}, u32[]{:S(2)}, u32[]{:S(2)}) collective-permute-start(bf16[288,128]{1,0:T(8,128)(2,1)S(1)} %get-tuple-element.34), channel_id=1, source_target_pairs={{0,13},{1,12},{2,15},{3,14},{4,9},{5,8},{6,11},{7,10},{8,5},{9,4},... | collective-permute-start | bytes 221192 | tf_op jit(solution)/shard_map/ppermute | solution.py:389
  45.2 8.1 %collective-permute-start.13 = (bf16[288,128]{1,0:T(8,128)(2,1)S(1)}, bf16[288,128]{1,0:T(8,128)(2,1)S(1)}, u32[]{:S(2)}, u32[]{:S(2)}) collective-permute-start(bf16[288,128]{1,0:T(8,128)(2,1)S(1)} %get-tuple-element.35), channel_id=1, source_target_pairs={{0,14},{1,15},{2,12},{3,13},{4,10},{5,11},{6,8},{7,9},{8,6},{9,7},... | collective-permute-start | bytes 221192 | tf_op jit(solution)/shard_map/ppermute | solution.py:389
  47.6 7.7 %collective-permute-start.14 = (bf16[288,128]{1,0:T(8,128)(2,1)S(1)}, bf16[288,128]{1,0:T(8,128)(2,1)S(1)}, u32[]{:S(2)}, u32[]{:S(2)}) collective-permute-start(bf16[288,128]{1,0:T(8,128)(2,1)S(1)} %get-tuple-element.36), channel_id=1, source_target_pairs={{0,15},{1,14},{2,13},{3,12},{4,11},{5,10},{6,9},{7,8},{8,7},{9,6},... | collective-permute-start | bytes 221192 | tf_op jit(solution)/shard_map/ppermute | solution.py:389
  51.3 10.2 %collective-permute-start.23 = (bf16[2,512,128]{2,1,0:T(8,128)(2,1)}, bf16[2,512,128]{2,1,0:T(8,128)(2,1)S(1)}, u32[]{:S(2)}, u32[]{:S(2)}) collective-permute-start(bf16[2,512,128]{2,1,0:T(8,128)(2,1)} %get-tuple-element.47), channel_id=1, source_target_pairs={{0,2},{1,3},{2,0},{3,1},{4,6},{5,7},{6,4},{7,5},{8,10},{9,11},{10,... | collective-permute-start | bytes 786440 | tf_op jit(solution)/shard_map/ppermute | solution.py:389
  52.6 13.6 %collective-permute-start.24 = (bf16[2,512,128]{2,1,0:T(8,128)(2,1)}, bf16[2,512,128]{2,1,0:T(8,128)(2,1)S(1)}, u32[]{:S(2)}, u32[]{:S(2)}) collective-permute-start(bf16[2,512,128]{2,1,0:T(8,128)(2,1)} %get-tuple-element.48), channel_id=1, source_target_pairs={{0,3},{1,2},{2,1},{3,0},{4,7},{5,6},{6,5},{7,4},{8,11},{9,10},{10,... | collective-permute-start | bytes 786440 | tf_op jit(solution)/shard_map/ppermute | solution.py:389
  53.3 12.9 %collective-permute-start.25 = (bf16[2,512,128]{2,1,0:T(8,128)(2,1)}, bf16[2,512,128]{2,1,0:T(8,128)(2,1)S(1)}, u32[]{:S(2)}, u32[]{:S(2)}) collective-permute-start(bf16[2,512,128]{2,1,0:T(8,128)(2,1)} %get-tuple-element.49), channel_id=1, source_target_pairs={{0,4},{1,5},{2,6},{3,7},{4,0},{5,1},{6,2},{7,3},{8,12},{9,13},{10,... | collective-permute-start | bytes 786440 | tf_op jit(solution)/shard_map/ppermute | solution.py:389
  55.3 12.6 %collective-permute-start.26 = (bf16[2,512,128]{2,1,0:T(8,128)(2,1)}, bf16[2,512,128]{2,1,0:T(8,128)(2,1)S(1)}, u32[]{:S(2)}, u32[]{:S(2)}) collective-permute-start(bf16[2,512,128]{2,1,0:T(8,128)(2,1)} %get-tuple-element.50), channel_id=1, source_target_pairs={{0,5},{1,4},{2,7},{3,6},{4,1},{5,0},{6,3},{7,2},{8,13},{9,12},{10,... | collective-permute-start | bytes 786440 | tf_op jit(solution)/shard_map/ppermute | solution.py:389
  57.3 17.3 %collective-permute-start.27 = (bf16[2,512,128]{2,1,0:T(8,128)(2,1)}, bf16[2,512,128]{2,1,0:T(8,128)(2,1)S(1)}, u32[]{:S(2)}, u32[]{:S(2)}) collective-permute-start(bf16[2,512,128]{2,1,0:T(8,128)(2,1)} %get-tuple-element.51), channel_id=1, source_target_pairs={{0,6},{1,7},{2,4},{3,5},{4,2},{5,3},{6,0},{7,1},{8,14},{9,15},{10,... | collective-permute-start | bytes 786440 | tf_op jit(solution)/shard_map/ppermute | solution.py:389
  61.5 17.3 %collective-permute-start.28 = (bf16[2,512,128]{2,1,0:T(8,128)(2,1)}, bf16[2,512,128]{2,1,0:T(8,128)(2,1)S(1)}, u32[]{:S(2)}, u32[]{:S(2)}) collective-permute-start(bf16[2,512,128]{2,1,0:T(8,128)(2,1)} %get-tuple-element.52), channel_id=1, source_target_pairs={{0,7},{1,6},{2,5},{3,4},{4,3},{5,2},{6,1},{7,0},{8,15},{9,14},{10,... | collective-permute-start | bytes 786440 | tf_op jit(solution)/shard_map/ppermute | solution.py:389
  96.6 53.0 %all-to-all-start.1 = ((bf16[16,136,128]{2,1,0:T(8,128)(2,1)}), bf16[16,136,128]{2,1,0:T(8,128)(2,1)S(1)}, u32[]{:S(2)}, u32[]{:S(2)}) async-start(bf16[16,136,128]{2,1,0:T(8,128)(2,1)} %shard_map.68), calls=%async_computation.1 | async-start | bytes 1114112 | tf_op jit(solution)/shard_map/all_to_all | solution.py:432
  103.2 12.0 %collective-permute-start.16 = (bf16[2,512,128]{2,1,0:T(8,128)(2,1)S(1)}, bf16[2,512,128]{2,1,0:T(8,128)(2,1)S(1)}, u32[]{:S(2)}, u32[]{:S(2)}) collective-permute-start(bf16[2,512,128]{2,1,0:T(8,128)(2,1)S(1)} %get-tuple-element.39), channel_id=1, source_target_pairs={{0,2},{1,3},{2,0},{3,1},{4,6},{5,7},{6,4},{7,5},{8,10},{9,11},{10,... | collective-permute-start | bytes 786440 | tf_op jit(solution)/shard_map/ppermute | solution.py:389
  104.8 15.3 %collective-permute-start.17 = (bf16[2,512,128]{2,1,0:T(8,128)(2,1)S(1)}, bf16[2,512,128]{2,1,0:T(8,128)(2,1)S(1)}, u32[]{:S(2)}, u32[]{:S(2)}) collective-permute-start(bf16[2,512,128]{2,1,0:T(8,128)(2,1)S(1)} %get-tuple-element.40), channel_id=1, source_target_pairs={{0,3},{1,2},{2,1},{3,0},{4,7},{5,6},{6,5},{7,4},{8,11},{9,10},{10,... | collective-permute-start | bytes 786440 | tf_op jit(solution)/shard_map/ppermute | solution.py:389
  104.8 15.3 %collective-permute-start.18 = (bf16[2,512,128]{2,1,0:T(8,128)(2,1)S(1)}, bf16[2,512,128]{2,1,0:T(8,128)(2,1)S(1)}, u32[]{:S(2)}, u32[]{:S(2)}) collective-permute-start(bf16[2,512,128]{2,1,0:T(8,128)(2,1)S(1)} %get-tuple-element.41), channel_id=1, source_target_pairs={{0,4},{1,5},{2,6},{3,7},{4,0},{5,1},{6,2},{7,3},{8,12},{9,13},{10,... | collective-permute-start | bytes 786440 | tf_op jit(solution)/shard_map/ppermute | solution.py:389
  106.6 16.2 %collective-permute-start.19 = (bf16[2,512,128]{2,1,0:T(8,128)(2,1)S(1)}, bf16[2,512,128]{2,1,0:T(8,128)(2,1)S(1)}, u32[]{:S(2)}, u32[]{:S(2)}) collective-permute-start(bf16[2,512,128]{2,1,0:T(8,128)(2,1)S(1)} %get-tuple-element.42), channel_id=1, source_target_pairs={{0,5},{1,4},{2,7},{3,6},{4,1},{5,0},{6,3},{7,2},{8,13},{9,12},{10,... | collective-permute-start | bytes 786440 | tf_op jit(solution)/shard_map/ppermute | solution.py:389
  106.7 23.3 %collective-permute-start.20 = (bf16[2,512,128]{2,1,0:T(8,128)(2,1)S(1)}, bf16[2,512,128]{2,1,0:T(8,128)(2,1)S(1)}, u32[]{:S(2)}, u32[]{:S(2)}) collective-permute-start(bf16[2,512,128]{2,1,0:T(8,128)(2,1)S(1)} %get-tuple-element.43), channel_id=1, source_target_pairs={{0,6},{1,7},{2,4},{3,5},{4,2},{5,3},{6,0},{7,1},{8,14},{9,15},{10,... | collective-permute-start | bytes 786440 | tf_op jit(solution)/shard_map/ppermute | solution.py:389
  115.3 20.1 %collective-permute-start.21 = (bf16[2,512,128]{2,1,0:T(8,128)(2,1)S(1)}, bf16[2,512,128]{2,1,0:T(8,128)(2,1)S(1)}, u32[]{:S(2)}, u32[]{:S(2)}) collective-permute-start(bf16[2,512,128]{2,1,0:T(8,128)(2,1)S(1)} %get-tuple-element.44), channel_id=1, source_target_pairs={{0,7},{1,6},{2,5},{3,4},{4,3},{5,2},{6,1},{7,0},{8,15},{9,14},{10,... | collective-permute-start | bytes 786440 | tf_op jit(solution)/shard_map/ppermute | solution.py:389
  149.6 18.4 %all-to-all-start = ((bf16[16,136,128]{2,1,0:T(8,128)(2,1)}), bf16[16,136,128]{2,1,0:T(8,128)(2,1)S(1)}, u32[]{:S(2)}, u32[]{:S(2)}) async-start(bf16[16,136,128]{2,1,0:T(8,128)(2,1)} %shard_map.66), calls=%async_computation | async-start | bytes 1114112 | tf_op jit(solution)/shard_map/all_to_all | solution.py:432
  (21 other events, 374.6 us)

commit v9 on v4

v9 whole, which is shorter than its diff:
```python
import functools
import math

import jax
import jax.numpy as jnp
from jax import lax
from jax.experimental import pallas as pl
from jax.experimental.pallas import tpu as pltpu
from jax.sharding import PartitionSpec as P


NEG = -1e30
STAT_ROWS = 8
SMALL_VMEM = 12 * 2**20
LARGE_VMEM = 56 * 2**20


VMEM_SPEC = pl.BlockSpec(memory_space=pltpu.VMEM)
HBM_SPEC = pl.BlockSpec(memory_space=pltpu.HBM)
SMEM_SPEC = pl.BlockSpec(memory_space=pltpu.SMEM)


def attend_kernel(*refs, blocks, tile, group_size, row_start):
    length_ref, place_ref, q_hbm = refs[:3]
    kv_refs = refs[3 : 3 + blocks]
    (
        fk_ref,
        fv_ref,
        out_hbm,
        q_ref,
        out_ref,
        keys,
        loaded,
        vals,
        bias,
        s0,
        s1,
        m0,
        m1,
        in_sems,
        q_sem,
        out_sem,
    ) = refs[3 + blocks :]
    per_source, dim = q_ref.shape[1:]
    block_slots = kv_refs[0].shape[1]
    chunk = bias.shape[0]
    slots = blocks * block_slots
    fresh = fk_ref.shape[0]
    rows = q_ref.shape[0] * per_source
    tiles = rows // tile
    span = tile // per_source
    ones = vals.shape[0] - dim
    scale = math.log2(math.e) / math.sqrt(dim)
    own, device_block = place_ref[0], place_ref[1]
    valid = jnp.clip(length_ref[0] - device_block * slots, 0, slots)
    fresh_shift = jnp.where(device_block == q_ref.shape[0] // blocks - 1, 0, -rows)

    copies = []
    for k, kv_ref in enumerate(kv_refs):
        at = pl.ds(pl.multiple_of((own ^ k) * block_slots, block_slots), block_slots)
        copies.append(pltpu.make_async_copy(kv_ref.at[1], loaded.at[at, :], in_sems.at[k, 1]))
    for k, kv_ref in enumerate(kv_refs):
        at = pl.ds(pl.multiple_of((own ^ k) * block_slots, block_slots), block_slots)
        copies.append(pltpu.make_async_copy(kv_ref.at[0], keys.at[at, :], in_sems.at[k, 0]))
    copies.append(pltpu.make_async_copy(q_hbm.at[:, row_start : row_start + per_source, :], q_ref, q_sem))
    for copy in copies:
        copy.start()

    vals[dim:, :] = jnp.ones((ones, slots + fresh), jnp.bfloat16)
    vals[:dim, slots:] = jnp.transpose(fv_ref[...])
    left = (valid - 1) % chunk + 1
    bias[...] = jnp.where(lax.broadcasted_iota(jnp.int32, bias.shape, 0) < left, 0.0, NEG)
    for copy in copies[:blocks]:
        copy.wait()
    for first in range(0, slots, block_slots):
        vals[:dim, first : first + block_slots] = jnp.transpose(loaded[first : first + block_slots, :])
    for copy in copies[blocks:]:
        copy.wait()

    def fold_max(scores, best):
        part = jnp.max(scores.reshape(-1, 8, tile), axis=0)
        return part if best is None else jnp.maximum(best, part)

    def score_chunk(t, j, count, s_ref, best):
        q = q_ref[pl.ds(t * span, span)].reshape(tile, dim)
        at = slice(j * chunk, (j + 1) * chunk) if j < count else slice(slots, slots + fresh)
        left_side = keys[at, :] if j < count else fk_ref[...]
        scores = lax.dot_general(left_side, q, (((1,), (1,)), ((), ())), preferred_element_type=jnp.float32)
        if j == count - 1:
            mask = bias[...]
            scores = scores + jnp.concatenate([mask] * (tile // mask.shape[1]), axis=1)
        elif j == count:
            token = (t * tile + lax.broadcasted_iota(jnp.int32, (1, tile), 1)) // group_size
            unit = lax.broadcasted_iota(jnp.int32, (fresh, 1), 0)
            scores = jnp.where(unit <= token + fresh_shift, scores, NEG)
        s_ref[at, :] = scores
        return fold_max(scores, best)

    def value_chunk(j, count, s_ref, top, acc):
        at = slice(j * chunk, (j + 1) * chunk) if j < count else slice(slots, slots + fresh)
        weights = jnp.exp2((s_ref[at, :] - top) * scale).astype(jnp.bfloat16)
        part = jnp.dot(vals[:, at], weights, preferred_element_type=jnp.float32)
        return part if acc is None else acc + part

    def finish(t, top, acc):
        total = acc[dim : dim + 1, :]
        out = acc[:dim, :] / total
        level = top * scale + jnp.log2(total)
        high = level.astype(jnp.bfloat16).astype(jnp.float32)
        mid = (level - high).astype(jnp.bfloat16).astype(jnp.float32)
        low = level - high - mid
        which = lax.broadcasted_iota(jnp.int32, (STAT_ROWS, tile), 0)
        stats = jnp.where(which == 0, high, jnp.where(which == 1, mid, low)).astype(jnp.bfloat16)
        for first in range(0, tile, dim):
            flat = jnp.transpose(out[:, first : first + dim]).astype(jnp.bfloat16)
            width = min(per_source, dim)
            for part in range(dim // width):
                source = t * span + (first + part * width) // per_source
                inside = (first + part * width) % per_source
                out_ref[source, inside : inside + width, :] = flat[part * width : (part + 1) * width, :]
                out_ref[source, per_source:, inside : inside + width] = stats[
                    :, first + part * width : first + (part + 1) * width
                ]

    def stage(t_next, s_next, m_next, t_now, s_now, m_now, count):
        best = None
        acc = None
        if t_now is not None:
            top = jnp.max(m_now[...], axis=0, keepdims=True)
        for j in range(count + 1):
            if t_next is not None:
                best = score_chunk(t_next, j, count, s_next, best)
            if t_now is not None:
                acc = value_chunk(j, count, s_now, top, acc)
        if t_next is not None:
            m_next[...] = best
        if t_now is not None:
            finish(t_now, top, acc)

    for count in range(slots // chunk + 1):

        @pl.when((valid > (count - 1) * chunk) & (valid <= count * chunk))
        def _(count=count):
            stage(0, s0, m0, None, None, None, count)

            def pair(i, carry):
                stage(2 * i + 1, s1, m1, 2 * i, s0, m0, count)
                stage(jnp.minimum(2 * i + 2, tiles - 1), s0, m0, 2 * i + 1, s1, m1, count)
                return carry

            lax.fori_loop(0, tiles // 2, pair, 0)

    result = pltpu.make_async_copy(out_ref, out_hbm, out_sem)
    result.start()
    result.wait()


def attend(length, place, head_q, kv_blocks, fresh, row_start, row_count, group_size):
    sources, _, dim = head_q.shape
    slots = len(kv_blocks) * kv_blocks[0].shape[1]
    rows = sources * row_count
    units = fresh[0].shape[0]
    tile = min(256, rows // 2)
    chunk = min(1024, slots)
    grant = 8 * tile * (slots + units) + 8 * slots * dim + 8 * rows * dim + SMALL_VMEM
    return pl.pallas_call(
        functools.partial(
            attend_kernel, blocks=len(kv_blocks), tile=tile, group_size=group_size, row_start=row_start
        ),
        in_specs=[SMEM_SPEC] * 2 + [HBM_SPEC] * (1 + len(kv_blocks)) + [VMEM_SPEC] * 2,
        out_specs=HBM_SPEC,
        scratch_shapes=[
            pltpu.VMEM((sources, row_count, dim), jnp.bfloat16),
            pltpu.VMEM((sources, row_count + STAT_ROWS, dim), jnp.bfloat16),
            pltpu.VMEM((slots, dim), jnp.bfloat16),
            pltpu.VMEM((slots, dim), jnp.bfloat16),
            pltpu.VMEM((dim + 16, slots + units), jnp.bfloat16),
            pltpu.VMEM((chunk, min(dim, tile)), jnp.float32),
            pltpu.VMEM((slots + units, tile), jnp.float32),
            pltpu.VMEM((slots + units, tile), jnp.float32),
            pltpu.VMEM((8, tile), jnp.float32),
            pltpu.VMEM((8, tile), jnp.float32),
            pltpu.SemaphoreType.DMA((len(kv_blocks), 2)),
            pltpu.SemaphoreType.DMA,
            pltpu.SemaphoreType.DMA,
        ],
        out_shape=jax.ShapeDtypeStruct((sources, row_count + STAT_ROWS, dim), jnp.bfloat16),
        compiler_params=pltpu.CompilerParams(vmem_limit_bytes=grant),
        cost_estimate=pl.CostEstimate(
            flops=4 * rows * slots * dim,
            bytes_accessed=4 * slots * dim + 4 * rows * dim,
            transcendentals=rows * slots,
        ),
    )(length, place, head_q, *kv_blocks, *fresh)


def merge_kernel(part_ref, *refs, group_size):
    out_ref = refs[-1]
    spread, heads, _, dim = part_ref.shape
    local_rows = out_ref.shape[1]
    per_source = local_rows * group_size
    levels = []
    for b in range(spread):
        stats = [
            part_ref[b, h, per_source : per_source + STAT_ROWS, :].astype(jnp.float32) for h in range(heads)
        ]
        levels.append(jnp.concatenate([x[0:1] + x[1:2] + x[2:3] for x in stats], axis=0))
    top = functools.reduce(jnp.maximum, levels)
    weights = [jnp.exp2(level - top) for level in levels]
    total = functools.reduce(jnp.add, weights)
    weights = [jnp.transpose(w / total) for w in weights]
    for h in range(heads):
        mixed = functools.reduce(
            jnp.add,
            [
                w[:per_source, h : h + 1] * part_ref[b, h, :per_source, :].astype(jnp.float32)
                for b, w in enumerate(weights)
            ],
        ).astype(jnp.bfloat16)
        out_ref[0, :, h * group_size : (h + 1) * group_size, :] = mixed.reshape(local_rows, group_size, dim)


def merge(parts, request, requests, local_rows, group_size, earlier):
    heads, dim = parts.shape[1], parts.shape[3]
    rest = [] if earlier is None else [earlier]
    return pl.pallas_call(
        functools.partial(merge_kernel, group_size=group_size),
        grid=(1,),
        in_specs=[pl.BlockSpec(parts.shape, lambda i: (0, 0, 0, 0))]
        + [pl.BlockSpec(memory_space=pl.ANY) for _ in rest],
        out_specs=pl.BlockSpec((1, local_rows, heads * group_size, dim), lambda i: (request, 0, 0, 0)),
        out_shape=jax.ShapeDtypeStruct((requests, local_rows, heads * group_size, dim), jnp.bfloat16),
        input_output_aliases={1: 0} if rest else {},
        compiler_params=pltpu.CompilerParams(vmem_limit_bytes=SMALL_VMEM),
    )(parts, *rest)


def pack_kernel(q_ref, fresh_ref, out_ref):
    requests, local_rows, heads, dim = q_ref.shape
    kv_heads = fresh_ref.shape[0]
    group_size = heads // kv_heads
    rows = requests * local_rows * group_size
    for d in range(out_ref.shape[0]):
        head = d % kv_heads
        out_ref[d, :rows, :] = q_ref[:, :, head * group_size : (head + 1) * group_size, :].reshape(rows, dim)
        out_ref[d, rows:, :] = fresh_ref[head]


def pack(queries, fresh, devices):
    requests, local_rows, heads, dim = queries.shape
    rows = requests * local_rows * (heads // fresh.shape[0]) + fresh.shape[1]
    return pl.pallas_call(
        pack_kernel,
        in_specs=[VMEM_SPEC, VMEM_SPEC],
        out_specs=VMEM_SPEC,
        out_shape=jax.ShapeDtypeStruct((devices, rows, dim), jnp.bfloat16),
        compiler_params=pltpu.CompilerParams(vmem_limit_bytes=SMALL_VMEM),
    )(queries, fresh)


def split_kernel(own_ref, k_hbm, v_hbm, *refs, request):
    loaded, held, sems = refs[-3:]
    copies = [
        pltpu.make_async_copy(hbm.at[request], loaded.at[i], sems.at[i]) for i, hbm in enumerate((k_hbm, v_hbm))
    ]
    for copy in copies:
        copy.start()
    for i, copy in enumerate(copies):
        copy.wait()
        held[:, i] = jnp.swapaxes(loaded[i], 0, 1)
    for k, out_ref in enumerate(refs[:-3]):
        out_ref[...] = held[own_ref[0] ^ k]


def split_heads(own, cache_k, cache_v, request, grant):
    _, slots, kv_heads, dim = cache_k.shape
    return pl.pallas_call(
        functools.partial(split_kernel, request=request),
        in_specs=[SMEM_SPEC, HBM_SPEC, HBM_SPEC],
        out_specs=[VMEM_SPEC] * kv_heads,
        out_shape=[jax.ShapeDtypeStruct((2, slots, dim), jnp.bfloat16)] * kv_heads,
        scratch_shapes=[
            pltpu.VMEM((2, slots, kv_heads, dim), jnp.bfloat16),
            pltpu.VMEM((kv_heads, 2, slots, dim), jnp.bfloat16),
            pltpu.SemaphoreType.DMA((2,)),
        ],
        compiler_params=pltpu.CompilerParams(vmem_limit_bytes=grant),
    )(own, cache_k, cache_v)


def attention(queries, new_k, new_v, cache_k, cache_v, cache_len):
    requests, local_rows, heads, head_dim = queries.shape
    kv_heads = cache_k.shape[2]
    group_size = heads // kv_heads
    devices_seq = lax.axis_size("seq")
    seq_index = lax.axis_index("seq")
    spread = devices_seq // kv_heads
    block = seq_index // kv_heads
    own = (seq_index % kv_heads).astype(jnp.int32)
    per_source = local_rows * group_size

    fresh = jnp.transpose(jnp.stack([new_k, new_v]), (3, 0, 1, 2, 4)).reshape(
        kv_heads, 2 * requests * local_rows, head_dim
    )
    head_q = lax.all_to_all(
        pack(queries, fresh, devices_seq), "seq", split_axis=0, concat_axis=0, tiled=True
    )
    head_fresh = head_q[:, requests * per_source :, :].reshape(
        devices_seq, 2, requests, local_rows, head_dim
    )
    head_fresh = jnp.transpose(head_fresh, (1, 2, 0, 3, 4)).reshape(
        2, requests, devices_seq * local_rows, head_dim
    )

    kv_blocks = []
    for r in range(requests):
        parts = split_heads(own[None], cache_k, cache_v, r, LARGE_VMEM if r == 0 else 2 * SMALL_VMEM)
        moved = [parts[0]]
        for k in range(1, kv_heads):
            moved.append(lax.ppermute(parts[k], "seq", [(i, i ^ k) for i in range(devices_seq)]))
        kv_blocks.append(moved)

    place = jnp.stack([own, block]).astype(jnp.int32)
    out = None
    for r in range(requests):
        part = attend(
            cache_len[r : r + 1],
            place,
            head_q,
            kv_blocks[r],
            (head_fresh[0, r], head_fresh[1, r]),
            r * per_source,
            per_source,
            group_size,
        )
        part = lax.all_to_all(part, "seq", split_axis=0, concat_axis=0, tiled=True)
        part = part.reshape(spread, kv_heads, per_source + STAT_ROWS, head_dim)
        out = merge(part, r, requests, local_rows, group_size, out)
    return out


def solution(mesh):
    in_specs = (
        P("groups", "seq", None, None),
        P("groups", "seq", None, None),
        P("groups", "seq", None, None),
        P("groups", "seq", None, None),
        P("groups", "seq", None, None),
        P("groups"),
    )
    out_specs = P("groups", "seq", None, None)
    return jax.shard_map(attention, mesh=mesh, in_specs=in_specs, out_specs=out_specs, check_vma=False)
```

time: 149 us -> 151 us (1.013)
  the two profiles are of different devices: /device:TPU:13 before, /device:TPU:0 now
where the time goes in v9:
time: 151 us; the launch traced here: 149 us
  waiting for transfers between devices  69.8 us (46%)
  Pallas kernels  34.4 us (23%)
  starting transfers between devices  28.8 us (19%)
  local copies, waits for them, and re-layouts  15.2 us (10%)
    ppermute x14, waiting for transfers between devices, attention(): lax.ppermute(parts[k], 'seq', [(i, i ^ k) for i in range(devices_seq)])  50.2 us
    pallas_call x2, Pallas kernels, attend(): pl.pallas_call(functools.partial(attend_kernel, blocks=len(kv_blocks), ti...  26.5 us
    unnamed x44, local copies, waits for them, and re-layouts  14.6 us
    ppermute x14, starting transfers between devices, attention(): lax.ppermute(parts[k], 'seq', [(i, i ^ k) for i in range(devices_seq)])  14.1 us
    all_to_all x2, waiting for transfers between devices, attention(): part = lax.all_to_all(part, 'seq', split_axis=0, concat_axis=0, tiled=True)  13.5 us
    all_to_all x1, starting transfers between devices, attention(): lax.all_to_all(pack(queries, fresh, devices_seq), 'seq', split_axis=0, co...  7.39 us
    all_to_all x2, starting transfers between devices, attention(): part = lax.all_to_all(part, 'seq', split_axis=0, concat_axis=0, tiled=True)  7.35 us
    all_to_all x1, waiting for transfers between devices, attention(): lax.all_to_all(pack(queries, fresh, devices_seq), 'seq', split_axis=0, co...  6.05 us
  transfers between devices with their start and end apart: 17, of which 13 were waited for; matrix products, arithmetic and copies ran while one was open for 0% of the time, Pallas kernels for 12%

profile of v9, /device:TPU:0, one launch (start us, length us, event | category | flops | bytes accessed | tf_op | source)
XLA Modules:
  0.0 149.3 jit_solution(8410614000438119816)
XLA Ops:
  3.0 7.4 %all-to-all-start = ((bf16[16,288,128]{2,1,0:T(8,128)(2,1)}), bf16[16,288,128]{2,1,0:T(8,128)(2,1)S(1)}, u32[]{:S(2)}, u32[]{:S(2)}) async-start(bf16[16,288,128]{2,1,0:T(8,128)(2,1)} %shard_map.64), calls=%async_computation | async-start | bytes 2359296 | tf_op jit(solution)/shard_map/all_to_all | solution.py:305
  10.4 3.3 %shard_map.67 = (bf16[2,512,128]{2,1,0:T(8,128)(2,1)}, bf16[2,512,128]{2,1,0:T(8,128)(2,1)}, bf16[2,512,128]{2,1,0:T(8,128)(2,1)}, bf16[2,512,128]{2,1,0:T(8,128...) custom-call(s32[1]{0:T(128)} %bitcast.own_ref, ...), custom_call_target="tpu_custom_call" | custom-call | tf_op jit(solution)/shard_map/pallas_call | solution.py:277
  14.1 1.6 %collective-permute-start.8 = (bf16[2,512,128]{2,1,0:T(8,128)(2,1)}, bf16[2,512,128]{2,1,0:T(8,128)(2,1)S(1)}, u32[]{:S(2)}, u32[]{:S(2)}) collective-permute-start(bf16[2,512,128]{2,1,0:T(8,128)(2,1)} %get-tuple-element.31), channel_id=1, source_target_pairs={{0,2},{1,3},{2,0},{3,1},{4,6},{5,7},{6,4},{7,5},{8,10},{9,11},{10,... | collective-permute-start | bytes 786440 | tf_op jit(solution)/shard_map/ppermute | solution.py:320
  15.8 1.7 %collective-permute-start.10 = (bf16[2,512,128]{2,1,0:T(8,128)(2,1)}, bf16[2,512,128]{2,1,0:T(8,128)(2,1)S(1)}, u32[]{:S(2)}, u32[]{:S(2)}) collective-permute-start(bf16[2,512,128]{2,1,0:T(8,128)(2,1)} %get-tuple-element.33), channel_id=1, source_target_pairs={{0,4},{1,5},{2,6},{3,7},{4,0},{5,1},{6,2},{7,3},{8,12},{9,13},{10,... | collective-permute-start | bytes 786440 | tf_op jit(solution)/shard_map/ppermute | solution.py:320
  18.2 2.5 %collective-permute-start.12 = (bf16[2,512,128]{2,1,0:T(8,128)(2,1)}, bf16[2,512,128]{2,1,0:T(8,128)(2,1)S(1)}, u32[]{:S(2)}, u32[]{:S(2)}) collective-permute-start(bf16[2,512,128]{2,1,0:T(8,128)(2,1)} %get-tuple-element.35), channel_id=1, source_target_pairs={{0,6},{1,7},{2,4},{3,5},{4,2},{5,3},{6,0},{7,1},{8,14},{9,15},{10,... | collective-permute-start | bytes 786440 | tf_op jit(solution)/shard_map/ppermute | solution.py:320
  20.7 9.0 %collective-permute-done.8.refs_5_ = bf16[2,512,128]{2,1,0:T(8,128)(2,1)S(1)} collective-permute-done((bf16[2,512,128]{2,1,0:T(8,128)(2,1)}, bf16[2,512,128]{2,1,0:T(8,128)(2,1)S(1)}, u32[]{:S(2)}, u32[]{:S(2)}) %collective-permute-start.8) | collective-permute-done | bytes 262176 | tf_op jit(solution)/shard_map/ppermute | solution.py:320
  29.8 6.1 %all-to-all-done.refs_2_ = bf16[16,288,128]{2,1,0:T(8,128)(2,1)S(1)} async-done(((bf16[16,288,128]{2,1,0:T(8,128)(2,1)}), bf16[16,288,128]{2,1,0:T(8,128)(2,1)S(1)}, u32[]{:S(2)}, u32[]{:S(2)}) %all-to-all-start) | async-done | bytes 1179680 | tf_op jit(solution)/shard_map/all_to_all | solution.py:305
  39.3 3.8 %collective-permute-done.11.refs_8_ = bf16[2,512,128]{2,1,0:T(8,128)(2,1)S(1)} collective-permute-done((bf16[2,512,128]{2,1,0:T(8,128)(2,1)}, bf16[2,512,128]{2,1,0:T(8,128)(2,1)S(1)}, u32[]{:S(2)}, u32[]{:S(2)}) %collective-permute-start.11) | collective-permute-done | bytes 262176 | tf_op jit(solution)/shard_map/ppermute | solution.py:320
  43.8 7.0 %collective-permute-done.12.refs_9_ = bf16[2,512,128]{2,1,0:T(8,128)(2,1)S(1)} collective-permute-done((bf16[2,512,128]{2,1,0:T(8,128)(2,1)}, bf16[2,512,128]{2,1,0:T(8,128)(2,1)S(1)}, u32[]{:S(2)}, u32[]{:S(2)}) %collective-permute-start.12) | collective-permute-done | bytes 262176 | tf_op jit(solution)/shard_map/ppermute | solution.py:320
  51.5 3.8 %collective-permute-done.13.refs_10_ = bf16[2,512,128]{2,1,0:T(8,128)(2,1)S(1)} collective-permute-done((bf16[2,512,128]{2,1,0:T(8,128)(2,1)}, bf16[2,512,128]{2,1,0:T(8,128)(2,1)S(1)}, u32[]{:S(2)}, u32[]{:S(2)}) %collective-permute-start.13) | collective-permute-done | bytes 262176 | tf_op jit(solution)/shard_map/ppermute | solution.py:320
  63.6 13.9 %shard_map.68 = bf16[16,136,128]{2,1,0:T(8,128)(2,1)S(1)} custom-call(s32[1]{0:T(128)} %get-tuple-element.41.refs_0_, s32[2]{0:T(128)S(1)} %pad_add_fusion.refs_1_, bf16[16,288,128]{2,1,0:T(8,128)(2,1)S(1)} %all-to-all-done.refs_2_, bf16[2,512,128]{2,1,0:T(8,128)(2,1)S(1)} %copy-done.6, bf16[2,512,128]{2,1,0:T(8,128)(2,1)S(1)} %copy-done.8, ...), custom_call_target="tpu_custom_call" | custom-call | flops 4294967296 | bytes 3145728 | tf_op jit(solution)/shard_map/pallas_call | solution.py:166
  78.3 3.8 %all-to-all-start.2 = ((bf16[16,136,128]{2,1,0:T(8,128)(2,1)}), bf16[16,136,128]{2,1,0:T(8,128)(2,1)S(1)}, u32[]{:S(2)}, u32[]{:S(2)}) async-start(bf16[16,136,128]{2,1,0:T(8,128)(2,1)} %copy-done.4), calls=%async_computation.2 | async-start | bytes 1114112 | tf_op jit(solution)/shard_map/all_to_all | solution.py:336
  82.0 1.6 %copy-done.1 = bf16[2,512,8,128]{3,2,1,0:T(8,128)(2,1)S(1)} copy-done((bf16[2,512,8,128]{3,2,1,0:T(8,128)(2,1)S(1)}, bf16[2,512,8,128]{3,2,1,0:T(8,128)(2,1)}, u32[]{:S(2)}) %copy-start.1) | copy-done | bytes 2097176
  85.0 1.4 collective-permute-start.1
  86.6 1.6 %collective-permute-start.3 = (bf16[2,512,128]{2,1,0:T(8,128)(2,1)S(1)}, bf16[2,512,128]{2,1,0:T(8,128)(2,1)S(1)}, u32[]{:S(2)}, u32[]{:S(2)}) collective-permute-start(bf16[2,512,128]{2,1,0:T(8,128)(2,1)S(1)} %get-tuple-element.25), channel_id=1, source_target_pairs={{0,4},{1,5},{2,6},{3,7},{4,0},{5,1},{6,2},{7,3},{8,12},{9,13},{10,... | collective-permute-start | bytes 786440 | tf_op jit(solution)/shard_map/ppermute | solution.py:320
  88.5 2.4 %collective-permute-start.5 = (bf16[2,512,128]{2,1,0:T(8,128)(2,1)S(1)}, bf16[2,512,128]{2,1,0:T(8,128)(2,1)S(1)}, u32[]{:S(2)}, u32[]{:S(2)}) collective-permute-start(bf16[2,512,128]{2,1,0:T(8,128)(2,1)S(1)} %get-tuple-element.27), channel_id=1, source_target_pairs={{0,6},{1,7},{2,4},{3,5},{4,2},{5,3},{6,0},{7,1},{8,14},{9,15},{10,... | collective-permute-start | bytes 786440 | tf_op jit(solution)/shard_map/ppermute | solution.py:320
  90.9 6.2 %collective-permute-done.1.refs_5_ = bf16[2,512,128]{2,1,0:T(8,128)(2,1)S(1)} collective-permute-done((bf16[2,512,128]{2,1,0:T(8,128)(2,1)S(1)}, bf16[2,512,128]{2,1,0:T(8,128)(2,1)S(1)}, u32[]{:S(2)}, u32[]{:S(2)}) %collective-permute-start.1) | collective-permute-done | bytes 262176 | tf_op jit(solution)/shard_map/ppermute | solution.py:320
  98.4 3.4 %collective-permute-done.2.refs_6_ = bf16[2,512,128]{2,1,0:T(8,128)(2,1)S(1)} collective-permute-done((bf16[2,512,128]{2,1,0:T(8,128)(2,1)S(1)}, bf16[2,512,128]{2,1,0:T(8,128)(2,1)S(1)}, u32[]{:S(2)}, u32[]{:S(2)}) %collective-permute-start.2) | collective-permute-done | bytes 262176 | tf_op jit(solution)/shard_map/ppermute | solution.py:320
  101.8 2.7 %collective-permute-done.4.refs_8_ = bf16[2,512,128]{2,1,0:T(8,128)(2,1)S(1)} collective-permute-done((bf16[2,512,128]{2,1,0:T(8,128)(2,1)S(1)}, bf16[2,512,128]{2,1,0:T(8,128)(2,1)S(1)}, u32[]{:S(2)}, u32[]{:S(2)}) %collective-permute-start.4) | collective-permute-done | bytes 262176 | tf_op jit(solution)/shard_map/ppermute | solution.py:320
  104.5 7.3 %collective-permute-done.5.refs_9_ = bf16[2,512,128]{2,1,0:T(8,128)(2,1)S(1)} collective-permute-done((bf16[2,512,128]{2,1,0:T(8,128)(2,1)S(1)}, bf16[2,512,128]{2,1,0:T(8,128)(2,1)S(1)}, u32[]{:S(2)}, u32[]{:S(2)}) %collective-permute-start.5) | collective-permute-done | bytes 262176 | tf_op jit(solution)/shard_map/ppermute | solution.py:320
  111.7 5.3 %collective-permute-done.6.refs_10_ = bf16[2,512,128]{2,1,0:T(8,128)(2,1)S(1)} collective-permute-done((bf16[2,512,128]{2,1,0:T(8,128)(2,1)S(1)}, bf16[2,512,128]{2,1,0:T(8,128)(2,1)S(1)}, u32[]{:S(2)}, u32[]{:S(2)}) %collective-permute-start.6) | collective-permute-done | bytes 262176 | tf_op jit(solution)/shard_map/ppermute | solution.py:320
  117.0 12.7 %shard_map.66 = bf16[16,136,128]{2,1,0:T(8,128)(2,1)} custom-call(s32[1]{0:T(128)} %get-tuple-element.42.refs_0_, s32[2]{0:T(128)S(1)} %pad_add_fusion.refs_1_, bf16[16,288,128]{2,1,0:T(8,128)(2,1)S(1)} %copy-done.3, bf16[2,512,128]{2,1,0:T(8,128)(2,1)S(1)} %get-tuple-element.21.refs_3_, bf16[2,512,128]{2,1,0:T(8,128)(2,1)S(1)} %collective-permute-done.refs_4_, ...), custom_call_target="tpu_custom_call" | custom-call | flops 4294967296 | bytes 3145728 | tf_op jit(solution)/shard_map/pallas_call | solution.py:166
  129.7 3.6 %all-to-all-start.1 = ((bf16[16,136,128]{2,1,0:T(8,128)(2,1)}), bf16[16,136,128]{2,1,0:T(8,128)(2,1)S(1)}, u32[]{:S(2)}, u32[]{:S(2)}) async-start(bf16[16,136,128]{2,1,0:T(8,128)(2,1)} %shard_map.66), calls=%async_computation.1 | async-start | bytes 1114112 | tf_op jit(solution)/shard_map/all_to_all | solution.py:336
  134.5 13.5 %all-to-all-done.1 = bf16[16,136,128]{2,1,0:T(8,128)(2,1)S(1)} async-done(((bf16[16,136,128]{2,1,0:T(8,128)(2,1)}), bf16[16,136,128]{2,1,0:T(8,128)(2,1)S(1)}, u32[]{:S(2)}, u32[]{:S(2)}) %all-to-all-start.1) | async-done | bytes 557088 | tf_op jit(solution)/shard_map/all_to_all | solution.py:336
  (68 shorter events, 23.8 us)
Async XLA Ops:
  3.0 32.9 %all-to-all-start = ((bf16[16,288,128]{2,1,0:T(8,128)(2,1)}), bf16[16,288,128]{2,1,0:T(8,128)(2,1)S(1)}, u32[]{:S(2)}, u32[]{:S(2)}) async-start(bf16[16,288,128]{2,1,0:T(8,128)(2,1)} %shard_map.64), calls=%async_computation | async-start | bytes 2359296 | tf_op jit(solution)/shard_map/all_to_all | solution.py:305
  10.4 7.3 %copy-start.21 = (s32[2]{0:T(128)S(1)}, s32[2]{0:T(128)}, u32[]{:S(2)}) copy-start(s32[2]{0:T(128)} %param.11) | copy-start | bytes 28
  13.7 4.5 %collective-permute-start.7 = (bf16[2,512,128]{2,1,0:T(8,128)(2,1)}, bf16[2,512,128]{2,1,0:T(8,128)(2,1)S(1)}, u32[]{:S(2)}, u32[]{:S(2)}) collective-permute-start(bf16[2,512,128]{2,1,0:T(8,128)(2,1)} %get-tuple-element.30), channel_id=1, source_target_pairs={{0,1},{1,0},{2,3},{3,2},{4,5},{5,4},{6,7},{7,6},{8,9},{9,8},{10,11... | collective-permute-start | bytes 786440 | tf_op jit(solution)/shard_map/ppermute | solution.py:320
  14.1 15.6 %collective-permute-start.8 = (bf16[2,512,128]{2,1,0:T(8,128)(2,1)}, bf16[2,512,128]{2,1,0:T(8,128)(2,1)S(1)}, u32[]{:S(2)}, u32[]{:S(2)}) collective-permute-start(bf16[2,512,128]{2,1,0:T(8,128)(2,1)} %get-tuple-element.31), channel_id=1, source_target_pairs={{0,2},{1,3},{2,0},{3,1},{4,6},{5,7},{6,4},{7,5},{8,10},{9,11},{10,... | collective-permute-start | bytes 786440 | tf_op jit(solution)/shard_map/ppermute | solution.py:320
  15.8 21.1 %collective-permute-start.9 = (bf16[2,512,128]{2,1,0:T(8,128)(2,1)}, bf16[2,512,128]{2,1,0:T(8,128)(2,1)S(1)}, u32[]{:S(2)}, u32[]{:S(2)}) collective-permute-start(bf16[2,512,128]{2,1,0:T(8,128)(2,1)} %get-tuple-element.32), channel_id=1, source_target_pairs={{0,3},{1,2},{2,1},{3,0},{4,7},{5,6},{6,5},{7,4},{8,11},{9,10},{10,... | collective-permute-start | bytes 786440 | tf_op jit(solution)/shard_map/ppermute | solution.py:320
  15.8 22.8 %collective-permute-start.10 = (bf16[2,512,128]{2,1,0:T(8,128)(2,1)}, bf16[2,512,128]{2,1,0:T(8,128)(2,1)S(1)}, u32[]{:S(2)}, u32[]{:S(2)}) collective-permute-start(bf16[2,512,128]{2,1,0:T(8,128)(2,1)} %get-tuple-element.33), channel_id=1, source_target_pairs={{0,4},{1,5},{2,6},{3,7},{4,0},{5,1},{6,2},{7,3},{8,12},{9,13},{10,... | collective-permute-start | bytes 786440 | tf_op jit(solution)/shard_map/ppermute | solution.py:320
  17.5 25.6 %collective-permute-start.11 = (bf16[2,512,128]{2,1,0:T(8,128)(2,1)}, bf16[2,512,128]{2,1,0:T(8,128)(2,1)S(1)}, u32[]{:S(2)}, u32[]{:S(2)}) collective-permute-start(bf16[2,512,128]{2,1,0:T(8,128)(2,1)} %get-tuple-element.34), channel_id=1, source_target_pairs={{0,5},{1,4},{2,7},{3,6},{4,1},{5,0},{6,3},{7,2},{8,13},{9,12},{10,... | collective-permute-start | bytes 786440 | tf_op jit(solution)/shard_map/ppermute | solution.py:320
  18.2 37.7 %copy-start.7 = (bf16[2,512,128]{2,1,0:T(8,128)(2,1)}, bf16[2,512,128]{2,1,0:T(8,128)(2,1)S(1)}, u32[]{:S(2)}) copy-start(bf16[2,512,128]{2,1,0:T(8,128)(2,1)S(1)} %collective-permute-done.7.refs_4_) | copy-start | bytes 786436
  18.2 32.6 %collective-permute-start.12 = (bf16[2,512,128]{2,1,0:T(8,128)(2,1)}, bf16[2,512,128]{2,1,0:T(8,128)(2,1)S(1)}, u32[]{:S(2)}, u32[]{:S(2)}) collective-permute-start(bf16[2,512,128]{2,1,0:T(8,128)(2,1)} %get-tuple-element.35), channel_id=1, source_target_pairs={{0,6},{1,7},{2,4},{3,5},{4,2},{5,3},{6,0},{7,1},{8,14},{9,15},{10,... | collective-permute-start | bytes 786440 | tf_op jit(solution)/shard_map/ppermute | solution.py:320
  29.7 26.2 %copy-start.9 = (bf16[2,512,128]{2,1,0:T(8,128)(2,1)}, bf16[2,512,128]{2,1,0:T(8,128)(2,1)S(1)}, u32[]{:S(2)}) copy-start(bf16[2,512,128]{2,1,0:T(8,128)(2,1)S(1)} %collective-permute-done.8.refs_5_) | copy-start | bytes 786436
  29.7 25.5 %collective-permute-start.13 = (bf16[2,512,128]{2,1,0:T(8,128)(2,1)}, bf16[2,512,128]{2,1,0:T(8,128)(2,1)S(1)}, u32[]{:S(2)}, u32[]{:S(2)}) collective-permute-start(bf16[2,512,128]{2,1,0:T(8,128)(2,1)} %get-tuple-element.36), channel_id=1, source_target_pairs={{0,7},{1,6},{2,5},{3,4},{4,3},{5,2},{6,1},{7,0},{8,15},{9,14},{10,... | collective-permute-start | bytes 786440 | tf_op jit(solution)/shard_map/ppermute | solution.py:320
  35.9 41.6 %copy-start.2 = (bf16[16,288,128]{2,1,0:T(8,128)(2,1)}, bf16[16,288,128]{2,1,0:T(8,128)(2,1)S(1)}, u32[]{:S(2)}) copy-start(bf16[16,288,128]{2,1,0:T(8,128)(2,1)S(1)} %all-to-all-done.refs_2_) | copy-start | bytes 3538948
  63.6 18.5 %copy-start = (bf16[2,512,8,128]{3,2,1,0:T(8,128)(2,1)S(1)}, bf16[2,512,8,128]{3,2,1,0:T(8,128)(2,1)}, u32[]{:S(2)}) copy-start(bf16[2,512,8,128]{3,2,1,0:T(8,128)(2,1)} %k_hbm.3) | copy-start | bytes 6291460
  78.3 51.4 %all-to-all-start.2 = ((bf16[16,136,128]{2,1,0:T(8,128)(2,1)}), bf16[16,136,128]{2,1,0:T(8,128)(2,1)S(1)}, u32[]{:S(2)}, u32[]{:S(2)}) async-start(bf16[16,136,128]{2,1,0:T(8,128)(2,1)} %copy-done.4), calls=%async_computation.2 | async-start | bytes 1114112 | tf_op jit(solution)/shard_map/all_to_all | solution.py:336
  82.0 1.6 %copy-start.1 = (bf16[2,512,8,128]{3,2,1,0:T(8,128)(2,1)S(1)}, bf16[2,512,8,128]{3,2,1,0:T(8,128)(2,1)}, u32[]{:S(2)}) copy-start(bf16[2,512,8,128]{3,2,1,0:T(8,128)(2,1)} %v_hbm.3) | copy-start | bytes 6291460
  83.6 33.4 %copy-start.3 = (bf16[16,288,128]{2,1,0:T(8,128)(2,1)S(1)}, bf16[16,288,128]{2,1,0:T(8,128)(2,1)}, u32[]{:S(2)}) copy-start(bf16[16,288,128]{2,1,0:T(8,128)(2,1)} %copy-done.2) | copy-start | bytes 3538948
  84.6 3.9 %collective-permute-start = (bf16[2,512,128]{2,1,0:T(8,128)(2,1)S(1)}, bf16[2,512,128]{2,1,0:T(8,128)(2,1)S(1)}, u32[]{:S(2)}, u32[]{:S(2)}) collective-permute-start(bf16[2,512,128]{2,1,0:T(8,128)(2,1)S(1)} %get-tuple-element.22), channel_id=1, source_target_pairs={{0,1},{1,0},{2,3},{3,2},{4,5},{5,4},{6,7},{7,6},{8,9},{9,8},{10,11... | collective-permute-start | bytes 786440 | tf_op jit(solution)/shard_map/ppermute | solution.py:320
  85.0 12.0 %collective-permute-start.1 = (bf16[2,512,128]{2,1,0:T(8,128)(2,1)S(1)}, bf16[2,512,128]{2,1,0:T(8,128)(2,1)S(1)}, u32[]{:S(2)}, u32[]{:S(2)}) collective-permute-start(bf16[2,512,128]{2,1,0:T(8,128)(2,1)S(1)} %get-tuple-element.23), channel_id=1, source_target_pairs={{0,2},{1,3},{2,0},{3,1},{4,6},{5,7},{6,4},{7,5},{8,10},{9,11},{10,... | collective-permute-start | bytes 786440 | tf_op jit(solution)/shard_map/ppermute | solution.py:320
  86.5 15.3 %collective-permute-start.2 = (bf16[2,512,128]{2,1,0:T(8,128)(2,1)S(1)}, bf16[2,512,128]{2,1,0:T(8,128)(2,1)S(1)}, u32[]{:S(2)}, u32[]{:S(2)}) collective-permute-start(bf16[2,512,128]{2,1,0:T(8,128)(2,1)S(1)} %get-tuple-element.24), channel_id=1, source_target_pairs={{0,3},{1,2},{2,1},{3,0},{4,7},{5,6},{6,5},{7,4},{8,11},{9,10},{10,... | collective-permute-start | bytes 786440 | tf_op jit(solution)/shard_map/ppermute | solution.py:320
  86.6 15.2 %collective-permute-start.3 = (bf16[2,512,128]{2,1,0:T(8,128)(2,1)S(1)}, bf16[2,512,128]{2,1,0:T(8,128)(2,1)S(1)}, u32[]{:S(2)}, u32[]{:S(2)}) collective-permute-start(bf16[2,512,128]{2,1,0:T(8,128)(2,1)S(1)} %get-tuple-element.25), channel_id=1, source_target_pairs={{0,4},{1,5},{2,6},{3,7},{4,0},{5,1},{6,2},{7,3},{8,12},{9,13},{10,... | collective-permute-start | bytes 786440 | tf_op jit(solution)/shard_map/ppermute | solution.py:320
  88.2 16.2 %collective-permute-start.4 = (bf16[2,512,128]{2,1,0:T(8,128)(2,1)S(1)}, bf16[2,512,128]{2,1,0:T(8,128)(2,1)S(1)}, u32[]{:S(2)}, u32[]{:S(2)}) collective-permute-start(bf16[2,512,128]{2,1,0:T(8,128)(2,1)S(1)} %get-tuple-element.26), channel_id=1, source_target_pairs={{0,5},{1,4},{2,7},{3,6},{4,1},{5,0},{6,3},{7,2},{8,13},{9,12},{10,... | collective-permute-start | bytes 786440 | tf_op jit(solution)/shard_map/ppermute | solution.py:320
  88.5 23.2 %collective-permute-start.5 = (bf16[2,512,128]{2,1,0:T(8,128)(2,1)S(1)}, bf16[2,512,128]{2,1,0:T(8,128)(2,1)S(1)}, u32[]{:S(2)}, u32[]{:S(2)}) collective-permute-start(bf16[2,512,128]{2,1,0:T(8,128)(2,1)S(1)} %get-tuple-element.27), channel_id=1, source_target_pairs={{0,6},{1,7},{2,4},{3,5},{4,2},{5,3},{6,0},{7,1},{8,14},{9,15},{10,... | collective-permute-start | bytes 786440 | tf_op jit(solution)/shard_map/ppermute | solution.py:320
  97.1 20.0 %collective-permute-start.6 = (bf16[2,512,128]{2,1,0:T(8,128)(2,1)S(1)}, bf16[2,512,128]{2,1,0:T(8,128)(2,1)S(1)}, u32[]{:S(2)}, u32[]{:S(2)}) collective-permute-start(bf16[2,512,128]{2,1,0:T(8,128)(2,1)S(1)} %get-tuple-element.28), channel_id=1, source_target_pairs={{0,7},{1,6},{2,5},{3,4},{4,3},{5,2},{6,1},{7,0},{8,15},{9,14},{10,... | collective-permute-start | bytes 786440 | tf_op jit(solution)/shard_map/ppermute | solution.py:320
  129.7 18.4 %all-to-all-start.1 = ((bf16[16,136,128]{2,1,0:T(8,128)(2,1)}), bf16[16,136,128]{2,1,0:T(8,128)(2,1)S(1)}, u32[]{:S(2)}, u32[]{:S(2)}) async-start(bf16[16,136,128]{2,1,0:T(8,128)(2,1)} %shard_map.66), calls=%async_computation.1 | async-start | bytes 1114112 | tf_op jit(solution)/shard_map/all_to_all | solution.py:336
  (15 other events, 13.0 us)

commit v10 on v7

--- a/solution.py
+++ b/solution.py
@@ -20,9 +20,9 @@
 SMEM_SPEC = pl.BlockSpec(memory_space=pltpu.SMEM)
 
 
-def attend_kernel(*refs, order, total_blocks, tile, group_size, row_start, with_fresh, with_state, final):
+def attend_kernel(*refs, order, blocks, tile, group_size, row_start, with_fresh, with_state, final):
     refs = list(refs)
-    info_ref, q_hbm = refs.pop(0), refs.pop(0)
+    length_ref, place_ref, q_hbm = refs.pop(0), refs.pop(0), refs.pop(0)
     kv_refs = [refs.pop(0) for _ in order]
     if with_fresh:
         fk_ref, fv_ref = refs.pop(0), refs.pop(0)
@@ -30,28 +30,27 @@
         acc_in, top_in = refs.pop(0), refs.pop(0)
     if final:
         out_hbm = refs.pop(0)
+        out_ref, out_sem = refs.pop(), refs.pop()
     else:
         acc_out, top_out = refs.pop(0), refs.pop(0)
-    if final:
-        out_ref, out_sem = refs.pop(), refs.pop()
-    if with_fresh:
-        fvals = refs.pop()
-    q_ref, keys, vals, s0, s1, m0, m1, in_sems, q_sem = refs
+    q_ref, keys, loaded, vals, bias, s0, s1, m0, m1, in_sems, q_sem = refs
     per_source, dim = q_ref.shape[1:]
     block_slots = kv_refs[0].shape[1]
-    chunk = 2 * block_slots
-    chunks = len(order) // 2
-    slots = chunks * chunk
+    chunk = bias.shape[0]
+    slots = len(order) * block_slots
+    chunks = slots // chunk
+    fresh = fk_ref.shape[0] if with_fresh else 0
     rows = q_ref.shape[0] * per_source
     tiles = rows // tile
     span = tile // per_source
+    ones = vals.shape[0] - dim
     scale = math.log2(math.e) / math.sqrt(dim)
-    valid = info_ref[0]
-    fresh_shift = info_ref[1]
-    own = info_ref[2]
+    own, device_block = place_ref[0], place_ref[1]
+    valid = jnp.clip(length_ref[0] - device_block * blocks * block_slots, 0, blocks * block_slots)
+    fresh_shift = jnp.where(device_block == q_ref.shape[0] // blocks - 1, 0, -rows)
 
     held = sorted({k // 2 for k in order})
-    absent = [c for c in range(total_blocks // 2) if c not in held]
+    absent = [c for c in range(blocks // 2) if c not in held]
 
     def rank_of(index):
         rank = index
@@ -59,19 +58,16 @@
             rank = rank - jnp.where((own // 2) ^ c < index, 1, 0)
         return rank
 
-    copies = [pltpu.make_async_copy(q_hbm.at[:, row_start : row_start + per_source, :], q_ref, q_sem)]
+    value_copies = []
+    copies = []
     for i, k in enumerate(order):
         first = rank_of((own // 2) ^ (k // 2)) * chunk + ((own % 2) ^ (k % 2)) * block_slots
         at = pl.ds(pl.multiple_of(first, block_slots), block_slots)
+        value_copies.append(pltpu.make_async_copy(kv_refs[i].at[1], loaded.at[at, :], in_sems.at[i, 1]))
         copies.append(pltpu.make_async_copy(kv_refs[i].at[0], keys.at[at, :], in_sems.at[i, 0]))
-        copies.append(pltpu.make_async_copy(kv_refs[i].at[1], vals.at[at, :dim], in_sems.at[i, 1]))
-    for copy in copies:
+    copies.append(pltpu.make_async_copy(q_hbm.at[:, row_start : row_start + per_source, :], q_ref, q_sem))
+    for copy in value_copies + copies:
         copy.start()
-    vals[:, dim:] = jnp.ones((slots, dim), jnp.bfloat16)
-    if with_fresh:
-        fresh = fk_ref.shape[0]
-        fvals[:, :dim] = fv_ref[...]
-        fvals[:, dim:] = jnp.ones((fresh, dim), jnp.bfloat16)
 
     filled = jnp.int32(0)
     last_valid = jnp.int32(0)
@@ -80,62 +76,61 @@
         filled = filled + jnp.where(left > 0, 1, 0)
         last_valid = jnp.where((left > 0) & (left < chunk), left, last_valid)
     last_valid = jnp.where(last_valid == 0, chunk, last_valid)
+
+    vals[dim:, :] = jnp.ones((ones, slots + fresh), jnp.bfloat16)
+    if with_fresh:
+        vals[:dim, slots:] = jnp.transpose(fv_ref[...])
+    bias[...] = jnp.where(lax.broadcasted_iota(jnp.int32, bias.shape, 0) < last_valid, 0.0, NEG)
+    for copy in value_copies:
+        copy.wait()
+    for first in range(0, slots, block_slots):
+        vals[:dim, first : first + block_slots] = jnp.transpose(loaded[first : first + block_slots, :])
     for copy in copies:
         copy.wait()
 
-    def product(a, b):
-        return lax.dot_general(a, b, (((1,), (1,)), ((), ())), preferred_element_type=jnp.float32)
-
-    def lane_max(scores, best):
-        for lane in range(scores.shape[1] // dim):
-            part = scores[:, lane * dim : (lane + 1) * dim]
-            best = part if best is None else jnp.maximum(best, part)
-        return best
+    def fold_max(scores, best):
+        part = jnp.max(scores.reshape(-1, 8, tile), axis=0)
+        return part if best is None else jnp.maximum(best, part)
 
     def score_chunk(t, j, count, s_ref, best):
         q = q_ref[pl.ds(t * span, span)].reshape(tile, dim)
-        if j < count:
-            scores = product(q, keys[j * chunk : (j + 1) * chunk, :])
-            if j == count - 1:
-                pos = lax.broadcasted_iota(jnp.int32, (1, chunk), 1)
-                scores = scores + jnp.where(pos < last_valid, 0.0, NEG)
-            s_ref[:, j * chunk : (j + 1) * chunk] = scores
-            return lane_max(scores, best)
-        scores = product(q, fk_ref[...])
-        token = (t * tile + lax.broadcasted_iota(jnp.int32, (tile, 1), 0)) // group_size
-        unit = lax.broadcasted_iota(jnp.int32, (1, fresh), 1)
-        scores = jnp.where(unit <= token + fresh_shift, scores, NEG)
-        s_ref[:, slots : slots + fresh] = scores
-        return lane_max(scores, best)
+        at = slice(j * chunk, (j + 1) * chunk) if j < count else slice(slots, slots + fresh)
+        left_side = keys[at, :] if j < count else fk_ref[...]
+        scores = lax.dot_general(left_side, q, (((1,), (1,)), ((), ())), preferred_element_type=jnp.float32)
+        if j == count - 1:
+            mask = bias[...]
+            scores = scores + jnp.concatenate([mask] * (tile // mask.shape[1]), axis=1)
+        elif j == count:
+            token = (t * tile + lax.broadcasted_iota(jnp.int32, (1, tile), 1)) // group_size
+            unit = lax.broadcasted_iota(jnp.int32, (fresh, 1), 0)
+            scores = jnp.where(unit <= token + fresh_shift, scores, NEG)
+        s_ref[at, :] = scores
+        return fold_max(scores, best)
 
     def value_chunk(j, count, s_ref, top, acc):
-        if j < count:
-            scores = s_ref[:, j * chunk : (j + 1) * chunk]
-            values = vals[j * chunk : (j + 1) * chunk, :]
-        else:
-            scores = s_ref[:, slots : slots + fresh]
-            values = fvals[...]
-        weights = jnp.exp2((scores - top) * scale).astype(jnp.bfloat16)
-        part = jnp.dot(weights, values, preferred_element_type=jnp.float32)
+        at = slice(j * chunk, (j + 1) * chunk) if j < count else slice(slots, slots + fresh)
+        weights = jnp.exp2((s_ref[at, :] - top) * scale).astype(jnp.bfloat16)
+        part = jnp.dot(vals[:, at], weights, preferred_element_type=jnp.float32)
         return part if acc is None else acc + part
 
     def finish(t, top, acc):
-        total = acc[:, dim:]
-        out = (acc[:, :dim] / total).astype(jnp.bfloat16)
-        out_ref[pl.ds(t * span, span), :per_source, :] = out.reshape(span, per_source, dim)
+        total = acc[dim : dim + 1, :]
+        out = acc[:dim, :] / total
         level = top * scale + jnp.log2(total)
+        high = level.astype(jnp.bfloat16).astype(jnp.float32)
+        mid = (level - high).astype(jnp.bfloat16).astype(jnp.float32)
+        low = level - high - mid
+        which = lax.broadcasted_iota(jnp.int32, (STAT_ROWS, tile), 0)
+        stats = jnp.where(which == 0, high, jnp.where(which == 1, mid, low)).astype(jnp.bfloat16)
         for first in range(0, tile, dim):
-            flat = jnp.transpose(level[first : first + dim, :STAT_ROWS])
-            high = flat.astype(jnp.bfloat16).astype(jnp.float32)
-            mid = (flat - high).astype(jnp.bfloat16).astype(jnp.float32)
-            low = flat - high - mid
-            which = lax.broadcasted_iota(jnp.int32, flat.shape, 0)
-            stats = jnp.where(which == 0, high, jnp.where(which == 1, mid, low)).astype(jnp.bfloat16)
+            flat = jnp.transpose(out[:, first : first + dim]).astype(jnp.bfloat16)
             width = min(per_source, dim)
             for part in range(dim // width):
-                row = first + part * width
-                out_ref[t * span + row // per_source, per_source:, :width] = stats[
-                    :, part * width : (part + 1) * width
+                source = t * span + (first + part * width) // per_source
+                inside = (first + part * width) % per_source
+                out_ref[source, inside : inside + width, :] = flat[part * width : (part + 1) * width, :]
+                out_ref[source, per_source:, inside : inside + width] = stats[
+                    :, first + part * width : first + (part + 1) * width
                 ]
 
     def stage(t_next, s_next, m_next, t_now, s_now, m_now, count):
@@ -144,11 +139,11 @@
         acc = None
         if t_now is not None:
             at = pl.ds(pl.multiple_of(t_now * tile, tile), tile)
-            top = jnp.max(m_now[...], axis=1, keepdims=True) if pieces else None
+            top = jnp.max(m_now[...], axis=0, keepdims=True) if pieces else None
             if with_state:
-                before = top_in[at, :1]
+                before = top_in[:, at][:1]
                 top = before if top is None else jnp.maximum(top, before)
-                acc = acc_in[at, :] * jnp.exp2((before - top) * scale)
+                acc = acc_in[:, at] * jnp.exp2((before - top) * scale)
         for j in range(pieces):
             if t_next is not None:
                 best = score_chunk(t_next, j, count, s_next, best)
@@ -160,8 +155,8 @@
             if final:
                 finish(t_now, top, acc)
             else:
-                acc_out[at, :] = acc
-                top_out[at, :] = jnp.broadcast_to(top, (tile, dim))
+                acc_out[:, at] = acc
+                top_out[:, at] = jnp.broadcast_to(top, (8, tile))
 
     for count in range(chunks + 1):
 
@@ -182,29 +177,32 @@
         result.wait()
 
 
-def attend(info, head_q, kv_blocks, order, fresh, state, final, row_start, row_count, group_size):
+def attend(length, place, head_q, kv_blocks, order, fresh, state, final, row_start, row_count, group_size):
     sources, _, dim = head_q.shape
     slots = len(order) * kv_blocks[0].shape[1]
     rows = sources * row_count
     units = 0 if fresh is None else fresh[0].shape[0]
     tile = min(256, rows // 2)
-    operands = [info, head_q] + [kv_blocks[k] for k in order]
-    in_specs = [SMEM_SPEC] + [HBM_SPEC] * (1 + len(order))
+    chunk = 2 * kv_blocks[0].shape[1]
+    depth = dim + 16
+    operands = [length, place, head_q] + [kv_blocks[k] for k in order]
+    in_specs = [SMEM_SPEC] * 2 + [HBM_SPEC] * (1 + len(order))
     scratch = [
         pltpu.VMEM((sources, row_count, dim), jnp.bfloat16),
         pltpu.VMEM((slots, dim), jnp.bfloat16),
-        pltpu.VMEM((slots, 2 * dim), jnp.bfloat16),
-        pltpu.VMEM((tile, slots + units), jnp.float32),
-        pltpu.VMEM((tile, slots + units), jnp.float32),
-        pltpu.VMEM((tile, dim), jnp.float32),
-        pltpu.VMEM((tile, dim), jnp.float32),
+        pltpu.VMEM((slots, dim), jnp.bfloat16),
+        pltpu.VMEM((depth, slots + units), jnp.bfloat16),
+        pltpu.VMEM((chunk, min(dim, tile)), jnp.float32),
+        pltpu.VMEM((slots + units, tile), jnp.float32),
+        pltpu.VMEM((slots + units, tile), jnp.float32),
+        pltpu.VMEM((8, tile), jnp.float32),
+        pltpu.VMEM((8, tile), jnp.float32),
         pltpu.SemaphoreType.DMA((len(order), 2)),
         pltpu.SemaphoreType.DMA,
     ]
     if fresh is not None:
         operands += list(fresh)
         in_specs += [VMEM_SPEC] * 2
-        scratch.append(pltpu.VMEM((units, 2 * dim), jnp.bfloat16))
     if state is not None:
         operands += list(state)
         in_specs += [VMEM_SPEC] * 2
@@ -214,16 +212,16 @@
         scratch += [pltpu.SemaphoreType.DMA, pltpu.VMEM(out_shape.shape, jnp.bfloat16)]
     else:
         out_shape = [
-            jax.ShapeDtypeStruct((rows, 2 * dim), jnp.float32),
-            jax.ShapeDtypeStruct((rows, dim), jnp.float32),
+            jax.ShapeDtypeStruct((depth, rows), jnp.float32),
+            jax.ShapeDtypeStruct((8, rows), jnp.float32),
         ]
         out_specs = [VMEM_SPEC] * 2
-    grant = 8 * tile * (slots + units) + 6 * slots * dim + 24 * rows * dim + SMALL_VMEM
+    grant = 8 * tile * (slots + units) + 8 * slots * dim + 12 * rows * dim + SMALL_VMEM
     return pl.pallas_call(
         functools.partial(
             attend_kernel,
             order=order,
-            total_blocks=len(kv_blocks),
+            blocks=len(kv_blocks),
             tile=tile,
             group_size=group_size,
             row_start=row_start,
@@ -340,7 +338,6 @@
 
 def attention(queries, new_k, new_v, cache_k, cache_v, cache_len):
     requests, local_rows, heads, head_dim = queries.shape
-    slots = cache_k.shape[1]
     kv_heads = cache_k.shape[2]
     group_size = heads // kv_heads
     devices_seq = lax.axis_size("seq")
@@ -371,16 +368,14 @@
             moved.append(lax.ppermute(parts[k], "seq", [(i, i ^ k) for i in range(devices_seq)]))
         kv_blocks.append(moved)
 
+    early = kv_heads - 2
+    place = jnp.stack([own, block]).astype(jnp.int32)
     out = None
     for r in range(requests):
-        held = kv_heads * slots
-        valid = jnp.clip(cache_len[r] - block * held, 0, held)
-        fresh_shift = jnp.where(block == spread - 1, 0, -devices_seq * local_rows)
-        info = jnp.stack([valid, fresh_shift, own]).astype(jnp.int32)
         rows = (r * per_source, per_source, group_size)
-        part = attend(
-            info, head_q, kv_blocks[r], tuple(range(kv_heads)), (head_fresh[0, r], head_fresh[1, r]), None, True, *rows
-        )
+        common = (cache_len[r : r + 1], place, head_q, kv_blocks[r])
+        state = attend(*common, tuple(range(early)), (head_fresh[0, r], head_fresh[1, r]), None, False, *rows)
+        part = attend(*common, tuple(range(early, kv_heads)), None, state, True, *rows)
         part = lax.all_to_all(part, "seq", split_axis=0, concat_axis=0, tiled=True)
         part = part.reshape(spread, kv_heads, per_source + STAT_ROWS, head_dim)
         out = merge(part, r, requests, local_rows, group_size, out)

time: 156 us -> 129 us (0.83)
  the two profiles are of different devices: /device:TPU:13 before, /device:TPU:0 now
where the time goes in v10:
time: 129 us; the launch traced here: 127 us
  waiting for transfers between devices  47.2 us (37%)
  Pallas kernels  39.6 us (31%)
  starting transfers between devices  34.1 us (26%)
  local copies, waits for them, and re-layouts  5.04 us (4%)
    pallas_call x4, Pallas kernels, attend(): pl.pallas_call(functools.partial(attend_kernel, order=order, blocks=len(k...  31.7 us
    all_to_all x1, waiting for transfers between devices, attention(): lax.all_to_all(pack(queries, fresh, devices_seq), 'seq', split_axis=0, co...  17.6 us
    ppermute x14, starting transfers between devices, attention(): lax.ppermute(parts[k], 'seq', [(i, i ^ k) for i in range(devices_seq)])  17.1 us
    ppermute x14, waiting for transfers between devices, attention(): lax.ppermute(parts[k], 'seq', [(i, i ^ k) for i in range(devices_seq)])  16 us
    all_to_all x2, waiting for transfers between devices, attention(): part = lax.all_to_all(part, 'seq', split_axis=0, concat_axis=0, tiled=True)  13.5 us
    all_to_all x2, starting transfers between devices, attention(): part = lax.all_to_all(part, 'seq', split_axis=0, concat_axis=0, tiled=True)  9.61 us
    all_to_all x1, starting transfers between devices, attention(): lax.all_to_all(pack(queries, fresh, devices_seq), 'seq', split_axis=0, co...  7.39 us
    unnamed x16, local copies, waits for them, and re-layouts  4.39 us
  transfers between devices with their start and end apart: 17, of which 8 were waited for; matrix products, arithmetic and copies ran while one was open for 1% of the time, Pallas kernels for 24%

profile of v10, /device:TPU:0, one launch (start us, length us, event | category | flops | bytes accessed | tf_op | source)
XLA Modules:
  0.0 127.0 jit_solution(17461098601016233045)
XLA Ops:
  3.0 7.4 %all-to-all-start = ((bf16[16,288,128]{2,1,0:T(8,128)(2,1)}), bf16[16,288,128]{2,1,0:T(8,128)(2,1)S(1)}, u32[]{:S(2)}, u32[]{:S(2)}) async-start(bf16[16,288,128]{2,1,0:T(8,128)(2,1)} %shard_map.64), calls=%async_computation | async-start | bytes 2359296 | tf_op jit(solution)/shard_map/all_to_all | solution.py:353
  10.4 3.3 %shard_map.68 = (bf16[2,512,128]{2,1,0:T(8,128)(2,1)}, bf16[2,512,128]{2,1,0:T(8,128)(2,1)}, bf16[2,512,128]{2,1,0:T(8,128)(2,1)}, bf16[2,512,128]{2,1,0:T(8,128...) custom-call(s32[1]{0:T(128)} %bitcast.own_ref, ...), custom_call_target="tpu_custom_call" | custom-call | tf_op jit(solution)/shard_map/pallas_call | solution.py:325
  14.1 1.6 %collective-permute-start.10 = (bf16[2,512,128]{2,1,0:T(8,128)(2,1)}, bf16[2,512,128]{2,1,0:T(8,128)(2,1)S(1)}, u32[]{:S(2)}, u32[]{:S(2)}) collective-permute-start(bf16[2,512,128]{2,1,0:T(8,128)(2,1)} %get-tuple-element.39), channel_id=1, source_target_pairs={{0,2},{1,3},{2,0},{3,1},{4,6},{5,7},{6,4},{7,5},{8,10},{9,11},{10,... | collective-permute-start | bytes 786440 | tf_op jit(solution)/shard_map/ppermute | solution.py:368
  15.8 1.7 %collective-permute-start.12 = (bf16[2,512,128]{2,1,0:T(8,128)(2,1)}, bf16[2,512,128]{2,1,0:T(8,128)(2,1)S(1)}, u32[]{:S(2)}, u32[]{:S(2)}) collective-permute-start(bf16[2,512,128]{2,1,0:T(8,128)(2,1)} %get-tuple-element.41), channel_id=1, source_target_pairs={{0,4},{1,5},{2,6},{3,7},{4,0},{5,1},{6,2},{7,3},{8,12},{9,13},{10,... | collective-permute-start | bytes 786440 | tf_op jit(solution)/shard_map/ppermute | solution.py:368
  18.3 17.6 %all-to-all-done.refs_2_ = bf16[16,288,128]{2,1,0:T(8,128)(2,1)S(1)} async-done(((bf16[16,288,128]{2,1,0:T(8,128)(2,1)}), bf16[16,288,128]{2,1,0:T(8,128)(2,1)S(1)}, u32[]{:S(2)}, u32[]{:S(2)}) %all-to-all-start) | async-done | bytes 1179680 | tf_op jit(solution)/shard_map/all_to_all | solution.py:353
  35.9 4.9 %collective-permute-start.7 = (bf16[2,512,128]{2,1,0:T(8,128)(2,1)}, bf16[2,512,128]{2,1,0:T(8,128)(2,1)S(1)}, u32[]{:S(2)}, u32[]{:S(2)}) collective-permute-start(bf16[2,512,128]{2,1,0:T(8,128)(2,1)} %get-tuple-element.35), channel_id=1, source_target_pairs={{0,6},{1,7},{2,4},{3,5},{4,2},{5,3},{6,0},{7,1},{8,14},{9,15},{10,... | collective-permute-start | bytes 786440 | tf_op jit(solution)/shard_map/ppermute | solution.py:368
  41.2 1.9 %collective-permute-done.13.refs_8_ = bf16[2,512,128]{2,1,0:T(8,128)(2,1)S(1)} collective-permute-done((bf16[2,512,128]{2,1,0:T(8,128)(2,1)}, bf16[2,512,128]{2,1,0:T(8,128)(2,1)S(1)}, u32[]{:S(2)}, u32[]{:S(2)}) %collective-permute-start.13) | collective-permute-done | bytes 262176 | tf_op jit(solution)/shard_map/ppermute | solution.py:368
  44.0 10.8 %shard_map.69 = (f32[144,2048]{1,0:T(8,128)S(1)}, f32[8,2048]{1,0:T(8,128)S(1)}) custom-call(s32[1]{0:T(128)} %get-tuple-element.49.refs_0_, s32[2]{0:T(128)S(1)} %pad_add_fusion.refs_1_, bf16[16,288,128]{2,1,0:T(8,128)(2,1)S(1)} %all-to-all-done.refs_2_, bf16[2,512,128]{2,1,0:T(8,128)(2,1)S(1)} %copy-done.6, ...), custom_call_target="tpu_custom_call" | custom-call | flops 3221225472 | bytes 2621440 | tf_op jit(solution)/shard_map/pallas_call | solution.py:220
  55.2 6.5 %shard_map.70 = bf16[16,136,128]{2,1,0:T(8,128)(2,1)S(1)} custom-call(s32[1]{0:T(128)} %get-tuple-element.49.refs_0_, s32[2]{0:T(128)S(1)} %pad_add_fusion.refs_1_, bf16[16,288,128]{2,1,0:T(8,128)(2,1)S(1)} %all-to-all-done.refs_2_, bf16[2,512,128]{2,1,0:T(8,128)(2,1)S(1)} %collective-permute-done.7.refs_3_, ...), custom_call_target="tpu_custom_call" | custom-call | flops 1073741824 | bytes 1572864 | tf_op jit(solution)/shard_map/pallas_call | solution.py:220
  62.6 4.1 %all-to-all-start.2 = ((bf16[16,136,128]{2,1,0:T(8,128)(2,1)}), bf16[16,136,128]{2,1,0:T(8,128)(2,1)S(1)}, u32[]{:S(2)}, u32[]{:S(2)}) async-start(bf16[16,136,128]{2,1,0:T(8,128)(2,1)} %copy-done.4), calls=%async_computation.2 | async-start | bytes 1114112 | tf_op jit(solution)/shard_map/all_to_all | solution.py:379
  66.7 1.6 %copy-done.1 = bf16[2,512,8,128]{3,2,1,0:T(8,128)(2,1)S(1)} copy-done((bf16[2,512,8,128]{3,2,1,0:T(8,128)(2,1)S(1)}, bf16[2,512,8,128]{3,2,1,0:T(8,128)(2,1)}, u32[]{:S(2)}) %copy-start.1) | copy-done | bytes 2097176
  69.8 1.6 %collective-permute-start.3 = (bf16[2,512,128]{2,1,0:T(8,128)(2,1)S(1)}, bf16[2,512,128]{2,1,0:T(8,128)(2,1)S(1)}, u32[]{:S(2)}, u32[]{:S(2)}) collective-permute-start(bf16[2,512,128]{2,1,0:T(8,128)(2,1)S(1)} %get-tuple-element.29), channel_id=1, source_target_pairs={{0,2},{1,3},{2,0},{3,1},{4,6},{5,7},{6,4},{7,5},{8,10},{9,11},{10,... | collective-permute-start | bytes 786440 | tf_op jit(solution)/shard_map/ppermute | solution.py:368
  71.4 1.7 %collective-permute-start.5 = (bf16[2,512,128]{2,1,0:T(8,128)(2,1)S(1)}, bf16[2,512,128]{2,1,0:T(8,128)(2,1)S(1)}, u32[]{:S(2)}, u32[]{:S(2)}) collective-permute-start(bf16[2,512,128]{2,1,0:T(8,128)(2,1)S(1)} %get-tuple-element.31), channel_id=1, source_target_pairs={{0,4},{1,5},{2,6},{3,7},{4,0},{5,1},{6,2},{7,3},{8,12},{9,13},{10,... | collective-permute-start | bytes 786440 | tf_op jit(solution)/shard_map/ppermute | solution.py:368
  73.3 2.5 %collective-permute-start = (bf16[2,512,128]{2,1,0:T(8,128)(2,1)S(1)}, bf16[2,512,128]{2,1,0:T(8,128)(2,1)S(1)}, u32[]{:S(2)}, u32[]{:S(2)}) collective-permute-start(bf16[2,512,128]{2,1,0:T(8,128)(2,1)S(1)} %get-tuple-element.25), channel_id=1, source_target_pairs={{0,6},{1,7},{2,4},{3,5},{4,2},{5,3},{6,0},{7,1},{8,14},{9,15},{10,... | collective-permute-start | bytes 786440 | tf_op jit(solution)/shard_map/ppermute | solution.py:368
  75.8 6.1 %collective-permute-done.3.refs_5_ = bf16[2,512,128]{2,1,0:T(8,128)(2,1)S(1)} collective-permute-done((bf16[2,512,128]{2,1,0:T(8,128)(2,1)S(1)}, bf16[2,512,128]{2,1,0:T(8,128)(2,1)S(1)}, u32[]{:S(2)}, u32[]{:S(2)}) %collective-permute-start.3) | collective-permute-done | bytes 262176 | tf_op jit(solution)/shard_map/ppermute | solution.py:368
  81.9 1.4 %collective-permute-start.1 = (bf16[2,512,128]{2,1,0:T(8,128)(2,1)S(1)}, bf16[2,512,128]{2,1,0:T(8,128)(2,1)S(1)}, u32[]{:S(2)}, u32[]{:S(2)}) collective-permute-start(bf16[2,512,128]{2,1,0:T(8,128)(2,1)S(1)} %get-tuple-element.26), channel_id=1, source_target_pairs={{0,7},{1,6},{2,5},{3,4},{4,3},{5,2},{6,1},{7,0},{8,15},{9,14},{10,... | collective-permute-start | bytes 786440 | tf_op jit(solution)/shard_map/ppermute | solution.py:368
  83.3 3.4 %collective-permute-done.4.refs_6_ = bf16[2,512,128]{2,1,0:T(8,128)(2,1)S(1)} collective-permute-done((bf16[2,512,128]{2,1,0:T(8,128)(2,1)S(1)}, bf16[2,512,128]{2,1,0:T(8,128)(2,1)S(1)}, u32[]{:S(2)}, u32[]{:S(2)}) %collective-permute-start.4) | collective-permute-done | bytes 262176 | tf_op jit(solution)/shard_map/ppermute | solution.py:368
  86.7 2.7 %collective-permute-done.6.refs_8_ = bf16[2,512,128]{2,1,0:T(8,128)(2,1)S(1)} collective-permute-done((bf16[2,512,128]{2,1,0:T(8,128)(2,1)S(1)}, bf16[2,512,128]{2,1,0:T(8,128)(2,1)S(1)}, u32[]{:S(2)}, u32[]{:S(2)}) %collective-permute-start.6) | collective-permute-done | bytes 262176 | tf_op jit(solution)/shard_map/ppermute | solution.py:368
  89.4 11.0 %shard_map.66 = (f32[144,2048]{1,0:T(8,128)S(1)}, f32[8,2048]{1,0:T(8,128)S(1)}) custom-call(s32[1]{0:T(128)} %get-tuple-element.50.refs_0_, s32[2]{0:T(128)S(1)} %pad_add_fusion.refs_1_, bf16[16,288,128]{2,1,0:T(8,128)(2,1)S(1)} %copy-done.3, bf16[2,512,128]{2,1,0:T(8,128)(2,1)S(1)} %get-tuple-element.27.refs_3_, ...), custom_call_target="tpu_custom_call" | custom-call | flops 3221225472 | bytes 2621440 | tf_op jit(solution)/shard_map/pallas_call | solution.py:220
  100.4 1.6 %collective-permute-done.1.refs_4_ = bf16[2,512,128]{2,1,0:T(8,128)(2,1)S(1)} collective-permute-done((bf16[2,512,128]{2,1,0:T(8,128)(2,1)S(1)}, bf16[2,512,128]{2,1,0:T(8,128)(2,1)S(1)}, u32[]{:S(2)}, u32[]{:S(2)}) %collective-permute-start.1) | collective-permute-done | bytes 262176 | tf_op jit(solution)/shard_map/ppermute | solution.py:368
  101.9 3.4 %shard_map.67 = bf16[16,136,128]{2,1,0:T(8,128)(2,1)} custom-call(s32[1]{0:T(128)} %get-tuple-element.50.refs_0_, s32[2]{0:T(128)S(1)} %pad_add_fusion.refs_1_, bf16[16,288,128]{2,1,0:T(8,128)(2,1)S(1)} %copy-done.3, bf16[2,512,128]{2,1,0:T(8,128)(2,1)S(1)} %collective-permute-done.refs_3_, bf16[2,512,128]{2,1,0:T(8,128)(2,1)S(1)} %collective-permute-done.1.refs_4_, ...), custom_call_target="tpu_custom_call" | custom-call | flops 1073741824 | bytes 1572864 | tf_op jit(solution)/shard_map/pallas_call | solution.py:220
  105.4 5.5 %all-to-all-start.1 = ((bf16[16,136,128]{2,1,0:T(8,128)(2,1)}), bf16[16,136,128]{2,1,0:T(8,128)(2,1)S(1)}, u32[]{:S(2)}, u32[]{:S(2)}) async-start(bf16[16,136,128]{2,1,0:T(8,128)(2,1)} %shard_map.67), calls=%async_computation.1 | async-start | bytes 1114112 | tf_op jit(solution)/shard_map/all_to_all | solution.py:379
  110.9 1.3 shard_map.71.refs_0_
  112.1 13.5 %all-to-all-done.1 = bf16[16,136,128]{2,1,0:T(8,128)(2,1)S(1)} async-done(((bf16[16,136,128]{2,1,0:T(8,128)(2,1)}), bf16[16,136,128]{2,1,0:T(8,128)(2,1)S(1)}, u32[]{:S(2)}, u32[]{:S(2)}) %all-to-all-start.1) | async-done | bytes 557088 | tf_op jit(solution)/shard_map/all_to_all | solution.py:379
  (42 shorter events, 9.7 us)
Async XLA Ops:
  0.8 1.0 copy-start.5
  3.0 32.9 %all-to-all-start = ((bf16[16,288,128]{2,1,0:T(8,128)(2,1)}), bf16[16,288,128]{2,1,0:T(8,128)(2,1)S(1)}, u32[]{:S(2)}, u32[]{:S(2)}) async-start(bf16[16,288,128]{2,1,0:T(8,128)(2,1)} %shard_map.64), calls=%async_computation | async-start | bytes 2359296 | tf_op jit(solution)/shard_map/all_to_all | solution.py:353
  10.4 7.3 %copy-start.7 = (s32[2]{0:T(128)S(1)}, s32[2]{0:T(128)}, u32[]{:S(2)}) copy-start(s32[2]{0:T(128)} %param.11) | copy-start | bytes 28
  13.7 22.3 %collective-permute-start.9 = (bf16[2,512,128]{2,1,0:T(8,128)(2,1)}, bf16[2,512,128]{2,1,0:T(8,128)(2,1)S(1)}, u32[]{:S(2)}, u32[]{:S(2)}) collective-permute-start(bf16[2,512,128]{2,1,0:T(8,128)(2,1)} %get-tuple-element.38), channel_id=1, source_target_pairs={{0,1},{1,0},{2,3},{3,2},{4,5},{5,4},{6,7},{7,6},{8,9},{9,8},{10,11... | collective-permute-start | bytes 786440 | tf_op jit(solution)/shard_map/ppermute | solution.py:368
  14.1 26.7 %collective-permute-start.10 = (bf16[2,512,128]{2,1,0:T(8,128)(2,1)}, bf16[2,512,128]{2,1,0:T(8,128)(2,1)S(1)}, u32[]{:S(2)}, u32[]{:S(2)}) collective-permute-start(bf16[2,512,128]{2,1,0:T(8,128)(2,1)} %get-tuple-element.39), channel_id=1, source_target_pairs={{0,2},{1,3},{2,0},{3,1},{4,6},{5,7},{6,4},{7,5},{8,10},{9,11},{10,... | collective-permute-start | bytes 786440 | tf_op jit(solution)/shard_map/ppermute | solution.py:368
  15.8 25.4 %collective-permute-start.11 = (bf16[2,512,128]{2,1,0:T(8,128)(2,1)}, bf16[2,512,128]{2,1,0:T(8,128)(2,1)S(1)}, u32[]{:S(2)}, u32[]{:S(2)}) collective-permute-start(bf16[2,512,128]{2,1,0:T(8,128)(2,1)} %get-tuple-element.40), channel_id=1, source_target_pairs={{0,3},{1,2},{2,1},{3,0},{4,7},{5,6},{6,5},{7,4},{8,11},{9,10},{10,... | collective-permute-start | bytes 786440 | tf_op jit(solution)/shard_map/ppermute | solution.py:368
  15.8 25.4 %collective-permute-start.12 = (bf16[2,512,128]{2,1,0:T(8,128)(2,1)}, bf16[2,512,128]{2,1,0:T(8,128)(2,1)S(1)}, u32[]{:S(2)}, u32[]{:S(2)}) collective-permute-start(bf16[2,512,128]{2,1,0:T(8,128)(2,1)} %get-tuple-element.41), channel_id=1, source_target_pairs={{0,4},{1,5},{2,6},{3,7},{4,0},{5,1},{6,2},{7,3},{8,12},{9,13},{10,... | collective-permute-start | bytes 786440 | tf_op jit(solution)/shard_map/ppermute | solution.py:368
  17.5 25.6 %collective-permute-start.13 = (bf16[2,512,128]{2,1,0:T(8,128)(2,1)}, bf16[2,512,128]{2,1,0:T(8,128)(2,1)S(1)}, u32[]{:S(2)}, u32[]{:S(2)}) collective-permute-start(bf16[2,512,128]{2,1,0:T(8,128)(2,1)} %get-tuple-element.42), channel_id=1, source_target_pairs={{0,5},{1,4},{2,7},{3,6},{4,1},{5,0},{6,3},{7,2},{8,13},{9,12},{10,... | collective-permute-start | bytes 786440 | tf_op jit(solution)/shard_map/ppermute | solution.py:368
  35.9 19.4 %copy-start.2 = (bf16[16,288,128]{2,1,0:T(8,128)(2,1)}, bf16[16,288,128]{2,1,0:T(8,128)(2,1)S(1)}, u32[]{:S(2)}) copy-start(bf16[16,288,128]{2,1,0:T(8,128)(2,1)S(1)} %all-to-all-done.refs_2_) | copy-start | bytes 3538948
  35.9 18.9 %collective-permute-start.7 = (bf16[2,512,128]{2,1,0:T(8,128)(2,1)}, bf16[2,512,128]{2,1,0:T(8,128)(2,1)S(1)}, u32[]{:S(2)}, u32[]{:S(2)}) collective-permute-start(bf16[2,512,128]{2,1,0:T(8,128)(2,1)} %get-tuple-element.35), channel_id=1, source_target_pairs={{0,6},{1,7},{2,4},{3,5},{4,2},{5,3},{6,0},{7,1},{8,14},{9,15},{10,... | collective-permute-start | bytes 786440 | tf_op jit(solution)/shard_map/ppermute | solution.py:368
  40.8 14.4 %collective-permute-start.8 = (bf16[2,512,128]{2,1,0:T(8,128)(2,1)}, bf16[2,512,128]{2,1,0:T(8,128)(2,1)S(1)}, u32[]{:S(2)}, u32[]{:S(2)}) collective-permute-start(bf16[2,512,128]{2,1,0:T(8,128)(2,1)} %get-tuple-element.36), channel_id=1, source_target_pairs={{0,7},{1,6},{2,5},{3,4},{4,3},{5,2},{6,1},{7,0},{8,15},{9,14},{10,... | collective-permute-start | bytes 786440 | tf_op jit(solution)/shard_map/ppermute | solution.py:368
  43.1 1.0 copy-start.6
  55.2 11.4 %copy-start = (bf16[2,512,8,128]{3,2,1,0:T(8,128)(2,1)S(1)}, bf16[2,512,8,128]{3,2,1,0:T(8,128)(2,1)}, u32[]{:S(2)}) copy-start(bf16[2,512,8,128]{3,2,1,0:T(8,128)(2,1)} %k_hbm.3) | copy-start | bytes 6291460
  62.6 42.8 %all-to-all-start.2 = ((bf16[16,136,128]{2,1,0:T(8,128)(2,1)}), bf16[16,136,128]{2,1,0:T(8,128)(2,1)S(1)}, u32[]{:S(2)}, u32[]{:S(2)}) async-start(bf16[16,136,128]{2,1,0:T(8,128)(2,1)} %copy-done.4), calls=%async_computation.2 | async-start | bytes 1114112 | tf_op jit(solution)/shard_map/all_to_all | solution.py:379
  66.7 1.6 %copy-start.1 = (bf16[2,512,8,128]{3,2,1,0:T(8,128)(2,1)S(1)}, bf16[2,512,8,128]{3,2,1,0:T(8,128)(2,1)}, u32[]{:S(2)}) copy-start(bf16[2,512,8,128]{3,2,1,0:T(8,128)(2,1)} %v_hbm.3) | copy-start | bytes 6291460
  68.3 21.1 %copy-start.3 = (bf16[16,288,128]{2,1,0:T(8,128)(2,1)S(1)}, bf16[16,288,128]{2,1,0:T(8,128)(2,1)}, u32[]{:S(2)}) copy-start(bf16[16,288,128]{2,1,0:T(8,128)(2,1)} %copy-done.2) | copy-start | bytes 3538948
  69.3 4.0 %collective-permute-start.2 = (bf16[2,512,128]{2,1,0:T(8,128)(2,1)S(1)}, bf16[2,512,128]{2,1,0:T(8,128)(2,1)S(1)}, u32[]{:S(2)}, u32[]{:S(2)}) collective-permute-start(bf16[2,512,128]{2,1,0:T(8,128)(2,1)S(1)} %get-tuple-element.28), channel_id=1, source_target_pairs={{0,1},{1,0},{2,3},{3,2},{4,5},{5,4},{6,7},{7,6},{8,9},{9,8},{10,11... | collective-permute-start | bytes 786440 | tf_op jit(solution)/shard_map/ppermute | solution.py:368
  69.8 12.1 %collective-permute-start.3 = (bf16[2,512,128]{2,1,0:T(8,128)(2,1)S(1)}, bf16[2,512,128]{2,1,0:T(8,128)(2,1)S(1)}, u32[]{:S(2)}, u32[]{:S(2)}) collective-permute-start(bf16[2,512,128]{2,1,0:T(8,128)(2,1)S(1)} %get-tuple-element.29), channel_id=1, source_target_pairs={{0,2},{1,3},{2,0},{3,1},{4,6},{5,7},{6,4},{7,5},{8,10},{9,11},{10,... | collective-permute-start | bytes 786440 | tf_op jit(solution)/shard_map/ppermute | solution.py:368
  71.4 15.3 %collective-permute-start.4 = (bf16[2,512,128]{2,1,0:T(8,128)(2,1)S(1)}, bf16[2,512,128]{2,1,0:T(8,128)(2,1)S(1)}, u32[]{:S(2)}, u32[]{:S(2)}) collective-permute-start(bf16[2,512,128]{2,1,0:T(8,128)(2,1)S(1)} %get-tuple-element.30), channel_id=1, source_target_pairs={{0,3},{1,2},{2,1},{3,0},{4,7},{5,6},{6,5},{7,4},{8,11},{9,10},{10,... | collective-permute-start | bytes 786440 | tf_op jit(solution)/shard_map/ppermute | solution.py:368
  71.4 15.3 %collective-permute-start.5 = (bf16[2,512,128]{2,1,0:T(8,128)(2,1)S(1)}, bf16[2,512,128]{2,1,0:T(8,128)(2,1)S(1)}, u32[]{:S(2)}, u32[]{:S(2)}) collective-permute-start(bf16[2,512,128]{2,1,0:T(8,128)(2,1)S(1)} %get-tuple-element.31), channel_id=1, source_target_pairs={{0,4},{1,5},{2,6},{3,7},{4,0},{5,1},{6,2},{7,3},{8,12},{9,13},{10,... | collective-permute-start | bytes 786440 | tf_op jit(solution)/shard_map/ppermute | solution.py:368
  73.2 16.2 %collective-permute-start.6 = (bf16[2,512,128]{2,1,0:T(8,128)(2,1)S(1)}, bf16[2,512,128]{2,1,0:T(8,128)(2,1)S(1)}, u32[]{:S(2)}, u32[]{:S(2)}) collective-permute-start(bf16[2,512,128]{2,1,0:T(8,128)(2,1)S(1)} %get-tuple-element.32), channel_id=1, source_target_pairs={{0,5},{1,4},{2,7},{3,6},{4,1},{5,0},{6,3},{7,2},{8,13},{9,12},{10,... | collective-permute-start | bytes 786440 | tf_op jit(solution)/shard_map/ppermute | solution.py:368
  73.3 27.1 %collective-permute-start = (bf16[2,512,128]{2,1,0:T(8,128)(2,1)S(1)}, bf16[2,512,128]{2,1,0:T(8,128)(2,1)S(1)}, u32[]{:S(2)}, u32[]{:S(2)}) collective-permute-start(bf16[2,512,128]{2,1,0:T(8,128)(2,1)S(1)} %get-tuple-element.25), channel_id=1, source_target_pairs={{0,6},{1,7},{2,4},{3,5},{4,2},{5,3},{6,0},{7,1},{8,14},{9,15},{10,... | collective-permute-start | bytes 786440 | tf_op jit(solution)/shard_map/ppermute | solution.py:368
  81.9 20.1 %collective-permute-start.1 = (bf16[2,512,128]{2,1,0:T(8,128)(2,1)S(1)}, bf16[2,512,128]{2,1,0:T(8,128)(2,1)S(1)}, u32[]{:S(2)}, u32[]{:S(2)}) collective-permute-start(bf16[2,512,128]{2,1,0:T(8,128)(2,1)S(1)} %get-tuple-element.26), channel_id=1, source_target_pairs={{0,7},{1,6},{2,5},{3,4},{4,3},{5,2},{6,1},{7,0},{8,15},{9,14},{10,... | collective-permute-start | bytes 786440 | tf_op jit(solution)/shard_map/ppermute | solution.py:368
  105.4 20.3 %all-to-all-start.1 = ((bf16[16,136,128]{2,1,0:T(8,128)(2,1)}), bf16[16,136,128]{2,1,0:T(8,128)(2,1)S(1)}, u32[]{:S(2)}, u32[]{:S(2)}) async-start(bf16[16,136,128]{2,1,0:T(8,128)(2,1)} %shard_map.67), calls=%async_computation.1 | async-start | bytes 1114112 | tf_op jit(solution)/shard_map/all_to_all | solution.py:379
  (1 other events, 0.8 us)

commit v11 on v10

--- a/solution.py
+++ b/solution.py
@@ -81,12 +81,12 @@
     if with_fresh:
         vals[:dim, slots:] = jnp.transpose(fv_ref[...])
     bias[...] = jnp.where(lax.broadcasted_iota(jnp.int32, bias.shape, 0) < last_valid, 0.0, NEG)
-    for copy in value_copies:
+    for copy in copies + value_copies:
         copy.wait()
-    for first in range(0, slots, block_slots):
-        vals[:dim, first : first + block_slots] = jnp.transpose(loaded[first : first + block_slots, :])
-    for copy in copies:
-        copy.wait()
+
+    def turn_values(count):
+        for first in range(0, count * chunk, block_slots):
+            vals[:dim, first : first + block_slots] = jnp.transpose(loaded[first : first + block_slots, :])
 
     def fold_max(scores, best):
         part = jnp.max(scores.reshape(-1, 8, tile), axis=0)
@@ -115,7 +115,7 @@
 
     def finish(t, top, acc):
         total = acc[dim : dim + 1, :]
-        out = acc[:dim, :] / total
+        out = (acc[:dim, :] * (1.0 / total)).astype(jnp.bfloat16)
         level = top * scale + jnp.log2(total)
         high = level.astype(jnp.bfloat16).astype(jnp.float32)
         mid = (level - high).astype(jnp.bfloat16).astype(jnp.float32)
@@ -123,7 +123,7 @@
         which = lax.broadcasted_iota(jnp.int32, (STAT_ROWS, tile), 0)
         stats = jnp.where(which == 0, high, jnp.where(which == 1, mid, low)).astype(jnp.bfloat16)
         for first in range(0, tile, dim):
-            flat = jnp.transpose(out[:, first : first + dim]).astype(jnp.bfloat16)
+            flat = jnp.transpose(out[:, first : first + dim])
             width = min(per_source, dim)
             for part in range(dim // width):
                 source = t * span + (first + part * width) // per_source
@@ -163,6 +163,7 @@
         @pl.when(filled == count)
         def _(count=count):
             stage(0, s0, m0, None, None, None, count)
+            turn_values(count)
 
             def pair(i, carry):
                 stage(2 * i + 1, s1, m1, 2 * i, s0, m0, count)
@@ -368,14 +369,13 @@
             moved.append(lax.ppermute(parts[k], "seq", [(i, i ^ k) for i in range(devices_seq)]))
         kv_blocks.append(moved)
 
-    early = kv_heads - 2
     place = jnp.stack([own, block]).astype(jnp.int32)
     out = None
     for r in range(requests):
         rows = (r * per_source, per_source, group_size)
         common = (cache_len[r : r + 1], place, head_q, kv_blocks[r])
-        state = attend(*common, tuple(range(early)), (head_fresh[0, r], head_fresh[1, r]), None, False, *rows)
-        part = attend(*common, tuple(range(early, kv_heads)), None, state, True, *rows)
+        fresh_r = (head_fresh[0, r], head_fresh[1, r])
+        part = attend(*common, tuple(range(kv_heads)), fresh_r, None, True, *rows)
         part = lax.all_to_all(part, "seq", split_axis=0, concat_axis=0, tiled=True)
         part = part.reshape(spread, kv_heads, per_source + STAT_ROWS, head_dim)
         out = merge(part, r, requests, local_rows, group_size, out)

time: 129 us -> 150 us (1.16)
  waiting for transfers between devices: 47.2 us -> 69.8 us
  local copies, waits for them, and re-layouts: 5.04 us -> 15.2 us
  Pallas kernels: 39.6 us -> 33.5 us
  starting transfers between devices: 34.1 us -> 28.8 us
    ppermute x14, waiting for transfers between devices: 16 us -> 50.2 us  [attention(): lax.ppermute(parts[k], 'seq', [(i, i ^ k) for i in range(devices_seq)])]
    all_to_all x1, waiting for transfers between devices: 17.6 us -> 6.05 us  [attention(): lax.all_to_all(pack(queries, fresh, devices_seq), 'seq', split_axis=0, co...]
    unnamed x16 -> x44, local copies, waits for them, and re-layouts: 4.39 us -> 14.6 us
    pallas_call x4 -> x2, Pallas kernels: 31.7 us -> 25.6 us  [attend(): pl.pallas_call(functools.partial(attend_kernel, order=order, blocks=len(k...]
    ppermute x14, starting transfers between devices: 17.1 us -> 14.1 us  [attention(): lax.ppermute(parts[k], 'seq', [(i, i ^ k) for i in range(devices_seq)])]
    all_to_all x2, starting transfers between devices: 9.61 us -> 7.35 us  [attention(): part = lax.all_to_all(part, 'seq', split_axis=0, concat_axis=0, tiled=True)]
  transfers between devices with their start and end apart: 17 -> 17, of which waited for: 8 -> 13; matrix products, arithmetic and copies ran while one was open for 1% -> 0% of each run, Pallas kernels for 24% -> 12%
where the time goes in v11:
time: 150 us; the launch traced here: 148 us
  waiting for transfers between devices  69.8 us (47%)
  Pallas kernels  33.5 us (22%)
  starting transfers between devices  28.8 us (19%)
  local copies, waits for them, and re-layouts  15.2 us (10%)
    ppermute x14, waiting for transfers between devices, attention(): lax.ppermute(parts[k], 'seq', [(i, i ^ k) for i in range(devices_seq)])  50.2 us
    pallas_call x2, Pallas kernels, attend(): pl.pallas_call(functools.partial(attend_kernel, order=order, blocks=len(k...  25.6 us
    unnamed x44, local copies, waits for them, and re-layouts  14.6 us
    ppermute x14, starting transfers between devices, attention(): lax.ppermute(parts[k], 'seq', [(i, i ^ k) for i in range(devices_seq)])  14.1 us
    all_to_all x2, waiting for transfers between devices, attention(): part = lax.all_to_all(part, 'seq', split_axis=0, concat_axis=0, tiled=True)  13.5 us
    all_to_all x1, starting transfers between devices, attention(): lax.all_to_all(pack(queries, fresh, devices_seq), 'seq', split_axis=0, co...  7.39 us
    all_to_all x2, starting transfers between devices, attention(): part = lax.all_to_all(part, 'seq', split_axis=0, concat_axis=0, tiled=True)  7.35 us
    all_to_all x1, waiting for transfers between devices, attention(): lax.all_to_all(pack(queries, fresh, devices_seq), 'seq', split_axis=0, co...  6.05 us
  transfers between devices with their start and end apart: 17, of which 13 were waited for; matrix products, arithmetic and copies ran while one was open for 0% of the time, Pallas kernels for 12%

profile of v11, /device:TPU:0, one launch (start us, length us, event | category | flops | bytes accessed | tf_op | source)
XLA Modules:
  0.0 148.4 jit_solution(15222031789853265339)
XLA Ops:
  3.0 7.4 %all-to-all-start = ((bf16[16,288,128]{2,1,0:T(8,128)(2,1)}), bf16[16,288,128]{2,1,0:T(8,128)(2,1)S(1)}, u32[]{:S(2)}, u32[]{:S(2)}) async-start(bf16[16,288,128]{2,1,0:T(8,128)(2,1)} %shard_map.64), calls=%async_computation | async-start | bytes 2359296 | tf_op jit(solution)/shard_map/all_to_all | solution.py:354
  10.4 3.3 %shard_map.67 = (bf16[2,512,128]{2,1,0:T(8,128)(2,1)}, bf16[2,512,128]{2,1,0:T(8,128)(2,1)}, bf16[2,512,128]{2,1,0:T(8,128)(2,1)}, bf16[2,512,128]{2,1,0:T(8,128...) custom-call(s32[1]{0:T(128)} %bitcast.own_ref, ...), custom_call_target="tpu_custom_call" | custom-call | tf_op jit(solution)/shard_map/pallas_call | solution.py:326
  14.1 1.6 %collective-permute-start.8 = (bf16[2,512,128]{2,1,0:T(8,128)(2,1)}, bf16[2,512,128]{2,1,0:T(8,128)(2,1)S(1)}, u32[]{:S(2)}, u32[]{:S(2)}) collective-permute-start(bf16[2,512,128]{2,1,0:T(8,128)(2,1)} %get-tuple-element.31), channel_id=1, source_target_pairs={{0,2},{1,3},{2,0},{3,1},{4,6},{5,7},{6,4},{7,5},{8,10},{9,11},{10,... | collective-permute-start | bytes 786440 | tf_op jit(solution)/shard_map/ppermute | solution.py:369
  15.8 1.7 %collective-permute-start.10 = (bf16[2,512,128]{2,1,0:T(8,128)(2,1)}, bf16[2,512,128]{2,1,0:T(8,128)(2,1)S(1)}, u32[]{:S(2)}, u32[]{:S(2)}) collective-permute-start(bf16[2,512,128]{2,1,0:T(8,128)(2,1)} %get-tuple-element.33), channel_id=1, source_target_pairs={{0,4},{1,5},{2,6},{3,7},{4,0},{5,1},{6,2},{7,3},{8,12},{9,13},{10,... | collective-permute-start | bytes 786440 | tf_op jit(solution)/shard_map/ppermute | solution.py:369
  18.2 2.5 %collective-permute-start.12 = (bf16[2,512,128]{2,1,0:T(8,128)(2,1)}, bf16[2,512,128]{2,1,0:T(8,128)(2,1)S(1)}, u32[]{:S(2)}, u32[]{:S(2)}) collective-permute-start(bf16[2,512,128]{2,1,0:T(8,128)(2,1)} %get-tuple-element.35), channel_id=1, source_target_pairs={{0,6},{1,7},{2,4},{3,5},{4,2},{5,3},{6,0},{7,1},{8,14},{9,15},{10,... | collective-permute-start | bytes 786440 | tf_op jit(solution)/shard_map/ppermute | solution.py:369
  20.7 9.0 %collective-permute-done.8.refs_5_ = bf16[2,512,128]{2,1,0:T(8,128)(2,1)S(1)} collective-permute-done((bf16[2,512,128]{2,1,0:T(8,128)(2,1)}, bf16[2,512,128]{2,1,0:T(8,128)(2,1)S(1)}, u32[]{:S(2)}, u32[]{:S(2)}) %collective-permute-start.8) | collective-permute-done | bytes 262176 | tf_op jit(solution)/shard_map/ppermute | solution.py:369
  29.8 6.1 %all-to-all-done.refs_2_ = bf16[16,288,128]{2,1,0:T(8,128)(2,1)S(1)} async-done(((bf16[16,288,128]{2,1,0:T(8,128)(2,1)}), bf16[16,288,128]{2,1,0:T(8,128)(2,1)S(1)}, u32[]{:S(2)}, u32[]{:S(2)}) %all-to-all-start) | async-done | bytes 1179680 | tf_op jit(solution)/shard_map/all_to_all | solution.py:354
  39.3 3.8 %collective-permute-done.11.refs_8_ = bf16[2,512,128]{2,1,0:T(8,128)(2,1)S(1)} collective-permute-done((bf16[2,512,128]{2,1,0:T(8,128)(2,1)}, bf16[2,512,128]{2,1,0:T(8,128)(2,1)S(1)}, u32[]{:S(2)}, u32[]{:S(2)}) %collective-permute-start.11) | collective-permute-done | bytes 262176 | tf_op jit(solution)/shard_map/ppermute | solution.py:369
  43.8 7.0 %collective-permute-done.12.refs_9_ = bf16[2,512,128]{2,1,0:T(8,128)(2,1)S(1)} collective-permute-done((bf16[2,512,128]{2,1,0:T(8,128)(2,1)}, bf16[2,512,128]{2,1,0:T(8,128)(2,1)S(1)}, u32[]{:S(2)}, u32[]{:S(2)}) %collective-permute-start.12) | collective-permute-done | bytes 262176 | tf_op jit(solution)/shard_map/ppermute | solution.py:369
  51.5 3.8 %collective-permute-done.13.refs_10_ = bf16[2,512,128]{2,1,0:T(8,128)(2,1)S(1)} collective-permute-done((bf16[2,512,128]{2,1,0:T(8,128)(2,1)}, bf16[2,512,128]{2,1,0:T(8,128)(2,1)S(1)}, u32[]{:S(2)}, u32[]{:S(2)}) %collective-permute-start.13) | collective-permute-done | bytes 262176 | tf_op jit(solution)/shard_map/ppermute | solution.py:369
  63.6 13.4 %shard_map.68 = bf16[16,136,128]{2,1,0:T(8,128)(2,1)S(1)} custom-call(s32[1]{0:T(128)} %get-tuple-element.41.refs_0_, s32[2]{0:T(128)S(1)} %pad_add_fusion.refs_1_, bf16[16,288,128]{2,1,0:T(8,128)(2,1)S(1)} %all-to-all-done.refs_2_, bf16[2,512,128]{2,1,0:T(8,128)(2,1)S(1)} %copy-done.6, bf16[2,512,128]{2,1,0:T(8,128)(2,1)S(1)} %copy-done.8, ...), custom_call_target="tpu_custom_call" | custom-call | flops 4294967296 | bytes 3145728 | tf_op jit(solution)/shard_map/pallas_call | solution.py:221
  77.8 3.8 %all-to-all-start.2 = ((bf16[16,136,128]{2,1,0:T(8,128)(2,1)}), bf16[16,136,128]{2,1,0:T(8,128)(2,1)S(1)}, u32[]{:S(2)}, u32[]{:S(2)}) async-start(bf16[16,136,128]{2,1,0:T(8,128)(2,1)} %copy-done.4), calls=%async_computation.2 | async-start | bytes 1114112 | tf_op jit(solution)/shard_map/all_to_all | solution.py:379
  81.6 1.6 %copy-done.1 = bf16[2,512,8,128]{3,2,1,0:T(8,128)(2,1)S(1)} copy-done((bf16[2,512,8,128]{3,2,1,0:T(8,128)(2,1)S(1)}, bf16[2,512,8,128]{3,2,1,0:T(8,128)(2,1)}, u32[]{:S(2)}) %copy-start.1) | copy-done | bytes 2097176
  84.5 1.5 collective-permute-start.1
  86.1 1.6 %collective-permute-start.3 = (bf16[2,512,128]{2,1,0:T(8,128)(2,1)S(1)}, bf16[2,512,128]{2,1,0:T(8,128)(2,1)S(1)}, u32[]{:S(2)}, u32[]{:S(2)}) collective-permute-start(bf16[2,512,128]{2,1,0:T(8,128)(2,1)S(1)} %get-tuple-element.25), channel_id=1, source_target_pairs={{0,4},{1,5},{2,6},{3,7},{4,0},{5,1},{6,2},{7,3},{8,12},{9,13},{10,... | collective-permute-start | bytes 786440 | tf_op jit(solution)/shard_map/ppermute | solution.py:369
  88.0 2.4 %collective-permute-start.5 = (bf16[2,512,128]{2,1,0:T(8,128)(2,1)S(1)}, bf16[2,512,128]{2,1,0:T(8,128)(2,1)S(1)}, u32[]{:S(2)}, u32[]{:S(2)}) collective-permute-start(bf16[2,512,128]{2,1,0:T(8,128)(2,1)S(1)} %get-tuple-element.27), channel_id=1, source_target_pairs={{0,6},{1,7},{2,4},{3,5},{4,2},{5,3},{6,0},{7,1},{8,14},{9,15},{10,... | collective-permute-start | bytes 786440 | tf_op jit(solution)/shard_map/ppermute | solution.py:369
  90.4 6.2 %collective-permute-done.1.refs_5_ = bf16[2,512,128]{2,1,0:T(8,128)(2,1)S(1)} collective-permute-done((bf16[2,512,128]{2,1,0:T(8,128)(2,1)S(1)}, bf16[2,512,128]{2,1,0:T(8,128)(2,1)S(1)}, u32[]{:S(2)}, u32[]{:S(2)}) %collective-permute-start.1) | collective-permute-done | bytes 262176 | tf_op jit(solution)/shard_map/ppermute | solution.py:369
  97.9 3.4 %collective-permute-done.2.refs_6_ = bf16[2,512,128]{2,1,0:T(8,128)(2,1)S(1)} collective-permute-done((bf16[2,512,128]{2,1,0:T(8,128)(2,1)S(1)}, bf16[2,512,128]{2,1,0:T(8,128)(2,1)S(1)}, u32[]{:S(2)}, u32[]{:S(2)}) %collective-permute-start.2) | collective-permute-done | bytes 262176 | tf_op jit(solution)/shard_map/ppermute | solution.py:369
  101.3 2.6 %collective-permute-done.4.refs_8_ = bf16[2,512,128]{2,1,0:T(8,128)(2,1)S(1)} collective-permute-done((bf16[2,512,128]{2,1,0:T(8,128)(2,1)S(1)}, bf16[2,512,128]{2,1,0:T(8,128)(2,1)S(1)}, u32[]{:S(2)}, u32[]{:S(2)}) %collective-permute-start.4) | collective-permute-done | bytes 262176 | tf_op jit(solution)/shard_map/ppermute | solution.py:369
  104.0 7.3 %collective-permute-done.5.refs_9_ = bf16[2,512,128]{2,1,0:T(8,128)(2,1)S(1)} collective-permute-done((bf16[2,512,128]{2,1,0:T(8,128)(2,1)S(1)}, bf16[2,512,128]{2,1,0:T(8,128)(2,1)S(1)}, u32[]{:S(2)}, u32[]{:S(2)}) %collective-permute-start.5) | collective-permute-done | bytes 262176 | tf_op jit(solution)/shard_map/ppermute | solution.py:369
  111.2 5.3 %collective-permute-done.6.refs_10_ = bf16[2,512,128]{2,1,0:T(8,128)(2,1)S(1)} collective-permute-done((bf16[2,512,128]{2,1,0:T(8,128)(2,1)S(1)}, bf16[2,512,128]{2,1,0:T(8,128)(2,1)S(1)}, u32[]{:S(2)}, u32[]{:S(2)}) %collective-permute-start.6) | collective-permute-done | bytes 262176 | tf_op jit(solution)/shard_map/ppermute | solution.py:369
  116.5 12.2 %shard_map.66 = bf16[16,136,128]{2,1,0:T(8,128)(2,1)} custom-call(s32[1]{0:T(128)} %get-tuple-element.42.refs_0_, s32[2]{0:T(128)S(1)} %pad_add_fusion.refs_1_, bf16[16,288,128]{2,1,0:T(8,128)(2,1)S(1)} %copy-done.3, bf16[2,512,128]{2,1,0:T(8,128)(2,1)S(1)} %get-tuple-element.21.refs_3_, bf16[2,512,128]{2,1,0:T(8,128)(2,1)S(1)} %collective-permute-done.refs_4_, ...), custom_call_target="tpu_custom_call" | custom-call | flops 4294967296 | bytes 3145728 | tf_op jit(solution)/shard_map/pallas_call | solution.py:221
  128.8 3.6 %all-to-all-start.1 = ((bf16[16,136,128]{2,1,0:T(8,128)(2,1)}), bf16[16,136,128]{2,1,0:T(8,128)(2,1)S(1)}, u32[]{:S(2)}, u32[]{:S(2)}) async-start(bf16[16,136,128]{2,1,0:T(8,128)(2,1)} %shard_map.66), calls=%async_computation.1 | async-start | bytes 1114112 | tf_op jit(solution)/shard_map/all_to_all | solution.py:379
  133.6 13.5 %all-to-all-done.1 = bf16[16,136,128]{2,1,0:T(8,128)(2,1)S(1)} async-done(((bf16[16,136,128]{2,1,0:T(8,128)(2,1)}), bf16[16,136,128]{2,1,0:T(8,128)(2,1)S(1)}, u32[]{:S(2)}, u32[]{:S(2)}) %all-to-all-start.1) | async-done | bytes 557088 | tf_op jit(solution)/shard_map/all_to_all | solution.py:379
  (68 shorter events, 23.8 us)
Async XLA Ops:
  3.0 32.9 %all-to-all-start = ((bf16[16,288,128]{2,1,0:T(8,128)(2,1)}), bf16[16,288,128]{2,1,0:T(8,128)(2,1)S(1)}, u32[]{:S(2)}, u32[]{:S(2)}) async-start(bf16[16,288,128]{2,1,0:T(8,128)(2,1)} %shard_map.64), calls=%async_computation | async-start | bytes 2359296 | tf_op jit(solution)/shard_map/all_to_all | solution.py:354
  10.4 7.3 %copy-start.21 = (s32[2]{0:T(128)S(1)}, s32[2]{0:T(128)}, u32[]{:S(2)}) copy-start(s32[2]{0:T(128)} %param.11) | copy-start | bytes 28
  13.7 4.5 %collective-permute-start.7 = (bf16[2,512,128]{2,1,0:T(8,128)(2,1)}, bf16[2,512,128]{2,1,0:T(8,128)(2,1)S(1)}, u32[]{:S(2)}, u32[]{:S(2)}) collective-permute-start(bf16[2,512,128]{2,1,0:T(8,128)(2,1)} %get-tuple-element.30), channel_id=1, source_target_pairs={{0,1},{1,0},{2,3},{3,2},{4,5},{5,4},{6,7},{7,6},{8,9},{9,8},{10,11... | collective-permute-start | bytes 786440 | tf_op jit(solution)/shard_map/ppermute | solution.py:369
  14.1 15.6 %collective-permute-start.8 = (bf16[2,512,128]{2,1,0:T(8,128)(2,1)}, bf16[2,512,128]{2,1,0:T(8,128)(2,1)S(1)}, u32[]{:S(2)}, u32[]{:S(2)}) collective-permute-start(bf16[2,512,128]{2,1,0:T(8,128)(2,1)} %get-tuple-element.31), channel_id=1, source_target_pairs={{0,2},{1,3},{2,0},{3,1},{4,6},{5,7},{6,4},{7,5},{8,10},{9,11},{10,... | collective-permute-start | bytes 786440 | tf_op jit(solution)/shard_map/ppermute | solution.py:369
  15.8 21.1 %collective-permute-start.9 = (bf16[2,512,128]{2,1,0:T(8,128)(2,1)}, bf16[2,512,128]{2,1,0:T(8,128)(2,1)S(1)}, u32[]{:S(2)}, u32[]{:S(2)}) collective-permute-start(bf16[2,512,128]{2,1,0:T(8,128)(2,1)} %get-tuple-element.32), channel_id=1, source_target_pairs={{0,3},{1,2},{2,1},{3,0},{4,7},{5,6},{6,5},{7,4},{8,11},{9,10},{10,... | collective-permute-start | bytes 786440 | tf_op jit(solution)/shard_map/ppermute | solution.py:369
  15.8 22.8 %collective-permute-start.10 = (bf16[2,512,128]{2,1,0:T(8,128)(2,1)}, bf16[2,512,128]{2,1,0:T(8,128)(2,1)S(1)}, u32[]{:S(2)}, u32[]{:S(2)}) collective-permute-start(bf16[2,512,128]{2,1,0:T(8,128)(2,1)} %get-tuple-element.33), channel_id=1, source_target_pairs={{0,4},{1,5},{2,6},{3,7},{4,0},{5,1},{6,2},{7,3},{8,12},{9,13},{10,... | collective-permute-start | bytes 786440 | tf_op jit(solution)/shard_map/ppermute | solution.py:369
  17.5 25.6 %collective-permute-start.11 = (bf16[2,512,128]{2,1,0:T(8,128)(2,1)}, bf16[2,512,128]{2,1,0:T(8,128)(2,1)S(1)}, u32[]{:S(2)}, u32[]{:S(2)}) collective-permute-start(bf16[2,512,128]{2,1,0:T(8,128)(2,1)} %get-tuple-element.34), channel_id=1, source_target_pairs={{0,5},{1,4},{2,7},{3,6},{4,1},{5,0},{6,3},{7,2},{8,13},{9,12},{10,... | collective-permute-start | bytes 786440 | tf_op jit(solution)/shard_map/ppermute | solution.py:369
  18.2 37.7 %copy-start.7 = (bf16[2,512,128]{2,1,0:T(8,128)(2,1)}, bf16[2,512,128]{2,1,0:T(8,128)(2,1)S(1)}, u32[]{:S(2)}) copy-start(bf16[2,512,128]{2,1,0:T(8,128)(2,1)S(1)} %collective-permute-done.7.refs_4_) | copy-start | bytes 786436
  18.2 32.6 %collective-permute-start.12 = (bf16[2,512,128]{2,1,0:T(8,128)(2,1)}, bf16[2,512,128]{2,1,0:T(8,128)(2,1)S(1)}, u32[]{:S(2)}, u32[]{:S(2)}) collective-permute-start(bf16[2,512,128]{2,1,0:T(8,128)(2,1)} %get-tuple-element.35), channel_id=1, source_target_pairs={{0,6},{1,7},{2,4},{3,5},{4,2},{5,3},{6,0},{7,1},{8,14},{9,15},{10,... | collective-permute-start | bytes 786440 | tf_op jit(solution)/shard_map/ppermute | solution.py:369
  29.7 26.2 %copy-start.9 = (bf16[2,512,128]{2,1,0:T(8,128)(2,1)}, bf16[2,512,128]{2,1,0:T(8,128)(2,1)S(1)}, u32[]{:S(2)}) copy-start(bf16[2,512,128]{2,1,0:T(8,128)(2,1)S(1)} %collective-permute-done.8.refs_5_) | copy-start | bytes 786436
  29.7 25.5 %collective-permute-start.13 = (bf16[2,512,128]{2,1,0:T(8,128)(2,1)}, bf16[2,512,128]{2,1,0:T(8,128)(2,1)S(1)}, u32[]{:S(2)}, u32[]{:S(2)}) collective-permute-start(bf16[2,512,128]{2,1,0:T(8,128)(2,1)} %get-tuple-element.36), channel_id=1, source_target_pairs={{0,7},{1,6},{2,5},{3,4},{4,3},{5,2},{6,1},{7,0},{8,15},{9,14},{10,... | collective-permute-start | bytes 786440 | tf_op jit(solution)/shard_map/ppermute | solution.py:369
  35.9 41.1 %copy-start.2 = (bf16[16,288,128]{2,1,0:T(8,128)(2,1)}, bf16[16,288,128]{2,1,0:T(8,128)(2,1)S(1)}, u32[]{:S(2)}) copy-start(bf16[16,288,128]{2,1,0:T(8,128)(2,1)S(1)} %all-to-all-done.refs_2_) | copy-start | bytes 3538948
  63.6 18.0 %copy-start = (bf16[2,512,8,128]{3,2,1,0:T(8,128)(2,1)S(1)}, bf16[2,512,8,128]{3,2,1,0:T(8,128)(2,1)}, u32[]{:S(2)}) copy-start(bf16[2,512,8,128]{3,2,1,0:T(8,128)(2,1)} %k_hbm.3) | copy-start | bytes 6291460
  77.8 51.0 %all-to-all-start.2 = ((bf16[16,136,128]{2,1,0:T(8,128)(2,1)}), bf16[16,136,128]{2,1,0:T(8,128)(2,1)S(1)}, u32[]{:S(2)}, u32[]{:S(2)}) async-start(bf16[16,136,128]{2,1,0:T(8,128)(2,1)} %copy-done.4), calls=%async_computation.2 | async-start | bytes 1114112 | tf_op jit(solution)/shard_map/all_to_all | solution.py:379
  81.5 1.6 %copy-start.1 = (bf16[2,512,8,128]{3,2,1,0:T(8,128)(2,1)S(1)}, bf16[2,512,8,128]{3,2,1,0:T(8,128)(2,1)}, u32[]{:S(2)}) copy-start(bf16[2,512,8,128]{3,2,1,0:T(8,128)(2,1)} %v_hbm.3) | copy-start | bytes 6291460
  83.1 33.4 %copy-start.3 = (bf16[16,288,128]{2,1,0:T(8,128)(2,1)S(1)}, bf16[16,288,128]{2,1,0:T(8,128)(2,1)}, u32[]{:S(2)}) copy-start(bf16[16,288,128]{2,1,0:T(8,128)(2,1)} %copy-done.2) | copy-start | bytes 3538948
  84.2 3.9 %collective-permute-start = (bf16[2,512,128]{2,1,0:T(8,128)(2,1)S(1)}, bf16[2,512,128]{2,1,0:T(8,128)(2,1)S(1)}, u32[]{:S(2)}, u32[]{:S(2)}) collective-permute-start(bf16[2,512,128]{2,1,0:T(8,128)(2,1)S(1)} %get-tuple-element.22), channel_id=1, source_target_pairs={{0,1},{1,0},{2,3},{3,2},{4,5},{5,4},{6,7},{7,6},{8,9},{9,8},{10,11... | collective-permute-start | bytes 786440 | tf_op jit(solution)/shard_map/ppermute | solution.py:369
  84.5 12.0 %collective-permute-start.1 = (bf16[2,512,128]{2,1,0:T(8,128)(2,1)S(1)}, bf16[2,512,128]{2,1,0:T(8,128)(2,1)S(1)}, u32[]{:S(2)}, u32[]{:S(2)}) collective-permute-start(bf16[2,512,128]{2,1,0:T(8,128)(2,1)S(1)} %get-tuple-element.23), channel_id=1, source_target_pairs={{0,2},{1,3},{2,0},{3,1},{4,6},{5,7},{6,4},{7,5},{8,10},{9,11},{10,... | collective-permute-start | bytes 786440 | tf_op jit(solution)/shard_map/ppermute | solution.py:369
  86.0 15.3 %collective-permute-start.2 = (bf16[2,512,128]{2,1,0:T(8,128)(2,1)S(1)}, bf16[2,512,128]{2,1,0:T(8,128)(2,1)S(1)}, u32[]{:S(2)}, u32[]{:S(2)}) collective-permute-start(bf16[2,512,128]{2,1,0:T(8,128)(2,1)S(1)} %get-tuple-element.24), channel_id=1, source_target_pairs={{0,3},{1,2},{2,1},{3,0},{4,7},{5,6},{6,5},{7,4},{8,11},{9,10},{10,... | collective-permute-start | bytes 786440 | tf_op jit(solution)/shard_map/ppermute | solution.py:369
  86.1 15.2 %collective-permute-start.3 = (bf16[2,512,128]{2,1,0:T(8,128)(2,1)S(1)}, bf16[2,512,128]{2,1,0:T(8,128)(2,1)S(1)}, u32[]{:S(2)}, u32[]{:S(2)}) collective-permute-start(bf16[2,512,128]{2,1,0:T(8,128)(2,1)S(1)} %get-tuple-element.25), channel_id=1, source_target_pairs={{0,4},{1,5},{2,6},{3,7},{4,0},{5,1},{6,2},{7,3},{8,12},{9,13},{10,... | collective-permute-start | bytes 786440 | tf_op jit(solution)/shard_map/ppermute | solution.py:369
  87.7 16.2 %collective-permute-start.4 = (bf16[2,512,128]{2,1,0:T(8,128)(2,1)S(1)}, bf16[2,512,128]{2,1,0:T(8,128)(2,1)S(1)}, u32[]{:S(2)}, u32[]{:S(2)}) collective-permute-start(bf16[2,512,128]{2,1,0:T(8,128)(2,1)S(1)} %get-tuple-element.26), channel_id=1, source_target_pairs={{0,5},{1,4},{2,7},{3,6},{4,1},{5,0},{6,3},{7,2},{8,13},{9,12},{10,... | collective-permute-start | bytes 786440 | tf_op jit(solution)/shard_map/ppermute | solution.py:369
  88.0 23.2 %collective-permute-start.5 = (bf16[2,512,128]{2,1,0:T(8,128)(2,1)S(1)}, bf16[2,512,128]{2,1,0:T(8,128)(2,1)S(1)}, u32[]{:S(2)}, u32[]{:S(2)}) collective-permute-start(bf16[2,512,128]{2,1,0:T(8,128)(2,1)S(1)} %get-tuple-element.27), channel_id=1, source_target_pairs={{0,6},{1,7},{2,4},{3,5},{4,2},{5,3},{6,0},{7,1},{8,14},{9,15},{10,... | collective-permute-start | bytes 786440 | tf_op jit(solution)/shard_map/ppermute | solution.py:369
  96.6 20.0 %collective-permute-start.6 = (bf16[2,512,128]{2,1,0:T(8,128)(2,1)S(1)}, bf16[2,512,128]{2,1,0:T(8,128)(2,1)S(1)}, u32[]{:S(2)}, u32[]{:S(2)}) collective-permute-start(bf16[2,512,128]{2,1,0:T(8,128)(2,1)S(1)} %get-tuple-element.28), channel_id=1, source_target_pairs={{0,7},{1,6},{2,5},{3,4},{4,3},{5,2},{6,1},{7,0},{8,15},{9,14},{10,... | collective-permute-start | bytes 786440 | tf_op jit(solution)/shard_map/ppermute | solution.py:369
  128.8 18.4 %all-to-all-start.1 = ((bf16[16,136,128]{2,1,0:T(8,128)(2,1)}), bf16[16,136,128]{2,1,0:T(8,128)(2,1)S(1)}, u32[]{:S(2)}, u32[]{:S(2)}) async-start(bf16[16,136,128]{2,1,0:T(8,128)(2,1)} %shard_map.66), calls=%async_computation.1 | async-start | bytes 1114112 | tf_op jit(solution)/shard_map/all_to_all | solution.py:379
  (15 other events, 13.0 us)

commit v12 on v11

--- a/solution.py
+++ b/solution.py
@@ -375,7 +375,12 @@
         rows = (r * per_source, per_source, group_size)
         common = (cache_len[r : r + 1], place, head_q, kv_blocks[r])
         fresh_r = (head_fresh[0, r], head_fresh[1, r])
-        part = attend(*common, tuple(range(kv_heads)), fresh_r, None, True, *rows)
+        state, first = None, 0
+        if r == requests - 1:
+            first = kv_heads - 2
+            state = attend(*common, tuple(range(first)), fresh_r, None, False, *rows)
+            fresh_r = None
+        part = attend(*common, tuple(range(first, kv_heads)), fresh_r, state, True, *rows)
         part = lax.all_to_all(part, "seq", split_axis=0, concat_axis=0, tiled=True)
         part = part.reshape(spread, kv_heads, per_source + STAT_ROWS, head_dim)
         out = merge(part, r, requests, local_rows, group_size, out)

time: 150 us -> 143 us (0.953)
  waiting for transfers between devices: 69.8 us -> 59.2 us
  starting transfers between devices: 28.8 us -> 30.6 us
  Pallas kernels: 33.5 us -> 35.1 us
    ppermute x14, waiting for transfers between devices: 50.2 us -> 39.6 us  [attention(): lax.ppermute(parts[k], 'seq', [(i, i ^ k) for i in range(devices_seq)])]
    all_to_all x2, starting transfers between devices: 7.35 us -> 9.09 us  [attention(): part = lax.all_to_all(part, 'seq', split_axis=0, concat_axis=0, tiled=True)]
    pallas_call x2 -> x3, Pallas kernels: 25.6 us -> 27.1 us  [attend(): pl.pallas_call(functools.partial(attend_kernel, order=order, blocks=len(k...]
  transfers between devices with their start and end apart: 17 -> 17, of which waited for: 13 -> 12; matrix products, arithmetic and copies ran while one was open for 0% -> 1% of each run, Pallas kernels for 12% -> 14%
where the time goes in v12:
time: 143 us; the launch traced here: 141 us
  waiting for transfers between devices  59.2 us (41%)
  Pallas kernels  35.1 us (25%)
  starting transfers between devices  30.6 us (21%)
  local copies, waits for them, and re-layouts  15.3 us (11%)
    ppermute x14, waiting for transfers between devices, attention(): lax.ppermute(parts[k], 'seq', [(i, i ^ k) for i in range(devices_seq)])  39.6 us
    pallas_call x3, Pallas kernels, attend(): pl.pallas_call(functools.partial(attend_kernel, order=order, blocks=len(k...  27.1 us
    unnamed x44, local copies, waits for them, and re-layouts  14.6 us
    ppermute x14, starting transfers between devices, attention(): lax.ppermute(parts[k], 'seq', [(i, i ^ k) for i in range(devices_seq)])  14.1 us
    all_to_all x2, waiting for transfers between devices, attention(): part = lax.all_to_all(part, 'seq', split_axis=0, concat_axis=0, tiled=True)  13.5 us
    all_to_all x2, starting transfers between devices, attention(): part = lax.all_to_all(part, 'seq', split_axis=0, concat_axis=0, tiled=True)  9.09 us
    all_to_all x1, starting transfers between devices, attention(): lax.all_to_all(pack(queries, fresh, devices_seq), 'seq', split_axis=0, co...  7.39 us
    all_to_all x1, waiting for transfers between devices, attention(): lax.all_to_all(pack(queries, fresh, devices_seq), 'seq', split_axis=0, co...  6.05 us
  transfers between devices with their start and end apart: 17, of which 12 were waited for; matrix products, arithmetic and copies ran while one was open for 1% of the time, Pallas kernels for 14%

profile of v12, /device:TPU:0, one launch (start us, length us, event | category | flops | bytes accessed | tf_op | source)
XLA Modules:
  0.0 141.2 jit_solution(9787052962534025366)
XLA Ops:
  3.0 7.4 %all-to-all-start = ((bf16[16,288,128]{2,1,0:T(8,128)(2,1)}), bf16[16,288,128]{2,1,0:T(8,128)(2,1)S(1)}, u32[]{:S(2)}, u32[]{:S(2)}) async-start(bf16[16,288,128]{2,1,0:T(8,128)(2,1)} %shard_map.64), calls=%async_computation | async-start | bytes 2359296 | tf_op jit(solution)/shard_map/all_to_all | solution.py:354
  10.4 3.3 %shard_map.68 = (bf16[2,512,128]{2,1,0:T(8,128)(2,1)}, bf16[2,512,128]{2,1,0:T(8,128)(2,1)}, bf16[2,512,128]{2,1,0:T(8,128)(2,1)}, bf16[2,512,128]{2,1,0:T(8,128...) custom-call(s32[1]{0:T(128)} %bitcast.own_ref, ...), custom_call_target="tpu_custom_call" | custom-call | tf_op jit(solution)/shard_map/pallas_call | solution.py:326
  14.1 1.6 %collective-permute-start.8 = (bf16[2,512,128]{2,1,0:T(8,128)(2,1)}, bf16[2,512,128]{2,1,0:T(8,128)(2,1)S(1)}, u32[]{:S(2)}, u32[]{:S(2)}) collective-permute-start(bf16[2,512,128]{2,1,0:T(8,128)(2,1)} %get-tuple-element.35), channel_id=1, source_target_pairs={{0,2},{1,3},{2,0},{3,1},{4,6},{5,7},{6,4},{7,5},{8,10},{9,11},{10,... | collective-permute-start | bytes 786440 | tf_op jit(solution)/shard_map/ppermute | solution.py:369
  15.8 1.7 %collective-permute-start.10 = (bf16[2,512,128]{2,1,0:T(8,128)(2,1)}, bf16[2,512,128]{2,1,0:T(8,128)(2,1)S(1)}, u32[]{:S(2)}, u32[]{:S(2)}) collective-permute-start(bf16[2,512,128]{2,1,0:T(8,128)(2,1)} %get-tuple-element.37), channel_id=1, source_target_pairs={{0,4},{1,5},{2,6},{3,7},{4,0},{5,1},{6,2},{7,3},{8,12},{9,13},{10,... | collective-permute-start | bytes 786440 | tf_op jit(solution)/shard_map/ppermute | solution.py:369
  18.3 2.5 %collective-permute-start.12 = (bf16[2,512,128]{2,1,0:T(8,128)(2,1)}, bf16[2,512,128]{2,1,0:T(8,128)(2,1)S(1)}, u32[]{:S(2)}, u32[]{:S(2)}) collective-permute-start(bf16[2,512,128]{2,1,0:T(8,128)(2,1)} %get-tuple-element.39), channel_id=1, source_target_pairs={{0,6},{1,7},{2,4},{3,5},{4,2},{5,3},{6,0},{7,1},{8,14},{9,15},{10,... | collective-permute-start | bytes 786440 | tf_op jit(solution)/shard_map/ppermute | solution.py:369
  20.8 8.9 %collective-permute-done.8.refs_5_ = bf16[2,512,128]{2,1,0:T(8,128)(2,1)S(1)} collective-permute-done((bf16[2,512,128]{2,1,0:T(8,128)(2,1)}, bf16[2,512,128]{2,1,0:T(8,128)(2,1)S(1)}, u32[]{:S(2)}, u32[]{:S(2)}) %collective-permute-start.8) | collective-permute-done | bytes 262176 | tf_op jit(solution)/shard_map/ppermute | solution.py:369
  29.8 6.1 %all-to-all-done.refs_2_ = bf16[16,288,128]{2,1,0:T(8,128)(2,1)S(1)} async-done(((bf16[16,288,128]{2,1,0:T(8,128)(2,1)}), bf16[16,288,128]{2,1,0:T(8,128)(2,1)S(1)}, u32[]{:S(2)}, u32[]{:S(2)}) %all-to-all-start) | async-done | bytes 1179680 | tf_op jit(solution)/shard_map/all_to_all | solution.py:354
  39.3 3.8 %collective-permute-done.11.refs_8_ = bf16[2,512,128]{2,1,0:T(8,128)(2,1)S(1)} collective-permute-done((bf16[2,512,128]{2,1,0:T(8,128)(2,1)}, bf16[2,512,128]{2,1,0:T(8,128)(2,1)S(1)}, u32[]{:S(2)}, u32[]{:S(2)}) %collective-permute-start.11) | collective-permute-done | bytes 262176 | tf_op jit(solution)/shard_map/ppermute | solution.py:369
  43.8 7.0 %collective-permute-done.12.refs_9_ = bf16[2,512,128]{2,1,0:T(8,128)(2,1)S(1)} collective-permute-done((bf16[2,512,128]{2,1,0:T(8,128)(2,1)}, bf16[2,512,128]{2,1,0:T(8,128)(2,1)S(1)}, u32[]{:S(2)}, u32[]{:S(2)}) %collective-permute-start.12) | collective-permute-done | bytes 262176 | tf_op jit(solution)/shard_map/ppermute | solution.py:369
  51.5 3.8 %collective-permute-done.13.refs_10_ = bf16[2,512,128]{2,1,0:T(8,128)(2,1)S(1)} collective-permute-done((bf16[2,512,128]{2,1,0:T(8,128)(2,1)}, bf16[2,512,128]{2,1,0:T(8,128)(2,1)S(1)}, u32[]{:S(2)}, u32[]{:S(2)}) %collective-permute-start.13) | collective-permute-done | bytes 262176 | tf_op jit(solution)/shard_map/ppermute | solution.py:369
  63.6 13.4 %shard_map.69 = bf16[16,136,128]{2,1,0:T(8,128)(2,1)S(1)} custom-call(s32[1]{0:T(128)} %get-tuple-element.45.refs_0_, s32[2]{0:T(128)S(1)} %pad_add_fusion.refs_1_, bf16[16,288,128]{2,1,0:T(8,128)(2,1)S(1)} %all-to-all-done.refs_2_, bf16[2,512,128]{2,1,0:T(8,128)(2,1)S(1)} %copy-done.6, bf16[2,512,128]{2,1,0:T(8,128)(2,1)S(1)} %copy-done.8, ...), custom_call_target="tpu_custom_call" | custom-call | flops 4294967296 | bytes 3145728 | tf_op jit(solution)/shard_map/pallas_call | solution.py:221
  77.8 3.8 %all-to-all-start.2 = ((bf16[16,136,128]{2,1,0:T(8,128)(2,1)}), bf16[16,136,128]{2,1,0:T(8,128)(2,1)S(1)}, u32[]{:S(2)}, u32[]{:S(2)}) async-start(bf16[16,136,128]{2,1,0:T(8,128)(2,1)} %copy-done.4), calls=%async_computation.2 | async-start | bytes 1114112 | tf_op jit(solution)/shard_map/all_to_all | solution.py:384
  81.6 1.6 %copy-done.1 = bf16[2,512,8,128]{3,2,1,0:T(8,128)(2,1)S(1)} copy-done((bf16[2,512,8,128]{3,2,1,0:T(8,128)(2,1)S(1)}, bf16[2,512,8,128]{3,2,1,0:T(8,128)(2,1)}, u32[]{:S(2)}) %copy-start.1) | copy-done | bytes 2097176
  84.5 1.5 %collective-permute-start.3 = (bf16[2,512,128]{2,1,0:T(8,128)(2,1)S(1)}, bf16[2,512,128]{2,1,0:T(8,128)(2,1)S(1)}, u32[]{:S(2)}, u32[]{:S(2)}) collective-permute-start(bf16[2,512,128]{2,1,0:T(8,128)(2,1)S(1)} %get-tuple-element.27), channel_id=1, source_target_pairs={{0,2},{1,3},{2,0},{3,1},{4,6},{5,7},{6,4},{7,5},{8,10},{9,11},{10,... | collective-permute-start | bytes 786440 | tf_op jit(solution)/shard_map/ppermute | solution.py:369
  86.1 1.6 %collective-permute-start.5 = (bf16[2,512,128]{2,1,0:T(8,128)(2,1)S(1)}, bf16[2,512,128]{2,1,0:T(8,128)(2,1)S(1)}, u32[]{:S(2)}, u32[]{:S(2)}) collective-permute-start(bf16[2,512,128]{2,1,0:T(8,128)(2,1)S(1)} %get-tuple-element.29), channel_id=1, source_target_pairs={{0,4},{1,5},{2,6},{3,7},{4,0},{5,1},{6,2},{7,3},{8,12},{9,13},{10,... | collective-permute-start | bytes 786440 | tf_op jit(solution)/shard_map/ppermute | solution.py:369
  88.0 2.4 %collective-permute-start = (bf16[2,512,128]{2,1,0:T(8,128)(2,1)S(1)}, bf16[2,512,128]{2,1,0:T(8,128)(2,1)S(1)}, u32[]{:S(2)}, u32[]{:S(2)}) collective-permute-start(bf16[2,512,128]{2,1,0:T(8,128)(2,1)S(1)} %get-tuple-element.23), channel_id=1, source_target_pairs={{0,6},{1,7},{2,4},{3,5},{4,2},{5,3},{6,0},{7,1},{8,14},{9,15},{10,... | collective-permute-start | bytes 786440 | tf_op jit(solution)/shard_map/ppermute | solution.py:369
  90.4 6.1 %collective-permute-done.3.refs_5_ = bf16[2,512,128]{2,1,0:T(8,128)(2,1)S(1)} collective-permute-done((bf16[2,512,128]{2,1,0:T(8,128)(2,1)S(1)}, bf16[2,512,128]{2,1,0:T(8,128)(2,1)S(1)}, u32[]{:S(2)}, u32[]{:S(2)}) %collective-permute-start.3) | collective-permute-done | bytes 262176 | tf_op jit(solution)/shard_map/ppermute | solution.py:369
  97.9 3.4 %collective-permute-done.4.refs_6_ = bf16[2,512,128]{2,1,0:T(8,128)(2,1)S(1)} collective-permute-done((bf16[2,512,128]{2,1,0:T(8,128)(2,1)S(1)}, bf16[2,512,128]{2,1,0:T(8,128)(2,1)S(1)}, u32[]{:S(2)}, u32[]{:S(2)}) %collective-permute-start.4) | collective-permute-done | bytes 262176 | tf_op jit(solution)/shard_map/ppermute | solution.py:369
  101.3 2.6 %collective-permute-done.6.refs_8_ = bf16[2,512,128]{2,1,0:T(8,128)(2,1)S(1)} collective-permute-done((bf16[2,512,128]{2,1,0:T(8,128)(2,1)S(1)}, bf16[2,512,128]{2,1,0:T(8,128)(2,1)S(1)}, u32[]{:S(2)}, u32[]{:S(2)}) %collective-permute-start.6) | collective-permute-done | bytes 262176 | tf_op jit(solution)/shard_map/ppermute | solution.py:369
  104.0 10.5 %shard_map.66 = (f32[144,2048]{1,0:T(8,128)S(1)}, f32[8,2048]{1,0:T(8,128)S(1)}) custom-call(s32[1]{0:T(128)} %get-tuple-element.46.refs_0_, s32[2]{0:T(128)S(1)} %pad_add_fusion.refs_1_, bf16[16,288,128]{2,1,0:T(8,128)(2,1)S(1)} %copy-done.3, bf16[2,512,128]{2,1,0:T(8,128)(2,1)S(1)} %get-tuple-element.25.refs_3_, ...), custom_call_target="tpu_custom_call" | custom-call | flops 3221225472 | bytes 2621440 | tf_op jit(solution)/shard_map/pallas_call | solution.py:221
  114.5 2.0 %collective-permute-done.1.refs_4_ = bf16[2,512,128]{2,1,0:T(8,128)(2,1)S(1)} collective-permute-done((bf16[2,512,128]{2,1,0:T(8,128)(2,1)S(1)}, bf16[2,512,128]{2,1,0:T(8,128)(2,1)S(1)}, u32[]{:S(2)}, u32[]{:S(2)}) %collective-permute-start.1) | collective-permute-done | bytes 262176 | tf_op jit(solution)/shard_map/ppermute | solution.py:369
  116.5 3.2 %shard_map.67 = bf16[16,136,128]{2,1,0:T(8,128)(2,1)} custom-call(s32[1]{0:T(128)} %get-tuple-element.46.refs_0_, s32[2]{0:T(128)S(1)} %pad_add_fusion.refs_1_, bf16[16,288,128]{2,1,0:T(8,128)(2,1)S(1)} %copy-done.3, bf16[2,512,128]{2,1,0:T(8,128)(2,1)S(1)} %collective-permute-done.refs_3_, bf16[2,512,128]{2,1,0:T(8,128)(2,1)S(1)} %collective-permute-done.1.refs_4_, ...), custom_call_target="tpu_custom_call" | custom-call | flops 1073741824 | bytes 1572864 | tf_op jit(solution)/shard_map/pallas_call | solution.py:221
  119.8 5.3 %all-to-all-start.1 = ((bf16[16,136,128]{2,1,0:T(8,128)(2,1)}), bf16[16,136,128]{2,1,0:T(8,128)(2,1)S(1)}, u32[]{:S(2)}, u32[]{:S(2)}) async-start(bf16[16,136,128]{2,1,0:T(8,128)(2,1)} %shard_map.67), calls=%async_computation.1 | async-start | bytes 1114112 | tf_op jit(solution)/shard_map/all_to_all | solution.py:384
  126.4 13.5 %all-to-all-done.1 = bf16[16,136,128]{2,1,0:T(8,128)(2,1)S(1)} async-done(((bf16[16,136,128]{2,1,0:T(8,128)(2,1)}), bf16[16,136,128]{2,1,0:T(8,128)(2,1)S(1)}, u32[]{:S(2)}, u32[]{:S(2)}) %all-to-all-start.1) | async-done | bytes 557088 | tf_op jit(solution)/shard_map/all_to_all | solution.py:384
  (69 shorter events, 23.9 us)
Async XLA Ops:
  3.0 32.9 %all-to-all-start = ((bf16[16,288,128]{2,1,0:T(8,128)(2,1)}), bf16[16,288,128]{2,1,0:T(8,128)(2,1)S(1)}, u32[]{:S(2)}, u32[]{:S(2)}) async-start(bf16[16,288,128]{2,1,0:T(8,128)(2,1)} %shard_map.64), calls=%async_computation | async-start | bytes 2359296 | tf_op jit(solution)/shard_map/all_to_all | solution.py:354
  10.4 7.3 %copy-start.21 = (s32[2]{0:T(128)S(1)}, s32[2]{0:T(128)}, u32[]{:S(2)}) copy-start(s32[2]{0:T(128)} %param.11) | copy-start | bytes 28
  13.7 4.6 %collective-permute-start.7 = (bf16[2,512,128]{2,1,0:T(8,128)(2,1)}, bf16[2,512,128]{2,1,0:T(8,128)(2,1)S(1)}, u32[]{:S(2)}, u32[]{:S(2)}) collective-permute-start(bf16[2,512,128]{2,1,0:T(8,128)(2,1)} %get-tuple-element.34), channel_id=1, source_target_pairs={{0,1},{1,0},{2,3},{3,2},{4,5},{5,4},{6,7},{7,6},{8,9},{9,8},{10,11... | collective-permute-start | bytes 786440 | tf_op jit(solution)/shard_map/ppermute | solution.py:369
  14.1 15.6 %collective-permute-start.8 = (bf16[2,512,128]{2,1,0:T(8,128)(2,1)}, bf16[2,512,128]{2,1,0:T(8,128)(2,1)S(1)}, u32[]{:S(2)}, u32[]{:S(2)}) collective-permute-start(bf16[2,512,128]{2,1,0:T(8,128)(2,1)} %get-tuple-element.35), channel_id=1, source_target_pairs={{0,2},{1,3},{2,0},{3,1},{4,6},{5,7},{6,4},{7,5},{8,10},{9,11},{10,... | collective-permute-start | bytes 786440 | tf_op jit(solution)/shard_map/ppermute | solution.py:369
  15.8 21.0 %collective-permute-start.9 = (bf16[2,512,128]{2,1,0:T(8,128)(2,1)}, bf16[2,512,128]{2,1,0:T(8,128)(2,1)S(1)}, u32[]{:S(2)}, u32[]{:S(2)}) collective-permute-start(bf16[2,512,128]{2,1,0:T(8,128)(2,1)} %get-tuple-element.36), channel_id=1, source_target_pairs={{0,3},{1,2},{2,1},{3,0},{4,7},{5,6},{6,5},{7,4},{8,11},{9,10},{10,... | collective-permute-start | bytes 786440 | tf_op jit(solution)/shard_map/ppermute | solution.py:369
  15.8 22.8 %collective-permute-start.10 = (bf16[2,512,128]{2,1,0:T(8,128)(2,1)}, bf16[2,512,128]{2,1,0:T(8,128)(2,1)S(1)}, u32[]{:S(2)}, u32[]{:S(2)}) collective-permute-start(bf16[2,512,128]{2,1,0:T(8,128)(2,1)} %get-tuple-element.37), channel_id=1, source_target_pairs={{0,4},{1,5},{2,6},{3,7},{4,0},{5,1},{6,2},{7,3},{8,12},{9,13},{10,... | collective-permute-start | bytes 786440 | tf_op jit(solution)/shard_map/ppermute | solution.py:369
  17.5 25.6 %collective-permute-start.11 = (bf16[2,512,128]{2,1,0:T(8,128)(2,1)}, bf16[2,512,128]{2,1,0:T(8,128)(2,1)S(1)}, u32[]{:S(2)}, u32[]{:S(2)}) collective-permute-start(bf16[2,512,128]{2,1,0:T(8,128)(2,1)} %get-tuple-element.38), channel_id=1, source_target_pairs={{0,5},{1,4},{2,7},{3,6},{4,1},{5,0},{6,3},{7,2},{8,13},{9,12},{10,... | collective-permute-start | bytes 786440 | tf_op jit(solution)/shard_map/ppermute | solution.py:369
  18.3 37.7 %copy-start.7 = (bf16[2,512,128]{2,1,0:T(8,128)(2,1)}, bf16[2,512,128]{2,1,0:T(8,128)(2,1)S(1)}, u32[]{:S(2)}) copy-start(bf16[2,512,128]{2,1,0:T(8,128)(2,1)S(1)} %collective-permute-done.7.refs_4_) | copy-start | bytes 786436
  18.3 32.5 %collective-permute-start.12 = (bf16[2,512,128]{2,1,0:T(8,128)(2,1)}, bf16[2,512,128]{2,1,0:T(8,128)(2,1)S(1)}, u32[]{:S(2)}, u32[]{:S(2)}) collective-permute-start(bf16[2,512,128]{2,1,0:T(8,128)(2,1)} %get-tuple-element.39), channel_id=1, source_target_pairs={{0,6},{1,7},{2,4},{3,5},{4,2},{5,3},{6,0},{7,1},{8,14},{9,15},{10,... | collective-permute-start | bytes 786440 | tf_op jit(solution)/shard_map/ppermute | solution.py:369
  29.7 26.2 %copy-start.9 = (bf16[2,512,128]{2,1,0:T(8,128)(2,1)}, bf16[2,512,128]{2,1,0:T(8,128)(2,1)S(1)}, u32[]{:S(2)}) copy-start(bf16[2,512,128]{2,1,0:T(8,128)(2,1)S(1)} %collective-permute-done.8.refs_5_) | copy-start | bytes 786436
  29.7 25.5 %collective-permute-start.13 = (bf16[2,512,128]{2,1,0:T(8,128)(2,1)}, bf16[2,512,128]{2,1,0:T(8,128)(2,1)S(1)}, u32[]{:S(2)}, u32[]{:S(2)}) collective-permute-start(bf16[2,512,128]{2,1,0:T(8,128)(2,1)} %get-tuple-element.40), channel_id=1, source_target_pairs={{0,7},{1,6},{2,5},{3,4},{4,3},{5,2},{6,1},{7,0},{8,15},{9,14},{10,... | collective-permute-start | bytes 786440 | tf_op jit(solution)/shard_map/ppermute | solution.py:369
  35.9 41.1 %copy-start.2 = (bf16[16,288,128]{2,1,0:T(8,128)(2,1)}, bf16[16,288,128]{2,1,0:T(8,128)(2,1)S(1)}, u32[]{:S(2)}) copy-start(bf16[16,288,128]{2,1,0:T(8,128)(2,1)S(1)} %all-to-all-done.refs_2_) | copy-start | bytes 3538948
  63.6 18.0 %copy-start = (bf16[2,512,8,128]{3,2,1,0:T(8,128)(2,1)S(1)}, bf16[2,512,8,128]{3,2,1,0:T(8,128)(2,1)}, u32[]{:S(2)}) copy-start(bf16[2,512,8,128]{3,2,1,0:T(8,128)(2,1)} %k_hbm.3) | copy-start | bytes 6291460
  77.8 42.0 %all-to-all-start.2 = ((bf16[16,136,128]{2,1,0:T(8,128)(2,1)}), bf16[16,136,128]{2,1,0:T(8,128)(2,1)S(1)}, u32[]{:S(2)}, u32[]{:S(2)}) async-start(bf16[16,136,128]{2,1,0:T(8,128)(2,1)} %copy-done.4), calls=%async_computation.2 | async-start | bytes 1114112 | tf_op jit(solution)/shard_map/all_to_all | solution.py:384
  81.5 1.6 %copy-start.1 = (bf16[2,512,8,128]{3,2,1,0:T(8,128)(2,1)S(1)}, bf16[2,512,8,128]{3,2,1,0:T(8,128)(2,1)}, u32[]{:S(2)}) copy-start(bf16[2,512,8,128]{3,2,1,0:T(8,128)(2,1)} %v_hbm.3) | copy-start | bytes 6291460
  83.1 20.8 %copy-start.3 = (bf16[16,288,128]{2,1,0:T(8,128)(2,1)S(1)}, bf16[16,288,128]{2,1,0:T(8,128)(2,1)}, u32[]{:S(2)}) copy-start(bf16[16,288,128]{2,1,0:T(8,128)(2,1)} %copy-done.2) | copy-start | bytes 3538948
  84.2 3.9 %collective-permute-start.2 = (bf16[2,512,128]{2,1,0:T(8,128)(2,1)S(1)}, bf16[2,512,128]{2,1,0:T(8,128)(2,1)S(1)}, u32[]{:S(2)}, u32[]{:S(2)}) collective-permute-start(bf16[2,512,128]{2,1,0:T(8,128)(2,1)S(1)} %get-tuple-element.26), channel_id=1, source_target_pairs={{0,1},{1,0},{2,3},{3,2},{4,5},{5,4},{6,7},{7,6},{8,9},{9,8},{10,11... | collective-permute-start | bytes 786440 | tf_op jit(solution)/shard_map/ppermute | solution.py:369
  84.5 12.0 %collective-permute-start.3 = (bf16[2,512,128]{2,1,0:T(8,128)(2,1)S(1)}, bf16[2,512,128]{2,1,0:T(8,128)(2,1)S(1)}, u32[]{:S(2)}, u32[]{:S(2)}) collective-permute-start(bf16[2,512,128]{2,1,0:T(8,128)(2,1)S(1)} %get-tuple-element.27), channel_id=1, source_target_pairs={{0,2},{1,3},{2,0},{3,1},{4,6},{5,7},{6,4},{7,5},{8,10},{9,11},{10,... | collective-permute-start | bytes 786440 | tf_op jit(solution)/shard_map/ppermute | solution.py:369
  86.0 15.3 %collective-permute-start.4 = (bf16[2,512,128]{2,1,0:T(8,128)(2,1)S(1)}, bf16[2,512,128]{2,1,0:T(8,128)(2,1)S(1)}, u32[]{:S(2)}, u32[]{:S(2)}) collective-permute-start(bf16[2,512,128]{2,1,0:T(8,128)(2,1)S(1)} %get-tuple-element.28), channel_id=1, source_target_pairs={{0,3},{1,2},{2,1},{3,0},{4,7},{5,6},{6,5},{7,4},{8,11},{9,10},{10,... | collective-permute-start | bytes 786440 | tf_op jit(solution)/shard_map/ppermute | solution.py:369
  86.1 15.2 %collective-permute-start.5 = (bf16[2,512,128]{2,1,0:T(8,128)(2,1)S(1)}, bf16[2,512,128]{2,1,0:T(8,128)(2,1)S(1)}, u32[]{:S(2)}, u32[]{:S(2)}) collective-permute-start(bf16[2,512,128]{2,1,0:T(8,128)(2,1)S(1)} %get-tuple-element.29), channel_id=1, source_target_pairs={{0,4},{1,5},{2,6},{3,7},{4,0},{5,1},{6,2},{7,3},{8,12},{9,13},{10,... | collective-permute-start | bytes 786440 | tf_op jit(solution)/shard_map/ppermute | solution.py:369
  87.7 16.2 %collective-permute-start.6 = (bf16[2,512,128]{2,1,0:T(8,128)(2,1)S(1)}, bf16[2,512,128]{2,1,0:T(8,128)(2,1)S(1)}, u32[]{:S(2)}, u32[]{:S(2)}) collective-permute-start(bf16[2,512,128]{2,1,0:T(8,128)(2,1)S(1)} %get-tuple-element.30), channel_id=1, source_target_pairs={{0,5},{1,4},{2,7},{3,6},{4,1},{5,0},{6,3},{7,2},{8,13},{9,12},{10,... | collective-permute-start | bytes 786440 | tf_op jit(solution)/shard_map/ppermute | solution.py:369
  88.0 26.5 %collective-permute-start = (bf16[2,512,128]{2,1,0:T(8,128)(2,1)S(1)}, bf16[2,512,128]{2,1,0:T(8,128)(2,1)S(1)}, u32[]{:S(2)}, u32[]{:S(2)}) collective-permute-start(bf16[2,512,128]{2,1,0:T(8,128)(2,1)S(1)} %get-tuple-element.23), channel_id=1, source_target_pairs={{0,6},{1,7},{2,4},{3,5},{4,2},{5,3},{6,0},{7,1},{8,14},{9,15},{10,... | collective-permute-start | bytes 786440 | tf_op jit(solution)/shard_map/ppermute | solution.py:369
  96.5 20.0 %collective-permute-start.1 = (bf16[2,512,128]{2,1,0:T(8,128)(2,1)S(1)}, bf16[2,512,128]{2,1,0:T(8,128)(2,1)S(1)}, u32[]{:S(2)}, u32[]{:S(2)}) collective-permute-start(bf16[2,512,128]{2,1,0:T(8,128)(2,1)S(1)} %get-tuple-element.24), channel_id=1, source_target_pairs={{0,7},{1,6},{2,5},{3,4},{4,3},{5,2},{6,1},{7,0},{8,15},{9,14},{10,... | collective-permute-start | bytes 786440 | tf_op jit(solution)/shard_map/ppermute | solution.py:369
  119.8 20.1 %all-to-all-start.1 = ((bf16[16,136,128]{2,1,0:T(8,128)(2,1)}), bf16[16,136,128]{2,1,0:T(8,128)(2,1)S(1)}, u32[]{:S(2)}, u32[]{:S(2)}) async-start(bf16[16,136,128]{2,1,0:T(8,128)(2,1)} %shard_map.67), calls=%async_computation.1 | async-start | bytes 1114112 | tf_op jit(solution)/shard_map/all_to_all | solution.py:384
  (15 other events, 13.0 us)
